TPU v7x, 32 devices: a whole 2x2x4 slice. The times are simulated.
32 devices in a mesh: dp: 8 (over z, y), seq: 4 (over x, core).
Axes of the slice: x: 2, y: 2, z: 4, core: 2. Of those that a mesh axis runs over, the one named last changes fastest.
Arguments:
- hidden: bfloat16 [16, 2048, 768], P('dp', 'seq'), may hold values from -6 to 6
- lengths: int32 [16], P('dp'), may hold values from 512 to 2048
- norm_gain: float32 [768], P(('dp', 'seq')), may hold values from 0.5 to 1.5
- in_weight: float32 [768, 3352], P(('dp', 'seq')), may hold values from -0.21875 to 0.21875
- conv_weight: float32 [4, 1792], P(None, ('dp', 'seq')), may hold values from -3 to 3
- conv_bias: float32 [1792], P(('dp', 'seq')), may hold values from -2.5 to 2.5
- step_bias: float32 [24], replicated, may hold values from -10 to -5
- decay_log: float32 [24], replicated, may hold values from 0 to 1
- skip_gain: float32 [24], replicated, may hold values from 0.5 to 1.5
- gate_gain: float32 [1536], P(('dp', 'seq')), may hold values from 0.5 to 1.5
- out_weight: float32 [1536, 768], P(('dp', 'seq')), may hold values from -0.15625 to 0.15625
- cotangent: bfloat16 [16, 2048, 768], P('dp', 'seq'), may hold values from -6 to 6
Outputs:
- output: bfloat16 [16, 2048, 768], P('dp', 'seq')
- grad_hidden: bfloat16 [16, 2048, 768], P('dp', 'seq')
- grad_norm_gain: float32 [768], P(('dp', 'seq'))
- grad_in_weight: float32 [768, 3352], P(('dp', 'seq'))
- grad_conv_weight: float32 [4, 1792], P(None, ('dp', 'seq'))
- grad_conv_bias: float32 [1792], P(('dp', 'seq'))
- grad_step_bias: float32 [24], replicated
- grad_decay_log: float32 [24], replicated
- grad_skip_gain: float32 [24], replicated
- grad_gate_gain: float32 [1536], P(('dp', 'seq'))
- grad_out_weight: float32 [1536, 768], P(('dp', 'seq'))
All inputs are finite; a program needn't handle non-finite values.
Results may differ from a plain program's by a relative error of at most 0.00435.
The roundings to bfloat16 on the way count: a program that leaves them out, or rounds other values in their place, can miss the bound.
Values may be sent and summed in bfloat16 or wider, within the bound.
No kernel may reach another device: no remote copies, remote signals or barrier semaphores. Data moves between devices by JAX's collectives and lax.ppermute only.
A program may use at most 192 MiB of HBM per device.

v0:
```python
import jax
import jax.numpy as jnp
from jax import lax
from jax.sharding import PartitionSpec as P

H = 24
P_SIZE = 64
N = 128
KW = 4
Q = 256
DI = 1536
CD = 1792


epsilon = 1e-05


def from_behind(block, axis, distance):
    devices = range(lax.axis_size(axis))
    route = [(i - distance, i) for i in devices if i - distance in devices]
    return lax.ppermute(block, axis, route)


def rms_scale(values):
    return lax.rsqrt(jnp.mean(values * values, axis=-1, keepdims=True) + epsilon)


def decay_matrix(cum_group):
    width_q = cum_group.shape[-1]
    lower = jnp.arange(width_q)[:, None] >= jnp.arange(width_q)[None, :]
    gap = jnp.where(lower[None], cum_group[:, :, None] - cum_group[:, None, :], 0.0)
    return jnp.where(lower[None], jnp.exp(gap), 0.0)


def intra_forward(group_item):
    x_group, b_group, c_group, step_group, cum_group = group_item
    scores = jnp.einsum("qn,rn->qr", c_group, b_group, preferred_element_type=jnp.float32)
    mixing = (scores[None] * decay_matrix(cum_group) * step_group[:, None, :]).astype(jnp.bfloat16)
    return jnp.einsum("hqr,rhp->qhp", mixing, x_group, preferred_element_type=jnp.float32)


def intra_backward(group_item):
    x_group, b_group, c_group, step_group, cum_group, grad_group = group_item
    scores = jnp.einsum("qn,rn->qr", c_group, b_group, preferred_element_type=jnp.float32)
    spread = decay_matrix(cum_group)
    rate_weight = spread * step_group[:, None, :]
    mixing = (scores[None] * rate_weight).astype(jnp.bfloat16)
    grad_mixing = jnp.einsum(
        "qhp,rhp->hqr", grad_group, x_group, preferred_element_type=jnp.float32
    )
    grad_x = jnp.einsum("hqr,qhp->rhp", mixing, grad_group, preferred_element_type=jnp.float32)
    grad_scores = jnp.sum(grad_mixing * rate_weight, axis=0).astype(jnp.bfloat16)
    grad_c = jnp.einsum("qr,rn->qn", grad_scores, b_group, preferred_element_type=jnp.float32)
    grad_b = jnp.einsum("qr,qn->rn", grad_scores, c_group, preferred_element_type=jnp.float32)
    through = grad_mixing * scores[None] * spread
    cum_flow = through * step_group[:, None, :]
    grad_cum = jnp.sum(cum_flow, axis=2) - jnp.sum(cum_flow, axis=1)
    return (grad_x, grad_b, grad_c, jnp.sum(through, axis=1), grad_cum)


def per_device(
    hidden,
    lengths,
    norm_gain,
    in_weight,
    conv_weight,
    conv_bias,
    step_bias,
    decay_log,
    skip_gain,
    gate_gain,
    out_weight,
    cotangent,
):
    seq_count, piece_len, model_width = hidden.shape
    group_count = piece_len // Q
    block_count = seq_count * group_count
    token_rows = seq_count * piece_len
    halo_width = KW - 1
    shards = (
        norm_gain.astype(jnp.bfloat16),
        in_weight.astype(jnp.bfloat16),
        conv_weight.astype(jnp.bfloat16),
        conv_bias.astype(jnp.bfloat16),
        gate_gain.astype(jnp.bfloat16),
        out_weight.astype(jnp.bfloat16),
    )
    gathered = (
        lax.all_gather(shards[0], ("dp", "seq"), axis=0, tiled=True),
        lax.all_gather(shards[1], ("dp", "seq"), axis=0, tiled=True),
        lax.all_gather(shards[2], ("dp", "seq"), axis=1, tiled=True),
        lax.all_gather(shards[3], ("dp", "seq"), axis=0, tiled=True),
        lax.all_gather(shards[4], ("dp", "seq"), axis=0, tiled=True),
        lax.all_gather(shards[5], ("dp", "seq"), axis=0, tiled=True),
    )
    gain_in, in_full, kernel_full, bias_full, gain_gate, out_full = gathered
    positions = lax.axis_index("seq") * piece_len + jnp.arange(piece_len, dtype=jnp.int32)
    valid_mask = (positions[None, :] < lengths[:, None]).astype(jnp.float32)
    x_float = hidden.astype(jnp.float32)
    scale_in = rms_scale(x_float)
    normed = (
        (x_float * scale_in * gain_in.astype(jnp.float32))
        .astype(jnp.bfloat16)
        .reshape(token_rows, model_width)
    )
    projected = jnp.dot(normed, in_full, preferred_element_type=jnp.float32).reshape(
        seq_count, piece_len, -1
    )
    gate_z = projected[..., :DI]
    conv_in = projected[..., DI : DI + CD].astype(jnp.bfloat16)
    dt_raw = projected[..., DI + CD :]
    rim_rows = from_behind(conv_in[:, piece_len - halo_width :, :], "seq", 1)
    extended = jnp.concatenate([rim_rows, conv_in], axis=1)
    kernel = kernel_full.astype(jnp.float32)
    pre_act = bias_full.astype(jnp.float32) + sum(
        (
            kernel[offset] * extended[:, offset : offset + piece_len].astype(jnp.float32)
            for offset in range(KW)
        )
    )
    conv_out = jax.nn.silu(pre_act)
    x_heads = conv_out[..., :DI].astype(jnp.bfloat16).reshape(block_count, Q, H, P_SIZE)
    b_rows = conv_out[..., DI : DI + N].astype(jnp.bfloat16).reshape(block_count, Q, N)
    c_rows = conv_out[..., DI + N :].astype(jnp.bfloat16).reshape(block_count, Q, N)
    step_size = jax.nn.softplus(dt_raw + step_bias)
    decay_rate = jnp.exp(decay_log)
    step_blocks = step_size.reshape(block_count, Q, H).transpose(0, 2, 1)
    cum_decay = jnp.cumsum(-step_blocks * decay_rate[None, :, None], axis=2)
    intra_out = lax.map(intra_forward, (x_heads, b_rows, c_rows, step_blocks, cum_decay))
    tail_weight = jnp.exp(cum_decay[:, :, -1:] - cum_decay) * step_blocks
    b_scaled = (b_rows[:, None].astype(jnp.float32) * tail_weight[..., None]).astype(jnp.bfloat16)
    local_state = jnp.einsum(
        "bhqn,bqhp->bhnp", b_scaled, x_heads, preferred_element_type=jnp.float32
    )
    block_decay = jnp.exp(cum_decay[:, :, -1])
    group_decay = block_decay.reshape(seq_count, group_count, H)
    local_parts = local_state.reshape(seq_count, group_count, H, N, P_SIZE)
    running = jnp.zeros((seq_count, H, N, P_SIZE), jnp.float32)
    carried = jnp.ones((seq_count, H), jnp.float32)
    start_list = []
    prefix_list = []
    for block_index in range(group_count):
        start_list.append(running)
        prefix_list.append(carried)
        running = group_decay[:, block_index, :, None, None] * running + local_parts[:, block_index]
        carried = carried * group_decay[:, block_index]
    incoming = jnp.zeros_like(running)
    for rounds in range(lax.axis_size("seq") - 1):
        incoming = from_behind(carried[:, :, None, None] * incoming + running, "seq", 1)
    group_starts = jnp.stack(
        [
            start_list[block_index] + prefix_list[block_index][:, :, None, None] * incoming
            for block_index in range(group_count)
        ],
        axis=1,
    ).reshape(block_count, H, N, P_SIZE)
    growth = jnp.exp(cum_decay)
    c_scaled = c_rows[:, None].astype(jnp.float32) * growth[..., None]
    c_low = c_scaled.astype(jnp.bfloat16)
    starts_low = group_starts.astype(jnp.bfloat16)
    inter_out = jnp.einsum("bhqn,bhnp->bqhp", c_low, starts_low, preferred_element_type=jnp.float32)
    ssm_out = (
        intra_out + inter_out + skip_gain[None, None, :, None] * x_heads.astype(jnp.float32)
    ).reshape(seq_count, piece_len, DI)
    gate_sig = jax.nn.sigmoid(gate_z)
    gated_out = ssm_out * gate_z * gate_sig
    scale_gate = rms_scale(gated_out)
    gated_norm = (
        (gated_out * scale_gate * gain_gate.astype(jnp.float32))
        .astype(jnp.bfloat16)
        .reshape(token_rows, DI)
    )
    branch = jnp.dot(gated_norm, out_full, preferred_element_type=jnp.float32).reshape(
        seq_count, piece_len, model_width
    )
    output = (x_float + valid_mask[..., None] * branch).astype(jnp.bfloat16)
    back_shards = (shards[0], shards[1], shards[2], shards[4], shards[5])
    back_weights = (
        lax.all_gather(back_shards[0], ("dp", "seq"), axis=0, tiled=True),
        lax.all_gather(back_shards[1], ("dp", "seq"), axis=0, tiled=True),
        lax.all_gather(back_shards[2], ("dp", "seq"), axis=1, tiled=True),
        lax.all_gather(back_shards[3], ("dp", "seq"), axis=0, tiled=True),
        lax.all_gather(back_shards[4], ("dp", "seq"), axis=0, tiled=True),
    )
    gain_in_back, in_back, kernel_back, gain_gate_back, out_back = back_weights
    d_branch = (
        (cotangent.astype(jnp.float32) * valid_mask[..., None])
        .astype(jnp.bfloat16)
        .reshape(token_rows, model_width)
    )
    grad_out = jnp.einsum("tk,td->kd", gated_norm, d_branch, preferred_element_type=jnp.float32)
    grad_norm_out = jnp.einsum(
        "td,kd->tk", d_branch, out_back, preferred_element_type=jnp.float32
    ).reshape(seq_count, piece_len, DI)
    grad_gate_gain = jnp.sum(grad_norm_out * gated_out * scale_gate, axis=(0, 1))
    scaled_back = grad_norm_out * gain_gate_back.astype(jnp.float32)
    grad_gated = scale_gate * scaled_back - gated_out * (
        scale_gate * scale_gate * scale_gate
    ) * jnp.mean(scaled_back * gated_out, axis=-1, keepdims=True)
    grad_ssm = (grad_gated * gate_z * gate_sig).astype(jnp.bfloat16)
    grad_gate_z = grad_gated * ssm_out * gate_sig * (1.0 + gate_z * (1.0 - gate_sig))
    grad_blocks = grad_ssm.reshape(block_count, Q, H, P_SIZE)
    grad_skip = jnp.einsum("bqhp,bqhp->h", grad_blocks, x_heads, preferred_element_type=jnp.float32)
    intra_x, intra_b, intra_c, intra_step, intra_cum = lax.map(
        intra_backward, (x_heads, b_rows, c_rows, step_blocks, cum_decay, grad_blocks)
    )
    grad_in_y = jnp.einsum(
        "bhqn,bqhp->bhnp", c_low, grad_blocks, preferred_element_type=jnp.float32
    ).reshape(seq_count, group_count, H, N, P_SIZE)
    back_running = jnp.zeros((seq_count, H, N, P_SIZE), jnp.float32)
    for block_index in reversed(range(group_count)):
        back_running = (
            group_decay[:, block_index, :, None, None] * back_running + grad_in_y[:, block_index]
        )
    arriving = jnp.zeros_like(back_running)
    for rounds in range(lax.axis_size("seq") - 1):
        arriving = from_behind(carried[:, :, None, None] * arriving + back_running, "seq", -1)
    end_list = [None] * group_count
    following = arriving
    for block_index in reversed(range(group_count)):
        end_list[block_index] = following
        following = (
            group_decay[:, block_index, :, None, None] * following + grad_in_y[:, block_index]
        )
    grad_end = jnp.stack(end_list, axis=1).reshape(block_count, H, N, P_SIZE)
    grad_last = jnp.sum(grad_end * group_starts, axis=(2, 3)) * block_decay
    grad_local = grad_end.astype(jnp.bfloat16)
    grad_b_scaled = jnp.einsum(
        "bqhp,bhnp->bhqn", x_heads, grad_local, preferred_element_type=jnp.float32
    )
    grad_x_heads = (
        skip_gain[None, None, :, None] * grad_blocks.astype(jnp.float32)
        + intra_x
        + jnp.einsum("bhqn,bhnp->bqhp", b_scaled, grad_local, preferred_element_type=jnp.float32)
    )
    grad_b = intra_b + jnp.einsum("bhqn,bhq->bqn", grad_b_scaled, tail_weight)
    grad_tail = jnp.einsum("bhqn,bqn->bhq", grad_b_scaled, b_rows.astype(jnp.float32))
    tail_flow = grad_tail * tail_weight
    grad_step = intra_step + grad_tail * jnp.exp(cum_decay[:, :, -1:] - cum_decay)
    grad_c_scaled = jnp.einsum(
        "bqhp,bhnp->bhqn", grad_blocks, starts_low, preferred_element_type=jnp.float32
    )
    grad_c = intra_c + jnp.einsum("bhqn,bhq->bqn", grad_c_scaled, growth)
    grad_cum = intra_cum - tail_flow + jnp.einsum("bhqn,bhqn->bhq", grad_c_scaled, c_scaled)
    grad_cum = grad_cum.at[:, :, -1].add(grad_last + jnp.sum(tail_flow, axis=2))
    grad_log = lax.cumsum(grad_cum, axis=2, reverse=True)
    grad_step = grad_step - grad_log * decay_rate[None, :, None]
    grad_decay = -jnp.sum(grad_log * step_blocks, axis=(0, 2)) * decay_rate
    grad_step_tokens = grad_step.transpose(0, 2, 1).reshape(seq_count, piece_len, H)
    grad_dt_raw = grad_step_tokens * jax.nn.sigmoid(dt_raw + step_bias)
    grad_step_bias = jnp.sum(grad_dt_raw, axis=(0, 1))
    grad_conv_out = jnp.concatenate(
        [
            grad_x_heads.reshape(seq_count, piece_len, DI),
            grad_b.reshape(seq_count, piece_len, N),
            grad_c.reshape(seq_count, piece_len, N),
        ],
        axis=-1,
    )
    pre_sig = jax.nn.sigmoid(pre_act)
    grad_pre = grad_conv_out * pre_sig * (1.0 + pre_act * (1.0 - pre_sig))
    grad_conv_bias = jnp.sum(grad_pre, axis=(0, 1))
    grad_kernel = jnp.stack(
        [
            jnp.sum(
                grad_pre * extended[:, offset : offset + piece_len].astype(jnp.float32), axis=(0, 1)
            )
            for offset in range(KW)
        ],
        axis=0,
    )
    kernel_float = kernel_back.astype(jnp.float32)
    grad_ext = sum(
        (
            jnp.pad(
                kernel_float[offset] * grad_pre, ((0, 0), (offset, halo_width - offset), (0, 0))
            )
            for offset in range(KW)
        )
    )
    returned = from_behind(grad_ext[:, :halo_width].astype(jnp.bfloat16), "seq", -1).astype(
        jnp.float32
    )
    grad_conv_in = grad_ext[:, halo_width:] + jnp.pad(
        returned, ((0, 0), (piece_len - halo_width, 0), (0, 0))
    )
    grad_proj = (
        jnp.concatenate([grad_gate_z, grad_conv_in, grad_dt_raw], axis=-1)
        .astype(jnp.bfloat16)
        .reshape(token_rows, -1)
    )
    grad_in = jnp.einsum("td,te->de", normed, grad_proj, preferred_element_type=jnp.float32)
    grad_normed = jnp.einsum(
        "te,de->td", grad_proj, in_back, preferred_element_type=jnp.float32
    ).reshape(seq_count, piece_len, model_width)
    grad_norm_gain = jnp.sum(grad_normed * x_float * scale_in, axis=(0, 1))
    scaled_in = grad_normed * gain_in_back.astype(jnp.float32)
    grad_x_in = scale_in * scaled_in - x_float * (scale_in * scale_in * scale_in) * jnp.mean(
        scaled_in * x_float, axis=-1, keepdims=True
    )
    grad_hidden = (cotangent.astype(jnp.float32) + grad_x_in).astype(jnp.bfloat16)
    owned_grads = (
        lax.psum_scatter(grad_norm_gain, ("dp", "seq"), scatter_dimension=0, tiled=True),
        lax.psum_scatter(grad_in, ("dp", "seq"), scatter_dimension=0, tiled=True),
        lax.psum_scatter(grad_kernel, ("dp", "seq"), scatter_dimension=1, tiled=True),
        lax.psum_scatter(grad_conv_bias, ("dp", "seq"), scatter_dimension=0, tiled=True),
        lax.psum_scatter(grad_gate_gain, ("dp", "seq"), scatter_dimension=0, tiled=True),
        lax.psum_scatter(grad_out, ("dp", "seq"), scatter_dimension=0, tiled=True),
    )
    head_totals = lax.psum((grad_step_bias, grad_decay, grad_skip), ("dp", "seq"))
    return (
        output,
        grad_hidden,
        owned_grads[0],
        owned_grads[1],
        owned_grads[2],
        owned_grads[3],
        head_totals[0],
        head_totals[1],
        head_totals[2],
        owned_grads[4],
        owned_grads[5],
    )


def solution(mesh):
    return jax.shard_map(
        per_device,
        mesh=mesh,
        in_specs=(
            P("dp", "seq", None),
            P("dp"),
            P(("dp", "seq")),
            P(("dp", "seq"), None),
            P(None, ("dp", "seq")),
            P(("dp", "seq")),
            P(),
            P(),
            P(),
            P(("dp", "seq")),
            P(("dp", "seq"), None),
            P("dp", "seq", None),
        ),
        out_specs=(
            P("dp", "seq", None),
            P("dp", "seq", None),
            P(("dp", "seq")),
            P(("dp", "seq"), None),
            P(None, ("dp", "seq")),
            P(("dp", "seq")),
            P(),
            P(),
            P(),
            P(("dp", "seq")),
            P(("dp", "seq"), None),
        ),
        check_vma=False,
    )
```

profile of v0, /device:TPU:0, one launch (start us, length us, event | category | flops | bytes accessed | tf_op | source)
XLA Modules:
  0.0 761.8 jit_solution(16280473056816043643)
XLA Ops:
  12.2 42.3 %all-reduce.14 = (bf16[768]{0:T(1024)(128)(2,1)S(1)}, bf16[1792]{0:T(1024)(128)(2,1)S(1)}, bf16[1536]{0:T(1024)(128)(2,1)S(1)}) all-reduce(bf16[768]{0:T(1024)(128)(2,1)S(1)} %dynamic-update-slice.4, bf16[1792]{0:T(1024)(128)(2,1)S(1)} %dynamic-update-slice.3, ...), channel_id=1, replica_groups=mesh['dp'=8,'seq'=4] {'dp','seq'}, use_global_device_ids=true, to_apply=%add.6 | all-reduce | flops 4096 | bytes 16384
  55.2 40.5 %all-gather = bf16[32,56,4]{1,2,0:T(4,128)(2,1)S(1)} all-gather(bf16[1,56,4]{1,2,0:T(4,128)(2,1)S(1)} %convert_bitcast_fusion), channel_id=1, replica_groups=mesh['dp'=8,'seq'=4] {'dp','seq'}, dimensions={0}, use_global_device_ids=true | all-gather | bytes 14784 | tf_op jit(solution)/shard_map/all_gather | solution.py:91
  98.4 12.8 %fusion.145 = (bf16[2,512,3352]{1,2,0:T(8,128)(2,1)}, f32[2,512,3352]{1,2,0:T(8,128)}) fusion(bf16[768,3352]{1,0:T(8,128)(2,1)} %all-gather.4.cloned.1.call-done, bf16[2,512,768]{2,1,0:T(8,128)(2,1)} %param.18, f32[768]{0:T(1024)S(1)} %convert_element_type.157, f32[2,512]{1,0:T(2,128)S(1)} %get-tuple-element.308), kind=kOutput, calls=%fused_computation.256 | convolution fusion | flops 5278818304 | bytes 27323392 | tf_op jit(solution)/shard_map/dot_general | solution.py:106
  127.1 12.4 %multiply_convert_fusion.14 = (bf16[2,512,1792]{1,2,0:T(8,128)(2,1)S(1)}, f32[2,512,1792]{1,2,0:T(8,128)}) fusion(bf16[2,512,1792]{1,2,0:T(8,128)(2,1)} %slice.154, f32[1792]{0:T(1024)S(1)} %get-tuple-element.225, bf16[2,3,1792]{1,2,0:T(8,128)(2,1)S(1)} %copy.159, f32[1792]{0:T(1024)S(1)} %get-tuple-element.226, f32[1792]{0:T(1024)S(1)} %get-tuple-element.227, ...), kind=kLoop, calls=%fused_computation.107 | loop fusion | flops 47710208 | bytes 14737408 | tf_op jit(solution)/shard_map/convert.8
  140.6 14.5 %copy.160 = bf16[2,512,1536]{1,0,2:T(2,128)(2,1)} copy(bf16[2,512,1536]{1,2,0:T(8,128)(2,1)S(1)} %slice.162) | data formatting | bytes 6291456 | tf_op jit(solution)/shard_map/slice | solution.py:122
  155.1 7.4 reshape.307
  163.7 5.4 fusion.60
  175.8 17.4 %collective-permute-start.2 = (f32[2,24,128,64]{2,3,1,0:T(8,128)}, f32[2,24,128,64]{2,3,1,0:T(8,128)}, u32[]{:S(2)}, u32[]{:S(2)}) collective-permute-start(f32[2,24,128,64]{2,3,1,0:T(8,128)} %multiply_add_fusion.3), channel_id=1, source_target_pairs={{0,1},{1,2},{2,3},{4,5},{5,6},{6,7},{8,9},{9,10},{10,11},{12,13},{... | collective-permute-start | bytes 4718600 | tf_op jit(solution)/shard_map/ppermute | solution.py:21
  203.6 15.8 %collective-permute-start.3 = (f32[2,24,128,64]{2,3,1,0:T(8,128)}, f32[2,24,128,64]{2,3,1,0:T(8,128)}, u32[]{:S(2)}, u32[]{:S(2)}) collective-permute-start(f32[2,24,128,64]{2,3,1,0:T(8,128)} %multiply_add_fusion.2), channel_id=1, source_target_pairs={{0,1},{1,2},{2,3},{4,5},{5,6},{6,7},{8,9},{9,10},{10,11},{12,13},{... | collective-permute-start | bytes 4718600 | tf_op jit(solution)/shard_map/ppermute | solution.py:21
  222.9 25.0 %while.29 = (s32[]{:T(128)}, f32[4,256,24,64]{1,3,2,0:T(8,128)}, bf16[4,256,24,64]{1,3,2,0:T(8,128)(2,1)}, bf16[4,256,128]{2,1,0:T(8,128)(2,1)}, bf16[4,256,128]...) while((s32[]{:T(128)}, f32[4,256,24,64]{1,3,2,0:T(8,128)}, ...), condition=%wide.region_4.5_spmd, body=%wide.region_3.4_spmd.sunk | while | flops 227606528 | bytes 3319905 | solution.py:129
  224.7 4.4 bitcast_dynamic-update-slice_fusion.7
  231.0 4.4 bitcast_dynamic-update-slice_fusion.7
  237.2 4.4 bitcast_dynamic-update-slice_fusion.7
  243.4 4.4 bitcast_dynamic-update-slice_fusion.7
  258.2 7.7 %copy.179 = f32[4,256,24,64]{1,0,3,2:T(4,128)} copy(f32[4,256,24,64]{1,3,2,0:T(8,128)S(1)} %fusion.74) | data formatting | bytes 12582912 | tf_op jit(solution)/shard_map/add | solution.py:163
  265.9 9.3 %reshape.314 = f32[2,512,1536]{1,0,2:T(2,128)} reshape(f32[4,256,24,64]{1,0,3,2:T(4,128)} %copy.179) | data formatting | bytes 12582912 | tf_op jit(solution)/shard_map/reshape | solution.py:164
  275.1 7.4 multiply_reduce_fusion.5
  282.6 10.6 %multiply_reduce_fusion.3 = (f32[1536]{0:T(1024)}, f32[2,512]{1,0:T(2,128)S(1)}, f32[2,512,1536]{1,2,0:T(8,128)}) fusion(f32[2,512,1536]{1,2,0:T(8,128)} %get-tuple-element.282, f32[2,512]{1,0:T(2,128)S(1)} %get-tuple-element.310, f32[1536]{0:T(1024)S(1)} %convert_element_type.172, bf16[1536,768]{1,0:T(8,128)(2,1)} %all-gather.6.cloned.1.call-done, ...), kind=kOutput, calls=%fused_computation.121 | convolution fusion | flops 2427713024 | bytes 16539648 | tf_op jit(solution)/shard_map/td,kd->tk/dot_general | solution.py:192
  293.2 8.8 %multiply_convert_fusion.16 = (bf16[2,512,1536]{1,2,0:T(8,128)(2,1)}, bf16[2,512,1536]{1,2,0:T(8,128)(2,1)S(1)}) fusion(f32[2,512,1536]{1,0,2:T(2,128)S(1)} %copy-done, f32[2,512,3352]{1,2,0:T(8,128)} %get-tuple-element.316, f32[2,512]{1,0:T(2,128)S(1)} %broadcast_multiply_fusion.4, f32[2,512,1536]{1,2,0:T(8,128)S(1)} %copy-done.2, ...), kind=kLoop, calls=%fused_computation.123 | loop fusion | flops 28311552 | bytes 31475712 | tf_op jit(solution)/shard_map/convert.2
  302.0 14.4 %copy.184 = bf16[2,512,1536]{1,0,2:T(2,128)(2,1)} copy(bf16[2,512,1536]{1,2,0:T(8,128)(2,1)S(1)} %get-tuple-element.294) | data formatting | bytes 6291456 | tf_op jit(solution)/shard_map/convert_element_type | solution.py:200
  316.4 8.6 %reshape.315 = bf16[4,256,24,64]{1,0,3,2:T(4,128)(2,1)} reshape(bf16[2,512,1536]{1,0,2:T(2,128)(2,1)} %copy.184) | data formatting | bytes 6291456 | tf_op jit(solution)/shard_map/reshape | solution.py:202
  325.0 8.2 %fusion.61 = f32[4,24,128,64]{2,3,1,0:T(8,128)S(1)} fusion(f32[4,24,256]{2,1,0:T(8,128)} %fusion.129, f32[4,256,128]{2,1,0:T(8,128)} %copy-done.23, bf16[4,256,24,64]{1,0,3,2:T(4,128)(2,1)} %reshape.315), kind=kOutput, calls=%fused_computation.92 | convolution fusion | flops 408944640 | bytes 6914048 | tf_op jit(solution)/shard_map/bhqn,bqhp->bhnp/dot_general | solution.py:207
  334.9 4.8 collective-permute-done.4
  349.0 7.7 %convolution_bitcast_fusion.3 = f32[1536,768]{1,0:T(8,128)} fusion(bf16[2,512,768]{2,1,0:T(8,128)(2,1)S(1)} %copy-done.28, f32[2,512]{1,0:T(2,128)} %copy-done.68, f32[2,512,1536]{1,2,0:T(8,128)} %get-tuple-element.282, f32[1536]{0:T(1024)} %copy-done.52, f32[2,512]{1,0:T(2,128)} %copy-done.65), kind=kOutput, calls=%fused_computation.148 | convolution fusion | flops 2422996992 | bytes 12597248 | tf_op jit(solution)/shard_map/tk,td->kd/dot_general | solution.py:191
  356.8 6.4 collective-permute-done.5
  371.2 61.4 %while.30 = (s32[]{:T(128)}, f32[4,256,24,64]{1,3,2,0:T(8,128)}, f32[4,256,128]{2,1,0:T(8,128)}, f32[4,256,128]{2,1,0:T(8,128)}, f32[4,24,256]{2,1,0:T(8,128)}, ...) while((s32[]{:T(128)}, f32[4,256,24,64]{1,3,2,0:T(8,128)}, ...), condition=%wide.region_12.13_spmd, body=%wide.region_7.12_spmd.sunk | while | flops 481284096 | bytes 6280337 | solution.py:204
  373.7 5.5 multiply_reduce_fusion.8
  389.1 5.5 multiply_reduce_fusion.8
  404.5 5.5 multiply_reduce_fusion.8
  419.8 5.5 multiply_reduce_fusion.8
  436.4 10.9 %fusion.52 = (f32[4,24,256]{2,1,0:T(8,128)}, bf16[4,24,256,128]{3,2,1,0:T(8,128)(2,1)S(1)}) fusion(f32[4,24,256]{2,1,0:T(8,128)S(1)} %copy-done.36, f32[4,256,128]{2,1,0:T(8,128)} %copy-done.23, bf16[4,24,128,64]{2,3,1,0:T(8,128)(2,1)} %bitcast.288, bf16[4,256,24,64]{1,0,3,2:T(4,128)(2,1)} %reshape.315), kind=kOutput, calls=%fused_computation.73 | convolution fusion | flops 415211520 | bytes 11730944 | tf_op jit(solution)/shard_map/bqhp,bhnp->bhqn/dot_general | solution.py:240
  464.0 4.8 fusion.55
  475.7 7.3 bitcast_add_fusion
  483.0 7.5 copy.193
  490.5 9.5 %reshape.317 = f32[2,512,1536]{1,0,2:T(2,128)} reshape(f32[4,256,24,64]{1,0,3,2:T(4,128)} %copy.193) | data formatting | bytes 12582912 | tf_op jit(solution)/shard_map/reshape | solution.py:254
  500.1 6.7 copy.196
  510.6 10.0 %reduce-window.16 = f32[4,24,2,128]{3,1,2,0:T(8,128)S(1)} reduce-window(f32[4,24,2,128]{3,1,2,0:T(8,128)S(1)} %copy.206, f32[]{:T(128)} %constant.98.clone.1), window={size=1x1x1x128 pad=0_0x0_0x0_0x0_127}, to_apply=%region_15.16 | reduce-window | flops 3121152 | bytes 196612 | tf_op jit(solution)/shard_map/reduce-window.2
  526.8 19.6 %fusion.137 = (f32[1792]{0:T(1024)}, f32[1792]{0:T(1024)}, f32[1792]{0:T(1024)}, f32[1792]{0:T(1024)}, f32[1792]{0:T(1024)}, /*index=5*/f32[2,512,1792]{1,2,0:T(8,128)S(1)}) fusion(bf16[2,512,3352]{1,2,0:T(8,128)(2,1)} %get-tuple-element.315, bf16[2,512,1792]{1,2,0:T(8,128)(2,1)} %slice.154, bf16[2,3,1792]{1,2,0:T(8,128)(2,1)} %copy-done.8, ...), kind=kLoop, calls=%fused_computation.252 | loop fusion | flops 58711296 | bytes 29417472 | tf_op jit(solution)/shard_map/reduce_sum | solution.py:262
  546.4 9.2 %broadcast_multiply_fusion.3 = (f32[2,512,1792]{1,2,0:T(8,128)S(1)}, f32[2,512,1792]{1,2,0:T(8,128)}, f32[2,512,1792]{1,2,0:T(8,128)}, f32[2,512,1792]{1,2,0:T(8,128)}) fusion(f32[2,512,1792]{1,2,0:T(8,128)S(1)} %get-tuple-element.278, f32[1792]{0:T(1024)S(1)} %copy-done.40, f32[1792]{0:T(1024)} %copy-done.41, f32[1792]{0:T(1024)} %copy-done.42, ...), kind=kLoop, calls=%fused_computation.155 | loop fusion | flops 7340032 | bytes 36728832 | tf_op jit(solution)/shard_map/mul | solution.py:276
  555.6 11.4 %pad_add_fusion = f32[2,515,1792]{1,2,0:T(8,128)S(1)} fusion(f32[2,512,1792]{1,2,0:T(8,128)} %get-tuple-element.296, f32[2,512,1792]{1,2,0:T(8,128)} %get-tuple-element.297, f32[2,512,1792]{1,2,0:T(8,128)} %get-tuple-element.298, f32[2,512,1792]{1,2,0:T(8,128)S(1)} %get-tuple-element.295), kind=kLoop, calls=%fused_computation.81 | loop fusion | flops 5537280 | bytes 36743168 | tf_op jit(solution)/shard_map/add | solution.py:273
  576.0 17.6 %collective-permute-done.7 = bf16[2,3,1792]{2,0,1:T(2,128)(2,1)S(1)} collective-permute-done((bf16[2,3,1792]{2,0,1:T(2,128)(2,1)S(1)}, bf16[2,3,1792]{2,0,1:T(2,128)(2,1)S(1)}, u32[]{:S(2)}, u32[]{:S(2)}) %collective-permute-start.7) | collective-permute-done | bytes 21536 | tf_op jit(solution)/shard_map/ppermute | solution.py:21
  594.9 5.6 fusion.71
  602.4 12.1 %convolution_bitcast_fusion.2 = f32[768,3352]{1,0:T(8,128)} fusion(bf16[2,512,24]{1,2,0:T(8,128)(2,1)S(1)} %get-tuple-element.277, bf16[2,512,1792]{1,2,0:T(8,128)(2,1)S(1)} %fusion.71, bf16[2,512,1536]{1,2,0:T(8,128)(2,1)} %get-tuple-element.293, bf16[2,512,768]{2,1,0:T(8,128)(2,1)S(1)} %copy-done.12, f32[768]{0:T(1024)S(1)} %copy-done.62, ...), kind=kOutput, calls=%fused_computation.94 | convolution fusion | flops 5295980544 | bytes 18742272 | tf_op jit(solution)/shard_map/td,te->de/dot_general | solution.py:292
  614.6 4.2 fusion.73
  618.9 7.6 fusion.94
  626.8 11.0 %fusion.99 = (f32[768]{0:T(1024)S(1)}, f32[2,512]{1,0:T(2,128)S(1)}, f32[2,512,768]{2,1,0:T(8,128)}) fusion(bf16[2,512,768]{2,1,0:T(8,128)(2,1)S(1)} %copy-done.13, f32[2,512]{1,0:T(2,128)S(1)} %copy-done.60, f32[768]{0:T(1024)S(1)} %copy-done.62, bf16[768,3352]{1,0:T(8,128)(2,1)} %all-gather.4.cloned.1.call-done, ...), kind=kOutput, calls=%fused_computation.166 | convolution fusion | flops 5298337792 | bytes 16746496 | tf_op jit(solution)/shard_map/te,de->td/dot_general | solution.py:293
  637.8 39.0 %all-reduce.13 = (f32[768]{0:T(1024)S(1)}, f32[4,1792]{1,0:T(4,128)S(1)}, f32[1792]{0:T(1024)S(1)}, f32[24]{0:T(128)}, f32[24]{0:T(128)}, /*index=5*/f32[24]{0:T(128)}, f32[1536]{0:T(1024)S(1)}) all-reduce(f32[768]{0:T(1024)S(1)} %get-tuple-element.222, ...), channel_id=2, replica_groups=mesh['dp'=8,'seq'=4] {'dp','seq'}, use_global_device_ids=true, to_apply=%region_19.20.clone | all-reduce | flops 11336 | bytes 90688
  682.6 72.5 %reduce-scatter.8.cloned.1.call-done = f32[24,3352]{1,0:T(8,128)} async-done(((f32[768,3352]{1,0:T(8,128)}), f32[24,3352]{1,0:T(8,128)}) %reduce-scatter.8.cloned.1.call-update) | async-done | bytes 321808
  (344 shorter events, 177.7 us)
Async XLA Ops:
  7.2 91.2 %all-gather.4.cloned.1.call-start = ((), (), s32[]{:S(2)}) async-start(), calls=%async_computation.2 | async-start | bytes 5474304 | tf_op jit(solution)/shard_map/all_gather | solution.py:90
  8.9 273.7 %all-gather.6.cloned.1.call-start = ((), (), s32[]{:S(2)}) async-start(), calls=%async_computation.3 | async-start | bytes 2433024 | tf_op jit(solution)/shard_map/all_gather | solution.py:94
  9.6 103.8 %copy-start.72 = (f32[24]{0:T(128)}, f32[24]{0:T(128)S(1)}, u32[]{:S(2)}) copy-start(f32[24]{0:T(128)S(1)} %exp.45) | copy-start | bytes 292
  54.5 56.7 %copy-start.61 = (f32[768]{0:T(1024)}, f32[768]{0:T(1024)S(1)}, u32[]{:S(2)}) copy-start(f32[768]{0:T(1024)S(1)} %convert_element_type.157) | copy-start | bytes 9220
  96.0 31.1 %copy-start.39 = (f32[1792]{0:T(1024)}, f32[1792]{0:T(1024)S(1)}, u32[]{:S(2)}) copy-start(f32[1792]{0:T(1024)S(1)} %get-tuple-element.224) | copy-start | bytes 21508
  96.0 31.1 %copy-start.41 = (f32[1792]{0:T(1024)}, f32[1792]{0:T(1024)S(1)}, u32[]{:S(2)}) copy-start(f32[1792]{0:T(1024)S(1)} %get-tuple-element.225) | copy-start | bytes 21508
  96.0 31.1 %copy-start.42 = (f32[1792]{0:T(1024)}, f32[1792]{0:T(1024)S(1)}, u32[]{:S(2)}) copy-start(f32[1792]{0:T(1024)S(1)} %get-tuple-element.226) | copy-start | bytes 21508
  96.0 31.1 %copy-start.43 = (f32[1792]{0:T(1024)}, f32[1792]{0:T(1024)S(1)}, u32[]{:S(2)}) copy-start(f32[1792]{0:T(1024)S(1)} %get-tuple-element.227) | copy-start | bytes 21508
  98.4 12.8 %copy-start.59 = (f32[2,512]{1,0:T(2,128)}, f32[2,512]{1,0:T(2,128)S(1)}, u32[]{:S(2)}) copy-start(f32[2,512]{1,0:T(2,128)S(1)} %get-tuple-element.308) | copy-start | bytes 12292
  98.4 12.8 %copy-start.70 = (f32[24]{0:T(128)S(1)}, f32[24]{0:T(128)}, u32[]{:S(2)}) copy-start(f32[24]{0:T(128)} %param.24) | copy-start | bytes 292
  113.4 12.3 %copy-start.7 = (f32[4,256,24]{2,0,1:T(4,128)}, f32[4,256,24]{2,0,1:T(4,128)S(1)}, u32[]{:S(2)}) copy-start(f32[4,256,24]{2,0,1:T(4,128)S(1)} %copy.164) | copy-start | bytes 294916
  116.3 79.3 %copy-start.44 = (f32[4,24,2]{1,2,0:T(2,128)}, f32[4,24,2]{1,2,0:T(2,128)S(1)}, u32[]{:S(2)}) copy-start(f32[4,24,2]{1,2,0:T(2,128)S(1)} %copy.167) | copy-start | bytes 2308
  116.4 10.2 %copy-start.27 = (f32[4,24,256]{2,1,0:T(8,128)}, f32[4,24,256]{2,1,0:T(8,128)S(1)}, u32[]{:S(2)}) copy-start(f32[4,24,256]{2,1,0:T(8,128)S(1)} %copy_bitcast_fusion) | copy-start | bytes 294916
  116.7 52.5 %copy-start.63 = (f32[2,1,24]{2,1,0:T(1,128)}, f32[2,1,24]{2,1,0:T(1,128)S(1)}, u32[]{:S(2)}) copy-start(f32[2,1,24]{2,1,0:T(1,128)S(1)} %get-tuple-element.311) | copy-start | bytes 580
  116.9 22.7 %copy-start.16 = (f32[4,24,256]{1,0,2:T(4,128)}, f32[4,24,256]{1,0,2:T(4,128)S(1)}, u32[]{:S(2)}) copy-start(f32[4,24,256]{1,0,2:T(4,128)S(1)} %bitcast_multiply_fusion.4) | copy-start | bytes 294916
  119.1 7.4 collective-permute-start
  121.6 218.2 %copy-start.54 = (f32[2,24]{1,0:T(2,128)}, f32[2,24]{1,0:T(2,128)S(1)}, u32[]{:S(2)}) copy-start(f32[2,24]{1,0:T(2,128)S(1)} %get-tuple-element.286) | copy-start | bytes 580
  127.1 12.5 %copy-start.8 = (bf16[2,3,1792]{1,2,0:T(8,128)(2,1)}, bf16[2,3,1792]{1,2,0:T(8,128)(2,1)S(1)}, u32[]{:S(2)}) copy-start(bf16[2,3,1792]{1,2,0:T(8,128)(2,1)S(1)} %copy.159) | copy-start | bytes 64516
  169.1 24.1 %copy-start.37 = (f32[48,768]{1,0:T(8,128)S(1)}, f32[48,768]{1,0:T(8,128)}, u32[]{:S(2)}) copy-start(f32[48,768]{1,0:T(8,128)} %param.28) | copy-start | bytes 442372
  169.1 24.8 %copy-start.74 = (s32[2]{0:T(128)S(1)}, s32[2]{0:T(128)}, u32[]{:S(2)}) copy-start(s32[2]{0:T(128)} %param.19) | copy-start | bytes 28
  169.5 4.9 collective-permute-start.1
  175.8 24.5 %collective-permute-start.2 = (f32[2,24,128,64]{2,3,1,0:T(8,128)}, f32[2,24,128,64]{2,3,1,0:T(8,128)}, u32[]{:S(2)}, u32[]{:S(2)}) collective-permute-start(f32[2,24,128,64]{2,3,1,0:T(8,128)} %multiply_add_fusion.3), channel_id=1, source_target_pairs={{0,1},{1,2},{2,3},{4,5},{5,6},{6,7},{8,9},{9,10},{10,11},{12,13},{... | collective-permute-start | bytes 4718600 | tf_op jit(solution)/shard_map/ppermute | solution.py:21
  193.9 488.7 %reduce-scatter.6.cloned.1.call-start = ((), (), s32[]{:S(2)}) async-start(), calls=%async_computation.4 | async-start | bytes 4866048 | tf_op jit(solution)/shard_map/reduce_scatter | solution.py:308
  193.9 99.3 %copy-start.52 = (f32[1536]{0:T(1024)}, f32[1536]{0:T(1024)S(1)}, u32[]{:S(2)}) copy-start(f32[1536]{0:T(1024)S(1)} %convert_element_type.172) | copy-start | bytes 18436
  194.0 88.6 %copy-start.68 = (f32[2,512]{1,0:T(2,128)}, f32[2,512]{1,0:T(2,128)S(1)}, u32[]{:S(2)}) copy-start(f32[2,512]{1,0:T(2,128)S(1)} %compare_convert_fusion) | copy-start | bytes 12292
  203.6 45.4 %collective-permute-start.3 = (f32[2,24,128,64]{2,3,1,0:T(8,128)}, f32[2,24,128,64]{2,3,1,0:T(8,128)}, u32[]{:S(2)}, u32[]{:S(2)}) collective-permute-start(f32[2,24,128,64]{2,3,1,0:T(8,128)} %multiply_add_fusion.2), channel_id=1, source_target_pairs={{0,1},{1,2},{2,3},{4,5},{5,6},{6,7},{8,9},{9,10},{10,11},{12,13},{... | collective-permute-start | bytes 4718600 | tf_op jit(solution)/shard_map/ppermute | solution.py:21
  282.6 10.7 %copy-start.65 = (f32[2,512]{1,0:T(2,128)}, f32[2,512]{1,0:T(2,128)S(1)}, u32[]{:S(2)}) copy-start(f32[2,512]{1,0:T(2,128)S(1)} %get-tuple-element.310) | copy-start | bytes 12292
  282.6 10.6 %copy-start = (f32[2,512,1536]{1,0,2:T(2,128)S(1)}, f32[2,512,1536]{1,0,2:T(2,128)}, u32[]{:S(2)}) copy-start(f32[2,512,1536]{1,0,2:T(2,128)} %reshape.314) | copy-start | bytes 18874372
  282.6 10.6 %copy-start.2 = (f32[2,512,1536]{1,2,0:T(8,128)S(1)}, f32[2,512,1536]{1,2,0:T(8,128)}, u32[]{:S(2)}) copy-start(f32[2,512,1536]{1,2,0:T(8,128)} %get-tuple-element.282) | copy-start | bytes 18874372
  333.6 6.2 collective-permute-start.4
  341.2 22.1 %collective-permute-start.5 = (f32[2,24,128,64]{2,3,1,0:T(8,128)}, f32[2,24,128,64]{2,3,1,0:T(8,128)}, u32[]{:S(2)}, u32[]{:S(2)}) collective-permute-start(f32[2,24,128,64]{2,3,1,0:T(8,128)} %multiply_add_fusion.1), channel_id=1, source_target_pairs={{1,0},{2,1},{3,2},{5,4},{6,5},{7,6},{9,8},{10,9},{11,10},{13,12},{... | collective-permute-start | bytes 4718600 | tf_op jit(solution)/shard_map/ppermute | solution.py:21
  349.0 14.2 %copy-start.55 = (f32[2,24]{1,0:T(2,128)S(1)}, f32[2,24]{1,0:T(2,128)}, u32[]{:S(2)}) copy-start(f32[2,24]{1,0:T(2,128)} %copy-done.54) | copy-start | bytes 580
  356.7 398.4 %reduce-scatter.8.cloned.1.call-start = ((), (), s32[]{:S(2)}) async-start(), calls=%async_computation.5 | async-start | bytes 10948608
  366.5 88.7 %collective-permute-start.6 = (f32[2,24,128,64]{2,3,1,0:T(8,128)}, f32[2,24,128,64]{2,3,1,0:T(8,128)}, u32[]{:S(2)}, u32[]{:S(2)}) collective-permute-start(f32[2,24,128,64]{2,3,1,0:T(8,128)} %multiply_add_fusion), channel_id=1, source_target_pairs={{1,0},{2,1},{3,2},{5,4},{6,5},{7,6},{9,8},{10,9},{11,10},{13,12},{... | collective-permute-start | bytes 4718600 | tf_op jit(solution)/shard_map/ppermute | solution.py:21
  371.2 65.2 %copy-start.36 = (f32[4,24,256]{2,1,0:T(8,128)S(1)}, f32[4,24,256]{2,1,0:T(8,128)}, u32[]{:S(2)}) copy-start(f32[4,24,256]{2,1,0:T(8,128)} %fusion.129) | copy-start | bytes 294916
  436.4 10.9 %copy-start.33 = (bf16[4,24,256,1]{1,3,2,0:T(2,128)(2,1)S(1)}, bf16[4,24,256,1]{1,3,2,0:T(2,128)(2,1)}, u32[]{:S(2)}) copy-start(bf16[4,24,256,1]{1,3,2,0:T(2,128)(2,1)} %copy.222) | copy-start | bytes 147460
  500.0 21.8 %copy-start.57 = (f32[4,24]{1,0:T(4,128)S(1)}, f32[4,24]{1,0:T(4,128)}, u32[]{:S(2)}) copy-start(f32[4,24]{1,0:T(4,128)} %copy-done.56) | copy-start | bytes 1156
  500.0 21.7 %copy-start.73 = (f32[24]{0:T(128)S(1)}, f32[24]{0:T(128)}, u32[]{:S(2)}) copy-start(f32[24]{0:T(128)} %copy-done.72) | copy-start | bytes 292
  526.8 19.6 %copy-start.40 = (f32[1792]{0:T(1024)S(1)}, f32[1792]{0:T(1024)}, u32[]{:S(2)}) copy-start(f32[1792]{0:T(1024)} %copy-done.39) | copy-start | bytes 21508
  555.6 19.2 %copy-start.71 = (f32[24]{0:T(128)S(1)}, f32[24]{0:T(128)}, u32[]{:S(2)}) copy-start(f32[24]{0:T(128)} %param.24) | copy-start | bytes 292
  573.1 20.5 %collective-permute-start.7 = (bf16[2,3,1792]{2,0,1:T(2,128)(2,1)S(1)}, bf16[2,3,1792]{2,0,1:T(2,128)(2,1)S(1)}, u32[]{:S(2)}, u32[]{:S(2)}) collective-permute-start(bf16[2,3,1792]{2,0,1:T(2,128)(2,1)S(1)} %copy.199), channel_id=1, source_target_pairs={{1,0},{2,1},{3,2},{5,4},{6,5},{7,6},{9,8},{10,9},{11,10},{13,12},{... | collective-permute-start | bytes 64520 | tf_op jit(solution)/shard_map/ppermute | solution.py:21
  576.0 26.4 %copy-start.60 = (f32[2,512]{1,0:T(2,128)S(1)}, f32[2,512]{1,0:T(2,128)}, u32[]{:S(2)}) copy-start(f32[2,512]{1,0:T(2,128)} %copy-done.59) | copy-start | bytes 12292
  576.0 26.4 %copy-start.62 = (f32[768]{0:T(1024)S(1)}, f32[768]{0:T(1024)}, u32[]{:S(2)}) copy-start(f32[768]{0:T(1024)} %copy-done.61) | copy-start | bytes 9220
  626.7 11.1 %copy-start.47 = (f32[1792]{0:T(1024)S(1)}, f32[1792]{0:T(1024)}, u32[]{:S(2)}) copy-start(f32[1792]{0:T(1024)} %get-tuple-element.217) | copy-start | bytes 21508
  626.7 11.1 %copy-start.67 = (f32[1536]{0:T(1024)S(1)}, f32[1536]{0:T(1024)}, u32[]{:S(2)}) copy-start(f32[1536]{0:T(1024)} %get-tuple-element.212) | copy-start | bytes 18436
  626.7 52.5 %copy-start.14 = (bf16[2,512,768]{2,1,0:T(8,128)(2,1)S(1)}, bf16[2,512,768]{2,1,0:T(8,128)(2,1)}, u32[]{:S(2)}) copy-start(bf16[2,512,768]{2,1,0:T(8,128)(2,1)} %param.18) | copy-start | bytes 4718596
  626.7 52.5 %copy-start.29 = (bf16[2,512,768]{2,1,0:T(8,128)(2,1)S(1)}, bf16[2,512,768]{2,1,0:T(8,128)(2,1)}, u32[]{:S(2)}) copy-start(bf16[2,512,768]{2,1,0:T(8,128)(2,1)} %param.29) | copy-start | bytes 4718596
  626.8 52.5 %copy-start.58 = (f32[2,512]{1,0:T(2,128)S(1)}, f32[2,512]{1,0:T(2,128)}, u32[]{:S(2)}) copy-start(f32[2,512]{1,0:T(2,128)} %get-tuple-element.307) | copy-start | bytes 12292
  (43 other events, 234.7 us)
Sparse Core Ops, SparseCore 0:
  11.5 68.4 all-gather.3
  194.0 55.1 all-gather.5
  356.9 123.4 reduce-scatter.5
  614.7 140.3 reduce-scatter.7
where the time goes:
time: 772 us; the launch traced here: 762 us
  matrix products  187 us (24%)
  local copies, waits for them, and re-layouts  152 us (20%)
  other arithmetic  138 us (18%)
  blocking collectives  122 us (16%)
  waiting for transfers between devices  104 us (13%)
  starting transfers between devices  43.3 us (6%)
  between operations  15.2 us (2%)
    unnamed x2, blocking collectives  81.3 us
    unnamed x5, waiting for transfers between devices  72.6 us
    ppermute x8, starting transfers between devices, from_behind(): return lax.ppermute(block, axis, route)  43.2 us
    all_gather x1, blocking collectives, per_device(): lax.all_gather(shards[2], ('dp', 'seq'), axis=1, tiled=True)  40.5 us
    another operation x12, other arithmetic  39.2 us
    ppermute x8, waiting for transfers between devices, from_behind(): return lax.ppermute(block, axis, route)  31.8 us
    dot_general x4, matrix products, intra_backward(): jnp.einsum('qhp,rhp->hqr', grad_group, x_group, preferred_element_type=jn...  22 us
    reduce_sum x1, other arithmetic, per_device(): grad_conv_bias = jnp.sum(grad_pre, axis=(0, 1))  19.6 us
  transfers between devices with their start and end apart: 12, of which 5 were waited for; matrix products, arithmetic and copies ran while one was open for 46% of the time, Pallas kernels for 0%

commit v1 on v0

v1 whole, which is shorter than its diff:
```python
import functools

import jax
import jax.numpy as jnp
from jax import lax
from jax.experimental import pallas as pl
from jax.experimental.pallas import tpu as pltpu
from jax.sharding import PartitionSpec as P

H = 24
P_SIZE = 64
N = 128
KW = 4
Q = 256
DI = 1536
CD = 1792
HL = 128
CW = CD + HL
CH = 256
HALF = 128
RIM = 16
PIECES = 32
NEG = -1e30

epsilon = 1e-05
low = jnp.bfloat16
f32 = jnp.float32
axes = ("dp", "seq")


def dot(left, right, dims):
    return lax.dot_general(left, right, (dims, ((), ())), preferred_element_type=f32)


def nn(left, right):
    return dot(left, right, ((1,), (0,)))


def nt(left, right):
    return dot(left, right, ((1,), (1,)))


def tn(left, right):
    return dot(left, right, ((0,), (0,)))


def split(value):
    top = value.astype(low)
    return top, (value - top.astype(f32)).astype(low)


def spread(parts, table):
    return nn(parts[0], table) + nn(parts[1], table)


def gather_heads(value, table):
    return spread(split(value), table)


def running_sum(value, reverse):
    rows = value.shape[0]
    at = lax.broadcasted_iota(jnp.int32, value.shape, 0)
    step = 1
    while step < rows:
        if reverse:
            value = value + jnp.where(at < rows - step, pltpu.roll(value, rows - step, 0), 0.0)
        else:
            value = value + jnp.where(at >= step, pltpu.roll(value, step, 0), 0.0)
        step *= 2
    return value


def softplus(value):
    tail = jnp.exp(-jnp.abs(value))
    series = tail * (1.0 - tail * (0.5 - tail * (1.0 / 3.0 - tail * (0.25 - tail * 0.2))))
    return jnp.maximum(value, 0.0) + jnp.where(tail < 0.03125, series, jnp.log(1.0 + tail))


def fold8(value):
    return jnp.sum(value.reshape(value.shape[0] // 8, 8, value.shape[1]), axis=0)


def pair_rows(me, own, other):
    first = (me & 1) == 0
    return jnp.concatenate([jnp.where(first, own, other), jnp.where(first, other, own)], axis=0)


def source_of(me, place):
    return me ^ ((place // 4) * 2) ^ ((place % 4) * 8)


def place_of(piece):
    return ((piece >> 1) & 3) * 4 + (piece >> 3)


def conv_kernel(
    groups, scal, x, halo, wa, wb, gain, cw, cb, sb, rate, e,
    nrm_o, nrmt_o, cie_o, xh_o, xs_o, wx_o, bc_o, step_o, cum_o, dtb_o, cumt_o,
    sloc_o, pre_o, r_o, tot_o, wc_o,
    nrm, cs, run, dec,
):
    block = pl.program_id(0)
    fresh = block % groups == 0

    @pl.when(block == 0)
    def assemble():
        me = scal[0]

        def one(place, carry):
            chip = source_of(me, place) >> 1
            own, other = wa[place].astype(f32), wb[place].astype(f32)
            wc_o[pl.ds(pl.multiple_of(chip * 48, 16), 48), :] = pair_rows(me, own, other).astype(low)
            return carry

        lax.fori_loop(0, PIECES // 2, one, 0)

    def normed(rows):
        wide = rows.astype(f32)
        scale = lax.rsqrt(jnp.mean(wide * wide, axis=-1, keepdims=True) + epsilon)
        return (wide * scale * gain[...]).astype(low)

    nrm[0:RIM, :] = normed(halo[...])
    for r in range(0, Q, 32):
        nrm[RIM + r : RIM + r + 32, :] = normed(x[r : r + 32, :])
    nrm_o[...] = nrm[RIM:, :]
    nrmt_o[...] = nrm[RIM:, :].T

    for c in range(0, CD, CH):
        cols = slice(c, c + CH)
        conv_in = nn(nrm[...], wc_o[:, cols]).astype(low)
        cie_o[:, cols] = conv_in
        cs[...] = conv_in.astype(f32)
        for r in range(0, Q, 32):
            taps = cw[0:1, cols] * cs[RIM - 3 + r : RIM + 29 + r, :]
            for k in range(1, KW):
                taps = taps + cw[k : k + 1, cols] * cs[RIM - 3 + k + r : RIM + 29 + k + r, :]
            pre = cb[:, cols] + taps
            act = (pre * jax.nn.sigmoid(pre)).astype(low)
            if c < DI:
                xh_o[r : r + 32, cols] = act
            else:
                bc_o[r : r + 32, :] = act

    dtb = nn(nrm[RIM:, :], wc_o[:, CD:CW]) + sb[...]
    step = softplus(dtb)
    cum = running_sum(-step * rate[...], False)
    step_o[...] = step
    cum_o[...] = cum
    dtb_o[...] = dtb
    cumt_o[...] = cum.T[0:H, :]
    last = cum[Q - 1 : Q, :]
    steps = split(step)
    tails = split(jnp.exp(last - cum) * step)
    decays = split(jnp.broadcast_to(jnp.exp(last), (8, HL)))
    for c in range(0, DI, CH):
        cols = slice(c, c + CH)
        table = e[:, cols]
        wide = xh_o[:, cols].astype(f32)
        xs_o[:, cols] = (spread(steps, table) * wide).astype(low)
        weighted = (spread(tails, table) * wide).astype(low)
        wx_o[:, cols] = weighted
        local = tn(bc_o[:, 0:N], weighted)
        decay = spread(decays, table)
        before = jnp.where(fresh, 0.0, run[:, cols])
        sloc_o[:, cols] = before
        after = decay[0:1, :] * before + local
        run[:, cols] = after
        r_o[:, cols] = after
        product = jnp.where(fresh, 1.0, dec[:, cols])
        pre_o[:, cols] = product
        product = product * decay
        dec[:, cols] = product
        tot_o[:, cols] = product


def intra_kernel(bc, xs, cum, cumt, o, sc):
    sc[...] = nt(bc[:, N : 2 * N], bc[:, 0:N])
    at = lax.broadcasted_iota(jnp.int32, (HALF, HALF), 0)
    to = lax.broadcasted_iota(jnp.int32, (HALF, HALF), 1)
    lower = at >= to
    left = lax.broadcasted_iota(jnp.int32, (Q, HALF), 1) < P_SIZE
    for pair in range(H // 2):
        cols = slice(pair * HALF, (pair + 1) * HALF)
        x_pair = xs[:, cols]
        tops, bottoms = [], []
        for h in (2 * pair, 2 * pair + 1):
            row = cumt[h : h + 1, :]
            upper_col, lower_col = cum[0:HALF, h : h + 1], cum[HALF:, h : h + 1]
            m00 = sc[0:HALF, 0:HALF] * jnp.exp(jnp.where(lower, upper_col - row[:, 0:HALF], NEG))
            m10 = sc[HALF:, 0:HALF] * jnp.exp(lower_col - row[:, 0:HALF])
            m11 = sc[HALF:, HALF:] * jnp.exp(jnp.where(lower, lower_col - row[:, HALF:], NEG))
            tops.append(nn(m00.astype(low), x_pair[0:HALF, :]))
            bottoms.append(nn(jnp.concatenate([m10.astype(low), m11.astype(low)], axis=1), x_pair))
        o[0:HALF, cols] = jnp.where(left[0:HALF], tops[0], tops[1])
        o[HALF:, cols] = jnp.where(left[0:HALF], bottoms[0], bottoms[1])


def valid_column(scal, groups, block):
    seq, group = block // groups, block % groups
    at = scal[1] * (groups * Q) + group * Q + lax.broadcasted_iota(jnp.int32, (Q, 1), 0)
    return (at < scal[2 + seq]).astype(f32)


def project_kernel(groups, scal, nrm, cot, wa, wb, z_o, dn_o, db_o, wz_o, wo_o):
    block = pl.program_id(0)

    @pl.when(block == 0)
    def assemble():
        me = scal[0]

        def halves(packed):
            return jnp.concatenate([packed[:, 0 : DI // 2], packed[:, DI // 2 :]], axis=0)

        def one(place, carry):
            chip = source_of(me, place) >> 1
            own, other = wa[place, 0].astype(f32), wb[place, 0].astype(f32)
            wz_o[pl.ds(pl.multiple_of(chip * 48, 16), 48), :] = pair_rows(me, own, other).astype(low)
            own, other = halves(wa[place, 1].astype(f32)), halves(wb[place, 1].astype(f32))
            wo_o[pl.ds(pl.multiple_of(chip * 96, 16), 96), :] = pair_rows(me, own, other).astype(low)
            return carry

        lax.fori_loop(0, PIECES // 2, one, 0)

    db_o[...] = (cot[...].astype(f32) * valid_column(scal, groups, block)).astype(low)
    for c in range(0, DI, CH):
        z_o[:, c : c + CH] = nn(nrm[...], wz_o[:, c : c + CH])
        dn_o[:, c : c + CH] = nt(db_o[...], wo_o[c : c + CH, :])


def gate_kernel(
    groups, scal, intra, xh, bc, cum, sloc, pre, inc, z, dn, hid, wo, gg, skip, e, et,
    out_o, dz_o, dy_o, gdy_o, gn_o, sbf_o, rs_o, dloc_o, suf_o, rd_o, tot_o, gacc_o, kacc_o,
    yi_s, ge_s, pr_s, y_s, sg_s, gt_s, run, dec,
):
    at = pl.program_id(0)
    fresh = at % groups == 0
    block = (at // groups) * groups + groups - 1 - at % groups

    @pl.when(at == 0)
    def start():
        gacc_o[...] = jnp.zeros_like(gacc_o)
        kacc_o[...] = jnp.zeros_like(kacc_o)

    c_rows = bc[:, N : 2 * N]
    growth = split(jnp.exp(cum[...]))
    for c in range(0, DI, CH):
        cols = slice(c, c + CH)
        begin = (sloc[:, cols] + pre[0:1, cols] * inc[:, cols].astype(f32)).astype(low)
        sbf_o[:, cols] = begin
        wide = spread(growth, e[:, cols])
        ge_s[:, cols] = wide
        yi_s[:, cols] = intra[:, cols] + wide * nn(c_rows, begin)

    def body(i, carry):
        rows = pl.ds(pl.multiple_of(i * 16, 16), 16)
        squares = jnp.zeros((16, HALF), f32)
        crosses = jnp.zeros((16, HALF), f32)
        for c in range(0, DI, HALF):
            cols = slice(c, c + HALF)
            zv = z[rows, cols]
            y = yi_s[rows, cols] + skip[:, cols] * xh[rows, cols].astype(f32)
            sig = jax.nn.sigmoid(zv)
            gated = y * (zv * sig)
            squares = squares + gated * gated
            crosses = crosses + (dn[rows, cols] * gg[:, cols]) * gated
            y_s[:, cols] = y
            sg_s[:, cols] = sig
            gt_s[:, cols] = gated
        scale = lax.rsqrt(jnp.sum(squares, axis=1, keepdims=True) / DI + epsilon)
        shift = scale * scale * scale * (jnp.sum(crosses, axis=1, keepdims=True) / DI)
        for c in range(0, DI, HALF):
            cols = slice(c, c + HALF)
            zv, y, sig, gated = z[rows, cols], y_s[:, cols], sg_s[:, cols], gt_s[:, cols]
            wide = dn[rows, cols]
            normal = gated * scale
            gn_o[rows, cols] = (normal * gg[:, cols]).astype(low)
            gacc_o[:, cols] += wide * normal
            d_gated = scale * (wide * gg[:, cols]) - gated * shift
            d_sig = d_gated * sig
            dz_o[rows, cols] = (d_sig * y * (1.0 + zv * (1.0 - sig))).astype(low)
            d_low = (d_sig * zv).astype(low)
            dy_o[rows, cols] = d_low
            d_y = d_low.astype(f32)
            kacc_o[:, cols] += d_y * xh[rows, cols].astype(f32)
            gdy_o[rows, cols] = (ge_s[rows, cols] * d_y).astype(low)
            pr_s[rows, cols] = d_y * yi_s[rows, cols]
        return carry

    lax.fori_loop(0, Q // 16, body, 0)

    valid = valid_column(scal, groups, block)
    for c in range(0, DI // 2, CH):
        branch = nn(gn_o[...], wo[:, c : c + CH])
        out_o[:, c : c + CH] = (hid[:, c : c + CH].astype(f32) + valid * branch).astype(low)
    decays = split(jnp.broadcast_to(jnp.exp(cum[Q - 1 : Q, :]), (8, HL)))
    sums = jnp.zeros((Q, HL), f32)
    for c in range(0, DI, CH):
        cols = slice(c, c + CH)
        sums = sums + gather_heads(pr_s[:, cols], et[cols, :])
        decay = spread(decays, e[:, cols])
        before = jnp.where(fresh, 0.0, run[:, cols])
        dloc_o[:, cols] = before
        after = decay[0:1, :] * before + tn(c_rows, gdy_o[:, cols])
        run[:, cols] = after
        rd_o[:, cols] = after
        product = jnp.where(fresh, 1.0, dec[:, cols])
        suf_o[:, cols] = product
        product = product * decay
        dec[:, cols] = product
        tot_o[:, cols] = product
    rs_o[...] = sums


def intra_back_kernel(bc, xs, xh, dy, step, cum, cumt, skip, e, et, dx_o, dbc_o, rs_o, sc, acc):
    sc[...] = nt(bc[:, 0:N], bc[:, N : 2 * N])
    acc[...] = jnp.zeros_like(acc)
    at = lax.broadcasted_iota(jnp.int32, (HALF, HALF), 0)
    to = lax.broadcasted_iota(jnp.int32, (HALF, HALF), 1)
    upper = at <= to
    left = lax.broadcasted_iota(jnp.int32, (Q, HALF), 1) < P_SIZE
    steps = split(step[...])
    sums = jnp.zeros((Q, HL), f32)
    for pair in range(H // 2):
        cols = slice(pair * HALF, (pair + 1) * HALF)
        dy_pair = dy[:, cols]
        x_pair = xs[:, cols]
        tops, bottoms = [], []
        for h in (2 * pair, 2 * pair + 1):
            keep = left if h % 2 == 0 else jnp.logical_not(left)
            x_half = jnp.where(keep, x_pair, jnp.zeros_like(x_pair))
            row = cumt[h : h + 1, :]
            first_col, second_col = cum[0:HALF, h : h + 1], cum[HALF:, h : h + 1]
            l00 = jnp.exp(jnp.where(upper, row[:, 0:HALF] - first_col, NEG))
            l01 = jnp.exp(row[:, HALF:] - first_col)
            l11 = jnp.exp(jnp.where(upper, row[:, HALF:] - second_col, NEG))
            m00 = (sc[0:HALF, 0:HALF] * l00).astype(low)
            m01 = (sc[0:HALF, HALF:] * l01).astype(low)
            m11 = (sc[HALF:, HALF:] * l11).astype(low)
            tops.append(nn(jnp.concatenate([m00, m01], axis=1), dy_pair))
            bottoms.append(nn(m11, dy_pair[HALF:, :]))
            grown = nt(x_half[0:HALF, :], dy_pair)
            acc[0:HALF, 0:HALF] += grown[:, 0:HALF] * l00
            acc[0:HALF, HALF:] += grown[:, HALF:] * l01
            acc[HALF:, HALF:] += nt(x_half[HALF:, :], dy_pair[HALF:, :]) * l11
        flow = jnp.concatenate(
            [
                jnp.where(left[0:HALF], tops[0], tops[1]),
                jnp.where(left[0:HALF], bottoms[0], bottoms[1]),
            ],
            axis=0,
        )
        sums = sums + gather_heads(flow * xh[:, cols].astype(f32), et[cols, :])
        dx_o[:, cols] = spread(steps, e[:, cols]) * flow + skip[:, cols] * dy_pair.astype(f32)
    rs_o[...] = sums
    scores = acc[...].astype(low)
    dbc_o[:, 0:N] = nn(scores, bc[:, N : 2 * N])
    dbc_o[:, N : 2 * N] = tn(scores, bc[:, 0:N])


def conv_back_kernel(
    groups, dloc, suf, inc, sbf, xh, wx, gdy, dx, dbc, bc, cum, step, dtb, rs1, rs2,
    cie, cw, cb, rate, e, et,
    dcv_o, kacc_o, hacc_o, head_o, tail_o,
    cs, ds, nxt,
):
    at = pl.program_id(0)
    fresh = at % groups == 0

    @pl.when(at == 0)
    def start():
        kacc_o[...] = jnp.zeros_like(kacc_o)
        hacc_o[...] = jnp.zeros_like(hacc_o)

    def conv_back(flow, c):
        cols = slice(c, c + CH)
        cs[...] = cie[:, cols].astype(f32)
        ds[0:8, :] = jnp.zeros((8, CH), f32)
        ds[8 + Q :, :] = jnp.where(fresh, 0.0, nxt[:, cols])
        taps = [cw[k : k + 1, cols] for k in range(KW)]
        sums = [jnp.zeros((8, CH), f32) for _ in range(KW + 1)]
        for r in range(0, Q, 32):
            views = [cs[RIM - 3 + k + r : RIM + 29 + k + r, :] for k in range(KW)]
            pre = taps[0] * views[0]
            for k in range(1, KW):
                pre = pre + taps[k] * views[k]
            pre = cb[:, cols] + pre
            sig = jax.nn.sigmoid(pre)
            d_pre = flow[r : r + 32, :] * (sig * (1.0 + pre * (1.0 - sig)))
            ds[8 + r : 40 + r, :] = d_pre
            for k in range(KW):
                sums[k] = sums[k] + fold8(d_pre * views[k])
            sums[KW] = sums[KW] + fold8(d_pre)
        nxt[:, cols] = ds[8:16, :]
        for k in range(KW + 1):
            kacc_o[8 * k : 8 * k + 8, cols] += sums[k]

        def back(begin, count):
            total = taps[0] * ds[begin + 11 : begin + 11 + count, :]
            for k in range(1, KW):
                total = total + taps[k] * ds[begin + 11 - k : begin + 11 - k + count, :]
            return total

        for r in range(0, Q, 32):
            dcv_o[r : r + 32, cols] = back(r, 32).astype(low)
        head_o[:, cols] = back(-8, 8)

        @pl.when(fresh)
        def keep():
            tail_o[:, cols] = back(Q - 16, 16)

    cumv = cum[...]
    stepv = step[...]
    last = cumv[Q - 1 : Q, :]
    fade = jnp.exp(last - cumv)
    tail = fade * stepv
    tails = split(tail)
    b_rows = bc[:, 0:N]
    d_b = dbc[:, 0:N]
    d_c = dbc[:, N : 2 * N]
    sums = jnp.zeros((Q, HL), f32)
    lasts = jnp.zeros((8, HL), f32)
    for c in range(0, DI, CH):
        cols = slice(c, c + CH)
        end = dloc[:, cols] + suf[0:1, cols] * inc[:, cols].astype(f32)
        end_low = end.astype(low)
        begin = sbf[:, cols]
        lasts = lasts + gather_heads(fold8(end * begin.astype(f32)), et[cols, :])
        reach = nn(b_rows, end_low)
        sums = sums + gather_heads(reach * xh[:, cols].astype(f32), et[cols, :])
        d_b = d_b + nt(wx[:, cols], end_low)
        d_c = d_c + nt(gdy[:, cols], begin)
        conv_back(dx[:, cols] + spread(tails, e[:, cols]) * reach, c)
    conv_back(jnp.concatenate([d_b, d_c], axis=1), DI)

    flow = sums * tail
    d_cum = rs1[...] - stepv * rs2[...] - flow
    d_last = jnp.exp(last) * jnp.sum(lasts, axis=0, keepdims=True)
    d_last = d_last + jnp.sum(flow, axis=0, keepdims=True)
    d_log = running_sum(d_cum, True) + d_last
    d_step = rs2[...] + sums * fade - d_log * rate[...]
    d_dt = d_step * jax.nn.sigmoid(dtb[...])
    dcv_o[:, CD:CW] = d_dt.astype(low)
    hacc_o[0:8, :] += fold8(d_dt)
    hacc_o[8:16, :] += fold8(d_log * stepv)


def store_pieces(me, total, first, count, height, write):
    for i in range(count):
        piece = (first + i) ^ me
        value = total[i * height : (i + 1) * height, :]
        place = place_of(piece)

        @pl.when((piece & 1) == 0)
        def mine():
            write(0, place, value)

        @pl.when((piece & 1) == 1)
        def sent():
            write(1, place, value)


def early_grad_kernel(scal, nrmt, dz, dzr, gn, db, wz, g0_o, g1_o, dn_o, part, wide):
    at = pl.program_id(0)
    me = scal[0]
    refs = (g0_o, g1_o)
    quarter = DI // 4
    cols = pl.ds(pl.multiple_of(at * quarter, HALF), quarter)
    part[...] = nn(nrmt[...], dz[...])

    def put_in(which, place, value):
        refs[which][place, 0, :, cols] = value.astype(low)

    store_pieces(me, part, 0, PIECES, 24, put_in)
    wide[...] = tn(gn[...], db[...])

    def put_out(which, place, value):
        packed = jnp.concatenate([value[0:24, :], value[24:48, :]], axis=1)
        refs[which][place, 1, :, :] = packed.astype(low)

    store_pieces(me, wide, at * 8, 8, 48, put_out)
    dn_o[...] = nt(dzr[...], wz[...])


def late_grad_kernel(scal, nrmt, dcv, g0_o, g1_o, part):
    refs = (g0_o, g1_o)
    part[...] = nn(nrmt[...], dcv[...])

    def put_in(which, place, value):
        refs[which][place, :, :] = value.astype(low)

    store_pieces(scal[0], part, 0, PIECES, 24, put_in)


def input_kernel(dcv, dnz, wc, x, cot, gain, gh_o, acc_o, total):
    @pl.when(pl.program_id(0) == 0)
    def start():
        acc_o[...] = jnp.zeros_like(acc_o)

    total[...] = dnz[...] + nt(dcv[...], wc[...])
    width = x.shape[1]
    for r in range(0, Q, 16):
        rows = slice(r, r + 16)
        wide = x[rows, :].astype(f32)
        scale = lax.rsqrt(jnp.mean(wide * wide, axis=-1, keepdims=True) + epsilon)
        flow = total[rows, :]
        acc_o[...] += fold8(flow * wide * scale)
        scaled = flow * gain[...]
        mean = jnp.sum(scaled * wide, axis=-1, keepdims=True) / width
        d_x = scale * scaled - wide * (scale * scale * scale * mean)
        gh_o[rows, :] = (cot[rows, :].astype(f32) + d_x).astype(low)


def call(kernel, grid, inputs, outputs, scratch, flops, name):
    in_specs = [spec for spec, _ in inputs]
    out_specs = [spec for spec, _, _ in outputs]
    out_shape = [jax.ShapeDtypeStruct(shape, kind) for _, shape, kind in outputs]
    moved = sum(value.size * value.dtype.itemsize for _, value in inputs)
    return pl.pallas_call(
        kernel,
        grid=(grid,),
        in_specs=in_specs,
        out_specs=out_specs,
        out_shape=out_shape,
        scratch_shapes=scratch,
        cost_estimate=pl.CostEstimate(flops=int(flops), transcendentals=0, bytes_accessed=moved),
        compiler_params=pltpu.CompilerParams(
            dimension_semantics=("arbitrary",), vmem_limit_bytes=56 * 1024 * 1024
        ),
        name=name,
    )(*[value for _, value in inputs])


def swap(value, mask):
    return lax.ppermute(value, axes, [(i, i ^ mask) for i in range(PIECES)])


def weave(value):
    line = jnp.stack([value] + [swap(value, mask) for mask in (8, 16, 24)])
    plane = jnp.stack([line] + [swap(line, mask) for mask in (2, 4, 6)])
    other = swap(plane, 1)
    flat = (PIECES // 2,) + value.shape
    return plane.reshape(flat), other.reshape(flat)


def canonical(pieces_own, pieces_other, me):
    both = jnp.concatenate([pieces_own, pieces_other])
    piece = jnp.arange(PIECES, dtype=jnp.int32) ^ me
    return both[(piece & 1) * (PIECES // 2) + place_of(piece)]


def unweave(kept, sent):
    shape = (4, 4) + kept.shape[1:]
    total = (kept.astype(f32) + swap(sent, 1).astype(f32)).reshape(shape)
    lows = total.astype(low)
    got = [swap(lows[j], mask).astype(f32) for j, mask in ((1, 2), (2, 4), (3, 6))]
    total = (total[0] + got[0]) + (got[1] + got[2])
    lows = total.astype(low)
    got = [swap(lows[j], mask).astype(f32) for j, mask in ((1, 8), (2, 16), (3, 24))]
    return (total[0] + got[0]) + (got[1] + got[2])


def total_over(value):
    value = value + swap(value, 1)
    for masks in ((2, 4, 6), (8, 16, 24)):
        got = [swap(value, mask) for mask in masks]
        value = (value + got[0]) + (got[1] + got[2])
    return value


def order_of_pieces():
    return [(j << 1) | (k << 3) for j in range(4) for k in range(4)]


def relay(ends, totals, forward):
    count = lax.axis_size("seq")
    incoming = jnp.zeros(ends.shape, f32)
    for hop in range(1, count):
        value = (totals[:, 0:1, :] * incoming + ends).astype(low)
        route = [(hop - 1, hop)] if forward else [(count - hop, count - hop - 1)]
        incoming = incoming + lax.ppermute(value, "seq", route).astype(f32)
    return incoming.astype(low)


def per_device(
    hidden,
    lengths,
    norm_gain,
    in_weight,
    conv_weight,
    conv_bias,
    step_bias,
    decay_log,
    skip_gain,
    gate_gain,
    out_weight,
    cotangent,
):
    seqs, piece_len, width = hidden.shape
    groups = piece_len // Q
    blocks = seqs * groups
    rows = seqs * piece_len
    devices = lax.axis_size(axes)
    quick = devices == PIECES
    place = lax.axis_index(axes).astype(jnp.int32)
    me = place if quick else jnp.zeros((), jnp.int32)
    seq_at = lax.axis_index("seq").astype(jnp.int32)
    scal = jnp.concatenate([me[None], seq_at[None], lengths.astype(jnp.int32)])

    rims = hidden[:, piece_len - RIM :, :]
    seq_size = lax.axis_size("seq")
    rim_in = lax.ppermute(rims, "seq", [(i, i + 1) for i in range(seq_size - 1)])
    inner = hidden.reshape(seqs, groups, Q, width)[:, : groups - 1, Q - RIM :, :]
    halo = jnp.concatenate([rim_in[:, None], inner], axis=1).reshape(blocks, RIM, width)

    small = jnp.concatenate(
        [norm_gain, conv_weight.reshape(-1), conv_bias, gate_gain]
    ).astype(low)
    w_low = in_weight.astype(low)
    o_low = out_weight.astype(low)
    first = jnp.concatenate(
        [w_low[:, DI:], jnp.zeros((w_low.shape[0], CW - (w_low.shape[1] - DI)), low)], axis=1
    )
    if quick:
        half = o_low.shape[0] // 2
        packed = jnp.concatenate([o_low[:half], o_low[half:]], axis=1)
        second = jnp.stack([w_low[:, :DI], packed])
        size = small.shape[0]
        padded = jnp.pad(small, (0, -size % HALF)).reshape(1, -1)
        smalls = canonical(*weave(padded), me)[:, 0, :size]
        ca, cb_pieces = weave(first)
        second, _ = lax.optimization_barrier((second, ca))
        za, zb = weave(second)
    else:
        smalls = lax.all_gather(small, axes, axis=0, tiled=False)
        order = jnp.array(order_of_pieces(), jnp.int32)
        whole = lax.all_gather(first, axes, axis=0, tiled=True).reshape(PIECES, -1, CW)
        ca, cb_pieces = whole[order], whole[order + 1]
        whole = lax.all_gather(w_low[:, :DI], axes, axis=0, tiled=True).reshape(PIECES, -1, DI)
        outs = lax.all_gather(o_low, axes, axis=0, tiled=True)
        outs = outs.reshape(PIECES, 2, -1, width).transpose(0, 2, 1, 3).reshape(PIECES, -1, DI)
        whole = jnp.stack([whole, outs], axis=1)
        za, zb = whole[order], whole[order + 1]
    smalls = smalls.astype(f32)
    cuts = [norm_gain.shape[0], KW * conv_weight.shape[1], conv_bias.shape[0], gate_gain.shape[0]]
    edges = [0, cuts[0], cuts[0] + cuts[1], cuts[0] + cuts[1] + cuts[2], sum(cuts)]
    gain_in = smalls[:, edges[0] : edges[1]].reshape(1, width)
    taps = smalls[:, edges[1] : edges[2]].reshape(devices, KW, -1)
    taps = taps.transpose(1, 0, 2).reshape(KW, CD)
    bias = smalls[:, edges[2] : edges[3]].reshape(1, CD)
    gain_gate = smalls[:, edges[3] : edges[4]].reshape(1, DI)

    rate = jnp.exp(decay_log)
    sb = jnp.pad(step_bias, (0, HL - H)).reshape(1, HL)
    rate_row = jnp.pad(rate, (0, HL - H)).reshape(1, HL)
    skip = jnp.repeat(skip_gain, P_SIZE).reshape(1, DI)
    heads = lax.broadcasted_iota(jnp.int32, (HL, DI), 0)
    e = (heads == lax.broadcasted_iota(jnp.int32, (HL, DI), 1) // P_SIZE).astype(low)
    heads = lax.broadcasted_iota(jnp.int32, (DI, HL), 1)
    et = (heads == lax.broadcasted_iota(jnp.int32, (DI, HL), 0) // P_SIZE).astype(low)

    def forth(i):
        return i

    def back(i):
        return (i // groups) * groups + groups - 1 - i % groups

    def tokens(cols, order):
        return pl.BlockSpec((Q, cols), lambda i: (order(i), 0))

    def per_block(height, cols, order):
        return pl.BlockSpec((None, height, cols), lambda i: (order(i), 0, 0))

    def per_seq(height, cols):
        return pl.BlockSpec((None, height, cols), lambda i: (i // groups, 0, 0))

    def fixed(*shape):
        zeros = (0,) * len(shape)
        return pl.BlockSpec(shape, lambda i: zeros, pipeline_mode=pl.Buffered(1))

    def kept(*shape):
        zeros = (0,) * len(shape)
        return pl.BlockSpec(shape, lambda i: zeros)

    scalars = pl.BlockSpec(memory_space=pltpu.SMEM)
    flat_hidden = hidden.reshape(rows, width)
    flat_cot = cotangent.reshape(rows, width)

    (nrm, nrmt, cie, xh, xs, wx, bc, step, cum, dtb, cumt, sloc, pre, ends, totals, wc) = call(
        functools.partial(conv_kernel, groups),
        blocks,
        [
            (scalars, scal),
            (tokens(width, forth), flat_hidden),
            (per_block(RIM, width, forth), halo),
            (fixed(*ca.shape), ca),
            (fixed(*ca.shape), cb_pieces),
            (fixed(1, width), gain_in),
            (fixed(KW, CD), taps),
            (fixed(1, CD), bias),
            (fixed(1, HL), sb),
            (fixed(1, HL), rate_row),
            (fixed(HL, DI), e),
        ],
        [
            (tokens(width, forth), (rows, width), low),
            (pl.BlockSpec((width, Q), lambda i: (0, i)), (width, rows), low),
            (per_block(Q + RIM, CD, forth), (blocks, Q + RIM, CD), low),
            (tokens(DI, forth), (rows, DI), low),
            (tokens(DI, forth), (rows, DI), low),
            (tokens(DI, forth), (rows, DI), low),
            (tokens(2 * N, forth), (rows, 2 * N), low),
            (tokens(HL, forth), (rows, HL), f32),
            (tokens(HL, forth), (rows, HL), f32),
            (tokens(HL, forth), (rows, HL), f32),
            (per_block(H, Q, forth), (blocks, H, Q), f32),
            (per_block(N, DI, forth), (blocks, N, DI), f32),
            (per_block(8, DI, forth), (blocks, 8, DI), f32),
            (per_seq(N, DI), (seqs, N, DI), f32),
            (per_seq(8, DI), (seqs, 8, DI), f32),
            (kept(width, CW), (width, CW), low),
        ],
        [
            pltpu.VMEM((Q + RIM, width), low),
            pltpu.VMEM((Q + RIM, CH), f32),
            pltpu.VMEM((N, DI), f32),
            pltpu.VMEM((8, DI), f32),
        ],
        2.0 * rows * width * CW,
        "conv",
    )

    incoming = relay(ends, totals, True)

    (intra,) = call(
        intra_kernel,
        blocks,
        [
            (tokens(2 * N, forth), bc),
            (tokens(DI, forth), xs),
            (tokens(HL, forth), cum),
            (per_block(H, Q, forth), cumt),
        ],
        [(tokens(DI, forth), (rows, DI), f32)],
        [pltpu.VMEM((Q, Q), f32)],
        2.0 * rows * Q * DI * 2,
        "intra",
    )

    (z, dn, db, wz, wo) = call(
        functools.partial(project_kernel, groups),
        blocks,
        [
            (scalars, scal),
            (tokens(width, forth), nrm),
            (tokens(width, forth), flat_cot),
            (fixed(*za.shape), za),
            (fixed(*za.shape), zb),
        ],
        [
            (tokens(DI, forth), (rows, DI), f32),
            (tokens(DI, forth), (rows, DI), f32),
            (tokens(width, forth), (rows, width), low),
            (kept(width, DI), (width, DI), low),
            (kept(DI, width), (DI, width), low),
        ],
        [],
        4.0 * rows * width * DI,
        "project",
    )

    (out, dz, dy, gdy, gn, sbf, rs1, dloc, suf, back_ends, back_totals, gacc, kacc) = call(
        functools.partial(gate_kernel, groups),
        blocks,
        [
            (scalars, scal),
            (tokens(DI, back), intra),
            (tokens(DI, back), xh),
            (tokens(2 * N, back), bc),
            (tokens(HL, back), cum),
            (per_block(N, DI, back), sloc),
            (per_block(8, DI, back), pre),
            (per_seq(N, DI), incoming),
            (tokens(DI, back), z),
            (tokens(DI, back), dn),
            (tokens(width, back), flat_hidden),
            (fixed(DI, width), wo),
            (fixed(1, DI), gain_gate),
            (fixed(1, DI), skip),
            (fixed(HL, DI), e),
            (fixed(DI, HL), et),
        ],
        [
            (tokens(width, back), (rows, width), low),
            (tokens(DI, back), (rows, DI), low),
            (tokens(DI, back), (rows, DI), low),
            (tokens(DI, back), (rows, DI), low),
            (tokens(DI, back), (rows, DI), low),
            (per_block(N, DI, back), (blocks, N, DI), low),
            (tokens(HL, back), (rows, HL), f32),
            (per_block(N, DI, back), (blocks, N, DI), f32),
            (per_block(8, DI, back), (blocks, 8, DI), f32),
            (per_seq(N, DI), (seqs, N, DI), f32),
            (per_seq(8, DI), (seqs, 8, DI), f32),
            (kept(16, DI), (16, DI), f32),
            (kept(16, DI), (16, DI), f32),
        ],
        [
            pltpu.VMEM((Q, DI), f32),
            pltpu.VMEM((Q, DI), f32),
            pltpu.VMEM((Q, DI), f32),
            pltpu.VMEM((16, DI), f32),
            pltpu.VMEM((16, DI), f32),
            pltpu.VMEM((16, DI), f32),
            pltpu.VMEM((N, DI), f32),
            pltpu.VMEM((8, DI), f32),
        ],
        4.0 * rows * width * DI,
        "gate",
    )

    back_incoming = relay(back_ends, back_totals, False)

    (dx, dbc, rs2) = call(
        intra_back_kernel,
        blocks,
        [
            (tokens(2 * N, forth), bc),
            (tokens(DI, forth), xs),
            (tokens(DI, forth), xh),
            (tokens(DI, forth), dy),
            (tokens(HL, forth), step),
            (tokens(HL, forth), cum),
            (per_block(H, Q, forth), cumt),
            (fixed(1, DI), skip),
            (fixed(HL, DI), e),
            (fixed(DI, HL), et),
        ],
        [
            (tokens(DI, forth), (rows, DI), f32),
            (tokens(2 * N, forth), (rows, 2 * N), f32),
            (tokens(HL, forth), (rows, HL), f32),
        ],
        [pltpu.VMEM((Q, Q), f32), pltpu.VMEM((Q, Q), f32)],
        4.0 * rows * Q * DI * 2,
        "intra_back",
    )

    share = rows // 4
    piece = (PIECES // 2, 2, width // PIECES, DI)
    (e0, e1, dnz) = call(
        early_grad_kernel,
        4,
        [
            (scalars, scal),
            (fixed(width, rows), nrmt),
            (pl.BlockSpec((rows, DI // 4), lambda i: (0, i)), dz),
            (pl.BlockSpec((share, DI), lambda i: (i, 0)), dz),
            (pl.BlockSpec((rows, DI // 4), lambda i: (0, i)), gn),
            (fixed(rows, width), db),
            (fixed(width, DI), wz),
        ],
        [
            (kept(*piece), piece, low),
            (kept(*piece), piece, low),
            (pl.BlockSpec((share, width), lambda i: (i, 0)), (rows, width), f32),
        ],
        [pltpu.VMEM((width, DI // 4), f32), pltpu.VMEM((DI // 4, width), f32)],
        6.0 * rows * width * DI,
        "early_grad",
    )

    (dcv, cacc, hacc, heads_out, tails_out) = call(
        functools.partial(conv_back_kernel, groups),
        blocks,
        [
            (per_block(N, DI, back), dloc),
            (per_block(8, DI, back), suf),
            (per_seq(N, DI), back_incoming),
            (per_block(N, DI, back), sbf),
            (tokens(DI, back), xh),
            (tokens(DI, back), wx),
            (tokens(DI, back), gdy),
            (tokens(DI, back), dx),
            (tokens(2 * N, back), dbc),
            (tokens(2 * N, back), bc),
            (tokens(HL, back), cum),
            (tokens(HL, back), step),
            (tokens(HL, back), dtb),
            (tokens(HL, back), rs1),
            (tokens(HL, back), rs2),
            (per_block(Q + RIM, CD, back), cie),
            (fixed(KW, CD), taps),
            (fixed(1, CD), bias),
            (fixed(1, HL), rate_row),
            (fixed(HL, DI), e),
            (fixed(DI, HL), et),
        ],
        [
            (tokens(CW, back), (rows, CW), low),
            (kept(8 * (KW + 1), CD), (8 * (KW + 1), CD), f32),
            (kept(16, HL), (16, HL), f32),
            (per_seq(8, CD), (seqs, 8, CD), f32),
            (per_seq(16, CD), (seqs, 16, CD), f32),
        ],
        [
            pltpu.VMEM((Q + RIM, CH), f32),
            pltpu.VMEM((Q + 16, CH), f32),
            pltpu.VMEM((8, CD), f32),
        ],
        6.0 * rows * N * DI,
        "conv_back",
    )

    returned = lax.ppermute(
        heads_out.astype(low), "seq", [(i, i - 1) for i in range(1, seq_size)]
    ).astype(f32)
    fixed_tail = jnp.concatenate(
        [tails_out[:, :8], tails_out[:, 8:] + returned], axis=1
    ).astype(low)
    dcv = dcv.reshape(seqs, piece_len, CW)
    dcv = dcv.at[:, piece_len - 16 :, :CD].set(fixed_tail).reshape(rows, CW)

    late = (PIECES // 2, width // PIECES, CW)
    late_spec = pl.BlockSpec((PIECES // 2, width // PIECES, CW // 5), lambda i: (0, 0, i))
    (l0, l1) = call(
        late_grad_kernel,
        5,
        [
            (scalars, scal),
            (fixed(width, rows), nrmt),
            (pl.BlockSpec((rows, CW // 5), lambda i: (0, i)), dcv),
        ],
        [(late_spec, late, low), (late_spec, late, low)],
        [pltpu.VMEM((width, CW // 5), f32)],
        2.0 * rows * width * CW,
        "late_grad",
    )

    (gh, nacc) = call(
        input_kernel,
        blocks,
        [
            (tokens(CW, forth), dcv),
            (tokens(width, forth), dnz),
            (fixed(width, CW), wc),
            (tokens(width, forth), flat_hidden),
            (tokens(width, forth), flat_cot),
            (fixed(1, width), gain_in),
        ],
        [
            (tokens(width, forth), (rows, width), low),
            (kept(8, width), (8, width), f32),
        ],
        [pltpu.VMEM((Q, width), f32)],
        2.0 * rows * width * CW,
        "input",
    )

    conv_sums = cacc.reshape(KW + 1, 8, CD).sum(axis=1)
    skips = kacc.sum(axis=0).reshape(H, P_SIZE).sum(axis=1)
    scalar_sums = jnp.concatenate(
        [hacc[0:8].sum(axis=0)[:H], -hacc[8:16].sum(axis=0)[:H] * rate, skips]
    )
    vector = jnp.concatenate(
        [nacc.sum(axis=0), conv_sums.reshape(-1), gacc.sum(axis=0), scalar_sums]
    )
    if quick:
        length = vector.shape[0]
        vector = total_over(jnp.pad(vector, (0, -length % (8 * HALF))).reshape(-1, HALF))
        vector = vector.reshape(-1)[:length]
        early = unweave(e0, e1)
        own_late = unweave(l0, l1)
        own_z, own_out = early[0], early[1]
        own_out = jnp.concatenate([own_out[:, : DI // 2], own_out[:, DI // 2 :]], axis=0)
    else:
        vector = lax.psum(vector, axes)
        order = jnp.array(order_of_pieces(), jnp.int32)
        inverse = jnp.argsort(jnp.concatenate([order, order + 1]))
        whole = jnp.concatenate([e0, e1])[inverse].astype(f32)
        outs = whole[:, 1].reshape(PIECES, -1, 2, width).transpose(0, 2, 1, 3).reshape(DI, width)
        own_z = lax.psum_scatter(
            whole[:, 0].reshape(width, DI), axes, scatter_dimension=0, tiled=True
        )
        own_out = lax.psum_scatter(outs, axes, scatter_dimension=0, tiled=True)
        whole = jnp.concatenate([l0, l1])[inverse].astype(f32).reshape(width, CW)
        own_late = lax.psum_scatter(whole, axes, scatter_dimension=0, tiled=True)

    def own(value, size, axis):
        return lax.dynamic_slice_in_dim(value, place * size, size, axis)

    at = width
    g_norm = own(vector[:at], cuts[0], 0)
    g_taps = own(vector[at : at + KW * CD].reshape(KW, CD), CD // devices, 1)
    at += KW * CD
    g_bias = own(vector[at : at + CD], CD // devices, 0)
    at += CD
    g_gate = own(vector[at : at + DI], cuts[3], 0)
    at += DI
    g_in = jnp.concatenate([own_z, own_late[:, : CD + H]], axis=1)
    return (
        out.reshape(hidden.shape),
        gh.reshape(hidden.shape),
        g_norm,
        g_in,
        g_taps,
        g_bias,
        vector[at : at + H],
        vector[at + H : at + 2 * H],
        vector[at + 2 * H : at + 3 * H],
        g_gate,
        own_out,
    )


def solution(mesh):
    return jax.shard_map(
        per_device,
        mesh=mesh,
        in_specs=(
            P("dp", "seq", None),
            P("dp"),
            P(("dp", "seq")),
            P(("dp", "seq"), None),
            P(None, ("dp", "seq")),
            P(("dp", "seq")),
            P(),
            P(),
            P(),
            P(("dp", "seq")),
            P(("dp", "seq"), None),
            P("dp", "seq", None),
        ),
        out_specs=(
            P("dp", "seq", None),
            P("dp", "seq", None),
            P(("dp", "seq")),
            P(("dp", "seq"), None),
            P(None, ("dp", "seq")),
            P(("dp", "seq")),
            P(),
            P(),
            P(),
            P(("dp", "seq")),
            P(("dp", "seq"), None),
        ),
        check_vma=False,
    )
```

time: 772 us -> 360 us (0.47); the launches traced: 762 us -> 358 us
  matrix products: 187 us -> 0 us
  Pallas kernels: 0 us -> 163 us
  local copies, waits for them, and re-layouts: 152 us -> 18.5 us
  blocking collectives: 122 us -> 0 us
  other arithmetic: 138 us -> 30.3 us
  waiting for transfers between devices: 104 us -> 53 us
  starting transfers between devices: 43.3 us -> 92.4 us
  between operations: 15.2 us -> 1.31 us
    dot_general x43 -> x0, matrix products: 187 us -> none  [the longest x4 22 us: intra_backward(): jnp.einsum('qhp,rhp->hqr', grad_group, x_group, preferred_element_type=jn...]
    pallas_call x0 -> x9, Pallas kernels: none -> 163 us  [call(): pl.pallas_call(kernel, grid=(grid,), in_specs=in_specs, out_specs=out_spe...]
    unnamed x2 -> x0, blocking collectives: 81.3 us -> none
    unnamed x5 -> x0, waiting for transfers between devices: 72.6 us -> none
    ppermute x8 -> x50, starting transfers between devices: 43.2 us -> 92.4 us  [the longest x42 84 us: swap(): return lax.ppermute(value, axes, [(i, i ^ mask) for i in range(PIECES)])]
    reshape x11 -> x15, local copies, waits for them, and re-layouts: 50.7 us -> 4.93 us  [the longest x1 1.37 us: per_device(): g_taps = own(vector[at:at + KW * CD].reshape(KW, CD), CD // devices, 1)]
    all_gather x1 -> x0, blocking collectives: 40.5 us -> none  [per_device(): lax.all_gather(shards[2], ('dp', 'seq'), axis=1, tiled=True)]
    another operation x16 -> x14, other arithmetic: 43.8 us -> 5.73 us
  transfers between devices with their start and end apart: 12 -> 50, of which waited for: 5 -> 17; matrix products, arithmetic and copies ran while one was open for 46% -> 11% of each run, Pallas kernels for 0% -> 38%
where the time goes in v1:
time: 360 us; the launch traced here: 358 us
  Pallas kernels  163 us (45%)
  starting transfers between devices  92.4 us (26%)
  waiting for transfers between devices  53 us (15%)
  other arithmetic  30.3 us (8%)
  local copies, waits for them, and re-layouts  18.5 us (5%)
    pallas_call x9, Pallas kernels, call(): pl.pallas_call(kernel, grid=(grid,), in_specs=in_specs, out_specs=out_spe...  163 us
    ppermute x42, starting transfers between devices, swap(): return lax.ppermute(value, axes, [(i, i ^ mask) for i in range(PIECES)])  84 us
    ppermute x42, waiting for transfers between devices, swap(): return lax.ppermute(value, axes, [(i, i ^ mask) for i in range(PIECES)])  52.9 us
  transfers between devices with their start and end apart: 50, of which 17 were waited for; matrix products, arithmetic and copies ran while one was open for 11% of the time, Pallas kernels for 38%

profile of v1, /device:TPU:0, one launch (start us, length us, event | category | flops | bytes accessed | tf_op | source)
XLA Modules:
  0.0 358.4 jit_solution(16877285136644766948)
XLA Ops:
  1.7 3.1 collective-permute-start.1
  4.8 2.6 collective-permute-start.2
  11.1 3.5 collective-permute-start.9
  17.2 1.6 collective-permute-start.4
  18.8 1.5 collective-permute-start.5
  21.6 7.2 %collective-permute-done.4 = bf16[4,24,1920]{2,1,0:T(8,128)(2,1)S(1)} collective-permute-done((bf16[4,24,1920]{2,1,0:T(8,128)(2,1)S(1)}, bf16[4,24,1920]{2,1,0:T(8,128)(2,1)S(1)}, u32[]{:S(2)}, u32[]{:S(2)}) %collective-permute-start.4) | collective-permute-done | bytes 368672 | tf_op jit(solution)/shard_map/ppermute | solution.py:534
  28.9 6.5 %collective-permute-done.5 = bf16[4,24,1920]{2,1,0:T(8,128)(2,1)S(1)} collective-permute-done((bf16[4,24,1920]{2,1,0:T(8,128)(2,1)S(1)}, bf16[4,24,1920]{2,1,0:T(8,128)(2,1)S(1)}, u32[]{:S(2)}, u32[]{:S(2)}) %collective-permute-start.5) | collective-permute-done | bytes 368672 | tf_op jit(solution)/shard_map/ppermute | solution.py:534
  38.8 2.4 collective-permute-start.12
  41.2 1.4 collective-permute-start.13
  42.8 2.9 collective-permute-done.13
  48.6 3.5 collective-permute-start.20
  55.7 6.4 %collective-permute-done.19 = bf16[2,24,1536]{2,1,0:T(8,128)(2,1)S(1)} collective-permute-done((bf16[2,24,1536]{2,1,0:T(8,128)(2,1)S(1)}, bf16[2,24,1536]{2,1,0:T(8,128)(2,1)S(1)}, u32[]{:S(2)}, u32[]{:S(2)}) %collective-permute-start.19) | collective-permute-done | bytes 147488 | tf_op jit(solution)/shard_map/ppermute | solution.py:534
  62.1 2.0 collective-permute-start.21
  64.2 1.5 collective-permute-start.23
  65.7 21.2 %conv.1 = (bf16[1024,768]{1,0:T(8,128)(2,1)}, bf16[768,1024]{1,0:T(8,128)(2,1)}, bf16[4,272,1792]{2,1,0:T(8,128)(2,1)}, bf16[1024,1536]{1,0:T(8,128)(2,1)}, bf16...) custom-call(s32[4]{0:T(128)} %pad_add_fusion.scal, ...), custom_call_target="tpu_custom_call" | custom-call | flops 3019898880 | bytes 5053456 | tf_op jit(solution)/shard_map/conv/pallas_call | solution.py:518
  87.9 1.5 add_convert_fusion.5
  89.4 1.3 collective-permute-start.15
  90.8 1.7 pad_maximum_fusion
  94.9 2.1 fusion.6.et
  98.6 8.1 %intra.1 = f32[1024,1536]{1,0:T(8,128)} custom-call(bf16[1024,256]{1,0:T(8,128)(2,1)} %get-tuple-element.73.bc, bf16[1024,1536]{1,0:T(8,128)(2,1)} %get-tuple-element.74.xs, f32[1024,128]{1,0:T(8,128)} %get-tuple-element.75.cum, f32[4,24,256]{2,1,0:T(8,128)} %get-tuple-element.76.cumt), custom_call_target="tpu_custom_call" | custom-call | flops 1610612736 | bytes 4292608 | tf_op jit(solution)/shard_map/intra/pallas_call | solution.py:518
  106.7 12.7 %project.1 = (f32[1024,1536]{1,0:T(8,128)}, f32[1024,1536]{1,0:T(8,128)}, bf16[1024,768]{1,0:T(8,128)(2,1)}, bf16[768,1536]{1,0:T(8,128)(2,1)}, bf16[1536,768]{1,0:T(8,128)(2,1)}) custom-call(s32[4]{0:T(128)} %pad_add_fusion.scal, bf16[1024,768]{1,0:T(8,128)(2,1)} %get-tuple-element.82.nrm, bf16[1024,768]{1,0:T(8,128)(2,1)} %bitcast.131, ...), custom_call_target="tpu_custom_call" | custom-call | flops 4831838208 | bytes 7864336 | tf_op jit(solution)/shard_map/project/pallas_call | solution.py:518
  120.5 28.4 %gate.1 = (bf16[1024,768]{1,0:T(8,128)(2,1)}, bf16[1024,1536]{1,0:T(8,128)(2,1)}, bf16[1024,1536]{1,0:T(8,128)(2,1)}, bf16[1024,1536]{1,0:T(8,128)(2,1)}, bf16[1...) custom-call(s32[4]{0:T(128)} %pad_add_fusion.scal, ...), custom_call_target="tpu_custom_call" | custom-call | flops 4831838208 | bytes 31928336 | tf_op jit(solution)/shard_map/gate/pallas_call | solution.py:518
  150.0 1.5 add_convert_fusion.2
  155.3 1.5 collective-permute-start.27
  156.8 19.1 %early_grad.1 = (bf16[16,2,24,1536]{3,2,1,0:T(8,128)(2,1)}, bf16[16,2,24,1536]{3,2,1,0:T(8,128)(2,1)}, f32[1024,768]{1,0:T(8,128)}) custom-call(s32[4]{0:T(128)} %pad_add_fusion.scal, bf16[768,1024]{1,0:T(8,128)(2,1)} %get-tuple-element.106.nrmt, bf16[1024,1536]{1,0:T(8,128)(2,1)} %get-tuple-element.107.dz.dzr, ...), custom_call_target="tpu_custom_call" | custom-call | flops 7247757312 | bytes 14942224 | tf_op jit(solution)/shard_map/early_grad/pallas_call | solution.py:518
  175.9 28.5 %collective-permute-start.36 = (bf16[16,2,24,1536]{3,2,1,0:T(8,128)(2,1)}, bf16[16,2,24,1536]{3,2,1,0:T(8,128)(2,1)}, u32[]{:S(2)}, u32[]{:S(2)}) collective-permute-start(bf16[16,2,24,1536]{3,2,1,0:T(8,128)(2,1)} %get-tuple-element.120), channel_id=1, source_target_pairs={{0,1},{1,0},{2,3},{3,2},{4,5},{5,4},{6,7},{7,6},{8,9},{9,8},{10,11... | collective-permute-start | bytes 7077896 | tf_op jit(solution)/shard_map/ppermute | solution.py:534
  204.7 18.9 %intra_back.1 = (f32[1024,1536]{1,0:T(8,128)}, f32[1024,256]{1,0:T(8,128)}, f32[1024,128]{1,0:T(8,128)}) custom-call(bf16[1024,256]{1,0:T(8,128)(2,1)} %get-tuple-element.73.bc, bf16[1024,1536]{1,0:T(8,128)(2,1)} %get-tuple-element.74.xs, bf16[1024,1536]{1,0:T(8,128)(2,1)} %get-tuple-element.77.xh, bf16[1024,1536]{1,0:T(8,128)(2,1)} %get-tuple-element.95.dy, ...), custom_call_target="tpu_custom_call" | custom-call | flops 3221225472 | bytes 11900928 | tf_op jit(solution)/shard_map/intra_back/pallas_call | solution.py:518
  224.8 35.4 %conv_back.1 = (bf16[1024,1920]{1,0:T(8,128)(2,1)}, f32[40,1792]{1,0:T(8,128)}, f32[16,128]{1,0:T(8,128)}, f32[2,8,1792]{2,1,0:T(8,128)}, f32[2,16,1792]{2,1,0:T(8,128)}) custom-call(f32[4,128,1536]{2,1,0:T(8,128)} %get-tuple-element.88.dloc, f32[4,8,1536]{2,1,0:T(8,128)} %get-tuple-element.89.suf, bf16[2,128,1536]{2,1,0:T(8,128)(2,1)} %add_convert_fusion.inc, ...), custom_call_target="tpu_custom_call" | custom-call | flops 1207959552 | bytes 30346752 | tf_op jit(solution)/shard_map/conv_back/pallas_call | solution.py:518
  266.7 9.7 %input.1 = (bf16[1024,768]{1,0:T(8,128)(2,1)}, f32[8,768]{1,0:T(8,128)}) custom-call(bf16[1024,1920]{1,0:T(8,128)(2,1)} %bitcast.129, f32[1024,768]{1,0:T(8,128)} %get-tuple-element.111.dnz, bf16[768,1920]{1,0:T(8,128)(2,1)} %get-tuple-element.112.wc, bf16[1024,768]{1,0:T(8,128)(2,1)} %bitcast.127, bf16[1024,768]{1,0:T(8,128)(2,1)} %bitcast.132, ...), custom_call_target="tpu_custom_call" | custom-call | flops 3019898880 | bytes 13175808 | tf_op jit(solution)/shard_map/input/pallas_call | solution.py:518
  277.3 1.6 collective-permute-start.29
  278.9 2.6 convert_add_fusion
  282.4 2.7 collective-permute-start.32
  287.9 3.2 collective-permute-start.33
  291.1 2.4 collective-permute-start.35
  293.5 9.3 %late_grad.1 = (bf16[16,24,1920]{2,1,0:T(8,128)(2,1)}, bf16[16,24,1920]{2,1,0:T(8,128)(2,1)}) custom-call(s32[4]{0:T(128)} %pad_add_fusion.scal, bf16[768,1024]{1,0:T(8,128)(2,1)} %get-tuple-element.106.nrmt, bf16[1024,1920]{1,0:T(8,128)(2,1)} %bitcast.130), custom_call_target="tpu_custom_call" | custom-call | flops 3019898880 | bytes 5505040 | tf_op jit(solution)/shard_map/late_grad/pallas_call | solution.py:518
  302.8 2.2 collective-permute-start.39
  305.7 11.1 %collective-permute-done.39 = bf16[4,2,24,1536]{3,2,1,0:T(8,128)(2,1)S(1)} collective-permute-done((bf16[4,2,24,1536]{3,2,1,0:T(8,128)(2,1)S(1)}, bf16[4,2,24,1536]{3,2,1,0:T(8,128)(2,1)S(1)}, u32[]{:S(2)}, u32[]{:S(2)}) %collective-permute-start.39) | collective-permute-done | bytes 589856 | tf_op jit(solution)/shard_map/ppermute | solution.py:534
  319.2 2.4 collective-permute-start.42
  322.8 1.4 reshape.242
  328.9 1.7 convert_add_fusion.1
  331.1 1.5 collective-permute-start.45
  332.6 1.7 collective-permute-start.46
  335.0 5.4 %collective-permute-done.44 = bf16[4,24,1920]{2,1,0:T(8,128)(2,1)S(1)} collective-permute-done((bf16[4,24,1920]{2,1,0:T(8,128)(2,1)S(1)}, bf16[4,24,1920]{2,1,0:T(8,128)(2,1)S(1)}, u32[]{:S(2)}, u32[]{:S(2)}) %collective-permute-start.44) | collective-permute-done | bytes 368672 | tf_op jit(solution)/shard_map/ppermute | solution.py:534
  341.2 3.9 %collective-permute-done.46 = bf16[4,24,1920]{2,1,0:T(8,128)(2,1)S(1)} collective-permute-done((bf16[4,24,1920]{2,1,0:T(8,128)(2,1)S(1)}, bf16[4,24,1920]{2,1,0:T(8,128)(2,1)S(1)}, u32[]{:S(2)}, u32[]{:S(2)}) %collective-permute-start.46) | collective-permute-done | bytes 368672 | tf_op jit(solution)/shard_map/ppermute | solution.py:534
  345.3 5.1 %collective-permute-start.47 = (bf16[24,1920]{1,0:T(8,128)(2,1)S(1)}, bf16[24,1920]{1,0:T(8,128)(2,1)S(1)}, u32[]{:S(2)}, u32[]{:S(2)}) collective-permute-start(bf16[24,1920]{1,0:T(8,128)(2,1)S(1)} %get-tuple-element.144), channel_id=1, source_target_pairs={{0,8},{1,9},{2,10},{3,11},{4,12},{5,13},{6,14},{7,15},{8,0},{9,1},... | collective-permute-start | bytes 276488 | tf_op jit(solution)/shard_map/ppermute | solution.py:534
  350.6 2.3 collective-permute-start.49
  352.9 1.7 collective-permute-done.47
  354.6 3.0 collective-permute-done.48
  (193 shorter events, 54.0 us)
Async XLA Ops:
  1.7 15.4 %collective-permute-start.1 = (bf16[24,1920]{1,0:T(8,128)(2,1)S(1)}, bf16[24,1920]{1,0:T(8,128)(2,1)S(1)}, u32[]{:S(2)}, u32[]{:S(2)}) collective-permute-start(bf16[24,1920]{1,0:T(8,128)(2,1)S(1)} %get-tuple-element.154), channel_id=1, source_target_pairs={{0,8},{1,9},{2,10},{3,11},{4,12},{5,13},{6,14},{7,15},{8,0},{9,1},... | collective-permute-start | bytes 276488 | tf_op jit(solution)/shard_map/ppermute | solution.py:534
  4.8 12.4 %collective-permute-start.2 = (bf16[24,1920]{1,0:T(8,128)(2,1)S(1)}, bf16[24,1920]{1,0:T(8,128)(2,1)S(1)}, u32[]{:S(2)}, u32[]{:S(2)}) collective-permute-start(bf16[24,1920]{1,0:T(8,128)(2,1)S(1)} %get-tuple-element.154), channel_id=1, source_target_pairs={{0,16},{1,17},{2,18},{3,19},{4,20},{5,21},{6,22},{7,23},{8,24},{9,... | collective-permute-start | bytes 276488 | tf_op jit(solution)/shard_map/ppermute | solution.py:534
  7.4 9.8 %collective-permute-start.3 = (bf16[24,1920]{1,0:T(8,128)(2,1)S(1)}, bf16[24,1920]{1,0:T(8,128)(2,1)S(1)}, u32[]{:S(2)}, u32[]{:S(2)}) collective-permute-start(bf16[24,1920]{1,0:T(8,128)(2,1)S(1)} %get-tuple-element.154), channel_id=1, source_target_pairs={{0,24},{1,25},{2,26},{3,27},{4,28},{5,29},{6,30},{7,31},{8,16},{9,... | collective-permute-start | bytes 276488 | tf_op jit(solution)/shard_map/ppermute | solution.py:534
  10.2 28.5 %collective-permute-start.8 = (bf16[1,384]{1,0:T(2,128)(2,1)S(1)}, bf16[1,384]{1,0:T(2,128)(2,1)S(1)}, u32[]{:S(2)}, u32[]{:S(2)}) collective-permute-start(bf16[1,384]{1,0:T(2,128)(2,1)S(1)} %reshape.221), channel_id=1, source_target_pairs={{0,8},{1,9},{2,10},{3,11},{4,12},{5,13},{6,14},{7,15},{8,0},{9,1},... | collective-permute-start | bytes 2312 | tf_op jit(solution)/shard_map/ppermute | solution.py:534
  11.1 27.6 %collective-permute-start.9 = (bf16[1,384]{1,0:T(2,128)(2,1)S(1)}, bf16[1,384]{1,0:T(2,128)(2,1)S(1)}, u32[]{:S(2)}, u32[]{:S(2)}) collective-permute-start(bf16[1,384]{1,0:T(2,128)(2,1)S(1)} %reshape.221), channel_id=1, source_target_pairs={{0,16},{1,17},{2,18},{3,19},{4,20},{5,21},{6,22},{7,23},{8,24},{9,... | collective-permute-start | bytes 2312 | tf_op jit(solution)/shard_map/ppermute | solution.py:534
  17.2 11.6 %collective-permute-start.4 = (bf16[4,24,1920]{2,1,0:T(8,128)(2,1)S(1)}, bf16[4,24,1920]{2,1,0:T(8,128)(2,1)S(1)}, u32[]{:S(2)}, u32[]{:S(2)}) collective-permute-start(bf16[4,24,1920]{2,1,0:T(8,128)(2,1)S(1)} %get-tuple-element.148), channel_id=1, source_target_pairs={{0,2},{1,3},{2,0},{3,1},{4,6},{5,7},{6,4},{7,5},{8,10},{9,11},{10,... | collective-permute-start | bytes 1105928 | tf_op jit(solution)/shard_map/ppermute | solution.py:534
  18.8 16.5 %collective-permute-start.5 = (bf16[4,24,1920]{2,1,0:T(8,128)(2,1)S(1)}, bf16[4,24,1920]{2,1,0:T(8,128)(2,1)S(1)}, u32[]{:S(2)}, u32[]{:S(2)}) collective-permute-start(bf16[4,24,1920]{2,1,0:T(8,128)(2,1)S(1)} %get-tuple-element.148), channel_id=1, source_target_pairs={{0,4},{1,5},{2,6},{3,7},{4,0},{5,1},{6,2},{7,3},{8,12},{9,13},{10,... | collective-permute-start | bytes 1105928 | tf_op jit(solution)/shard_map/ppermute | solution.py:534
  20.3 16.3 %collective-permute-start.6 = (bf16[4,24,1920]{2,1,0:T(8,128)(2,1)S(1)}, bf16[4,24,1920]{2,1,0:T(8,128)(2,1)S(1)}, u32[]{:S(2)}, u32[]{:S(2)}) collective-permute-start(bf16[4,24,1920]{2,1,0:T(8,128)(2,1)S(1)} %get-tuple-element.148), channel_id=1, source_target_pairs={{0,6},{1,7},{2,4},{3,5},{4,2},{5,3},{6,0},{7,1},{8,14},{9,15},{10,... | collective-permute-start | bytes 1105928 | tf_op jit(solution)/shard_map/ppermute | solution.py:534
  28.8 9.9 %collective-permute-start.10 = (bf16[1,384]{1,0:T(2,128)(2,1)S(1)}, bf16[1,384]{1,0:T(2,128)(2,1)S(1)}, u32[]{:S(2)}, u32[]{:S(2)}) collective-permute-start(bf16[1,384]{1,0:T(2,128)(2,1)S(1)} %reshape.221), channel_id=1, source_target_pairs={{0,24},{1,25},{2,26},{3,27},{4,28},{5,29},{6,30},{7,31},{8,16},{9,... | collective-permute-start | bytes 2312 | tf_op jit(solution)/shard_map/ppermute | solution.py:534
  35.3 19.1 %collective-permute-start = (bf16[2,16,768]{2,1,0:T(8,128)(2,1)S(1)}, bf16[2,16,768]{2,1,0:T(8,128)(2,1)S(1)}, u32[]{:S(2)}, u32[]{:S(2)}) collective-permute-start(bf16[2,16,768]{2,1,0:T(8,128)(2,1)S(1)} %slice.200), channel_id=1, source_target_pairs={{0,1},{1,2},{2,3},{4,5},{5,6},{6,7},{8,9},{9,10},{10,11},{12,13},{... | collective-permute-start | bytes 147464 | tf_op jit(solution)/shard_map/ppermute | solution.py:611
  36.9 28.8 %collective-permute-start.7 = (bf16[4,4,24,1920]{3,2,1,0:T(8,128)(2,1)S(1)}, bf16[4,4,24,1920]{3,2,1,0:T(8,128)(2,1)}, u32[]{:S(2)}, u32[]{:S(2)}) collective-permute-start(bf16[4,4,24,1920]{3,2,1,0:T(8,128)(2,1)S(1)} %pad_maximum_fusion.1), channel_id=1, source_target_pairs={{0,1},{1,0},{2,3},{3,2},{4,5},{5,4},{6,7},{7,6},{8,9},{9,8},{10,11... | collective-permute-start | bytes 4423688 | tf_op jit(solution)/shard_map/ppermute | solution.py:534
  38.7 3.9 %collective-permute-start.11 = (bf16[4,1,384]{2,0,1:T(4,128)(2,1)S(1)}, bf16[4,1,384]{2,0,1:T(4,128)(2,1)S(1)}, u32[]{:S(2)}, u32[]{:S(2)}) collective-permute-start(bf16[4,1,384]{2,0,1:T(4,128)(2,1)S(1)} %pad_maximum_fusion.9), channel_id=1, source_target_pairs={{0,2},{1,3},{2,0},{3,1},{4,6},{5,7},{6,4},{7,5},{8,10},{9,11},{10,... | collective-permute-start | bytes 9224 | tf_op jit(solution)/shard_map/ppermute | solution.py:534
  38.8 4.0 %collective-permute-start.12 = (bf16[4,1,384]{2,0,1:T(4,128)(2,1)S(1)}, bf16[4,1,384]{2,0,1:T(4,128)(2,1)S(1)}, u32[]{:S(2)}, u32[]{:S(2)}) collective-permute-start(bf16[4,1,384]{2,0,1:T(4,128)(2,1)S(1)} %pad_maximum_fusion.9), channel_id=1, source_target_pairs={{0,4},{1,5},{2,6},{3,7},{4,0},{5,1},{6,2},{7,3},{8,12},{9,13},{10,... | collective-permute-start | bytes 9224 | tf_op jit(solution)/shard_map/ppermute | solution.py:534
  41.2 4.5 %collective-permute-start.13 = (bf16[4,1,384]{2,0,1:T(4,128)(2,1)S(1)}, bf16[4,1,384]{2,0,1:T(4,128)(2,1)S(1)}, u32[]{:S(2)}, u32[]{:S(2)}) collective-permute-start(bf16[4,1,384]{2,0,1:T(4,128)(2,1)S(1)} %pad_maximum_fusion.9), channel_id=1, source_target_pairs={{0,6},{1,7},{2,4},{3,5},{4,2},{5,3},{6,0},{7,1},{8,14},{9,15},{10,... | collective-permute-start | bytes 9224 | tf_op jit(solution)/shard_map/ppermute | solution.py:534
  45.8 1.2 collective-permute-start.14
  47.7 8.0 %collective-permute-start.18 = (bf16[2,24,1536]{2,1,0:T(8,128)(2,1)S(1)}, bf16[2,24,1536]{2,1,0:T(8,128)(2,1)S(1)}, u32[]{:S(2)}, u32[]{:S(2)}) collective-permute-start(bf16[2,24,1536]{2,1,0:T(8,128)(2,1)S(1)} %pad_maximum_fusion.5), channel_id=1, source_target_pairs={{0,8},{1,9},{2,10},{3,11},{4,12},{5,13},{6,14},{7,15},{8,0},{9,1},... | collective-permute-start | bytes 442376 | tf_op jit(solution)/shard_map/ppermute | solution.py:534
  48.1 14.0 %collective-permute-start.19 = (bf16[2,24,1536]{2,1,0:T(8,128)(2,1)S(1)}, bf16[2,24,1536]{2,1,0:T(8,128)(2,1)S(1)}, u32[]{:S(2)}, u32[]{:S(2)}) collective-permute-start(bf16[2,24,1536]{2,1,0:T(8,128)(2,1)S(1)} %pad_maximum_fusion.5), channel_id=1, source_target_pairs={{0,16},{1,17},{2,18},{3,19},{4,20},{5,21},{6,22},{7,23},{8,24},{9,... | collective-permute-start | bytes 442376 | tf_op jit(solution)/shard_map/ppermute | solution.py:534
  48.6 13.5 %collective-permute-start.20 = (bf16[2,24,1536]{2,1,0:T(8,128)(2,1)S(1)}, bf16[2,24,1536]{2,1,0:T(8,128)(2,1)S(1)}, u32[]{:S(2)}, u32[]{:S(2)}) collective-permute-start(bf16[2,24,1536]{2,1,0:T(8,128)(2,1)S(1)} %pad_maximum_fusion.5), channel_id=1, source_target_pairs={{0,24},{1,25},{2,26},{3,27},{4,28},{5,29},{6,30},{7,31},{8,16},{9,... | collective-permute-start | bytes 442376 | tf_op jit(solution)/shard_map/ppermute | solution.py:534
  62.1 28.6 %collective-permute-start.21 = (bf16[4,2,24,1536]{3,2,1,0:T(8,128)(2,1)S(1)}, bf16[4,2,24,1536]{3,2,1,0:T(8,128)(2,1)S(1)}, u32[]{:S(2)}, u32[]{:S(2)}) collective-permute-start(bf16[4,2,24,1536]{3,2,1,0:T(8,128)(2,1)S(1)} %get-tuple-element.143), channel_id=1, source_target_pairs={{0,2},{1,3},{2,0},{3,1},{4,6},{5,7},{6,4},{7,5},{8,10},{9,11},{10,... | collective-permute-start | bytes 1769480 | tf_op jit(solution)/shard_map/ppermute | solution.py:534
  64.2 26.6 %collective-permute-start.22 = (bf16[4,2,24,1536]{3,2,1,0:T(8,128)(2,1)S(1)}, bf16[4,2,24,1536]{3,2,1,0:T(8,128)(2,1)S(1)}, u32[]{:S(2)}, u32[]{:S(2)}) collective-permute-start(bf16[4,2,24,1536]{3,2,1,0:T(8,128)(2,1)S(1)} %get-tuple-element.143), channel_id=1, source_target_pairs={{0,4},{1,5},{2,6},{3,7},{4,0},{5,1},{6,2},{7,3},{8,12},{9,13},{10,... | collective-permute-start | bytes 1769480 | tf_op jit(solution)/shard_map/ppermute | solution.py:534
  64.2 26.6 %collective-permute-start.23 = (bf16[4,2,24,1536]{3,2,1,0:T(8,128)(2,1)S(1)}, bf16[4,2,24,1536]{3,2,1,0:T(8,128)(2,1)S(1)}, u32[]{:S(2)}, u32[]{:S(2)}) collective-permute-start(bf16[4,2,24,1536]{3,2,1,0:T(8,128)(2,1)S(1)} %get-tuple-element.143), channel_id=1, source_target_pairs={{0,6},{1,7},{2,4},{3,5},{4,2},{5,3},{6,0},{7,1},{8,14},{9,15},{10,... | collective-permute-start | bytes 1769480 | tf_op jit(solution)/shard_map/ppermute | solution.py:534
  89.4 3.2 collective-permute-start.15
  92.5 14.2 %collective-permute-start.24 = (bf16[4,4,2,24,1536]{4,3,2,1,0:T(8,128)(2,1)}, bf16[4,4,2,24,1536]{4,3,2,1,0:T(8,128)(2,1)}, u32[]{:S(2)}, u32[]{:S(2)}) collective-permute-start(bf16[4,4,2,24,1536]{4,3,2,1,0:T(8,128)(2,1)} %pad_maximum_fusion), channel_id=1, source_target_pairs={{0,1},{1,0},{2,3},{3,2},{4,5},{5,4},{6,7},{7,6},{8,9},{9,8},{10,11... | collective-permute-start | bytes 7077896 | tf_op jit(solution)/shard_map/ppermute | solution.py:534
  94.0 25.4 %collective-permute-start.17 = (bf16[2,128,1536]{2,1,0:T(8,128)(2,1)S(1)}, bf16[2,128,1536]{2,1,0:T(8,128)(2,1)S(1)}, u32[]{:S(2)}, u32[]{:S(2)}) collective-permute-start(bf16[2,128,1536]{2,1,0:T(8,128)(2,1)S(1)} %add_convert_fusion.4), channel_id=1, source_target_pairs={{2,3},{6,7},{10,11},{14,15},{18,19},{22,23},{26,27},{30,31}} | collective-permute-start | bytes 2359304 | tf_op jit(solution)/shard_map/ppermute | solution.py:580
  151.5 0.7 collective-permute-start.25
  155.3 68.3 %collective-permute-start.27 = (bf16[2,128,1536]{2,1,0:T(8,128)(2,1)}, bf16[2,128,1536]{2,1,0:T(8,128)(2,1)S(1)}, u32[]{:S(2)}, u32[]{:S(2)}) collective-permute-start(bf16[2,128,1536]{2,1,0:T(8,128)(2,1)} %add_convert_fusion.1), channel_id=1, source_target_pairs={{1,0},{5,4},{9,8},{13,12},{17,16},{21,20},{25,24},{29,28}} | collective-permute-start | bytes 2359304 | tf_op jit(solution)/shard_map/ppermute | solution.py:580
  175.9 103.0 %collective-permute-start.36 = (bf16[16,2,24,1536]{3,2,1,0:T(8,128)(2,1)}, bf16[16,2,24,1536]{3,2,1,0:T(8,128)(2,1)}, u32[]{:S(2)}, u32[]{:S(2)}) collective-permute-start(bf16[16,2,24,1536]{3,2,1,0:T(8,128)(2,1)} %get-tuple-element.120), channel_id=1, source_target_pairs={{0,1},{1,0},{2,3},{3,2},{4,5},{5,4},{6,7},{7,6},{8,9},{9,8},{10,11... | collective-permute-start | bytes 7077896 | tf_op jit(solution)/shard_map/ppermute | solution.py:534
  261.2 4.0 %collective-permute-start.28 = (bf16[2,8,1792]{2,1,0:T(8,128)(2,1)S(1)}, bf16[2,8,1792]{2,1,0:T(8,128)(2,1)S(1)}, u32[]{:S(2)}, u32[]{:S(2)}) collective-permute-start(bf16[2,8,1792]{2,1,0:T(8,128)(2,1)S(1)} %convert_element_type.167), channel_id=1, source_target_pairs={{1,0},{2,1},{3,2},{5,4},{6,5},{7,6},{9,8},{10,9},{11,10},{13,12},{... | collective-permute-start | bytes 172040 | tf_op jit(solution)/shard_map/ppermute | solution.py:914
  277.3 4.2 %collective-permute-start.29 = (f32[96,128]{1,0:T(8,128)S(1)}, f32[96,128]{1,0:T(8,128)S(1)}, u32[]{:S(2)}, u32[]{:S(2)}) collective-permute-start(f32[96,128]{1,0:T(8,128)S(1)} %pad_bitcast_fusion), channel_id=1, source_target_pairs={{0,1},{1,0},{2,3},{3,2},{4,5},{5,4},{6,7},{7,6},{8,9},{9,8},{10,11... | collective-permute-start | bytes 147464 | tf_op jit(solution)/shard_map/ppermute | solution.py:534
  281.5 4.5 %collective-permute-start.30 = (f32[96,128]{1,0:T(8,128)S(1)}, f32[96,128]{1,0:T(8,128)S(1)}, u32[]{:S(2)}, u32[]{:S(2)}) collective-permute-start(f32[96,128]{1,0:T(8,128)S(1)} %fusion.23), channel_id=1, source_target_pairs={{0,2},{1,3},{2,0},{3,1},{4,6},{5,7},{6,4},{7,5},{8,10},{9,11},{10,... | collective-permute-start | bytes 147464 | tf_op jit(solution)/shard_map/ppermute | solution.py:534
  282.3 4.8 %collective-permute-start.31 = (f32[96,128]{1,0:T(8,128)S(1)}, f32[96,128]{1,0:T(8,128)S(1)}, u32[]{:S(2)}, u32[]{:S(2)}) collective-permute-start(f32[96,128]{1,0:T(8,128)S(1)} %fusion.23), channel_id=1, source_target_pairs={{0,4},{1,5},{2,6},{3,7},{4,0},{5,1},{6,2},{7,3},{8,12},{9,13},{10,... | collective-permute-start | bytes 147464 | tf_op jit(solution)/shard_map/ppermute | solution.py:534
  282.4 5.5 %collective-permute-start.32 = (f32[96,128]{1,0:T(8,128)S(1)}, f32[96,128]{1,0:T(8,128)S(1)}, u32[]{:S(2)}, u32[]{:S(2)}) collective-permute-start(f32[96,128]{1,0:T(8,128)S(1)} %fusion.23), channel_id=1, source_target_pairs={{0,6},{1,7},{2,4},{3,5},{4,2},{5,3},{6,0},{7,1},{8,14},{9,15},{10,... | collective-permute-start | bytes 147464 | tf_op jit(solution)/shard_map/ppermute | solution.py:534
  285.2 20.4 %collective-permute-start.37 = (bf16[4,2,24,1536]{3,2,1,0:T(8,128)(2,1)S(1)}, bf16[4,2,24,1536]{3,2,1,0:T(8,128)(2,1)S(1)}, u32[]{:S(2)}, u32[]{:S(2)}) collective-permute-start(bf16[4,2,24,1536]{3,2,1,0:T(8,128)(2,1)S(1)} %get-tuple-element.133), channel_id=1, source_target_pairs={{0,2},{1,3},{2,0},{3,1},{4,6},{5,7},{6,4},{7,5},{8,10},{9,11},{10,... | collective-permute-start | bytes 1769480 | tf_op jit(solution)/shard_map/ppermute | solution.py:534
  286.0 19.6 %collective-permute-start.38 = (bf16[4,2,24,1536]{3,2,1,0:T(8,128)(2,1)S(1)}, bf16[4,2,24,1536]{3,2,1,0:T(8,128)(2,1)S(1)}, u32[]{:S(2)}, u32[]{:S(2)}) collective-permute-start(bf16[4,2,24,1536]{3,2,1,0:T(8,128)(2,1)S(1)} %get-tuple-element.135), channel_id=1, source_target_pairs={{0,4},{1,5},{2,6},{3,7},{4,0},{5,1},{6,2},{7,3},{8,12},{9,13},{10,... | collective-permute-start | bytes 1769480 | tf_op jit(solution)/shard_map/ppermute | solution.py:534
  287.9 15.0 %collective-permute-start.33 = (f32[96,128]{1,0:T(8,128)S(1)}, f32[96,128]{1,0:T(8,128)S(1)}, u32[]{:S(2)}, u32[]{:S(2)}) collective-permute-start(f32[96,128]{1,0:T(8,128)S(1)} %add_add_fusion.1), channel_id=1, source_target_pairs={{0,8},{1,9},{2,10},{3,11},{4,12},{5,13},{6,14},{7,15},{8,0},{9,1},... | collective-permute-start | bytes 147464 | tf_op jit(solution)/shard_map/ppermute | solution.py:534
  291.1 14.0 %collective-permute-start.34 = (f32[96,128]{1,0:T(8,128)S(1)}, f32[96,128]{1,0:T(8,128)S(1)}, u32[]{:S(2)}, u32[]{:S(2)}) collective-permute-start(f32[96,128]{1,0:T(8,128)S(1)} %add_add_fusion.1), channel_id=1, source_target_pairs={{0,16},{1,17},{2,18},{3,19},{4,20},{5,21},{6,22},{7,23},{8,24},{9,... | collective-permute-start | bytes 147464 | tf_op jit(solution)/shard_map/ppermute | solution.py:534
  291.1 13.9 %collective-permute-start.35 = (f32[96,128]{1,0:T(8,128)S(1)}, f32[96,128]{1,0:T(8,128)S(1)}, u32[]{:S(2)}, u32[]{:S(2)}) collective-permute-start(f32[96,128]{1,0:T(8,128)S(1)} %add_add_fusion.1), channel_id=1, source_target_pairs={{0,24},{1,25},{2,26},{3,27},{4,28},{5,29},{6,30},{7,31},{8,16},{9,... | collective-permute-start | bytes 147464 | tf_op jit(solution)/shard_map/ppermute | solution.py:534
  302.8 13.9 %collective-permute-start.39 = (bf16[4,2,24,1536]{3,2,1,0:T(8,128)(2,1)S(1)}, bf16[4,2,24,1536]{3,2,1,0:T(8,128)(2,1)S(1)}, u32[]{:S(2)}, u32[]{:S(2)}) collective-permute-start(bf16[4,2,24,1536]{3,2,1,0:T(8,128)(2,1)S(1)} %get-tuple-element.134), channel_id=1, source_target_pairs={{0,6},{1,7},{2,4},{3,5},{4,2},{5,3},{6,0},{7,1},{8,14},{9,15},{10,... | collective-permute-start | bytes 1769480 | tf_op jit(solution)/shard_map/ppermute | solution.py:534
  305.0 23.9 %collective-permute-start.43 = (bf16[16,24,1920]{2,1,0:T(8,128)(2,1)}, bf16[16,24,1920]{2,1,0:T(8,128)(2,1)}, u32[]{:S(2)}, u32[]{:S(2)}) collective-permute-start(bf16[16,24,1920]{2,1,0:T(8,128)(2,1)} %get-tuple-element.122), channel_id=1, source_target_pairs={{0,1},{1,0},{2,3},{3,2},{4,5},{5,4},{6,7},{7,6},{8,9},{9,8},{10,11... | collective-permute-start | bytes 4423688 | tf_op jit(solution)/shard_map/ppermute | solution.py:534
  317.1 10.8 %collective-permute-start.40 = (bf16[2,24,1536]{2,1,0:T(8,128)(2,1)S(1)}, bf16[2,24,1536]{2,1,0:T(8,128)(2,1)S(1)}, u32[]{:S(2)}, u32[]{:S(2)}) collective-permute-start(bf16[2,24,1536]{2,1,0:T(8,128)(2,1)S(1)} %get-tuple-element.139), channel_id=1, source_target_pairs={{0,8},{1,9},{2,10},{3,11},{4,12},{5,13},{6,14},{7,15},{8,0},{9,1},... | collective-permute-start | bytes 442376 | tf_op jit(solution)/shard_map/ppermute | solution.py:534
  318.0 10.9 %collective-permute-start.41 = (bf16[2,24,1536]{2,1,0:T(8,128)(2,1)S(1)}, bf16[2,24,1536]{2,1,0:T(8,128)(2,1)S(1)}, u32[]{:S(2)}, u32[]{:S(2)}) collective-permute-start(bf16[2,24,1536]{2,1,0:T(8,128)(2,1)S(1)} %get-tuple-element.141), channel_id=1, source_target_pairs={{0,16},{1,17},{2,18},{3,19},{4,20},{5,21},{6,22},{7,23},{8,24},{9,... | collective-permute-start | bytes 442376 | tf_op jit(solution)/shard_map/ppermute | solution.py:534
  319.2 9.6 %collective-permute-start.42 = (bf16[2,24,1536]{2,1,0:T(8,128)(2,1)S(1)}, bf16[2,24,1536]{2,1,0:T(8,128)(2,1)S(1)}, u32[]{:S(2)}, u32[]{:S(2)}) collective-permute-start(bf16[2,24,1536]{2,1,0:T(8,128)(2,1)S(1)} %get-tuple-element.140), channel_id=1, source_target_pairs={{0,24},{1,25},{2,26},{3,27},{4,28},{5,29},{6,30},{7,31},{8,16},{9,... | collective-permute-start | bytes 442376 | tf_op jit(solution)/shard_map/ppermute | solution.py:534
  330.7 9.6 %collective-permute-start.44 = (bf16[4,24,1920]{2,1,0:T(8,128)(2,1)S(1)}, bf16[4,24,1920]{2,1,0:T(8,128)(2,1)S(1)}, u32[]{:S(2)}, u32[]{:S(2)}) collective-permute-start(bf16[4,24,1920]{2,1,0:T(8,128)(2,1)S(1)} %get-tuple-element.136), channel_id=1, source_target_pairs={{0,2},{1,3},{2,0},{3,1},{4,6},{5,7},{6,4},{7,5},{8,10},{9,11},{10,... | collective-permute-start | bytes 1105928 | tf_op jit(solution)/shard_map/ppermute | solution.py:534
  331.1 10.1 %collective-permute-start.45 = (bf16[4,24,1920]{2,1,0:T(8,128)(2,1)S(1)}, bf16[4,24,1920]{2,1,0:T(8,128)(2,1)S(1)}, u32[]{:S(2)}, u32[]{:S(2)}) collective-permute-start(bf16[4,24,1920]{2,1,0:T(8,128)(2,1)S(1)} %get-tuple-element.138), channel_id=1, source_target_pairs={{0,4},{1,5},{2,6},{3,7},{4,0},{5,1},{6,2},{7,3},{8,12},{9,13},{10,... | collective-permute-start | bytes 1105928 | tf_op jit(solution)/shard_map/ppermute | solution.py:534
  332.6 12.5 %collective-permute-start.46 = (bf16[4,24,1920]{2,1,0:T(8,128)(2,1)S(1)}, bf16[4,24,1920]{2,1,0:T(8,128)(2,1)S(1)}, u32[]{:S(2)}, u32[]{:S(2)}) collective-permute-start(bf16[4,24,1920]{2,1,0:T(8,128)(2,1)S(1)} %get-tuple-element.137), channel_id=1, source_target_pairs={{0,6},{1,7},{2,4},{3,5},{4,2},{5,3},{6,0},{7,1},{8,14},{9,15},{10,... | collective-permute-start | bytes 1105928 | tf_op jit(solution)/shard_map/ppermute | solution.py:534
  345.3 9.3 %collective-permute-start.47 = (bf16[24,1920]{1,0:T(8,128)(2,1)S(1)}, bf16[24,1920]{1,0:T(8,128)(2,1)S(1)}, u32[]{:S(2)}, u32[]{:S(2)}) collective-permute-start(bf16[24,1920]{1,0:T(8,128)(2,1)S(1)} %get-tuple-element.144), channel_id=1, source_target_pairs={{0,8},{1,9},{2,10},{3,11},{4,12},{5,13},{6,14},{7,15},{8,0},{9,1},... | collective-permute-start | bytes 276488 | tf_op jit(solution)/shard_map/ppermute | solution.py:534
  350.5 7.1 %collective-permute-start.48 = (bf16[24,1920]{1,0:T(8,128)(2,1)S(1)}, bf16[24,1920]{1,0:T(8,128)(2,1)S(1)}, u32[]{:S(2)}, u32[]{:S(2)}) collective-permute-start(bf16[24,1920]{1,0:T(8,128)(2,1)S(1)} %get-tuple-element.146), channel_id=1, source_target_pairs={{0,16},{1,17},{2,18},{3,19},{4,20},{5,21},{6,22},{7,23},{8,24},{9,... | collective-permute-start | bytes 276488 | tf_op jit(solution)/shard_map/ppermute | solution.py:534
  350.6 7.0 %collective-permute-start.49 = (bf16[24,1920]{1,0:T(8,128)(2,1)S(1)}, bf16[24,1920]{1,0:T(8,128)(2,1)S(1)}, u32[]{:S(2)}, u32[]{:S(2)}) collective-permute-start(bf16[24,1920]{1,0:T(8,128)(2,1)S(1)} %get-tuple-element.145), channel_id=1, source_target_pairs={{0,24},{1,25},{2,26},{3,27},{4,28},{5,29},{6,30},{7,31},{8,16},{9,... | collective-permute-start | bytes 276488 | tf_op jit(solution)/shard_map/ppermute | solution.py:534
  (13 other events, 234.6 us)

commit v2 on v1

v2 whole, which is shorter than its diff:
```python
import functools

import jax
import jax.numpy as jnp
import numpy as np
from jax import lax
from jax.experimental import pallas as pl
from jax.experimental.pallas import tpu as pltpu
from jax.sharding import PartitionSpec as P

H = 24
P_SIZE = 64
N = 128
KW = 4
Q = 256
E = 3352
DI = 1536
CD = 1792
HL = 128
CW = CD + HL
CH = 256
HALF = 128
RIM = 16
PIECES = 32
NEG = -1e30

epsilon = 1e-05
low = jnp.bfloat16
f32 = jnp.float32
axes = ("dp", "seq")


def onehot(rows, cols, first, period):
    table = np.zeros((rows, cols), np.float32)
    at = np.arange(cols)
    table[first + at % period, at] = 1.0
    return jnp.asarray(table, low)


def head_table():
    table = np.zeros((HL, DI), np.float32)
    at = np.arange(DI)
    table[at // P_SIZE, at] = 1.0
    table[HL // 2 + at // P_SIZE, at] = 1.0
    return table


def dot(left, right, dims):
    return lax.dot_general(left, right, (dims, ((), ())), preferred_element_type=f32)


def nn(left, right):
    return dot(left, right, ((1,), (0,)))


def nt(left, right):
    return dot(left, right, ((1,), (1,)))


def tn(left, right):
    return dot(left, right, ((0,), (0,)))


def pack(value):
    top = value.astype(low).astype(f32)
    rest = pltpu.roll(value - top, HL // 2, 1)
    lane = lax.broadcasted_iota(jnp.int32, value.shape, 1)
    return jnp.where(lane < HL // 2, top, rest).astype(low)


def spread(packed, table):
    return nn(packed, table)


def gather_heads(value, table):
    top = value.astype(low)
    return nn(top, table) + nn((value - top.astype(f32)).astype(low), table)


def running_sum(value, reverse):
    rows = value.shape[0]
    at = lax.broadcasted_iota(jnp.int32, value.shape, 0)
    step = 1
    while step < rows:
        if reverse:
            value = value + jnp.where(at < rows - step, pltpu.roll(value, rows - step, 0), 0.0)
        else:
            value = value + jnp.where(at >= step, pltpu.roll(value, step, 0), 0.0)
        step *= 2
    return value


def softplus(value):
    tail = jnp.exp(-jnp.abs(value))
    series = tail * (1.0 - tail * (0.5 - tail * (1.0 / 3.0 - tail * (0.25 - tail * 0.2))))
    return jnp.maximum(value, 0.0) + jnp.where(tail < 0.03125, series, jnp.log(1.0 + tail))


def fold8(value):
    return jnp.sum(value.reshape(value.shape[0] // 8, 8, value.shape[1]), axis=0)


def pair_rows(me, own, other):
    first = (me & 1) == 0
    return jnp.concatenate([jnp.where(first, own, other), jnp.where(first, other, own)], axis=0)


def source_of(me, place):
    return me ^ ((place // 4) * 2) ^ ((place % 4) * 8)


def place_of(piece):
    return ((piece >> 1) & 3) * 4 + (piece >> 3)


def conv_kernel(
    groups, scal, x, halo, wa, wb, t56, t48, t24, sb, rate, e,
    nrm_o, nrmt_o, cie_o, sp_o, xh_o, xs_o, wx_o, bc_o, step_o, cum_o, dtb_o, cumt_o,
    sloc_o, pre_o, r_o, tot_o, wc_o, taps_o, gain_o, gate_o,
    nrm, cs, run, dec, small,
):
    block = pl.program_id(0)
    fresh = block % groups == 0

    @pl.when(block == 0)
    def assemble():
        me = scal[0]

        def one(place, carry):
            chip = source_of(me, place) >> 1
            own, other = wa[place].astype(f32), wb[place].astype(f32)
            wc_o[pl.ds(pl.multiple_of(chip * 48, 16), 48), :] = pair_rows(me, own, other).astype(low)
            rows = pl.ds(pl.multiple_of(place * 8, 8), 8)
            small[0, rows, :] = own[0:8, CD:CW]
            small[1, rows, :] = other[0:8, CD:CW]
            return carry

        lax.fori_loop(0, PIECES // 2, one, 0)
        at = lax.broadcasted_iota(jnp.int32, (PIECES, 1), 0)
        slot = at & (PIECES // 2 - 1)
        ids = me ^ ((slot >> 2) << 1) ^ ((slot & 3) << 3) ^ (at >> 4)

        def row_of(k, table, size):
            pieces = [small[which, pl.ds(k, PIECES // 2, stride=8), :] for which in range(2)]
            wide = nn(jnp.concatenate(pieces, axis=0).astype(low), table)
            lane = lax.broadcasted_iota(jnp.int32, wide.shape, 1)
            inside = jnp.logical_and(lane >= ids * size, lane < (ids + 1) * size)
            return jnp.sum(jnp.where(inside, wide, 0.0), axis=0, keepdims=True)

        for k in range(KW + 1):
            taps_o[k : k + 1, :] = row_of(k, t56[...], CD // PIECES)
        gate_o[0:1, :] = row_of(0, t48[...], DI // PIECES)
        gain_o[0:1, :] = row_of(1, t24[...], gain_o.shape[1] // PIECES)

    def normed(rows):
        wide = rows.astype(f32)
        scale = lax.rsqrt(jnp.mean(wide * wide, axis=-1, keepdims=True) + epsilon)
        return (wide * scale * gain_o[0:1, :]).astype(low)

    nrm[0:RIM, :] = normed(halo[...])
    for r in range(0, Q, 32):
        nrm[RIM + r : RIM + r + 32, :] = normed(x[r : r + 32, :])
    nrm_o[...] = nrm[RIM:, :]
    nrmt_o[...] = nrm[RIM:, :].T

    for c in range(0, CD, CH):
        cols = slice(c, c + CH)
        conv_in = nn(nrm[...], wc_o[:, cols]).astype(low)
        cie_o[:, cols] = conv_in
        cs[...] = conv_in.astype(f32)
        for r in range(0, Q, 32):
            taps = taps_o[0:1, cols] * cs[RIM - 3 + r : RIM + 29 + r, :]
            for k in range(1, KW):
                taps = taps + taps_o[k : k + 1, cols] * cs[RIM - 3 + k + r : RIM + 29 + k + r, :]
            pre = taps_o[KW : KW + 1, cols] + taps
            sig = jax.nn.sigmoid(pre)
            act = (pre * sig).astype(low)
            sp_o[r : r + 32, cols] = sig * (1.0 + pre * (1.0 - sig))
            if c < DI:
                xh_o[r : r + 32, cols] = act
            else:
                bc_o[r : r + 32, :] = act

    dtb = nn(nrm[RIM:, :], wc_o[:, CD:CW]) + sb[...]
    step = softplus(dtb)
    cum = running_sum(-step * rate[...], False)
    step_o[...] = step
    cum_o[...] = cum
    dtb_o[...] = dtb
    cumt_o[...] = cum.T[0:H, :]
    last = cum[Q - 1 : Q, :]
    steps = pack(step)
    tails = pack(jnp.exp2(last - cum) * step)
    decays = pack(jnp.broadcast_to(jnp.exp2(last), (8, HL)))
    for c in range(0, DI, CH):
        cols = slice(c, c + CH)
        table = e[:, cols]
        wide = xh_o[:, cols].astype(f32)
        xs_o[:, cols] = (spread(steps, table) * wide).astype(low)
        weighted = (spread(tails, table) * wide).astype(low)
        wx_o[:, cols] = weighted
        local = tn(bc_o[:, 0:N], weighted)
        decay = spread(decays, table)
        before = jnp.where(fresh, 0.0, run[:, cols])
        sloc_o[:, cols] = before
        after = decay[0:1, :] * before + local
        run[:, cols] = after
        r_o[:, cols] = after
        product = jnp.where(fresh, 1.0, dec[:, cols])
        pre_o[:, cols] = product
        product = product * decay
        dec[:, cols] = product
        tot_o[:, cols] = product[0:1, :]


def intra_kernel(bc, xs, cum, cumt, o, sc):
    sc[...] = nt(bc[:, N : 2 * N], bc[:, 0:N])
    at = lax.broadcasted_iota(jnp.int32, (HALF, HALF), 0)
    to = lax.broadcasted_iota(jnp.int32, (HALF, HALF), 1)
    lower = at >= to
    left = lax.broadcasted_iota(jnp.int32, (Q, HALF), 1) < P_SIZE
    for pair in range(H // 2):
        cols = slice(pair * HALF, (pair + 1) * HALF)
        x_pair = xs[:, cols]
        tops, bottoms = [], []
        for h in (2 * pair, 2 * pair + 1):
            row = cumt[h : h + 1, :]
            upper_col, lower_col = cum[0:HALF, h : h + 1], cum[HALF:, h : h + 1]
            m00 = sc[0:HALF, 0:HALF] * jnp.exp2(jnp.where(lower, upper_col - row[:, 0:HALF], NEG))
            m10 = sc[HALF:, 0:HALF] * jnp.exp2(lower_col - row[:, 0:HALF])
            m11 = sc[HALF:, HALF:] * jnp.exp2(jnp.where(lower, lower_col - row[:, HALF:], NEG))
            tops.append(nn(m00.astype(low), x_pair[0:HALF, :]))
            bottoms.append(nn(jnp.concatenate([m10.astype(low), m11.astype(low)], axis=1), x_pair))
        o[0:HALF, cols] = jnp.where(left[0:HALF], tops[0], tops[1])
        o[HALF:, cols] = jnp.where(left[0:HALF], bottoms[0], bottoms[1])


def valid_column(scal, groups, block):
    seq, group = block // groups, block % groups
    at = scal[1] * (groups * Q) + group * Q + lax.broadcasted_iota(jnp.int32, (Q, 1), 0)
    return (at < scal[2 + seq]).astype(f32)


def project_kernel(groups, scal, nrm, cot, wa, wb, z_o, dn_o, db_o, wz_o, wo_o):
    block = pl.program_id(0)

    @pl.when(block == 0)
    def assemble():
        me = scal[0]

        def halves(packed):
            return jnp.concatenate([packed[:, 0 : DI // 2], packed[:, DI // 2 :]], axis=0)

        def one(place, carry):
            chip = source_of(me, place) >> 1
            own, other = wa[place, 0].astype(f32), wb[place, 0].astype(f32)
            wz_o[pl.ds(pl.multiple_of(chip * 48, 16), 48), :] = pair_rows(me, own, other).astype(low)
            own, other = halves(wa[place, 1].astype(f32)), halves(wb[place, 1].astype(f32))
            wo_o[pl.ds(pl.multiple_of(chip * 96, 16), 96), :] = pair_rows(me, own, other).astype(low)
            return carry

        lax.fori_loop(0, PIECES // 2, one, 0)

    db_o[...] = (cot[...].astype(f32) * valid_column(scal, groups, block)).astype(low)
    for c in range(0, DI, CH):
        z_o[:, c : c + CH] = nn(nrm[...], wz_o[:, c : c + CH])
        dn_o[:, c : c + CH] = nt(db_o[...], wo_o[c : c + CH, :])


def gate_kernel(
    groups, scal, intra, xh, bc, cum, sloc, pre, inc, z, dn, hid, wo, gg, skip, e, et,
    out_o, dz_o, dy_o, gdy_o, gn_o, sbf_o, rs_o, dloc_o, suf_o, rd_o, tot_o, gacc_o, kacc_o,
    yi_s, ge_s, pr_s, y_s, sg_s, gt_s, run, dec,
):
    at = pl.program_id(0)
    fresh = at % groups == 0
    block = (at // groups) * groups + groups - 1 - at % groups

    @pl.when(at == 0)
    def start():
        gacc_o[...] = jnp.zeros_like(gacc_o)
        kacc_o[...] = jnp.zeros_like(kacc_o)

    c_rows = bc[:, N : 2 * N]
    growth = pack(jnp.exp2(cum[...]))
    for c in range(0, DI, CH):
        cols = slice(c, c + CH)
        begin = (sloc[:, cols] + pre[0:1, cols] * inc[:, cols].astype(f32)).astype(low)
        sbf_o[:, cols] = begin
        wide = spread(growth, e[:, cols])
        ge_s[:, cols] = wide
        yi_s[:, cols] = intra[:, cols] + wide * nn(c_rows, begin)

    def body(i, carry):
        rows = pl.ds(pl.multiple_of(i * 32, 32), 32)
        squares = jnp.zeros((32, HALF), f32)
        crosses = jnp.zeros((32, HALF), f32)
        for c in range(0, DI, HALF):
            cols = slice(c, c + HALF)
            zv = z[rows, cols]
            y = yi_s[rows, cols] + skip[:, cols] * xh[rows, cols].astype(f32)
            sig = jax.nn.sigmoid(zv)
            gated = y * (zv * sig)
            squares = squares + gated * gated
            crosses = crosses + (dn[rows, cols] * gg[0:1, cols]) * gated
            y_s[:, cols] = y
            sg_s[:, cols] = sig
            gt_s[:, cols] = gated
        scale = lax.rsqrt(jnp.sum(squares, axis=1, keepdims=True) / DI + epsilon)
        shift = scale * scale * scale * (jnp.sum(crosses, axis=1, keepdims=True) / DI)
        for c in range(0, DI, HALF):
            cols = slice(c, c + HALF)
            zv, y, sig, gated = z[rows, cols], y_s[:, cols], sg_s[:, cols], gt_s[:, cols]
            wide = dn[rows, cols]
            normal = gated * scale
            gn_o[rows, cols] = (normal * gg[0:1, cols]).astype(low)
            gacc_o[:, cols] += fold8(wide * normal)
            d_gated = scale * (wide * gg[0:1, cols]) - gated * shift
            d_sig = d_gated * sig
            dz_o[rows, cols] = (d_sig * y * (1.0 + zv * (1.0 - sig))).astype(low)
            d_low = (d_sig * zv).astype(low)
            dy_o[rows, cols] = d_low
            d_y = d_low.astype(f32)
            kacc_o[:, cols] += fold8(d_y * xh[rows, cols].astype(f32))
            gdy_o[rows, cols] = (ge_s[rows, cols] * d_y).astype(low)
            pr_s[rows, cols] = d_y * yi_s[rows, cols]
        return carry

    lax.fori_loop(0, Q // 32, body, 0)

    valid = valid_column(scal, groups, block)
    for c in range(0, DI // 2, CH):
        branch = nn(gn_o[...], wo[:, c : c + CH])
        out_o[:, c : c + CH] = (hid[:, c : c + CH].astype(f32) + valid * branch).astype(low)
    decays = pack(jnp.broadcast_to(jnp.exp2(cum[Q - 1 : Q, :]), (8, HL)))
    sums = jnp.zeros((Q, HL), f32)
    for c in range(0, DI, CH):
        cols = slice(c, c + CH)
        sums = sums + gather_heads(pr_s[:, cols], et[cols, :])
        decay = spread(decays, e[:, cols])
        before = jnp.where(fresh, 0.0, run[:, cols])
        dloc_o[:, cols] = before
        after = decay[0:1, :] * before + tn(c_rows, gdy_o[:, cols])
        run[:, cols] = after
        rd_o[:, cols] = after
        product = jnp.where(fresh, 1.0, dec[:, cols])
        suf_o[:, cols] = product
        product = product * decay
        dec[:, cols] = product
        tot_o[:, cols] = product[0:1, :]
    rs_o[...] = sums


def intra_back_kernel(bc, xs, xh, dy, step, cum, cumt, skip, e, et, dx_o, dbc_o, rs_o, sc, acc):
    sc[...] = nt(bc[:, 0:N], bc[:, N : 2 * N])
    acc[...] = jnp.zeros_like(acc)
    at = lax.broadcasted_iota(jnp.int32, (HALF, HALF), 0)
    to = lax.broadcasted_iota(jnp.int32, (HALF, HALF), 1)
    upper = at <= to
    left = lax.broadcasted_iota(jnp.int32, (Q, HALF), 1) < P_SIZE
    steps = pack(step[...])
    sums = jnp.zeros((Q, HL), f32)
    for pair in range(H // 2):
        cols = slice(pair * HALF, (pair + 1) * HALF)
        dy_pair = dy[:, cols]
        x_pair = xs[:, cols]
        tops, bottoms, parts = [], [], []
        for h in (2 * pair, 2 * pair + 1):
            keep = left if h % 2 == 0 else jnp.logical_not(left)
            x_half = jnp.where(keep, x_pair, jnp.zeros_like(x_pair))
            row = cumt[h : h + 1, :]
            first_col, second_col = cum[0:HALF, h : h + 1], cum[HALF:, h : h + 1]
            l00 = jnp.exp2(jnp.where(upper, row[:, 0:HALF] - first_col, NEG))
            l01 = jnp.exp2(row[:, HALF:] - first_col)
            l11 = jnp.exp2(jnp.where(upper, row[:, HALF:] - second_col, NEG))
            m00 = (sc[0:HALF, 0:HALF] * l00).astype(low)
            m01 = (sc[0:HALF, HALF:] * l01).astype(low)
            m11 = (sc[HALF:, HALF:] * l11).astype(low)
            tops.append(nn(jnp.concatenate([m00, m01], axis=1), dy_pair))
            bottoms.append(nn(m11, dy_pair[HALF:, :]))
            grown = nt(x_half[0:HALF, :], dy_pair)
            last = nt(x_half[HALF:, :], dy_pair[HALF:, :])
            parts.append((grown[:, 0:HALF] * l00, grown[:, HALF:] * l01, last * l11))
        acc[0:HALF, 0:HALF] += parts[0][0] + parts[1][0]
        acc[0:HALF, HALF:] += parts[0][1] + parts[1][1]
        acc[HALF:, HALF:] += parts[0][2] + parts[1][2]
        flow = jnp.concatenate(
            [
                jnp.where(left[0:HALF], tops[0], tops[1]),
                jnp.where(left[0:HALF], bottoms[0], bottoms[1]),
            ],
            axis=0,
        )
        sums = sums + gather_heads(flow * xh[:, cols].astype(f32), et[cols, :])
        dx_o[:, cols] = spread(steps, e[:, cols]) * flow + skip[:, cols] * dy_pair.astype(f32)
    rs_o[...] = sums
    scores = acc[...].astype(low)
    dbc_o[:, 0:N] = nn(scores, bc[:, N : 2 * N])
    dbc_o[:, N : 2 * N] = tn(scores, bc[:, 0:N])


def conv_back_kernel(
    groups, dloc, suf, inc, sbf, xh, wx, gdy, dx, dbc, bc, cum, step, dtb, rs1, rs2,
    cie, sp, cw, rate, e, et,
    dcv_o, kacc_o, hacc_o, head_o, tail_o,
    ds, nxt,
):
    at = pl.program_id(0)
    fresh = at % groups == 0
    opening = at % groups == groups - 1

    @pl.when(at == 0)
    def start():
        kacc_o[...] = jnp.zeros_like(kacc_o)
        hacc_o[...] = jnp.zeros_like(hacc_o)

    def conv_back(flow, c):
        cols = slice(c, c + CH)
        ds[0:8, :] = jnp.zeros((8, CH), f32)
        ds[8 + Q :, :] = jnp.where(fresh, 0.0, nxt[:, cols])
        ds[8 : 8 + Q, :] = flow * sp[:, cols]
        nxt[:, cols] = ds[8:16, :]
        taps = [cw[k : k + 1, cols] for k in range(KW)]
        sums = [jnp.zeros((8, CH), f32) for _ in range(KW + 1)]

        def views_at(begin, count):
            return [ds[begin + 11 - k : begin + 11 - k + count, :] for k in range(KW)]

        def back(views):
            total = taps[0] * views[0]
            for k in range(1, KW):
                total = total + taps[k] * views[k]
            return total

        for r in range(0, Q, 32):
            views = views_at(r, 32)
            dcv_o[r : r + 32, cols] = back(views).astype(low)
            conv_in = cie[RIM + r : RIM + r + 32, cols].astype(f32)
            for k in range(KW):
                sums[k] = sums[k] + fold8(views[k] * conv_in)
            sums[KW] = sums[KW] + fold8(views[KW - 1])
        views = views_at(-8, 8)
        head_o[:, cols] = back(views).astype(low)
        conv_in = cie[0:RIM, cols].astype(f32)[8:16, :]
        for k in range(KW):
            kacc_o[8 * k : 8 * k + 8, cols] += sums[k] + jnp.where(opening, views[k] * conv_in, 0.0)
        kacc_o[8 * KW : 8 * KW + 8, cols] += sums[KW]

        @pl.when(fresh)
        def keep():
            tail_o[:, cols] = back(views_at(Q - 16, 16))

    cumv = cum[...]
    stepv = step[...]
    last = cumv[Q - 1 : Q, :]
    fade = jnp.exp2(last - cumv)
    tail = fade * stepv
    tails = pack(tail)
    b_rows = bc[:, 0:N]
    d_b = dbc[:, 0:N]
    d_c = dbc[:, N : 2 * N]
    sums = jnp.zeros((Q, HL), f32)
    lasts = jnp.zeros((8, HL), f32)
    for c in range(0, DI, CH):
        cols = slice(c, c + CH)
        end = dloc[:, cols] + suf[0:1, cols] * inc[:, cols].astype(f32)
        end_low = end.astype(low)
        begin = sbf[:, cols]
        lasts = lasts + gather_heads(fold8(end * begin.astype(f32)), et[cols, :])
        reach = nn(b_rows, end_low)
        sums = sums + gather_heads(reach * xh[:, cols].astype(f32), et[cols, :])
        d_b = d_b + nt(wx[:, cols], end_low)
        d_c = d_c + nt(gdy[:, cols], begin)
        conv_back(dx[:, cols] + spread(tails, e[:, cols]) * reach, c)
    conv_back(jnp.concatenate([d_b, d_c], axis=1), DI)

    flow = sums * tail
    d_cum = rs1[...] - stepv * rs2[...] - flow
    d_last = jnp.exp2(last) * jnp.sum(lasts, axis=0, keepdims=True)
    d_last = d_last + jnp.sum(flow, axis=0, keepdims=True)
    d_log = running_sum(d_cum, True) + d_last
    d_step = rs2[...] + sums * fade - d_log * rate[...]
    d_dt = d_step * jax.nn.sigmoid(dtb[...])
    lane = lax.broadcasted_iota(jnp.int32, d_dt.shape, 1)
    d_dt = jnp.where(lane < H, d_dt, 0.0)
    dcv_o[:, CD:CW] = d_dt.astype(low)
    head_o[:, CD:CW] = jnp.zeros((8, HL), low)

    @pl.when(fresh)
    def keep_step():
        tail_o[:, CD:CW] = d_dt[Q - 16 :, :]

    hacc_o[0:8, :] += fold8(d_dt)
    hacc_o[8:16, :] += fold8(d_log * stepv)


def piece_at(me, place, which):
    return source_of(me, place) ^ which


def early_grad_kernel(scal, nrmt, dz, dzr, gn, db, wz, g0_o, g1_o, dn_o, part, wide):
    at = pl.program_id(0)
    me = scal[0]
    refs = (g0_o, g1_o)
    quarter = DI // 4
    cols = pl.ds(pl.multiple_of(at * quarter, HALF), quarter)
    part[...] = nn(nrmt[...], dz[...])
    for place in range(PIECES // 2):
        for which in range(2):
            start = pl.multiple_of(piece_at(me, place, which) * 24, 8)
            refs[which][place, 0, :, cols] = part[pl.ds(start, 24), :].astype(low)
    wide[pl.ds(pl.multiple_of(at * quarter, HALF), quarter), :] = tn(gn[...], db[...])
    dn_o[...] = nt(dzr[...], wz[...])

    @pl.when(at == 3)
    def finish():
        for place in range(PIECES // 2):
            for which in range(2):
                start = pl.multiple_of(piece_at(me, place, which) * 48, 8)
                for half in range(2):
                    rows = pl.ds(start + 24 * half, 24)
                    span = slice(half * DI // 2, (half + 1) * DI // 2)
                    refs[which][place, 1, :, span] = wide[rows, :].astype(low)


def late_grad_kernel(scal, nrmt, dcv, tails, returned, g0_o, g1_o, fix_o, part):
    refs = (g0_o, g1_o)
    fix_o[...] = dcv[...]
    seqs = tails.shape[0]
    piece_len = dcv.shape[0] // seqs
    for seq in range(seqs):
        back = jnp.concatenate(
            [tails[seq, 0:8, :], tails[seq, 8:16, :] + returned[seq].astype(f32)], axis=0
        )
        fix_o[(seq + 1) * piece_len - 16 : (seq + 1) * piece_len, :] = back.astype(low)
    part[...] = nn(nrmt[...], fix_o[...])
    for place in range(PIECES // 2):
        for which in range(2):
            start = pl.multiple_of(piece_at(scal[0], place, which) * 24, 8)
            refs[which][place, :, :] = part[pl.ds(start, 24), :].astype(low)


def input_kernel(dcv, dnz, wc, x, cot, gain, past, gh_o, acc_o, total):
    @pl.when(pl.program_id(0) == 0)
    def start():
        acc_o[...] = jnp.zeros_like(acc_o)

    total[...] = dnz[...] + nt(dcv[...], wc[...])
    width = x.shape[1]
    for r in range(0, Q, 16):
        rows = slice(r, r + 16)
        wide = x[rows, :].astype(f32)
        scale = lax.rsqrt(jnp.mean(wide * wide, axis=-1, keepdims=True) + epsilon)
        flow = total[rows, :]
        acc_o[...] += fold8(flow * wide * scale)
        scaled = flow * gain[0:1, :]
        mean = jnp.sum(scaled * wide, axis=-1, keepdims=True) / width
        d_x = scale * scaled - wide * (scale * scale * scale * mean)
        gh_o[rows, :] = (cot[rows, :].astype(f32) + d_x).astype(low)


def call(kernel, grid, inputs, outputs, scratch, flops, name, aliases=None):
    in_specs = [spec for spec, _ in inputs]
    out_specs = [spec for spec, _, _ in outputs]
    out_shape = [jax.ShapeDtypeStruct(shape, kind) for _, shape, kind in outputs]
    moved = sum(value.size * value.dtype.itemsize for _, value in inputs)
    return pl.pallas_call(
        kernel,
        grid=(grid,),
        in_specs=in_specs,
        out_specs=out_specs,
        out_shape=out_shape,
        scratch_shapes=scratch,
        input_output_aliases=aliases or {},
        cost_estimate=pl.CostEstimate(flops=int(flops), transcendentals=0, bytes_accessed=moved),
        compiler_params=pltpu.CompilerParams(
            dimension_semantics=("arbitrary",), vmem_limit_bytes=56 * 1024 * 1024
        ),
        name=name,
    )(*[value for _, value in inputs])


def swap(value, mask):
    return lax.ppermute(value, axes, [(i, i ^ mask) for i in range(PIECES)])


def tie(value, *after):
    return lax.optimization_barrier((value,) + after)[0]


def along(value, masks):
    return jnp.stack([value] + [swap(value, mask) for mask in masks])


def ends_of(plane, value):
    flat = (PIECES // 2,) + value.shape
    return plane.reshape(flat), swap(plane, 1).reshape(flat)


def weave_first(first, second, rim):
    line = tie(along(first, (8, 16, 24)), rim)
    later = along(tie(second, line), (8, 16, 24))
    got = [tie(swap(line, mask), later) for mask in (2, 4, 6)]
    plane = jnp.stack([line] + got)
    return ends_of(plane, first), tie(later, plane)


def weave_second(line, value, token):
    got = [tie(swap(line, mask), token) for mask in (2, 4, 6)]
    plane = jnp.stack([line] + got)
    return ends_of(plane, value), plane


def parts_of(total):
    return total[0], [total[j].astype(low) for j in range(1, 4)]


def merge_core(kept, got):
    total = kept.astype(f32) + got.astype(f32)
    return parts_of(total.reshape((4, 4) + kept.shape[1:]))


def merge(keep, sends, masks, *after):
    got = [swap(value, mask) for value, mask in zip(sends, masks)]
    if after:
        got = lax.optimization_barrier((*got,) + after)[:3]
    got = [value.astype(f32) for value in got]
    return (keep + got[0]) + (got[1] + got[2])


def tie_all(keep, sends, *after):
    out = lax.optimization_barrier((keep, *sends) + after)
    return out[0], list(out[1:4])


def total_over(value):
    value = value + swap(value, 1)
    for masks in ((2, 4, 6), (8, 16, 24)):
        got = [swap(value, mask) for mask in masks]
        value = (value + got[0]) + (got[1] + got[2])
    return value


def extras(taps, bias, gate, norm):
    left = jnp.concatenate([taps, bias[:, None, :]], axis=1)
    norm = jnp.pad(norm, ((0, 0), (0, gate.shape[1] - norm.shape[1])))
    right = jnp.stack([gate, norm], axis=1)
    left = jnp.pad(left, ((0, 0), (0, 24 - left.shape[1]), (0, 0)))
    right = jnp.pad(right, ((0, 0), (0, 24 - right.shape[1]), (0, 0)))
    return jnp.concatenate([left, right], axis=2)


def order_of_pieces():
    return [(j << 1) | (k << 3) for j in range(4) for k in range(4)]


def relay(ends, totals, forward, fillers):
    count = lax.axis_size("seq")
    incoming = jnp.zeros(ends.shape, f32)
    results, got = [], None
    for hop in range(1, count):
        value = (totals * incoming + ends).astype(low)
        route = [(hop - 1, hop)] if forward else [(count - hop, count - hop - 1)]
        arrived = lax.ppermute(value, "seq", route)
        if fillers:
            made = fillers.pop(0)(got)
            results.append(made)
            arrived = tie(arrived, made[-1])
        got = arrived
        incoming = incoming + got.astype(f32)
    while fillers:
        results.append(fillers.pop(0)(got))
    return incoming.astype(low), results


def per_device(
    hidden,
    lengths,
    norm_gain,
    in_weight,
    conv_weight,
    conv_bias,
    step_bias,
    decay_log,
    skip_gain,
    gate_gain,
    out_weight,
    cotangent,
):
    seqs, piece_len, width = hidden.shape
    groups = piece_len // Q
    blocks = seqs * groups
    rows = seqs * piece_len
    devices = lax.axis_size(axes)
    quick = devices == PIECES
    place = lax.axis_index(axes).astype(jnp.int32)
    me = place if quick else jnp.zeros((), jnp.int32)
    seq_at = lax.axis_index("seq").astype(jnp.int32)
    scal = jnp.concatenate([me[None], seq_at[None], lengths.astype(jnp.int32)])

    rims = hidden[:, piece_len - RIM :, :]
    seq_size = lax.axis_size("seq")
    rim_in = lax.ppermute(rims, "seq", [(i, i + 1) for i in range(seq_size - 1)])
    inner = hidden.reshape(seqs, groups, Q, width)[:, : groups - 1, Q - RIM :, :]
    halo = jnp.concatenate([rim_in[:, None], inner], axis=1).reshape(blocks, RIM, width)

    w_low = in_weight.astype(low)
    o_low = out_weight.astype(low)
    if quick:
        half = o_low.shape[0] // 2
        packed = jnp.concatenate([o_low[:half], o_low[half:]], axis=1)
        second = jnp.stack([w_low[:, :DI], packed])
        first = jnp.concatenate(
            [
                in_weight[:, DI:],
                extras(
                    conv_weight[None], conv_bias[None], gate_gain[None], norm_gain[None]
                )[0],
            ],
            axis=1,
        ).astype(low)
        (ca, cb_pieces), second_line = weave_first(first, second, rim_in)
        begin = tie(scal, second_line)
    else:
        begin = scal
        order = jnp.array(order_of_pieces(), jnp.int32)
        rows_w = lax.all_gather(w_low, axes, axis=0, tiled=True).reshape(PIECES, -1, E)
        full_taps = lax.all_gather(conv_weight.astype(low), axes, axis=1, tiled=True)
        full = [
            lax.all_gather(value.astype(low), axes, axis=0, tiled=True).reshape(PIECES, -1)
            for value in (conv_bias, gate_gain, norm_gain)
        ]
        extra = extras(full_taps.reshape(KW, PIECES, -1).transpose(1, 0, 2), *full)
        whole = jnp.concatenate([rows_w[:, :, DI:], extra], axis=2)
        ca, cb_pieces = whole[order], whole[order + 1]
        outs = lax.all_gather(o_low, axes, axis=0, tiled=True)
        outs = outs.reshape(PIECES, 2, -1, width).transpose(0, 2, 1, 3).reshape(PIECES, -1, DI)
        whole = jnp.stack([rows_w[:, :, :DI], outs], axis=1)
        za, zb = whole[order], whole[order + 1]

    rate = jnp.exp(decay_log)
    log2_rate = rate * 1.4426950408889634
    sb = jnp.pad(step_bias, (0, HL - H)).reshape(1, HL)
    rate_row = jnp.pad(rate, (0, HL - H)).reshape(1, HL)
    log2_row = jnp.pad(log2_rate, (0, HL - H)).reshape(1, HL)
    skip = jnp.repeat(skip_gain, P_SIZE).reshape(1, DI)
    e = jnp.asarray(head_table(), low)
    et = jnp.asarray(np.pad(head_table()[: HL // 2].T, ((0, 0), (0, HL // 2))), low)
    t56 = onehot(HL, CD, H, CD // PIECES)
    t48 = onehot(HL, DI, 80, DI // PIECES)
    t24 = onehot(HL, width, 80, width // PIECES)

    def forth(i):
        return i

    def back(i):
        return (i // groups) * groups + groups - 1 - i % groups

    def tokens(cols, order):
        return pl.BlockSpec((Q, cols), lambda i: (order(i), 0))

    def per_block(height, cols, order):
        return pl.BlockSpec((None, height, cols), lambda i: (order(i), 0, 0))

    def per_seq(height, cols):
        return pl.BlockSpec((None, height, cols), lambda i: (i // groups, 0, 0))

    def fixed(*shape):
        zeros = (0,) * len(shape)
        return pl.BlockSpec(shape, lambda i: zeros, pipeline_mode=pl.Buffered(1))

    def kept(*shape):
        zeros = (0,) * len(shape)
        return pl.BlockSpec(shape, lambda i: zeros)

    scalars = pl.BlockSpec(memory_space=pltpu.SMEM)
    flat_hidden = hidden.reshape(rows, width)
    flat_cot = cotangent.reshape(rows, width)

    (nrm, nrmt, cie, sp, xh, xs, wx, bc, step, cum, dtb, cumt, sloc, pre, ends, totals, wc, taps, gain_in, gain_gate) = call(
        functools.partial(conv_kernel, groups),
        blocks,
        [
            (scalars, begin),
            (tokens(width, forth), flat_hidden),
            (per_block(RIM, width, forth), halo),
            (fixed(*ca.shape), ca),
            (fixed(*ca.shape), cb_pieces),
            (fixed(HL, CD), t56),
            (fixed(HL, DI), t48),
            (fixed(HL, width), t24),
            (fixed(1, HL), sb),
            (fixed(1, HL), log2_row),
            (fixed(HL, DI), e),
        ],
        [
            (tokens(width, forth), (rows, width), low),
            (pl.BlockSpec((width, Q), lambda i: (0, i)), (width, rows), low),
            (per_block(Q + RIM, CD, forth), (blocks, Q + RIM, CD), low),
            (tokens(CD, forth), (rows, CD), f32),
            (tokens(DI, forth), (rows, DI), low),
            (tokens(DI, forth), (rows, DI), low),
            (tokens(DI, forth), (rows, DI), low),
            (tokens(2 * N, forth), (rows, 2 * N), low),
            (tokens(HL, forth), (rows, HL), f32),
            (tokens(HL, forth), (rows, HL), f32),
            (tokens(HL, forth), (rows, HL), f32),
            (per_block(H, Q, forth), (blocks, H, Q), f32),
            (per_block(N, DI, forth), (blocks, N, DI), f32),
            (per_block(8, DI, forth), (blocks, 8, DI), f32),
            (per_seq(N, DI), (seqs, N, DI), f32),
            (per_seq(1, DI), (seqs, 1, DI), f32),
            (kept(width, CW), (width, CW), low),
            (kept(8, CD), (8, CD), f32),
            (kept(8, width), (8, width), f32),
            (kept(8, DI), (8, DI), f32),
        ],
        [
            pltpu.VMEM((Q + RIM, width), low),
            pltpu.VMEM((Q + RIM, CH), f32),
            pltpu.VMEM((N, DI), f32),
            pltpu.VMEM((8, DI), f32),
            pltpu.VMEM((2, HL, HL), f32),
        ],
        2.0 * rows * width * CW,
        "conv",
    )
    if quick:
        (za, zb), token = weave_second(second_line, second, cum)
        bc_after = tie(bc, token)
    else:
        bc_after = bc

    def intra_part(got):
        return call(
            intra_kernel,
            blocks,
            [
                (tokens(2 * N, forth), bc_after),
                (tokens(DI, forth), xs),
                (tokens(HL, forth), cum),
                (per_block(H, Q, forth), cumt),
            ],
            [(tokens(DI, forth), (rows, DI), f32)],
            [pltpu.VMEM((Q, Q), f32)],
            2.0 * rows * Q * DI * 2,
            "intra",
        )

    def after(value, got):
        return value if got is None else tie(value, got)

    def project_part(got):
        return call(
            functools.partial(project_kernel, groups),
            blocks,
            [
                (scalars, after(scal, got)),
                (tokens(width, forth), nrm),
                (tokens(width, forth), flat_cot),
                (fixed(*za.shape), za),
                (fixed(*za.shape), zb),
            ],
            [
                (tokens(DI, forth), (rows, DI), f32),
                (tokens(DI, forth), (rows, DI), f32),
                (tokens(width, forth), (rows, width), low),
                (kept(width, DI), (width, DI), low),
                (kept(DI, width), (DI, width), low),
            ],
            [],
            4.0 * rows * width * DI,
            "project",
        )

    incoming, ((intra,), (z, dn, db, wz, wo)) = relay(
        ends, totals, True, [intra_part, project_part]
    )

    (out, dz, dy, gdy, gn, sbf, rs1, dloc, suf, back_ends, back_totals, gacc, kacc) = call(
        functools.partial(gate_kernel, groups),
        blocks,
        [
            (scalars, scal),
            (tokens(DI, back), intra),
            (tokens(DI, back), xh),
            (tokens(2 * N, back), bc),
            (tokens(HL, back), cum),
            (per_block(N, DI, back), sloc),
            (per_block(8, DI, back), pre),
            (per_seq(N, DI), incoming),
            (tokens(DI, back), z),
            (tokens(DI, back), dn),
            (tokens(width, back), flat_hidden),
            (fixed(DI, width), wo),
            (fixed(8, DI), gain_gate),
            (fixed(1, DI), skip),
            (fixed(HL, DI), e),
            (fixed(DI, HL), et),
        ],
        [
            (tokens(width, back), (rows, width), low),
            (tokens(DI, back), (rows, DI), low),
            (tokens(DI, back), (rows, DI), low),
            (tokens(DI, back), (rows, DI), low),
            (tokens(DI, back), (rows, DI), low),
            (per_block(N, DI, back), (blocks, N, DI), low),
            (tokens(HL, back), (rows, HL), f32),
            (per_block(N, DI, back), (blocks, N, DI), f32),
            (per_block(8, DI, back), (blocks, 8, DI), f32),
            (per_seq(N, DI), (seqs, N, DI), f32),
            (per_seq(1, DI), (seqs, 1, DI), f32),
            (kept(8, DI), (8, DI), f32),
            (kept(8, DI), (8, DI), f32),
        ],
        [
            pltpu.VMEM((Q, DI), f32),
            pltpu.VMEM((Q, DI), f32),
            pltpu.VMEM((Q, DI), f32),
            pltpu.VMEM((32, DI), f32),
            pltpu.VMEM((32, DI), f32),
            pltpu.VMEM((32, DI), f32),
            pltpu.VMEM((N, DI), f32),
            pltpu.VMEM((8, DI), f32),
        ],
        4.0 * rows * width * DI,
        "gate",
    )

    def intra_back_part(got):
        return call(
            intra_back_kernel,
            blocks,
            [
                (tokens(2 * N, forth), after(bc, got)),
                (tokens(DI, forth), xs),
                (tokens(DI, forth), xh),
                (tokens(DI, forth), dy),
                (tokens(HL, forth), step),
                (tokens(HL, forth), cum),
                (per_block(H, Q, forth), cumt),
                (fixed(1, DI), skip),
                (fixed(HL, DI), e),
                (fixed(DI, HL), et),
            ],
            [
                (tokens(DI, forth), (rows, DI), f32),
                (tokens(2 * N, forth), (rows, 2 * N), f32),
                (tokens(HL, forth), (rows, HL), f32),
            ],
            [pltpu.VMEM((Q, Q), f32), pltpu.VMEM((Q, Q), f32)],
            4.0 * rows * Q * DI * 2,
            "intra_back",
        )

    share = rows // 4
    piece = (PIECES // 2, 2, width // PIECES, DI)

    def early_part(got):
        return call(
            early_grad_kernel,
            4,
            [
                (scalars, after(scal, got)),
                (fixed(width, rows), nrmt),
                (pl.BlockSpec((rows, DI // 4), lambda i: (0, i)), dz),
                (pl.BlockSpec((share, DI), lambda i: (i, 0)), dz),
                (pl.BlockSpec((rows, DI // 4), lambda i: (0, i)), gn),
                (fixed(rows, width), db),
                (fixed(width, DI), wz),
            ],
            [
                (kept(*piece), piece, low),
                (kept(*piece), piece, low),
                (pl.BlockSpec((share, width), lambda i: (i, 0)), (rows, width), f32),
            ],
            [pltpu.VMEM((width, DI // 4), f32), pltpu.VMEM((DI, width), f32)],
            6.0 * rows * width * DI,
            "early_grad",
        )

    back_incoming, ((e0, e1, dnz), (dx, dbc, rs2)) = relay(
        back_ends, back_totals, False, [early_part, intra_back_part]
    )
    if quick:
        early = merge_core(e0, tie(swap(e1, 1), rs2))
        back_incoming = tie(back_incoming, *early[1])

    (dcv, cacc, hacc, heads_out, tails_out) = call(
        functools.partial(conv_back_kernel, groups),
        blocks,
        [
            (per_block(N, DI, back), dloc),
            (per_block(8, DI, back), suf),
            (per_seq(N, DI), back_incoming),
            (per_block(N, DI, back), sbf),
            (tokens(DI, back), xh),
            (tokens(DI, back), wx),
            (tokens(DI, back), gdy),
            (tokens(DI, back), dx),
            (tokens(2 * N, back), dbc),
            (tokens(2 * N, back), bc),
            (tokens(HL, back), cum),
            (tokens(HL, back), step),
            (tokens(HL, back), dtb),
            (tokens(HL, back), rs1),
            (tokens(HL, back), rs2),
            (per_block(Q + RIM, CD, back), cie),
            (tokens(CD, back), sp),
            (fixed(8, CD), taps),
            (fixed(1, HL), rate_row),
            (fixed(HL, DI), e),
            (fixed(DI, HL), et),
        ],
        [
            (tokens(CW, back), (rows, CW), low),
            (kept(8 * (KW + 1), CD), (8 * (KW + 1), CD), f32),
            (kept(16, HL), (16, HL), f32),
            (per_seq(8, CW), (seqs, 8, CW), low),
            (per_seq(16, CW), (seqs, 16, CW), f32),
        ],
        [
            pltpu.VMEM((Q + 16, CH), f32),
            pltpu.VMEM((8, CD), f32),
        ],
        6.0 * rows * N * DI,
        "conv_back",
    )
    turn = scal
    if quick:
        early = parts_of(merge(*early, (2, 4, 6), hacc))
        turn = tie(scal, *early[1])
    returned = lax.ppermute(heads_out, "seq", [(i, i - 1) for i in range(1, seq_size)])

    late = (PIECES // 2, width // PIECES, CW)
    late_spec = pl.BlockSpec((PIECES // 2, width // PIECES, CW // 5), lambda i: (0, 0, i))
    (l0, l1, dcv) = call(
        late_grad_kernel,
        5,
        [
            (scalars, turn),
            (fixed(width, rows), nrmt),
            (pl.BlockSpec((rows, CW // 5), lambda i: (0, i)), dcv),
            (pl.BlockSpec((seqs, 16, CW // 5), lambda i: (0, 0, i)), tails_out),
            (pl.BlockSpec((seqs, 8, CW // 5), lambda i: (0, 0, i)), returned),
        ],
        [
            (late_spec, late, low),
            (late_spec, late, low),
            (pl.BlockSpec((rows, CW // 5), lambda i: (0, i)), (rows, CW), low),
        ],
        [pltpu.VMEM((width, CW // 5), f32)],
        2.0 * rows * width * CW,
        "late_grad",
    )

    def input_part(first, count, past, token):
        def order(i):
            return i + first

        return call(
            input_kernel,
            count,
            [
                (tokens(CW, order), dcv),
                (tokens(width, order), dnz),
                (fixed(width, CW), wc),
                (tokens(width, order), flat_hidden),
                (tokens(width, order), flat_cot),
                (fixed(8, width), gain_in if token is None else tie(gain_in, *token)),
                (pl.BlockSpec(memory_space=pl.ANY), past),
            ],
            [
                (tokens(width, order), (rows, width), low),
                (kept(8, width), (8, width), f32),
            ],
            [pltpu.VMEM((Q, width), f32)],
            2.0 * rows * width * CW * count / blocks,
            "input",
            {6: 0} if first else None,
        )

    half_blocks = blocks // 2
    if quick:
        gh, nacc = input_part(0, half_blocks, scal, None)
        late_sum = merge_core(l0, tie(swap(l1, 1), nacc))
        early = tie_all(*early, late_sum[1][0])
        gh, nacc2 = input_part(half_blocks, blocks - half_blocks, gh, late_sum[1])
        late_sum = parts_of(merge(*late_sum, (2, 4, 6), nacc2))
        early = merge(*early, (8, 16, 24), nacc2)
        late_sum = tie_all(*late_sum, early)
        nacc = nacc + nacc2
    else:
        gh, nacc = input_part(0, blocks, scal, None)

    conv_sums = cacc.reshape(KW + 1, 8, CD).sum(axis=1)
    skips = kacc.sum(axis=0).reshape(H, P_SIZE).sum(axis=1)
    scalar_sums = jnp.concatenate(
        [hacc[0:8].sum(axis=0)[:H], -hacc[8:16].sum(axis=0)[:H] * rate, skips]
    )
    vector = jnp.concatenate(
        [nacc.sum(axis=0), conv_sums.reshape(-1), gacc.sum(axis=0), scalar_sums]
    )
    if quick:
        length = vector.shape[0]
        vector = tie(vector, late_sum[1][0])
        vector = total_over(jnp.pad(vector, (0, -length % (8 * HALF))).reshape(-1, HALF))
        vector = vector.reshape(-1)[:length]
        own_late = merge(*late_sum, (8, 16, 24))
        own_z, own_out = early[0], early[1]
        own_out = jnp.concatenate([own_out[:, : DI // 2], own_out[:, DI // 2 :]], axis=0)
    else:
        vector = lax.psum(vector, axes)
        order = jnp.array(order_of_pieces(), jnp.int32)
        inverse = jnp.argsort(jnp.concatenate([order, order + 1]))
        whole = jnp.concatenate([e0, e1])[inverse].astype(f32)
        outs = whole[:, 1].reshape(PIECES, -1, 2, width).transpose(0, 2, 1, 3).reshape(DI, width)
        own_z = lax.psum_scatter(
            whole[:, 0].reshape(width, DI), axes, scatter_dimension=0, tiled=True
        )
        own_out = lax.psum_scatter(outs, axes, scatter_dimension=0, tiled=True)
        whole = jnp.concatenate([l0, l1])[inverse].astype(f32).reshape(width, CW)
        own_late = lax.psum_scatter(whole, axes, scatter_dimension=0, tiled=True)

    def own(value, size, axis):
        return lax.dynamic_slice_in_dim(value, place * size, size, axis)

    at = width
    g_norm = own(vector[:at], norm_gain.shape[0], 0)
    g_taps = own(vector[at : at + KW * CD].reshape(KW, CD), CD // devices, 1)
    at += KW * CD
    g_bias = own(vector[at : at + CD], CD // devices, 0)
    at += CD
    g_gate = own(vector[at : at + DI], gate_gain.shape[0], 0)
    at += DI
    g_in = jnp.concatenate([own_z, own_late[:, : CD + H]], axis=1)
    return (
        out.reshape(hidden.shape),
        gh.reshape(hidden.shape),
        g_norm,
        g_in,
        g_taps,
        g_bias,
        vector[at : at + H],
        vector[at + H : at + 2 * H],
        vector[at + 2 * H : at + 3 * H],
        g_gate,
        own_out,
    )


def solution(mesh):
    return jax.shard_map(
        per_device,
        mesh=mesh,
        in_specs=(
            P("dp", "seq", None),
            P("dp"),
            P(("dp", "seq")),
            P(("dp", "seq"), None),
            P(None, ("dp", "seq")),
            P(("dp", "seq")),
            P(),
            P(),
            P(),
            P(("dp", "seq")),
            P(("dp", "seq"), None),
            P("dp", "seq", None),
        ),
        out_specs=(
            P("dp", "seq", None),
            P("dp", "seq", None),
            P(("dp", "seq")),
            P(("dp", "seq"), None),
            P(None, ("dp", "seq")),
            P(("dp", "seq")),
            P(),
            P(),
            P(),
            P(("dp", "seq")),
            P(("dp", "seq"), None),
        ),
        check_vma=False,
    )
```

time: 360 us -> 282 us (0.78)
  starting transfers between devices: 92.4 us -> 55.2 us
  waiting for transfers between devices: 53 us -> 32.6 us
  other arithmetic: 30.3 us -> 20.7 us
  Pallas kernels: 163 us -> 155 us
    ppermute x42 -> x35, starting transfers between devices: 84 us -> 46.2 us  [swap(): return lax.ppermute(value, axes, [(i, i ^ mask) for i in range(PIECES)])]
    ppermute x42 -> x35, waiting for transfers between devices: 52.9 us -> 32.6 us  [swap(): return lax.ppermute(value, axes, [(i, i ^ mask) for i in range(PIECES)])]
    convert_element_type x15 -> x8, other arithmetic: 13.7 us -> 5.03 us  [the longest x6 2.67 us: relay(): value = (totals * incoming + ends).astype(low)]
    pallas_call x9 -> x10, Pallas kernels: 163 us -> 155 us  [call(): pl.pallas_call(kernel, grid=(grid,), in_specs=in_specs, out_specs=out_spe...]
  transfers between devices with their start and end apart: 50 -> 43, of which waited for: 17 -> 10; matrix products, arithmetic and copies ran while one was open for 11% -> 7% of each run, Pallas kernels for 38% -> 43%
where the time goes in v2:
time: 282 us; the launch traced here: 281 us
  Pallas kernels  155 us (55%)
  starting transfers between devices  55.2 us (20%)
  waiting for transfers between devices  32.6 us (12%)
  other arithmetic  20.7 us (7%)
  local copies, waits for them, and re-layouts  16.7 us (6%)
    pallas_call x10, Pallas kernels, call(): pl.pallas_call(kernel, grid=(grid,), in_specs=in_specs, out_specs=out_spe...  155 us
    ppermute x35, starting transfers between devices, swap(): return lax.ppermute(value, axes, [(i, i ^ mask) for i in range(PIECES)])  46.2 us
    ppermute x35, waiting for transfers between devices, swap(): return lax.ppermute(value, axes, [(i, i ^ mask) for i in range(PIECES)])  32.6 us
    ppermute x6, starting transfers between devices, relay(): arrived = lax.ppermute(value, 'seq', route)  6.22 us
  transfers between devices with their start and end apart: 43, of which 10 were waited for; matrix products, arithmetic and copies ran while one was open for 7% of the time, Pallas kernels for 43%

profile of v2, /device:TPU:0, one launch (start us, length us, event | category | flops | bytes accessed | tf_op | source)
XLA Modules:
  0.0 281.1 jit_solution(10412403522258655336)
XLA Ops:
  3.8 3.0 %collective-permute-start = (bf16[24,1920]{1,0:T(8,128)(2,1)S(1)}, bf16[24,1920]{1,0:T(8,128)(2,1)S(1)}, u32[]{:S(2)}, u32[]{:S(2)}) collective-permute-start(bf16[24,1920]{1,0:T(8,128)(2,1)S(1)} %pad_maximum_fusion.8), channel_id=1, source_target_pairs={{0,8},{1,9},{2,10},{3,11},{4,12},{5,13},{6,14},{7,15},{8,0},{9,1},... | collective-permute-start | bytes 276488 | tf_op jit(solution)/shard_map/ppermute | solution.py:584
  6.8 2.6 collective-permute-start.1
  10.2 1.3 collective-permute-start.3
  14.4 2.3 collective-permute-done.1
  16.8 1.6 collective-permute-start.4
  18.5 1.5 collective-permute-start.5
  19.9 1.3 collective-permute-start.6
  21.3 1.5 collective-permute-start.7
  22.8 1.5 collective-permute-start.8
  26.2 6.2 %collective-permute-done.5 = bf16[2,24,1536]{2,1,0:T(8,128)(2,1)S(1)} collective-permute-done((bf16[2,24,1536]{2,1,0:T(8,128)(2,1)S(1)}, bf16[2,24,1536]{2,1,0:T(8,128)(2,1)S(1)}, u32[]{:S(2)}, u32[]{:S(2)}) %collective-permute-start.5) | collective-permute-done | bytes 147488 | tf_op jit(solution)/shard_map/ppermute | solution.py:584
  32.8 7.2 %collective-permute-done.9 = bf16[4,24,1920]{2,1,0:T(8,128)(2,1)S(1)} collective-permute-done((bf16[4,24,1920]{2,1,0:T(8,128)(2,1)S(1)}, bf16[4,24,1920]{2,1,0:T(8,128)(2,1)S(1)}, u32[]{:S(2)}, u32[]{:S(2)}) %collective-permute-start.9) | collective-permute-done | bytes 368672 | tf_op jit(solution)/shard_map/ppermute | solution.py:584
  42.0 1.5 collective-permute-start.12
  46.5 24.1 %conv.1 = (bf16[1024,768]{1,0:T(8,128)(2,1)}, bf16[768,1024]{1,0:T(8,128)(2,1)}, bf16[4,272,1792]{2,1,0:T(8,128)(2,1)}, f32[1024,1792]{1,0:T(8,128)}, bf16[1024,...) custom-call(s32[4]{0:T(128)} %pad_add_fusion.scal.past, ...), custom_call_target="tpu_custom_call" | custom-call | flops 3019898880 | bytes 6063120 | tf_op jit(solution)/shard_map/conv/pallas_call | solution.py:567
  72.6 1.6 collective-permute-start.14
  74.1 8.0 %intra.1 = f32[1024,1536]{1,0:T(8,128)} custom-call(bf16[1024,256]{1,0:T(8,128)(2,1)} %get-tuple-element.147.bc, bf16[1024,1536]{1,0:T(8,128)(2,1)} %get-tuple-element.120.xs, f32[1024,128]{1,0:T(8,128)} %get-tuple-element.115.cum, f32[4,24,256]{2,1,0:T(8,128)} %get-tuple-element.121.cumt), custom_call_target="tpu_custom_call" | custom-call | flops 1610612736 | bytes 4292608 | tf_op jit(solution)/shard_map/intra/pallas_call | solution.py:567
  83.0 12.7 %project.1 = (f32[1024,1536]{1,0:T(8,128)}, f32[1024,1536]{1,0:T(8,128)}, bf16[1024,768]{1,0:T(8,128)(2,1)}, bf16[768,1536]{1,0:T(8,128)(2,1)}, bf16[1536,768]{1,0:T(8,128)(2,1)}) custom-call(s32[4]{0:T(128)} %pad_add_fusion.scal.past, bf16[1024,768]{1,0:T(8,128)(2,1)} %get-tuple-element.129.nrm, bf16[1024,768]{1,0:T(8,128)(2,1)} %bitcast.99, ...), custom_call_target="tpu_custom_call" | custom-call | flops 4831838208 | bytes 7864336 | tf_op jit(solution)/shard_map/project/pallas_call | solution.py:567
  98.9 24.9 %gate.1 = (bf16[1024,768]{1,0:T(8,128)(2,1)}, bf16[1024,1536]{1,0:T(8,128)(2,1)}, bf16[1024,1536]{1,0:T(8,128)(2,1)}, bf16[1024,1536]{1,0:T(8,128)(2,1)}, bf16[1...) custom-call(s32[4]{0:T(128)} %pad_add_fusion.scal.past, ...), custom_call_target="tpu_custom_call" | custom-call | flops 4831838208 | bytes 31971344 | tf_op jit(solution)/shard_map/gate/pallas_call | solution.py:567
  124.6 1.5 add_convert_fusion.2
  126.8 15.3 %early_grad.1 = (bf16[16,2,24,1536]{3,2,1,0:T(8,128)(2,1)}, bf16[16,2,24,1536]{3,2,1,0:T(8,128)(2,1)}, f32[1024,768]{1,0:T(8,128)}) custom-call(s32[4]{0:T(128)} %pad_add_fusion.scal.past, bf16[768,1024]{1,0:T(8,128)(2,1)} %get-tuple-element.136.nrmt, bf16[1024,1536]{1,0:T(8,128)(2,1)} %get-tuple-element.137.dz.dzr, ...), custom_call_target="tpu_custom_call" | custom-call | flops 7247757312 | bytes 14942224 | tf_op jit(solution)/shard_map/early_grad/pallas_call | solution.py:567
  142.1 1.3 collective-permute-start.18
  144.9 18.0 %intra_back.1 = (f32[1024,1536]{1,0:T(8,128)}, f32[1024,256]{1,0:T(8,128)}, f32[1024,128]{1,0:T(8,128)}) custom-call(bf16[1024,256]{1,0:T(8,128)(2,1)} %get-tuple-element.147.bc, bf16[1024,1536]{1,0:T(8,128)(2,1)} %get-tuple-element.120.xs, bf16[1024,1536]{1,0:T(8,128)(2,1)} %get-tuple-element.122.xh, bf16[1024,1536]{1,0:T(8,128)(2,1)} %get-tuple-element.148.dy, ...), custom_call_target="tpu_custom_call" | custom-call | flops 3221225472 | bytes 11900928 | tf_op jit(solution)/shard_map/intra_back/pallas_call | solution.py:567
  163.3 1.6 collective-permute-start.24
  165.0 1.4 copy-done.4
  166.4 2.6 convert_add_fusion
  170.2 2.5 collective-permute-start.20
  172.7 1.5 collective-permute-start.21
  175.4 29.6 %conv_back.1 = (bf16[1024,1920]{1,0:T(8,128)(2,1)}, f32[40,1792]{1,0:T(8,128)}, f32[16,128]{1,0:T(8,128)}, bf16[2,8,1920]{2,1,0:T(8,128)(2,1)}, f32[2,16,1920]{2,1,0:T(8,128)}) custom-call(f32[4,128,1536]{2,1,0:T(8,128)} %get-tuple-element.152.dloc, f32[4,8,1536]{2,1,0:T(8,128)} %get-tuple-element.153.suf, bf16[2,128,1536]{2,1,0:T(8,128)(2,1)} %add_convert_fusion.inc, ...), custom_call_target="tpu_custom_call" | custom-call | flops 1207959552 | bytes 37708288 | tf_op jit(solution)/shard_map/conv_back/pallas_call | solution.py:567
  205.0 1.6 collective-permute-start.25
  206.6 1.4 fusion.15
  209.4 9.5 %late_grad.1 = (bf16[16,24,1920]{2,1,0:T(8,128)(2,1)}, bf16[16,24,1920]{2,1,0:T(8,128)(2,1)}, bf16[1024,1920]{1,0:T(8,128)(2,1)}) custom-call(s32[4]{0:T(128)} %pad_add_fusion.scal.past, bf16[768,1024]{1,0:T(8,128)(2,1)} %get-tuple-element.136.nrmt, bf16[1024,1920]{1,0:T(8,128)(2,1)} %get-tuple-element.171.dcv, f32[2,16,1920]{2,1,0:T(8,128)} %get-tuple-element.172.tails, ...), custom_call_target="tpu_custom_call" | custom-call | flops 3019898880 | bytes 5812240 | tf_op jit(solution)/shard_map/late_grad/pallas_call | solution.py:567
  218.8 2.4 collective-permute-start.26
  221.6 6.2 %input.2 = (bf16[1024,768]{1,0:T(8,128)(2,1)}, f32[8,768]{1,0:T(8,128)}) custom-call(bf16[1024,1920]{1,0:T(8,128)(2,1)} %get-tuple-element.174.dcv, f32[1024,768]{1,0:T(8,128)} %get-tuple-element.145.dnz, bf16[768,1920]{1,0:T(8,128)(2,1)} %get-tuple-element.175.wc, bf16[1024,768]{1,0:T(8,128)(2,1)} %bitcast.97, bf16[1024,768]{1,0:T(8,128)(2,1)} %bitcast.100, ...), custom_call_target="tpu_custom_call" | custom-call | flops 1509949440 | bytes 13197328 | tf_op jit(solution)/shard_map/input/pallas_call | solution.py:567
  227.9 1.7 convert_add_fusion.1
  232.0 3.5 %collective-permute-start.31 = (bf16[2,24,1536]{2,1,0:T(8,128)(2,1)}, bf16[2,24,1536]{2,1,0:T(8,128)(2,1)}, u32[]{:S(2)}, u32[]{:S(2)}) collective-permute-start(bf16[2,24,1536]{2,1,0:T(8,128)(2,1)} %get-tuple-element.193), channel_id=1, source_target_pairs={{0,16},{1,17},{2,18},{3,19},{4,20},{5,21},{6,22},{7,23},{8,24},{9,... | collective-permute-start | bytes 442376 | tf_op jit(solution)/shard_map/ppermute | solution.py:584
  235.8 1.5 collective-permute-start.28
  237.3 6.2 %input.3 = (bf16[1024,768]{1,0:T(8,128)(2,1)}, f32[8,768]{1,0:T(8,128)}) custom-call(bf16[1024,1920]{1,0:T(8,128)(2,1)} %get-tuple-element.174.dcv, f32[1024,768]{1,0:T(8,128)} %get-tuple-element.145.dnz, bf16[768,1920]{1,0:T(8,128)(2,1)} %get-tuple-element.175.wc, bf16[1024,768]{1,0:T(8,128)(2,1)} %bitcast.98, ...), custom_call_target="tpu_custom_call", output_to_operand_aliasing={{0}: (6, {})} | custom-call | flops 1509949440 | bytes 14770176 | tf_op jit(solution)/shard_map/input/pallas_call | solution.py:567
  244.3 1.3 collective-permute-start.29
  245.6 1.3 collective-permute-done.31
  248.0 6.5 %collective-permute-done.29 = bf16[4,24,1920]{2,1,0:T(8,128)(2,1)S(1)} collective-permute-done((bf16[4,24,1920]{2,1,0:T(8,128)(2,1)}, bf16[4,24,1920]{2,1,0:T(8,128)(2,1)S(1)}, u32[]{:S(2)}, u32[]{:S(2)}) %collective-permute-start.29) | collective-permute-done | bytes 368672 | tf_op jit(solution)/shard_map/ppermute | solution.py:584
  254.5 1.3 fusion.13
  257.2 3.5 %collective-permute-start.41 = (bf16[24,1920]{1,0:T(8,128)(2,1)S(1)}, bf16[24,1920]{1,0:T(8,128)(2,1)S(1)}, u32[]{:S(2)}, u32[]{:S(2)}) collective-permute-start(bf16[24,1920]{1,0:T(8,128)(2,1)S(1)} %get-tuple-element.201), channel_id=1, source_target_pairs={{0,16},{1,17},{2,18},{3,19},{4,20},{5,21},{6,22},{7,23},{8,24},{9,... | collective-permute-start | bytes 276488 | tf_op jit(solution)/shard_map/ppermute | solution.py:584
  261.0 1.4 collective-permute-start.34
  263.0 1.7 collective-permute-start.36
  264.6 3.5 %collective-permute-done.41 = bf16[24,1920]{1,0:T(8,128)(2,1)S(1)} collective-permute-done((bf16[24,1920]{1,0:T(8,128)(2,1)S(1)}, bf16[24,1920]{1,0:T(8,128)(2,1)S(1)}, u32[]{:S(2)}, u32[]{:S(2)}) %collective-permute-start.41) | collective-permute-done | bytes 92192 | tf_op jit(solution)/shard_map/ppermute | solution.py:584
  268.2 2.2 collective-permute-start.37
  270.5 1.7 collective-permute-start.38
  273.6 3.1 %collective-permute-done.38 = f32[96,128]{1,0:T(8,128)S(1)} collective-permute-done((f32[96,128]{1,0:T(8,128)S(1)}, f32[96,128]{1,0:T(8,128)S(1)}, u32[]{:S(2)}, u32[]{:S(2)}) %collective-permute-start.38) | collective-permute-done | bytes 49184 | tf_op jit(solution)/shard_map/ppermute | solution.py:584
  276.7 1.3 collective-permute-done.39
  (164 shorter events, 38.7 us)
Async XLA Ops:
  3.8 10.7 %collective-permute-start = (bf16[24,1920]{1,0:T(8,128)(2,1)S(1)}, bf16[24,1920]{1,0:T(8,128)(2,1)S(1)}, u32[]{:S(2)}, u32[]{:S(2)}) collective-permute-start(bf16[24,1920]{1,0:T(8,128)(2,1)S(1)} %pad_maximum_fusion.8), channel_id=1, source_target_pairs={{0,8},{1,9},{2,10},{3,11},{4,12},{5,13},{6,14},{7,15},{8,0},{9,1},... | collective-permute-start | bytes 276488 | tf_op jit(solution)/shard_map/ppermute | solution.py:584
  6.8 10.0 %collective-permute-start.1 = (bf16[24,1920]{1,0:T(8,128)(2,1)S(1)}, bf16[24,1920]{1,0:T(8,128)(2,1)S(1)}, u32[]{:S(2)}, u32[]{:S(2)}) collective-permute-start(bf16[24,1920]{1,0:T(8,128)(2,1)S(1)} %pad_maximum_fusion.8), channel_id=1, source_target_pairs={{0,16},{1,17},{2,18},{3,19},{4,20},{5,21},{6,22},{7,23},{8,24},{9,... | collective-permute-start | bytes 276488 | tf_op jit(solution)/shard_map/ppermute | solution.py:584
  9.4 7.4 %collective-permute-start.2 = (bf16[24,1920]{1,0:T(8,128)(2,1)S(1)}, bf16[24,1920]{1,0:T(8,128)(2,1)S(1)}, u32[]{:S(2)}, u32[]{:S(2)}) collective-permute-start(bf16[24,1920]{1,0:T(8,128)(2,1)S(1)} %pad_maximum_fusion.8), channel_id=1, source_target_pairs={{0,24},{1,25},{2,26},{3,27},{4,28},{5,29},{6,30},{7,31},{8,16},{9,... | collective-permute-start | bytes 276488 | tf_op jit(solution)/shard_map/ppermute | solution.py:584
  10.2 6.6 %collective-permute-start.3 = (bf16[2,16,768]{2,1,0:T(8,128)(2,1)S(1)}, bf16[2,16,768]{2,1,0:T(8,128)(2,1)S(1)}, u32[]{:S(2)}, u32[]{:S(2)}) collective-permute-start(bf16[2,16,768]{2,1,0:T(8,128)(2,1)S(1)} %slice.156), channel_id=1, source_target_pairs={{0,1},{1,2},{2,3},{4,5},{5,6},{6,7},{8,9},{9,10},{10,11},{12,13},{... | collective-permute-start | bytes 147464 | tf_op jit(solution)/shard_map/ppermute | solution.py:703
  16.8 8.3 %collective-permute-start.4 = (bf16[2,24,1536]{2,1,0:T(8,128)(2,1)S(1)}, bf16[2,24,1536]{2,1,0:T(8,128)(2,1)S(1)}, u32[]{:S(2)}, u32[]{:S(2)}) collective-permute-start(bf16[2,24,1536]{2,1,0:T(8,128)(2,1)S(1)} %pad_maximum_fusion.5), channel_id=1, source_target_pairs={{0,8},{1,9},{2,10},{3,11},{4,12},{5,13},{6,14},{7,15},{8,0},{9,1},... | collective-permute-start | bytes 442376 | tf_op jit(solution)/shard_map/ppermute | solution.py:584
  18.5 14.0 %collective-permute-start.5 = (bf16[2,24,1536]{2,1,0:T(8,128)(2,1)S(1)}, bf16[2,24,1536]{2,1,0:T(8,128)(2,1)S(1)}, u32[]{:S(2)}, u32[]{:S(2)}) collective-permute-start(bf16[2,24,1536]{2,1,0:T(8,128)(2,1)S(1)} %pad_maximum_fusion.5), channel_id=1, source_target_pairs={{0,16},{1,17},{2,18},{3,19},{4,20},{5,21},{6,22},{7,23},{8,24},{9,... | collective-permute-start | bytes 442376 | tf_op jit(solution)/shard_map/ppermute | solution.py:584
  19.9 12.5 %collective-permute-start.6 = (bf16[2,24,1536]{2,1,0:T(8,128)(2,1)S(1)}, bf16[2,24,1536]{2,1,0:T(8,128)(2,1)S(1)}, u32[]{:S(2)}, u32[]{:S(2)}) collective-permute-start(bf16[2,24,1536]{2,1,0:T(8,128)(2,1)S(1)} %pad_maximum_fusion.5), channel_id=1, source_target_pairs={{0,24},{1,25},{2,26},{3,27},{4,28},{5,29},{6,30},{7,31},{8,16},{9,... | collective-permute-start | bytes 442376 | tf_op jit(solution)/shard_map/ppermute | solution.py:584
  21.3 11.5 %collective-permute-start.7 = (bf16[4,24,1920]{2,1,0:T(8,128)(2,1)S(1)}, bf16[4,24,1920]{2,1,0:T(8,128)(2,1)S(1)}, u32[]{:S(2)}, u32[]{:S(2)}) collective-permute-start(bf16[4,24,1920]{2,1,0:T(8,128)(2,1)S(1)} %pad_maximum_fusion.3), channel_id=1, source_target_pairs={{0,2},{1,3},{2,0},{3,1},{4,6},{5,7},{6,4},{7,5},{8,10},{9,11},{10,... | collective-permute-start | bytes 1105928 | tf_op jit(solution)/shard_map/ppermute | solution.py:584
  22.8 10.0 %collective-permute-start.8 = (bf16[4,24,1920]{2,1,0:T(8,128)(2,1)S(1)}, bf16[4,24,1920]{2,1,0:T(8,128)(2,1)S(1)}, u32[]{:S(2)}, u32[]{:S(2)}) collective-permute-start(bf16[4,24,1920]{2,1,0:T(8,128)(2,1)S(1)} %pad_maximum_fusion.3), channel_id=1, source_target_pairs={{0,4},{1,5},{2,6},{3,7},{4,0},{5,1},{6,2},{7,3},{8,12},{9,13},{10,... | collective-permute-start | bytes 1105928 | tf_op jit(solution)/shard_map/ppermute | solution.py:584
  25.1 14.9 %collective-permute-start.9 = (bf16[4,24,1920]{2,1,0:T(8,128)(2,1)S(1)}, bf16[4,24,1920]{2,1,0:T(8,128)(2,1)S(1)}, u32[]{:S(2)}, u32[]{:S(2)}) collective-permute-start(bf16[4,24,1920]{2,1,0:T(8,128)(2,1)S(1)} %pad_maximum_fusion.3), channel_id=1, source_target_pairs={{0,6},{1,7},{2,4},{3,5},{4,2},{5,3},{6,0},{7,1},{8,14},{9,15},{10,... | collective-permute-start | bytes 1105928 | tf_op jit(solution)/shard_map/ppermute | solution.py:584
  32.5 12.2 %copy-start.15 = (s32[2]{0:T(128)S(1)}, s32[2]{0:T(128)}, u32[]{:S(2)}) copy-start(s32[2]{0:T(128)} %param.18) | copy-start | bytes 28
  32.5 12.8 %copy-start.16 = (f32[24]{0:T(128)S(1)}, f32[24]{0:T(128)}, u32[]{:S(2)}) copy-start(f32[24]{0:T(128)} %param.23) | copy-start | bytes 292
  40.2 6.3 %collective-permute-start.10 = (bf16[4,4,24,1920]{3,2,1,0:T(8,128)(2,1)S(1)}, bf16[4,4,24,1920]{3,2,1,0:T(8,128)(2,1)}, u32[]{:S(2)}, u32[]{:S(2)}) collective-permute-start(bf16[4,4,24,1920]{3,2,1,0:T(8,128)(2,1)S(1)} %pad_maximum_fusion.1), channel_id=1, source_target_pairs={{0,1},{1,0},{2,3},{3,2},{4,5},{5,4},{6,7},{7,6},{8,9},{9,8},{10,11... | collective-permute-start | bytes 4423688 | tf_op jit(solution)/shard_map/ppermute | solution.py:584
  41.2 29.4 %collective-permute-start.11 = (bf16[4,2,24,1536]{3,2,1,0:T(8,128)(2,1)S(1)}, bf16[4,2,24,1536]{3,2,1,0:T(8,128)(2,1)S(1)}, u32[]{:S(2)}, u32[]{:S(2)}) collective-permute-start(bf16[4,2,24,1536]{3,2,1,0:T(8,128)(2,1)S(1)} %pad_maximum_fusion.2), channel_id=1, source_target_pairs={{0,2},{1,3},{2,0},{3,1},{4,6},{5,7},{6,4},{7,5},{8,10},{9,11},{10,... | collective-permute-start | bytes 1769480 | tf_op jit(solution)/shard_map/ppermute | solution.py:584
  42.0 28.6 %collective-permute-start.12 = (bf16[4,2,24,1536]{3,2,1,0:T(8,128)(2,1)S(1)}, bf16[4,2,24,1536]{3,2,1,0:T(8,128)(2,1)S(1)}, u32[]{:S(2)}, u32[]{:S(2)}) collective-permute-start(bf16[4,2,24,1536]{3,2,1,0:T(8,128)(2,1)S(1)} %pad_maximum_fusion.2), channel_id=1, source_target_pairs={{0,4},{1,5},{2,6},{3,7},{4,0},{5,1},{6,2},{7,3},{8,12},{9,13},{10,... | collective-permute-start | bytes 1769480 | tf_op jit(solution)/shard_map/ppermute | solution.py:584
  43.6 27.1 %collective-permute-start.13 = (bf16[4,2,24,1536]{3,2,1,0:T(8,128)(2,1)S(1)}, bf16[4,2,24,1536]{3,2,1,0:T(8,128)(2,1)S(1)}, u32[]{:S(2)}, u32[]{:S(2)}) collective-permute-start(bf16[4,2,24,1536]{3,2,1,0:T(8,128)(2,1)S(1)} %pad_maximum_fusion.2), channel_id=1, source_target_pairs={{0,6},{1,7},{2,4},{3,5},{4,2},{5,3},{6,0},{7,1},{8,14},{9,15},{10,... | collective-permute-start | bytes 1769480 | tf_op jit(solution)/shard_map/ppermute | solution.py:584
  71.0 12.0 %collective-permute-start.16 = (bf16[4,4,2,24,1536]{4,3,2,1,0:T(8,128)(2,1)S(1)}, bf16[4,4,2,24,1536]{4,3,2,1,0:T(8,128)(2,1)}, u32[]{:S(2)}, u32[]{:S(2)}) collective-permute-start(bf16[4,4,2,24,1536]{4,3,2,1,0:T(8,128)(2,1)S(1)} %pad_maximum_fusion), channel_id=1, source_target_pairs={{0,1},{1,0},{2,3},{3,2},{4,5},{5,4},{6,7},{7,6},{8,9},{9,8},{10,11... | collective-permute-start | bytes 7077896 | tf_op jit(solution)/shard_map/ppermute | solution.py:584
  72.6 9.5 %collective-permute-start.14 = (bf16[2,128,1536]{2,1,0:T(8,128)(2,1)S(1)}, bf16[2,128,1536]{2,1,0:T(8,128)(2,1)S(1)}, u32[]{:S(2)}, u32[]{:S(2)}) collective-permute-start(bf16[2,128,1536]{2,1,0:T(8,128)(2,1)S(1)} %add_convert_fusion.5), channel_id=1, source_target_pairs={{0,1},{4,5},{8,9},{12,13},{16,17},{20,21},{24,25},{28,29}} | collective-permute-start | bytes 2359304 | tf_op jit(solution)/shard_map/ppermute | solution.py:664
  82.3 13.4 %collective-permute-start.15 = (bf16[2,128,1536]{2,1,0:T(8,128)(2,1)S(1)}, bf16[2,128,1536]{2,1,0:T(8,128)(2,1)S(1)}, u32[]{:S(2)}, u32[]{:S(2)}) collective-permute-start(bf16[2,128,1536]{2,1,0:T(8,128)(2,1)S(1)} %fusion.1), channel_id=1, source_target_pairs={{1,2},{5,6},{9,10},{13,14},{17,18},{21,22},{25,26},{29,30}} | collective-permute-start | bytes 2359304 | tf_op jit(solution)/shard_map/ppermute | solution.py:664
  96.1 1.7 collective-permute-start.17
  126.1 17.4 %collective-permute-start.19 = (bf16[2,128,1536]{2,1,0:T(8,128)(2,1)S(1)}, bf16[2,128,1536]{2,1,0:T(8,128)(2,1)S(1)}, u32[]{:S(2)}, u32[]{:S(2)}) collective-permute-start(bf16[2,128,1536]{2,1,0:T(8,128)(2,1)S(1)} %add_convert_fusion.2), channel_id=1, source_target_pairs={{3,2},{7,6},{11,10},{15,14},{19,18},{23,22},{27,26},{31,30}} | collective-permute-start | bytes 2359304 | tf_op jit(solution)/shard_map/ppermute | solution.py:664
  126.8 16.7 %copy-start.11 = (f32[2,1,1536]{2,1,0:T(1,128)S(1)}, f32[2,1,1536]{2,1,0:T(1,128)}, u32[]{:S(2)}) copy-start(f32[2,1,1536]{2,1,0:T(1,128)} %get-tuple-element.143) | copy-start | bytes 36868
  126.8 16.7 %copy-start.1 = (f32[2,128,1536]{2,1,0:T(8,128)S(1)}, f32[2,128,1536]{2,1,0:T(8,128)}, u32[]{:S(2)}) copy-start(f32[2,128,1536]{2,1,0:T(8,128)} %get-tuple-element.144) | copy-start | bytes 4718596
  142.1 22.8 %collective-permute-start.18 = (bf16[16,2,24,1536]{3,2,1,0:T(8,128)(2,1)}, bf16[16,2,24,1536]{3,2,1,0:T(8,128)(2,1)S(1)}, u32[]{:S(2)}, u32[]{:S(2)}) collective-permute-start(bf16[16,2,24,1536]{3,2,1,0:T(8,128)(2,1)} %get-tuple-element.142), channel_id=1, source_target_pairs={{0,1},{1,0},{2,3},{3,2},{4,5},{5,4},{6,7},{7,6},{8,9},{9,8},{10,11... | collective-permute-start | bytes 7077896 | tf_op jit(solution)/shard_map/ppermute | solution.py:584
  143.7 19.3 %collective-permute-start.23 = (bf16[2,128,1536]{2,1,0:T(8,128)(2,1)S(1)}, bf16[2,128,1536]{2,1,0:T(8,128)(2,1)S(1)}, u32[]{:S(2)}, u32[]{:S(2)}) collective-permute-start(bf16[2,128,1536]{2,1,0:T(8,128)(2,1)S(1)} %fusion.3), channel_id=1, source_target_pairs={{2,1},{6,5},{10,9},{14,13},{18,17},{22,21},{26,25},{30,29}} | collective-permute-start | bytes 2359304 | tf_op jit(solution)/shard_map/ppermute | solution.py:664
  163.3 10.9 %collective-permute-start.24 = (bf16[2,128,1536]{2,1,0:T(8,128)(2,1)S(1)}, bf16[2,128,1536]{2,1,0:T(8,128)(2,1)S(1)}, u32[]{:S(2)}, u32[]{:S(2)}) collective-permute-start(bf16[2,128,1536]{2,1,0:T(8,128)(2,1)S(1)} %add_convert_fusion.1), channel_id=1, source_target_pairs={{1,0},{5,4},{9,8},{13,12},{17,16},{21,20},{25,24},{29,28}} | collective-permute-start | bytes 2359304 | tf_op jit(solution)/shard_map/ppermute | solution.py:664
  170.2 36.4 %collective-permute-start.20 = (bf16[4,2,24,1536]{3,2,1,0:T(8,128)(2,1)}, bf16[4,2,24,1536]{3,2,1,0:T(8,128)(2,1)S(1)}, u32[]{:S(2)}, u32[]{:S(2)}) collective-permute-start(bf16[4,2,24,1536]{3,2,1,0:T(8,128)(2,1)} %get-tuple-element.215), channel_id=1, source_target_pairs={{0,2},{1,3},{2,0},{3,1},{4,6},{5,7},{6,4},{7,5},{8,10},{9,11},{10,... | collective-permute-start | bytes 1769480 | tf_op jit(solution)/shard_map/ppermute | solution.py:584
  172.7 33.9 %collective-permute-start.21 = (bf16[4,2,24,1536]{3,2,1,0:T(8,128)(2,1)}, bf16[4,2,24,1536]{3,2,1,0:T(8,128)(2,1)S(1)}, u32[]{:S(2)}, u32[]{:S(2)}) collective-permute-start(bf16[4,2,24,1536]{3,2,1,0:T(8,128)(2,1)} %get-tuple-element.214), channel_id=1, source_target_pairs={{0,4},{1,5},{2,6},{3,7},{4,0},{5,1},{6,2},{7,3},{8,12},{9,13},{10,... | collective-permute-start | bytes 1769480 | tf_op jit(solution)/shard_map/ppermute | solution.py:584
  174.2 32.4 %collective-permute-start.22 = (bf16[4,2,24,1536]{3,2,1,0:T(8,128)(2,1)}, bf16[4,2,24,1536]{3,2,1,0:T(8,128)(2,1)}, u32[]{:S(2)}, u32[]{:S(2)}) collective-permute-start(bf16[4,2,24,1536]{3,2,1,0:T(8,128)(2,1)} %get-tuple-element.213), channel_id=1, source_target_pairs={{0,6},{1,7},{2,4},{3,5},{4,2},{5,3},{6,0},{7,1},{8,14},{9,15},{10,... | collective-permute-start | bytes 1769480 | tf_op jit(solution)/shard_map/ppermute | solution.py:584
  205.0 3.7 %collective-permute-start.25 = (bf16[2,8,1920]{2,1,0:T(8,128)(2,1)}, bf16[2,8,1920]{2,1,0:T(8,128)(2,1)S(1)}, u32[]{:S(2)}, u32[]{:S(2)}) collective-permute-start(bf16[2,8,1920]{2,1,0:T(8,128)(2,1)} %get-tuple-element.173), channel_id=1, source_target_pairs={{1,0},{2,1},{3,2},{5,4},{6,5},{7,6},{9,8},{10,9},{11,10},{13,12},{... | collective-permute-start | bytes 184328 | tf_op jit(solution)/shard_map/ppermute | solution.py:1033
  209.3 12.3 %copy-start.13 = (f32[16,128]{1,0:T(8,128)S(1)}, f32[16,128]{1,0:T(8,128)}, u32[]{:S(2)}) copy-start(f32[16,128]{1,0:T(8,128)} %get-tuple-element.166) | copy-start | bytes 24580
  218.8 9.1 %collective-permute-start.26 = (bf16[16,24,1920]{2,1,0:T(8,128)(2,1)}, bf16[16,24,1920]{2,1,0:T(8,128)(2,1)}, u32[]{:S(2)}, u32[]{:S(2)}) collective-permute-start(bf16[16,24,1920]{2,1,0:T(8,128)(2,1)} %get-tuple-element.178), channel_id=1, source_target_pairs={{0,1},{1,0},{2,3},{3,2},{4,5},{5,4},{6,7},{7,6},{8,9},{9,8},{10,11... | collective-permute-start | bytes 4423688 | tf_op jit(solution)/shard_map/ppermute | solution.py:584
  230.7 17.3 %collective-permute-start.27 = (bf16[4,24,1920]{2,1,0:T(8,128)(2,1)}, bf16[4,24,1920]{2,1,0:T(8,128)(2,1)}, u32[]{:S(2)}, u32[]{:S(2)}) collective-permute-start(bf16[4,24,1920]{2,1,0:T(8,128)(2,1)} %get-tuple-element.218), channel_id=1, source_target_pairs={{0,2},{1,3},{2,0},{3,1},{4,6},{5,7},{6,4},{7,5},{8,10},{9,11},{10,... | collective-permute-start | bytes 1105928 | tf_op jit(solution)/shard_map/ppermute | solution.py:584
  231.4 12.9 %collective-permute-start.30 = (bf16[2,24,1536]{2,1,0:T(8,128)(2,1)}, bf16[2,24,1536]{2,1,0:T(8,128)(2,1)}, u32[]{:S(2)}, u32[]{:S(2)}) collective-permute-start(bf16[2,24,1536]{2,1,0:T(8,128)(2,1)} %get-tuple-element.192), channel_id=1, source_target_pairs={{0,8},{1,9},{2,10},{3,11},{4,12},{5,13},{6,14},{7,15},{8,0},{9,1},... | collective-permute-start | bytes 442376 | tf_op jit(solution)/shard_map/ppermute | solution.py:584
  232.0 14.9 %collective-permute-start.31 = (bf16[2,24,1536]{2,1,0:T(8,128)(2,1)}, bf16[2,24,1536]{2,1,0:T(8,128)(2,1)}, u32[]{:S(2)}, u32[]{:S(2)}) collective-permute-start(bf16[2,24,1536]{2,1,0:T(8,128)(2,1)} %get-tuple-element.193), channel_id=1, source_target_pairs={{0,16},{1,17},{2,18},{3,19},{4,20},{5,21},{6,22},{7,23},{8,24},{9,... | collective-permute-start | bytes 442376 | tf_op jit(solution)/shard_map/ppermute | solution.py:584
  235.5 11.4 %collective-permute-start.32 = (bf16[2,24,1536]{2,1,0:T(8,128)(2,1)S(1)}, bf16[2,24,1536]{2,1,0:T(8,128)(2,1)}, u32[]{:S(2)}, u32[]{:S(2)}) collective-permute-start(bf16[2,24,1536]{2,1,0:T(8,128)(2,1)S(1)} %get-tuple-element.194), channel_id=1, source_target_pairs={{0,24},{1,25},{2,26},{3,27},{4,28},{5,29},{6,30},{7,31},{8,16},{9,... | collective-permute-start | bytes 442376 | tf_op jit(solution)/shard_map/ppermute | solution.py:584
  235.8 12.3 %collective-permute-start.28 = (bf16[4,24,1920]{2,1,0:T(8,128)(2,1)}, bf16[4,24,1920]{2,1,0:T(8,128)(2,1)}, u32[]{:S(2)}, u32[]{:S(2)}) collective-permute-start(bf16[4,24,1920]{2,1,0:T(8,128)(2,1)} %get-tuple-element.217), channel_id=1, source_target_pairs={{0,4},{1,5},{2,6},{3,7},{4,0},{5,1},{6,2},{7,3},{8,12},{9,13},{10,... | collective-permute-start | bytes 1105928 | tf_op jit(solution)/shard_map/ppermute | solution.py:584
  244.3 10.3 %collective-permute-start.29 = (bf16[4,24,1920]{2,1,0:T(8,128)(2,1)}, bf16[4,24,1920]{2,1,0:T(8,128)(2,1)S(1)}, u32[]{:S(2)}, u32[]{:S(2)}) collective-permute-start(bf16[4,24,1920]{2,1,0:T(8,128)(2,1)} %get-tuple-element.216), channel_id=1, source_target_pairs={{0,6},{1,7},{2,4},{3,5},{4,2},{5,3},{6,0},{7,1},{8,14},{9,15},{10,... | collective-permute-start | bytes 1105928 | tf_op jit(solution)/shard_map/ppermute | solution.py:584
  255.9 5.1 %collective-permute-start.33 = (f32[96,128]{1,0:T(8,128)S(1)}, f32[96,128]{1,0:T(8,128)S(1)}, u32[]{:S(2)}, u32[]{:S(2)}) collective-permute-start(f32[96,128]{1,0:T(8,128)S(1)} %pad_bitcast_fusion), channel_id=1, source_target_pairs={{0,1},{1,0},{2,3},{3,2},{4,5},{5,4},{6,7},{7,6},{8,9},{9,8},{10,11... | collective-permute-start | bytes 147464 | tf_op jit(solution)/shard_map/ppermute | solution.py:584
  256.6 6.3 %collective-permute-start.40 = (bf16[24,1920]{1,0:T(8,128)(2,1)S(1)}, bf16[24,1920]{1,0:T(8,128)(2,1)S(1)}, u32[]{:S(2)}, u32[]{:S(2)}) collective-permute-start(bf16[24,1920]{1,0:T(8,128)(2,1)S(1)} %get-tuple-element.198), channel_id=1, source_target_pairs={{0,8},{1,9},{2,10},{3,11},{4,12},{5,13},{6,14},{7,15},{8,0},{9,1},... | collective-permute-start | bytes 276488 | tf_op jit(solution)/shard_map/ppermute | solution.py:584
  257.2 10.9 %collective-permute-start.41 = (bf16[24,1920]{1,0:T(8,128)(2,1)S(1)}, bf16[24,1920]{1,0:T(8,128)(2,1)S(1)}, u32[]{:S(2)}, u32[]{:S(2)}) collective-permute-start(bf16[24,1920]{1,0:T(8,128)(2,1)S(1)} %get-tuple-element.201), channel_id=1, source_target_pairs={{0,16},{1,17},{2,18},{3,19},{4,20},{5,21},{6,22},{7,23},{8,24},{9,... | collective-permute-start | bytes 276488 | tf_op jit(solution)/shard_map/ppermute | solution.py:584
  260.8 7.4 %collective-permute-start.42 = (bf16[24,1920]{1,0:T(8,128)(2,1)S(1)}, bf16[24,1920]{1,0:T(8,128)(2,1)S(1)}, u32[]{:S(2)}, u32[]{:S(2)}) collective-permute-start(bf16[24,1920]{1,0:T(8,128)(2,1)S(1)} %get-tuple-element.202), channel_id=1, source_target_pairs={{0,24},{1,25},{2,26},{3,27},{4,28},{5,29},{6,30},{7,31},{8,16},{9,... | collective-permute-start | bytes 276488 | tf_op jit(solution)/shard_map/ppermute | solution.py:584
  261.0 7.1 %collective-permute-start.34 = (f32[96,128]{1,0:T(8,128)S(1)}, f32[96,128]{1,0:T(8,128)S(1)}, u32[]{:S(2)}, u32[]{:S(2)}) collective-permute-start(f32[96,128]{1,0:T(8,128)S(1)} %fusion.10), channel_id=1, source_target_pairs={{0,2},{1,3},{2,0},{3,1},{4,6},{5,7},{6,4},{7,5},{8,10},{9,11},{10,... | collective-permute-start | bytes 147464 | tf_op jit(solution)/shard_map/ppermute | solution.py:584
  262.4 5.8 %collective-permute-start.35 = (f32[96,128]{1,0:T(8,128)S(1)}, f32[96,128]{1,0:T(8,128)S(1)}, u32[]{:S(2)}, u32[]{:S(2)}) collective-permute-start(f32[96,128]{1,0:T(8,128)S(1)} %fusion.10), channel_id=1, source_target_pairs={{0,4},{1,5},{2,6},{3,7},{4,0},{5,1},{6,2},{7,3},{8,12},{9,13},{10,... | collective-permute-start | bytes 147464 | tf_op jit(solution)/shard_map/ppermute | solution.py:584
  263.0 5.3 %collective-permute-start.36 = (f32[96,128]{1,0:T(8,128)S(1)}, f32[96,128]{1,0:T(8,128)S(1)}, u32[]{:S(2)}, u32[]{:S(2)}) collective-permute-start(f32[96,128]{1,0:T(8,128)S(1)} %fusion.10), channel_id=1, source_target_pairs={{0,6},{1,7},{2,4},{3,5},{4,2},{5,3},{6,0},{7,1},{8,14},{9,15},{10,... | collective-permute-start | bytes 147464 | tf_op jit(solution)/shard_map/ppermute | solution.py:584
  268.2 5.4 %collective-permute-start.37 = (f32[96,128]{1,0:T(8,128)S(1)}, f32[96,128]{1,0:T(8,128)S(1)}, u32[]{:S(2)}, u32[]{:S(2)}) collective-permute-start(f32[96,128]{1,0:T(8,128)S(1)} %add_add_fusion.2), channel_id=1, source_target_pairs={{0,8},{1,9},{2,10},{3,11},{4,12},{5,13},{6,14},{7,15},{8,0},{9,1},... | collective-permute-start | bytes 147464 | tf_op jit(solution)/shard_map/ppermute | solution.py:584
  270.5 6.3 %collective-permute-start.38 = (f32[96,128]{1,0:T(8,128)S(1)}, f32[96,128]{1,0:T(8,128)S(1)}, u32[]{:S(2)}, u32[]{:S(2)}) collective-permute-start(f32[96,128]{1,0:T(8,128)S(1)} %add_add_fusion.2), channel_id=1, source_target_pairs={{0,16},{1,17},{2,18},{3,19},{4,20},{5,21},{6,22},{7,23},{8,24},{9,... | collective-permute-start | bytes 147464 | tf_op jit(solution)/shard_map/ppermute | solution.py:584
  272.1 5.9 %collective-permute-start.39 = (f32[96,128]{1,0:T(8,128)S(1)}, f32[96,128]{1,0:T(8,128)S(1)}, u32[]{:S(2)}, u32[]{:S(2)}) collective-permute-start(f32[96,128]{1,0:T(8,128)S(1)} %add_add_fusion.2), channel_id=1, source_target_pairs={{0,24},{1,25},{2,26},{3,27},{4,28},{5,29},{6,30},{7,31},{8,16},{9,... | collective-permute-start | bytes 147464 | tf_op jit(solution)/shard_map/ppermute | solution.py:584
  (14 other events, 83.8 us)

commit v3 on v2

--- a/solution.py
+++ b/solution.py
@@ -23,6 +23,17 @@
 RIM = 16
 PIECES = 32
 NEG = -1e30
+LIMITS = {
+    "conv": 56,
+    "intra": 56,
+    "project": 48,
+    "gate": 48,
+    "early_grad": 56,
+    "intra_back": 56,
+    "conv_back": 56,
+    "late_grad": 56,
+    "input": 56,
+}
 
 epsilon = 1e-05
 low = jnp.bfloat16
@@ -72,9 +83,24 @@
     return nn(packed, table)
 
 
+def spread_all(packed, table):
+    wide = nn(jnp.concatenate(packed, axis=0), table)
+    parts, at = [], 0
+    for value in packed:
+        parts.append(wide[at : at + value.shape[0], :])
+        at += value.shape[0]
+    return parts
+
+
+def gather_all(values, table):
+    tops = [value.astype(low) for value in values]
+    rests = [(value - top.astype(f32)).astype(low) for value, top in zip(values, tops)]
+    parts = spread_all(tops + rests, table)
+    return [parts[i] + parts[i + len(values)] for i in range(len(values))]
+
+
 def gather_heads(value, table):
-    top = value.astype(low)
-    return nn(top, table) + nn((value - top.astype(f32)).astype(low), table)
+    return gather_all([value], table)[0]
 
 
 def running_sum(value, reverse):
@@ -114,13 +140,14 @@
 
 
 def conv_kernel(
-    groups, scal, x, halo, wa, wb, t56, t48, t24, sb, rate, e,
+    groups, scal, x, halo, wa, wb, t56, t48, t24, par, e,
     nrm_o, nrmt_o, cie_o, sp_o, xh_o, xs_o, wx_o, bc_o, step_o, cum_o, dtb_o, cumt_o,
-    sloc_o, pre_o, r_o, tot_o, wc_o, taps_o, gain_o, gate_o,
-    nrm, cs, run, dec, small,
+    sloc_o, pre_o, r_o, rl_o, tot_o, wc_o, taps_o, gain_o, gate_o,
+    nrm, run, dec, small, *slots,
 ):
     block = pl.program_id(0)
     fresh = block % groups == 0
+    zero = scal[scal.shape[0] - 1]
 
     @pl.when(block == 0)
     def assemble():
@@ -167,23 +194,27 @@
         cols = slice(c, c + CH)
         conv_in = nn(nrm[...], wc_o[:, cols]).astype(low)
         cie_o[:, cols] = conv_in
-        cs[...] = conv_in.astype(f32)
-        for r in range(0, Q, 32):
-            taps = taps_o[0:1, cols] * cs[RIM - 3 + r : RIM + 29 + r, :]
-            for k in range(1, KW):
-                taps = taps + taps_o[k : k + 1, cols] * cs[RIM - 3 + k + r : RIM + 29 + k + r, :]
-            pre = taps_o[KW : KW + 1, cols] + taps
-            sig = jax.nn.sigmoid(pre)
-            act = (pre * sig).astype(low)
-            sp_o[r : r + 32, cols] = sig * (1.0 + pre * (1.0 - sig))
-            if c < DI:
-                xh_o[r : r + 32, cols] = act
-            else:
-                bc_o[r : r + 32, :] = act
-
-    dtb = nn(nrm[RIM:, :], wc_o[:, CD:CW]) + sb[...]
+        wide = conv_in.astype(f32)
+        for side in range(2):
+            span = slice(c + side * HALF, c + (side + 1) * HALF)
+            cs = slots[c // HALF + side]
+            cs[...] = wide[:, side * HALF : (side + 1) * HALF]
+            for r in range(0, Q, 64):
+                taps = taps_o[0:1, span] * cs[pl.ds(zero + (RIM - 3 + r), 64), :]
+                for k in range(1, KW):
+                    taps = taps + taps_o[k : k + 1, span] * cs[pl.ds(zero + (RIM - 3 + k + r), 64), :]
+                pre = taps_o[KW : KW + 1, span] + taps
+                sig = jax.nn.sigmoid(pre)
+                act = (pre * sig).astype(low)
+                sp_o[r : r + 64, span] = sig * (1.0 + pre * (1.0 - sig))
+                if c < DI:
+                    xh_o[r : r + 64, span] = act
+                else:
+                    bc_o[r : r + 64, side * HALF : (side + 1) * HALF] = act
+
+    dtb = nn(nrm[RIM:, :], wc_o[:, CD:CW]) + par[0:1, :]
     step = softplus(dtb)
-    cum = running_sum(-step * rate[...], False)
+    cum = running_sum(-step * par[1:2, :], False)
     step_o[...] = step
     cum_o[...] = cum
     dtb_o[...] = dtb
@@ -197,15 +228,16 @@
         table = e[:, cols]
         wide = xh_o[:, cols].astype(f32)
         xs_o[:, cols] = (spread(steps, table) * wide).astype(low)
-        weighted = (spread(tails, table) * wide).astype(low)
+        tail_e, decay = spread_all([tails, decays], table)
+        weighted = (tail_e * wide).astype(low)
         wx_o[:, cols] = weighted
         local = tn(bc_o[:, 0:N], weighted)
-        decay = spread(decays, table)
         before = jnp.where(fresh, 0.0, run[:, cols])
         sloc_o[:, cols] = before
         after = decay[0:1, :] * before + local
         run[:, cols] = after
         r_o[:, cols] = after
+        rl_o[:, cols] = after.astype(low)
         product = jnp.where(fresh, 1.0, dec[:, cols])
         pre_o[:, cols] = product
         product = product * decay
@@ -213,26 +245,34 @@
         tot_o[:, cols] = product[0:1, :]
 
 
+def block_rows(block):
+    return pl.ds(pl.multiple_of(block * Q, Q), Q)
+
+
 def intra_kernel(bc, xs, cum, cumt, o, sc):
     sc[...] = nt(bc[:, N : 2 * N], bc[:, 0:N])
     at = lax.broadcasted_iota(jnp.int32, (HALF, HALF), 0)
     to = lax.broadcasted_iota(jnp.int32, (HALF, HALF), 1)
     lower = at >= to
-    left = lax.broadcasted_iota(jnp.int32, (Q, HALF), 1) < P_SIZE
+    left = lax.broadcasted_iota(jnp.int32, (HALF, HALF), 1) < P_SIZE
     for pair in range(H // 2):
         cols = slice(pair * HALF, (pair + 1) * HALF)
         x_pair = xs[:, cols]
-        tops, bottoms = [], []
+        m00, m10, m11 = [], [], []
         for h in (2 * pair, 2 * pair + 1):
             row = cumt[h : h + 1, :]
             upper_col, lower_col = cum[0:HALF, h : h + 1], cum[HALF:, h : h + 1]
-            m00 = sc[0:HALF, 0:HALF] * jnp.exp2(jnp.where(lower, upper_col - row[:, 0:HALF], NEG))
-            m10 = sc[HALF:, 0:HALF] * jnp.exp2(lower_col - row[:, 0:HALF])
-            m11 = sc[HALF:, HALF:] * jnp.exp2(jnp.where(lower, lower_col - row[:, HALF:], NEG))
-            tops.append(nn(m00.astype(low), x_pair[0:HALF, :]))
-            bottoms.append(nn(jnp.concatenate([m10.astype(low), m11.astype(low)], axis=1), x_pair))
-        o[0:HALF, cols] = jnp.where(left[0:HALF], tops[0], tops[1])
-        o[HALF:, cols] = jnp.where(left[0:HALF], bottoms[0], bottoms[1])
+            l00 = jnp.exp2(jnp.where(lower, upper_col - row[:, 0:HALF], NEG))
+            m00.append((sc[0:HALF, 0:HALF] * l00).astype(low))
+            l10 = jnp.exp2(lower_col - row[:, 0:HALF])
+            m10.append((sc[HALF:, 0:HALF] * l10).astype(low))
+            l11 = jnp.exp2(jnp.where(lower, lower_col - row[:, HALF:], NEG))
+            m11.append((sc[HALF:, HALF:] * l11).astype(low))
+        top = nn(jnp.concatenate(m00, axis=0), x_pair[0:HALF, :])
+        sides = [jnp.concatenate([m10[i], m11[i]], axis=1) for i in range(2)]
+        bottom = nn(jnp.concatenate(sides, axis=0), x_pair)
+        o[0:HALF, cols] = jnp.where(left, top[0:HALF, :], top[HALF:, :])
+        o[HALF:, cols] = jnp.where(left, bottom[0:HALF, :], bottom[HALF:, :])
 
 
 def valid_column(scal, groups, block):
@@ -241,8 +281,9 @@
     return (at < scal[2 + seq]).astype(f32)
 
 
-def project_kernel(groups, scal, nrm, cot, wa, wb, z_o, dn_o, db_o, wz_o, wo_o):
+def project_kernel(groups, scal, nrm, cot, wa, wb, z_all, dn_all, db_o, wz_o, wo_o):
     block = pl.program_id(0)
+    z_o, dn_o = z_all.at[block_rows(block), :], dn_all.at[block_rows(block), :]
 
     @pl.when(block == 0)
     def assemble():
@@ -268,81 +309,87 @@
 
 
 def gate_kernel(
-    groups, scal, intra, xh, bc, cum, sloc, pre, inc, z, dn, hid, wo, gg, skip, e, et,
-    out_o, dz_o, dy_o, gdy_o, gn_o, sbf_o, rs_o, dloc_o, suf_o, rd_o, tot_o, gacc_o, kacc_o,
-    yi_s, ge_s, pr_s, y_s, sg_s, gt_s, run, dec,
+    groups, hops, scal, intra, xh, bc, cum, sloc, pre, *refs
 ):
+    inc = refs[:hops]
+    z_all, dn_all, hid, wo, gg, par, e, et = refs[hops : hops + 8]
+    (
+        out_o, dz_o, dy_o, gdy_o, gn_o, sbf_o, rs_o, dloc_o, suf_o, rd_o, rdl_o, tot_o, kacc_o,
+        yi_s, ge_s, pr_s, y_s, sg_s, gt_s, run, dec, skip, fall,
+    ) = refs[hops + 8 :]
     at = pl.program_id(0)
     fresh = at % groups == 0
     block = (at // groups) * groups + groups - 1 - at % groups
+    here = block_rows(block)
+    z, dn = z_all.at[here, :], dn_all.at[here, :]
 
     @pl.when(at == 0)
     def start():
-        gacc_o[...] = jnp.zeros_like(gacc_o)
         kacc_o[...] = jnp.zeros_like(kacc_o)
 
     c_rows = bc[:, N : 2 * N]
     growth = pack(jnp.exp2(cum[...]))
+    params = pack(par[...])
+    decays = pack(jnp.broadcast_to(jnp.exp2(cum[Q - 1 : Q, :]), (8, HL)))
     for c in range(0, DI, CH):
         cols = slice(c, c + CH)
-        begin = (sloc[:, cols] + pre[0:1, cols] * inc[:, cols].astype(f32)).astype(low)
+        begin = (sloc[:, cols] + pre[0:1, cols] * total_of(inc, cols)).astype(low)
         sbf_o[:, cols] = begin
-        wide = spread(growth, e[:, cols])
+        wide, skip[:, cols], fall[:, cols] = spread_all([growth, params, decays], e[:, cols])
         ge_s[:, cols] = wide
         yi_s[:, cols] = intra[:, cols] + wide * nn(c_rows, begin)
 
-    def body(i, carry):
-        rows = pl.ds(pl.multiple_of(i * 32, 32), 32)
+    def body(r):
+        rows = slice(r, r + 32)
         squares = jnp.zeros((32, HALF), f32)
         crosses = jnp.zeros((32, HALF), f32)
         for c in range(0, DI, HALF):
             cols = slice(c, c + HALF)
             zv = z[rows, cols]
-            y = yi_s[rows, cols] + skip[:, cols] * xh[rows, cols].astype(f32)
+            y = yi_s[rows, cols] + skip[3:4, cols] * xh[rows, cols].astype(f32)
             sig = jax.nn.sigmoid(zv)
             gated = y * (zv * sig)
             squares = squares + gated * gated
             crosses = crosses + (dn[rows, cols] * gg[0:1, cols]) * gated
-            y_s[:, cols] = y
-            sg_s[:, cols] = sig
-            gt_s[:, cols] = gated
+            y_s[rows, cols] = y
+            sg_s[rows, cols] = sig
+            gt_s[rows, cols] = gated
         scale = lax.rsqrt(jnp.sum(squares, axis=1, keepdims=True) / DI + epsilon)
         shift = scale * scale * scale * (jnp.sum(crosses, axis=1, keepdims=True) / DI)
         for c in range(0, DI, HALF):
             cols = slice(c, c + HALF)
-            zv, y, sig, gated = z[rows, cols], y_s[:, cols], sg_s[:, cols], gt_s[:, cols]
-            wide = dn[rows, cols]
-            normal = gated * scale
-            gn_o[rows, cols] = (normal * gg[0:1, cols]).astype(low)
-            gacc_o[:, cols] += fold8(wide * normal)
-            d_gated = scale * (wide * gg[0:1, cols]) - gated * shift
+            zv, y, sig, gated = z[rows, cols], y_s[rows, cols], sg_s[rows, cols], gt_s[rows, cols]
+            gained = gg[0:1, cols]
+            gn_o[rows, cols] = (gated * scale * gained).astype(low)
+            d_gated = scale * (dn[rows, cols] * gained) - gated * shift
             d_sig = d_gated * sig
-            dz_o[rows, cols] = (d_sig * y * (1.0 + zv * (1.0 - sig))).astype(low)
-            d_low = (d_sig * zv).astype(low)
+            d_wide = d_sig * zv
+            dz_o[rows, cols] = (y * (d_sig + d_wide * (1.0 - sig))).astype(low)
+            d_low = d_wide.astype(low)
             dy_o[rows, cols] = d_low
             d_y = d_low.astype(f32)
             kacc_o[:, cols] += fold8(d_y * xh[rows, cols].astype(f32))
             gdy_o[rows, cols] = (ge_s[rows, cols] * d_y).astype(low)
             pr_s[rows, cols] = d_y * yi_s[rows, cols]
-        return carry
-
-    lax.fori_loop(0, Q // 32, body, 0)
+
+    for r in range(0, Q, 32):
+        body(r)
 
     valid = valid_column(scal, groups, block)
     for c in range(0, DI // 2, CH):
         branch = nn(gn_o[...], wo[:, c : c + CH])
         out_o[:, c : c + CH] = (hid[:, c : c + CH].astype(f32) + valid * branch).astype(low)
-    decays = pack(jnp.broadcast_to(jnp.exp2(cum[Q - 1 : Q, :]), (8, HL)))
     sums = jnp.zeros((Q, HL), f32)
     for c in range(0, DI, CH):
         cols = slice(c, c + CH)
         sums = sums + gather_heads(pr_s[:, cols], et[cols, :])
-        decay = spread(decays, e[:, cols])
+        decay = fall[:, cols]
         before = jnp.where(fresh, 0.0, run[:, cols])
         dloc_o[:, cols] = before
         after = decay[0:1, :] * before + tn(c_rows, gdy_o[:, cols])
         run[:, cols] = after
         rd_o[:, cols] = after
+        rdl_o[:, cols] = after.astype(low)
         product = jnp.where(fresh, 1.0, dec[:, cols])
         suf_o[:, cols] = product
         product = product * decay
@@ -351,7 +398,7 @@
     rs_o[...] = sums
 
 
-def intra_back_kernel(bc, xs, xh, dy, step, cum, cumt, skip, e, et, dx_o, dbc_o, rs_o, sc, acc):
+def intra_back_kernel(bc, xs, xh, dy, step, cum, cumt, par, e, et, dx_o, dbc_o, rs_o, sc, acc):
     sc[...] = nt(bc[:, 0:N], bc[:, N : 2 * N])
     acc[...] = jnp.zeros_like(acc)
     at = lax.broadcasted_iota(jnp.int32, (HALF, HALF), 0)
@@ -359,40 +406,62 @@
     upper = at <= to
     left = lax.broadcasted_iota(jnp.int32, (Q, HALF), 1) < P_SIZE
     steps = pack(step[...])
+    params = pack(par[...])
     sums = jnp.zeros((Q, HL), f32)
-    for pair in range(H // 2):
-        cols = slice(pair * HALF, (pair + 1) * HALF)
-        dy_pair = dy[:, cols]
-        x_pair = xs[:, cols]
-        tops, bottoms, parts = [], [], []
-        for h in (2 * pair, 2 * pair + 1):
-            keep = left if h % 2 == 0 else jnp.logical_not(left)
-            x_half = jnp.where(keep, x_pair, jnp.zeros_like(x_pair))
-            row = cumt[h : h + 1, :]
-            first_col, second_col = cum[0:HALF, h : h + 1], cum[HALF:, h : h + 1]
-            l00 = jnp.exp2(jnp.where(upper, row[:, 0:HALF] - first_col, NEG))
-            l01 = jnp.exp2(row[:, HALF:] - first_col)
-            l11 = jnp.exp2(jnp.where(upper, row[:, HALF:] - second_col, NEG))
-            m00 = (sc[0:HALF, 0:HALF] * l00).astype(low)
-            m01 = (sc[0:HALF, HALF:] * l01).astype(low)
-            m11 = (sc[HALF:, HALF:] * l11).astype(low)
-            tops.append(nn(jnp.concatenate([m00, m01], axis=1), dy_pair))
-            bottoms.append(nn(m11, dy_pair[HALF:, :]))
-            grown = nt(x_half[0:HALF, :], dy_pair)
-            last = nt(x_half[HALF:, :], dy_pair[HALF:, :])
-            parts.append((grown[:, 0:HALF] * l00, grown[:, HALF:] * l01, last * l11))
-        acc[0:HALF, 0:HALF] += parts[0][0] + parts[1][0]
-        acc[0:HALF, HALF:] += parts[0][1] + parts[1][1]
-        acc[HALF:, HALF:] += parts[0][2] + parts[1][2]
-        flow = jnp.concatenate(
-            [
-                jnp.where(left[0:HALF], tops[0], tops[1]),
-                jnp.where(left[0:HALF], bottoms[0], bottoms[1]),
-            ],
-            axis=0,
-        )
+    for quad in range(H // 4):
+        flows = []
+        for pair in (2 * quad, 2 * quad + 1):
+            cols = slice(pair * HALF, (pair + 1) * HALF)
+            dy_pair = dy[:, cols]
+            x_pair = xs[:, cols]
+            heads = (2 * pair, 2 * pair + 1)
+            zeros = jnp.zeros_like(x_pair)
+            x_a, x_b = jnp.where(left, x_pair, zeros), jnp.where(left, zeros, x_pair)
+            rows = [cumt[h : h + 1, :] for h in heads]
+            x_top = jnp.concatenate([x_a[0:HALF, :], x_b[0:HALF, :]], axis=0)
+            grown = nt(x_top, dy_pair)
+            m00, m01, m11 = [], [], []
+            total = 0.0
+            for i, h in enumerate(heads):
+                first_col = cum[0:HALF, h : h + 1]
+                l00 = jnp.exp2(jnp.where(upper, rows[i][:, 0:HALF] - first_col, NEG))
+                m00.append((sc[0:HALF, 0:HALF] * l00).astype(low))
+                total = total + grown[i * HALF : (i + 1) * HALF, 0:HALF] * l00
+            acc[0:HALF, 0:HALF] += total
+            total = 0.0
+            for i, h in enumerate(heads):
+                first_col = cum[0:HALF, h : h + 1]
+                l01 = jnp.exp2(rows[i][:, HALF:] - first_col)
+                m01.append((sc[0:HALF, HALF:] * l01).astype(low))
+                total = total + grown[i * HALF : (i + 1) * HALF, HALF:] * l01
+            acc[0:HALF, HALF:] += total
+            sides = [jnp.concatenate([m00[i], m01[i]], axis=1) for i in range(2)]
+            top = nn(jnp.concatenate(sides, axis=0), dy_pair)
+            x_bottom = jnp.concatenate([x_a[HALF:, :], x_b[HALF:, :]], axis=0)
+            grown = nt(x_bottom, dy_pair[HALF:, :])
+            total = 0.0
+            for i, h in enumerate(heads):
+                second_col = cum[HALF:, h : h + 1]
+                l11 = jnp.exp2(jnp.where(upper, rows[i][:, HALF:] - second_col, NEG))
+                m11.append((sc[HALF:, HALF:] * l11).astype(low))
+                total = total + grown[i * HALF : (i + 1) * HALF, :] * l11
+            acc[HALF:, HALF:] += total
+            bottom = nn(jnp.concatenate(m11, axis=0), dy_pair[HALF:, :])
+            half_left = left[0:HALF]
+            flows.append(
+                jnp.concatenate(
+                    [
+                        jnp.where(half_left, top[0:HALF, :], top[HALF:, :]),
+                        jnp.where(half_left, bottom[0:HALF, :], bottom[HALF:, :]),
+                    ],
+                    axis=0,
+                )
+            )
+        cols = slice(quad * CH, (quad + 1) * CH)
+        flow = jnp.concatenate(flows, axis=1)
         sums = sums + gather_heads(flow * xh[:, cols].astype(f32), et[cols, :])
-        dx_o[:, cols] = spread(steps, e[:, cols]) * flow + skip[:, cols] * dy_pair.astype(f32)
+        step_e, skip = spread_all([steps, params], e[:, cols])
+        dx_o[:, cols] = step_e * flow + skip[3:4, :] * dy[:, cols].astype(f32)
     rs_o[...] = sums
     scores = acc[...].astype(low)
     dbc_o[:, 0:N] = nn(scores, bc[:, N : 2 * N])
@@ -400,14 +469,14 @@
 
 
 def conv_back_kernel(
-    groups, dloc, suf, inc, sbf, xh, wx, gdy, dx, dbc, bc, cum, step, dtb, rs1, rs2,
-    cie, sp, cw, rate, e, et,
-    dcv_o, kacc_o, hacc_o, head_o, tail_o,
-    ds, nxt,
+    groups, hops, scal, dloc, suf, sbf, xh, wx, gdy, dx, dbc, bc, cum, step, dtb, rs1, rs2, *refs
 ):
+    inc = refs[:hops]
+    cie, sp, cw, par, e, et, dcv_o, kacc_o, hacc_o, head_o, tail_o, nxt, *slots = refs[hops:]
     at = pl.program_id(0)
     fresh = at % groups == 0
     opening = at % groups == groups - 1
+    zero = scal[scal.shape[0] - 1]
 
     @pl.when(at == 0)
     def start():
@@ -415,16 +484,21 @@
         hacc_o[...] = jnp.zeros_like(hacc_o)
 
     def conv_back(flow, c):
-        cols = slice(c, c + CH)
-        ds[0:8, :] = jnp.zeros((8, CH), f32)
+        for side in range(2):
+            half_back(flow[:, side * HALF : (side + 1) * HALF], c + side * HALF)
+
+    def half_back(flow, c):
+        ds = slots[c // HALF]
+        cols = slice(c, c + HALF)
+        ds[0:8, :] = jnp.zeros((8, HALF), f32)
         ds[8 + Q :, :] = jnp.where(fresh, 0.0, nxt[:, cols])
         ds[8 : 8 + Q, :] = flow * sp[:, cols]
         nxt[:, cols] = ds[8:16, :]
         taps = [cw[k : k + 1, cols] for k in range(KW)]
-        sums = [jnp.zeros((8, CH), f32) for _ in range(KW + 1)]
+        sums = [jnp.zeros((8, HALF), f32) for _ in range(KW + 1)]
 
         def views_at(begin, count):
-            return [ds[begin + 11 - k : begin + 11 - k + count, :] for k in range(KW)]
+            return [ds[pl.ds(zero + (begin + 11 - k), count), :] for k in range(KW)]
 
         def back(views):
             total = taps[0] * views[0]
@@ -432,10 +506,10 @@
                 total = total + taps[k] * views[k]
             return total
 
-        for r in range(0, Q, 32):
-            views = views_at(r, 32)
-            dcv_o[r : r + 32, cols] = back(views).astype(low)
-            conv_in = cie[RIM + r : RIM + r + 32, cols].astype(f32)
+        for r in range(0, Q, 64):
+            views = views_at(r, 64)
+            dcv_o[r : r + 64, cols] = back(views).astype(low)
+            conv_in = cie[RIM + r : RIM + r + 64, cols].astype(f32)
             for k in range(KW):
                 sums[k] = sums[k] + fold8(views[k] * conv_in)
             sums[KW] = sums[KW] + fold8(views[KW - 1])
@@ -445,10 +519,6 @@
         for k in range(KW):
             kacc_o[8 * k : 8 * k + 8, cols] += sums[k] + jnp.where(opening, views[k] * conv_in, 0.0)
         kacc_o[8 * KW : 8 * KW + 8, cols] += sums[KW]
-
-        @pl.when(fresh)
-        def keep():
-            tail_o[:, cols] = back(views_at(Q - 16, 16))
 
     cumv = cum[...]
     stepv = step[...]
@@ -463,12 +533,13 @@
     lasts = jnp.zeros((8, HL), f32)
     for c in range(0, DI, CH):
         cols = slice(c, c + CH)
-        end = dloc[:, cols] + suf[0:1, cols] * inc[:, cols].astype(f32)
+        end = dloc[:, cols] + suf[0:1, cols] * total_of(inc, cols)
         end_low = end.astype(low)
         begin = sbf[:, cols]
-        lasts = lasts + gather_heads(fold8(end * begin.astype(f32)), et[cols, :])
         reach = nn(b_rows, end_low)
-        sums = sums + gather_heads(reach * xh[:, cols].astype(f32), et[cols, :])
+        held = [reach * xh[:, cols].astype(f32), fold8(end * begin.astype(f32))]
+        held = gather_all(held, et[cols, :])
+        sums, lasts = sums + held[0], lasts + held[1]
         d_b = d_b + nt(wx[:, cols], end_low)
         d_c = d_c + nt(gdy[:, cols], begin)
         conv_back(dx[:, cols] + spread(tails, e[:, cols]) * reach, c)
@@ -479,7 +550,7 @@
     d_last = jnp.exp2(last) * jnp.sum(lasts, axis=0, keepdims=True)
     d_last = d_last + jnp.sum(flow, axis=0, keepdims=True)
     d_log = running_sum(d_cum, True) + d_last
-    d_step = rs2[...] + sums * fade - d_log * rate[...]
+    d_step = rs2[...] + sums * fade - d_log * par[2:3, :]
     d_dt = d_step * jax.nn.sigmoid(dtb[...])
     lane = lax.broadcasted_iota(jnp.int32, d_dt.shape, 1)
     d_dt = jnp.where(lane < H, d_dt, 0.0)
@@ -487,8 +558,14 @@
     head_o[:, CD:CW] = jnp.zeros((8, HL), low)
 
     @pl.when(fresh)
-    def keep_step():
+    def keep():
         tail_o[:, CD:CW] = d_dt[Q - 16 :, :]
+        for slot, ds in enumerate(slots):
+            cols = slice(slot * HALF, (slot + 1) * HALF)
+            total = jnp.zeros((16, HALF), f32)
+            for k in range(KW):
+                total = total + cw[k : k + 1, cols] * ds[pl.ds(zero + (Q - 5 - k), 16), :]
+            tail_o[:, cols] = total
 
     hacc_o[0:8, :] += fold8(d_dt)
     hacc_o[8:16, :] += fold8(d_log * stepv)
@@ -498,19 +575,33 @@
     return source_of(me, place) ^ which
 
 
-def early_grad_kernel(scal, nrmt, dz, dzr, gn, db, wz, g0_o, g1_o, dn_o, part, wide):
+def fold_lanes(value):
+    total = value[:, 0:HALF]
+    for c in range(HALF, value.shape[1], HALF):
+        total = total + value[:, c : c + HALF]
+    return total
+
+
+def early_grad_kernel(scal, nrmt, dz, gn, db, wzc, wo, g0_o, g1_o, na_o, ga_o, part, wide):
     at = pl.program_id(0)
+
+    @pl.when(at == 0)
+    def start():
+        na_o[...] = jnp.zeros_like(na_o)
+
     me = scal[0]
     refs = (g0_o, g1_o)
     quarter = DI // 4
     cols = pl.ds(pl.multiple_of(at * quarter, HALF), quarter)
     part[...] = nn(nrmt[...], dz[...])
+    na_o[...] += fold_lanes(part[...] * wzc[...].astype(f32))
     for place in range(PIECES // 2):
         for which in range(2):
             start = pl.multiple_of(piece_at(me, place, which) * 24, 8)
             refs[which][place, 0, :, cols] = part[pl.ds(start, 24), :].astype(low)
-    wide[pl.ds(pl.multiple_of(at * quarter, HALF), quarter), :] = tn(gn[...], db[...])
-    dn_o[...] = nt(dzr[...], wz[...])
+    rows = pl.ds(pl.multiple_of(at * quarter, HALF), quarter)
+    wide[rows, :] = tn(gn[...], db[...])
+    ga_o[...] = fold_lanes(wide[rows, :] * wo[...].astype(f32))
 
     @pl.when(at == 3)
     def finish():
@@ -523,7 +614,26 @@
                     refs[which][place, 1, :, span] = wide[rows, :].astype(low)
 
 
-def late_grad_kernel(scal, nrmt, dcv, tails, returned, g0_o, g1_o, fix_o, part):
+def row_sums(value):
+    ones = jnp.ones((8, value.shape[1]), low)
+    total = 0.0
+    for _ in range(3):
+        top = value.astype(low)
+        total = total + nt(ones, top)
+        value = value - top.astype(f32)
+    return total[0:1, :]
+
+
+def late_grad_kernel(
+    scal, nrmt, dcv, wc, na, tails, returned, cacc, hacc, kacc, ga, par, et,
+    g0_o, g1_o, fix_o, vec_o, part, nl,
+):
+    at = pl.program_id(0)
+
+    @pl.when(at == 0)
+    def start():
+        nl[...] = na[...]
+
     refs = (g0_o, g1_o)
     fix_o[...] = dcv[...]
     seqs = tails.shape[0]
@@ -534,25 +644,44 @@
         )
         fix_o[(seq + 1) * piece_len - 16 : (seq + 1) * piece_len, :] = back.astype(low)
     part[...] = nn(nrmt[...], fix_o[...])
+    columns = at * fix_o.shape[1] + lax.broadcasted_iota(jnp.int32, (1, fix_o.shape[1]), 1)
+    weight = jnp.where(columns < CD + H, wc[...].astype(f32), 0.0)
+    nl[...] += fold_lanes(part[...] * weight)
     for place in range(PIECES // 2):
         for which in range(2):
             start = pl.multiple_of(piece_at(scal[0], place, which) * 24, 8)
             refs[which][place, :, :] = part[pl.ds(start, 24), :].astype(low)
 
-
-def input_kernel(dcv, dnz, wc, x, cot, gain, past, gh_o, acc_o, total):
-    @pl.when(pl.program_id(0) == 0)
-    def start():
-        acc_o[...] = jnp.zeros_like(acc_o)
-
-    total[...] = dnz[...] + nt(dcv[...], wc[...])
+    @pl.when(at == pl.num_programs(0) - 1)
+    def finish():
+        def put(first, row):
+            for c in range(0, row.shape[1], HALF):
+                vec_o[first + c // HALF : first + c // HALF + 1, :] = row[:, c : c + HALF]
+            return first + row.shape[1] // HALF
+
+        def column_sum(value):
+            return jnp.sum(value, axis=0, keepdims=True)
+
+        first = 0
+        for k in range(KW + 1):
+            first = put(first, column_sum(cacc[8 * k : 8 * k + 8, :]))
+        first = put(first, row_sums(ga[...]))
+        first = put(first, row_sums(nl[...]))
+        first = put(first, column_sum(hacc[0:8, :]))
+        first = put(first, -column_sum(hacc[8:16, :]) * par[2:3, :])
+        first = put(first, column_sum(gather_heads(kacc[...], et[...])))
+        vec_o[first:, :] = jnp.zeros((vec_o.shape[0] - first, HALF), f32)
+
+
+def input_kernel(dcv, dz, wc, wz, x, cot, gain, past, token, gh_o, done_o, total):
+    done_o[...] = jnp.zeros_like(done_o)
+    total[...] = nt(dz[...], wz[...]) + nt(dcv[...], wc[...])
     width = x.shape[1]
     for r in range(0, Q, 16):
         rows = slice(r, r + 16)
         wide = x[rows, :].astype(f32)
         scale = lax.rsqrt(jnp.mean(wide * wide, axis=-1, keepdims=True) + epsilon)
         flow = total[rows, :]
-        acc_o[...] += fold8(flow * wide * scale)
         scaled = flow * gain[0:1, :]
         mean = jnp.sum(scaled * wide, axis=-1, keepdims=True) / width
         d_x = scale * scaled - wide * (scale * scale * scale * mean)
@@ -561,9 +690,12 @@
 
 def call(kernel, grid, inputs, outputs, scratch, flops, name, aliases=None):
     in_specs = [spec for spec, _ in inputs]
-    out_specs = [spec for spec, _, _ in outputs]
-    out_shape = [jax.ShapeDtypeStruct(shape, kind) for _, shape, kind in outputs]
-    moved = sum(value.size * value.dtype.itemsize for _, value in inputs)
+    out_specs = [item[0] for item in outputs]
+    out_shape = [
+        pltpu.VMEM(item[1], item[2]) if len(item) > 3 else jax.ShapeDtypeStruct(item[1], item[2])
+        for item in outputs
+    ]
+    moved = 1 if flops == 1.0 else sum(value.size * value.dtype.itemsize for _, value in inputs)
     return pl.pallas_call(
         kernel,
         grid=(grid,),
@@ -574,10 +706,14 @@
         input_output_aliases=aliases or {},
         cost_estimate=pl.CostEstimate(flops=int(flops), transcendentals=0, bytes_accessed=moved),
         compiler_params=pltpu.CompilerParams(
-            dimension_semantics=("arbitrary",), vmem_limit_bytes=56 * 1024 * 1024
+            dimension_semantics=("arbitrary",), vmem_limit_bytes=LIMITS[name] * 1024 * 1024
         ),
         name=name,
     )(*[value for _, value in inputs])
+
+
+def near(value):
+    return pltpu.with_memory_space_constraint(value, pltpu.VMEM)
 
 
 def swap(value, mask):
@@ -633,12 +769,8 @@
     return out[0], list(out[1:4])
 
 
-def total_over(value):
-    value = value + swap(value, 1)
-    for masks in ((2, 4, 6), (8, 16, 24)):
-        got = [swap(value, mask) for mask in masks]
-        value = (value + got[0]) + (got[1] + got[2])
-    return value
+def rounded(value):
+    return value.astype(low).astype(f32)
 
 
 def extras(taps, bias, gate, norm):
@@ -654,12 +786,14 @@
     return [(j << 1) | (k << 3) for j in range(4) for k in range(4)]
 
 
-def relay(ends, totals, forward, fillers):
+def relay(ends, ends_low, totals, forward, fillers):
     count = lax.axis_size("seq")
-    incoming = jnp.zeros(ends.shape, f32)
-    results, got = [], None
+    incoming = None
+    results, arrivals, got = [], [], None
     for hop in range(1, count):
-        value = (totals * incoming + ends).astype(low)
+        value = ends_low
+        if incoming is not None:
+            value = (totals * incoming + ends).astype(low)
         route = [(hop - 1, hop)] if forward else [(count - hop, count - hop - 1)]
         arrived = lax.ppermute(value, "seq", route)
         if fillers:
@@ -667,10 +801,19 @@
             results.append(made)
             arrived = tie(arrived, made[-1])
         got = arrived
-        incoming = incoming + got.astype(f32)
+        arrivals.append(got)
+        wide = got.astype(f32)
+        incoming = wide if incoming is None else incoming + wide
     while fillers:
         results.append(fillers.pop(0)(got))
-    return incoming.astype(low), results
+    return arrivals or [jnp.zeros_like(ends_low)], results
+
+
+def total_of(refs, cols):
+    total = refs[0][:, cols].astype(f32)
+    for ref in refs[1:]:
+        total = total + ref[:, cols].astype(f32)
+    return total
 
 
 def per_device(
@@ -696,7 +839,7 @@
     place = lax.axis_index(axes).astype(jnp.int32)
     me = place if quick else jnp.zeros((), jnp.int32)
     seq_at = lax.axis_index("seq").astype(jnp.int32)
-    scal = jnp.concatenate([me[None], seq_at[None], lengths.astype(jnp.int32)])
+    scal = jnp.concatenate([me[None], seq_at[None], lengths.astype(jnp.int32), me[None] * 0])
 
     rims = hidden[:, piece_len - RIM :, :]
     seq_size = lax.axis_size("seq")
@@ -739,11 +882,9 @@
         za, zb = whole[order], whole[order + 1]
 
     rate = jnp.exp(decay_log)
-    log2_rate = rate * 1.4426950408889634
-    sb = jnp.pad(step_bias, (0, HL - H)).reshape(1, HL)
-    rate_row = jnp.pad(rate, (0, HL - H)).reshape(1, HL)
-    log2_row = jnp.pad(log2_rate, (0, HL - H)).reshape(1, HL)
-    skip = jnp.repeat(skip_gain, P_SIZE).reshape(1, DI)
+    par = jnp.pad(
+        jnp.stack([step_bias, rate * 1.4426950408889634, rate, skip_gain]), ((0, 4), (0, HL - H))
+    )
     e = jnp.asarray(head_table(), low)
     et = jnp.asarray(np.pad(head_table()[: HL // 2].T, ((0, 0), (0, HL // 2))), low)
     t56 = onehot(HL, CD, H, CD // PIECES)
@@ -774,10 +915,11 @@
         return pl.BlockSpec(shape, lambda i: zeros)
 
     scalars = pl.BlockSpec(memory_space=pltpu.SMEM)
+    whole = pl.BlockSpec(memory_space=pltpu.VMEM)
     flat_hidden = hidden.reshape(rows, width)
     flat_cot = cotangent.reshape(rows, width)
 
-    (nrm, nrmt, cie, sp, xh, xs, wx, bc, step, cum, dtb, cumt, sloc, pre, ends, totals, wc, taps, gain_in, gain_gate) = call(
+    (nrm, nrmt, cie, sp, xh, xs, wx, bc, step, cum, dtb, cumt, sloc, pre, ends, ends_low, totals, wc, taps, gain_in, gain_gate) = call(
         functools.partial(conv_kernel, groups),
         blocks,
         [
@@ -789,8 +931,7 @@
             (fixed(HL, CD), t56),
             (fixed(HL, DI), t48),
             (fixed(HL, width), t24),
-            (fixed(1, HL), sb),
-            (fixed(1, HL), log2_row),
+            (fixed(8, HL), par),
             (fixed(HL, DI), e),
         ],
         [
@@ -809,6 +950,7 @@
             (per_block(N, DI, forth), (blocks, N, DI), f32),
             (per_block(8, DI, forth), (blocks, 8, DI), f32),
             (per_seq(N, DI), (seqs, N, DI), f32),
+            (per_seq(N, DI), (seqs, N, DI), low),
             (per_seq(1, DI), (seqs, 1, DI), f32),
             (kept(width, CW), (width, CW), low),
             (kept(8, CD), (8, CD), f32),
@@ -817,10 +959,10 @@
         ],
         [
             pltpu.VMEM((Q + RIM, width), low),
-            pltpu.VMEM((Q + RIM, CH), f32),
             pltpu.VMEM((N, DI), f32),
             pltpu.VMEM((8, DI), f32),
             pltpu.VMEM((2, HL, HL), f32),
+            *[pltpu.VMEM((Q + RIM, HALF), f32)] * (CD // HALF),
         ],
         2.0 * rows * width * CW,
         "conv",
@@ -862,8 +1004,8 @@
                 (fixed(*za.shape), zb),
             ],
             [
-                (tokens(DI, forth), (rows, DI), f32),
-                (tokens(DI, forth), (rows, DI), f32),
+                (whole, (rows, DI), f32, near),
+                (whole, (rows, DI), f32, near),
                 (tokens(width, forth), (rows, width), low),
                 (kept(width, DI), (width, DI), low),
                 (kept(DI, width), (DI, width), low),
@@ -874,11 +1016,11 @@
         )
 
     incoming, ((intra,), (z, dn, db, wz, wo)) = relay(
-        ends, totals, True, [intra_part, project_part]
+        ends, ends_low, totals, True, [intra_part, project_part]
     )
 
-    (out, dz, dy, gdy, gn, sbf, rs1, dloc, suf, back_ends, back_totals, gacc, kacc) = call(
-        functools.partial(gate_kernel, groups),
+    (out, dz, dy, gdy, gn, sbf, rs1, dloc, suf, back_ends, back_ends_low, back_totals, kacc) = call(
+        functools.partial(gate_kernel, groups, len(incoming)),
         blocks,
         [
             (scalars, scal),
@@ -888,13 +1030,13 @@
             (tokens(HL, back), cum),
             (per_block(N, DI, back), sloc),
             (per_block(8, DI, back), pre),
-            (per_seq(N, DI), incoming),
-            (tokens(DI, back), z),
-            (tokens(DI, back), dn),
+            *[(per_seq(N, DI), value) for value in incoming],
+            (whole, near(z)),
+            (whole, near(dn)),
             (tokens(width, back), flat_hidden),
             (fixed(DI, width), wo),
             (fixed(8, DI), gain_gate),
-            (fixed(1, DI), skip),
+            (fixed(8, HL), par),
             (fixed(HL, DI), e),
             (fixed(DI, HL), et),
         ],
@@ -909,18 +1051,20 @@
             (per_block(N, DI, back), (blocks, N, DI), f32),
             (per_block(8, DI, back), (blocks, 8, DI), f32),
             (per_seq(N, DI), (seqs, N, DI), f32),
+            (per_seq(N, DI), (seqs, N, DI), low),
             (per_seq(1, DI), (seqs, 1, DI), f32),
-            (kept(8, DI), (8, DI), f32),
             (kept(8, DI), (8, DI), f32),
         ],
         [
             pltpu.VMEM((Q, DI), f32),
             pltpu.VMEM((Q, DI), f32),
             pltpu.VMEM((Q, DI), f32),
-            pltpu.VMEM((32, DI), f32),
-            pltpu.VMEM((32, DI), f32),
-            pltpu.VMEM((32, DI), f32),
+            pltpu.VMEM((Q, DI), f32),
+            pltpu.VMEM((Q, DI), f32),
+            pltpu.VMEM((Q, DI), f32),
             pltpu.VMEM((N, DI), f32),
+            pltpu.VMEM((8, DI), f32),
+            pltpu.VMEM((8, DI), f32),
             pltpu.VMEM((8, DI), f32),
         ],
         4.0 * rows * width * DI,
@@ -939,7 +1083,7 @@
                 (tokens(HL, forth), step),
                 (tokens(HL, forth), cum),
                 (per_block(H, Q, forth), cumt),
-                (fixed(1, DI), skip),
+                (fixed(8, HL), par),
                 (fixed(HL, DI), e),
                 (fixed(DI, HL), et),
             ],
@@ -953,7 +1097,6 @@
             "intra_back",
         )
 
-    share = rows // 4
     piece = (PIECES // 2, 2, width // PIECES, DI)
 
     def early_part(got):
@@ -964,35 +1107,36 @@
                 (scalars, after(scal, got)),
                 (fixed(width, rows), nrmt),
                 (pl.BlockSpec((rows, DI // 4), lambda i: (0, i)), dz),
-                (pl.BlockSpec((share, DI), lambda i: (i, 0)), dz),
                 (pl.BlockSpec((rows, DI // 4), lambda i: (0, i)), gn),
                 (fixed(rows, width), db),
-                (fixed(width, DI), wz),
+                (pl.BlockSpec((width, DI // 4), lambda i: (0, i)), wz),
+                (pl.BlockSpec((DI // 4, width), lambda i: (i, 0)), wo),
             ],
             [
                 (kept(*piece), piece, low),
                 (kept(*piece), piece, low),
-                (pl.BlockSpec((share, width), lambda i: (i, 0)), (rows, width), f32),
+                (kept(width, HALF), (width, HALF), f32),
+                (pl.BlockSpec((DI // 4, HALF), lambda i: (i, 0)), (DI, HALF), f32),
             ],
             [pltpu.VMEM((width, DI // 4), f32), pltpu.VMEM((DI, width), f32)],
             6.0 * rows * width * DI,
             "early_grad",
         )
 
-    back_incoming, ((e0, e1, dnz), (dx, dbc, rs2)) = relay(
-        back_ends, back_totals, False, [early_part, intra_back_part]
+    back_incoming, ((e0, e1, na, ga), (dx, dbc, rs2)) = relay(
+        back_ends, back_ends_low, back_totals, False, [early_part, intra_back_part]
     )
     if quick:
         early = merge_core(e0, tie(swap(e1, 1), rs2))
-        back_incoming = tie(back_incoming, *early[1])
+        back_incoming[-1] = tie(back_incoming[-1], *early[1])
 
     (dcv, cacc, hacc, heads_out, tails_out) = call(
-        functools.partial(conv_back_kernel, groups),
+        functools.partial(conv_back_kernel, groups, len(back_incoming)),
         blocks,
         [
+            (scalars, scal),
             (per_block(N, DI, back), dloc),
             (per_block(8, DI, back), suf),
-            (per_seq(N, DI), back_incoming),
             (per_block(N, DI, back), sbf),
             (tokens(DI, back), xh),
             (tokens(DI, back), wx),
@@ -1005,10 +1149,11 @@
             (tokens(HL, back), dtb),
             (tokens(HL, back), rs1),
             (tokens(HL, back), rs2),
+            *[(per_seq(N, DI), value) for value in back_incoming],
             (per_block(Q + RIM, CD, back), cie),
             (tokens(CD, back), sp),
             (fixed(8, CD), taps),
-            (fixed(1, HL), rate_row),
+            (fixed(8, HL), par),
             (fixed(HL, DI), e),
             (fixed(DI, HL), et),
         ],
@@ -1020,8 +1165,8 @@
             (per_seq(16, CW), (seqs, 16, CW), f32),
         ],
         [
-            pltpu.VMEM((Q + 16, CH), f32),
             pltpu.VMEM((8, CD), f32),
+            *[pltpu.VMEM((Q + 16, HALF), f32)] * (CD // HALF),
         ],
         6.0 * rows * N * DI,
         "conv_back",
@@ -1034,27 +1179,36 @@
 
     late = (PIECES // 2, width // PIECES, CW)
     late_spec = pl.BlockSpec((PIECES // 2, width // PIECES, CW // 5), lambda i: (0, 0, i))
-    (l0, l1, dcv) = call(
+    (l0, l1, dcv, vector) = call(
         late_grad_kernel,
         5,
         [
             (scalars, turn),
             (fixed(width, rows), nrmt),
             (pl.BlockSpec((rows, CW // 5), lambda i: (0, i)), dcv),
+            (pl.BlockSpec((width, CW // 5), lambda i: (0, i)), wc),
+            (fixed(width, HALF), na),
             (pl.BlockSpec((seqs, 16, CW // 5), lambda i: (0, 0, i)), tails_out),
             (pl.BlockSpec((seqs, 8, CW // 5), lambda i: (0, 0, i)), returned),
+            (fixed(8 * (KW + 1), CD), cacc),
+            (fixed(16, HL), hacc),
+            (fixed(8, DI), kacc),
+            (fixed(DI, HALF), ga),
+            (fixed(8, HL), par),
+            (fixed(DI, HL), et),
         ],
         [
             (late_spec, late, low),
             (late_spec, late, low),
             (pl.BlockSpec((rows, CW // 5), lambda i: (0, i)), (rows, CW), low),
+            (kept(96, HALF), (96, HALF), f32),
         ],
-        [pltpu.VMEM((width, CW // 5), f32)],
+        [pltpu.VMEM((width, CW // 5), f32), pltpu.VMEM((width, HALF), f32)],
         2.0 * rows * width * CW,
         "late_grad",
     )
 
-    def input_part(first, count, past, token):
+    def input_part(first, count, past, before, token):
         def order(i):
             return i + first
 
@@ -1063,49 +1217,46 @@
             count,
             [
                 (tokens(CW, order), dcv),
-                (tokens(width, order), dnz),
+                (tokens(DI, order), dz),
                 (fixed(width, CW), wc),
+                (fixed(width, DI), wz),
                 (tokens(width, order), flat_hidden),
                 (tokens(width, order), flat_cot),
                 (fixed(8, width), gain_in if token is None else tie(gain_in, *token)),
                 (pl.BlockSpec(memory_space=pl.ANY), past),
+                (pl.BlockSpec(memory_space=pl.ANY), before),
             ],
             [
                 (tokens(width, order), (rows, width), low),
-                (kept(8, width), (8, width), f32),
+                (kept(8, HALF), (8, HALF), f32),
             ],
             [pltpu.VMEM((Q, width), f32)],
-            2.0 * rows * width * CW * count / blocks,
+            1.0,
             "input",
-            {6: 0} if first else None,
+            {7: 0} if first else None,
         )
 
-    half_blocks = blocks // 2
+    half_blocks = max(blocks // 4, 1)
     if quick:
-        gh, nacc = input_part(0, half_blocks, scal, None)
-        late_sum = merge_core(l0, tie(swap(l1, 1), nacc))
+        late_got = swap(l1, 1)
+        vector_got = swap(vector, 1)
+        gh, done = input_part(0, half_blocks, scal, scal, None)
+        late_sum = merge_core(l0, tie(late_got, done))
+        vector = vector + tie(vector_got, done)
         early = tie_all(*early, late_sum[1][0])
-        gh, nacc2 = input_part(half_blocks, blocks - half_blocks, gh, late_sum[1])
-        late_sum = parts_of(merge(*late_sum, (2, 4, 6), nacc2))
-        early = merge(*early, (8, 16, 24), nacc2)
+        gh, done2 = input_part(half_blocks, blocks - half_blocks, gh, done, late_sum[1])
+        late_sum = parts_of(merge(*late_sum, (2, 4, 6), done2))
+        early = merge(*early, (8, 16, 24), late_sum[1][0])
         late_sum = tie_all(*late_sum, early)
-        nacc = nacc + nacc2
+        vector = tie(vector, late_sum[1][0])
+        got = [swap(vector, mask) for mask in (2, 4, 6)]
+        vector = (vector + got[0]) + (got[1] + got[2])
     else:
-        gh, nacc = input_part(0, blocks, scal, None)
-
-    conv_sums = cacc.reshape(KW + 1, 8, CD).sum(axis=1)
-    skips = kacc.sum(axis=0).reshape(H, P_SIZE).sum(axis=1)
-    scalar_sums = jnp.concatenate(
-        [hacc[0:8].sum(axis=0)[:H], -hacc[8:16].sum(axis=0)[:H] * rate, skips]
-    )
-    vector = jnp.concatenate(
-        [nacc.sum(axis=0), conv_sums.reshape(-1), gacc.sum(axis=0), scalar_sums]
-    )
+        gh, done = input_part(0, blocks, scal, scal, None)
+
     if quick:
-        length = vector.shape[0]
-        vector = tie(vector, late_sum[1][0])
-        vector = total_over(jnp.pad(vector, (0, -length % (8 * HALF))).reshape(-1, HALF))
-        vector = vector.reshape(-1)[:length]
+        got = [swap(vector, mask) for mask in (8, 16, 24)]
+        vector = (vector + got[0]) + (got[1] + got[2])
         own_late = merge(*late_sum, (8, 16, 24))
         own_z, own_out = early[0], early[1]
         own_out = jnp.concatenate([own_out[:, : DI // 2], own_out[:, DI // 2 :]], axis=0)
@@ -1125,14 +1276,16 @@
     def own(value, size, axis):
         return lax.dynamic_slice_in_dim(value, place * size, size, axis)
 
-    at = width
-    g_norm = own(vector[:at], norm_gain.shape[0], 0)
-    g_taps = own(vector[at : at + KW * CD].reshape(KW, CD), CD // devices, 1)
-    at += KW * CD
-    g_bias = own(vector[at : at + CD], CD // devices, 0)
-    at += CD
-    g_gate = own(vector[at : at + DI], gate_gain.shape[0], 0)
-    at += DI
+    tile = CD // HALF
+    g_taps = own(vector[: KW * tile].reshape(KW, CD), CD // devices, 1)
+    at = KW * tile
+    g_bias = own(vector[at : at + tile].reshape(-1), CD // devices, 0)
+    at += tile
+    g_gate = own(vector[at : at + DI // HALF].reshape(-1), gate_gain.shape[0], 0)
+    at += DI // HALF
+    g_norm = own(vector[at : at + width // HALF].reshape(-1), norm_gain.shape[0], 0)
+    at += width // HALF
+    g_gate, g_norm = g_gate / rounded(gate_gain), g_norm / rounded(norm_gain)
     g_in = jnp.concatenate([own_z, own_late[:, : CD + H]], axis=1)
     return (
         out.reshape(hidden.shape),
@@ -1141,9 +1294,9 @@
         g_in,
         g_taps,
         g_bias,
-        vector[at : at + H],
-        vector[at + H : at + 2 * H],
-        vector[at + 2 * H : at + 3 * H],
+        vector[at, :H],
+        vector[at + 1, :H],
+        vector[at + 2, :H],
         g_gate,
         own_out,
     )

time: 282 us -> 250 us (0.89)
  Pallas kernels: 155 us -> 134 us
  other arithmetic: 20.7 us -> 12.2 us
  local copies, waits for them, and re-layouts: 16.7 us -> 12.1 us
    pallas_call x10, Pallas kernels: 155 us -> 134 us  [call(): pl.pallas_call(kernel, grid=(grid,), in_specs=in_specs, out_specs=out_spe...]
  transfers between devices with their start and end apart: 43 -> 43, of which waited for: 10 -> 11; matrix products, arithmetic and copies ran while one was open for 7% -> 5% of each run, Pallas kernels for 43% -> 41%
where the time goes in v3:
time: 250 us; the launch traced here: 249 us
  Pallas kernels  134 us (54%)
  starting transfers between devices  55.4 us (22%)
  waiting for transfers between devices  34.1 us (14%)
  other arithmetic  12.2 us (5%)
  local copies, waits for them, and re-layouts  12.1 us (5%)
    pallas_call x10, Pallas kernels, call(): pl.pallas_call(kernel, grid=(grid,), in_specs=in_specs, out_specs=out_spe...  134 us
    ppermute x35, starting transfers between devices, swap(): return lax.ppermute(value, axes, [(i, i ^ mask) for i in range(PIECES)])  46.5 us
    ppermute x35, waiting for transfers between devices, swap(): return lax.ppermute(value, axes, [(i, i ^ mask) for i in range(PIECES)])  34.1 us
    ppermute x6, starting transfers between devices, relay(): arrived = lax.ppermute(value, 'seq', route)  6.34 us
  transfers between devices with their start and end apart: 43, of which 11 were waited for; matrix products, arithmetic and copies ran while one was open for 5% of the time, Pallas kernels for 41%

profile of v3, /device:TPU:0, one launch (start us, length us, event | category | flops | bytes accessed | tf_op | source)
XLA Modules:
  0.0 249.2 jit_solution(17216343075087592961)
XLA Ops:
  1.3 0.9 slice.223
  3.8 3.0 %collective-permute-start = (bf16[24,1920]{1,0:T(8,128)(2,1)S(1)}, bf16[24,1920]{1,0:T(8,128)(2,1)S(1)}, u32[]{:S(2)}, u32[]{:S(2)}) collective-permute-start(bf16[24,1920]{1,0:T(8,128)(2,1)S(1)} %pad_maximum_fusion.8), channel_id=1, source_target_pairs={{0,8},{1,9},{2,10},{3,11},{4,12},{5,13},{6,14},{7,15},{8,0},{9,1},... | collective-permute-start | bytes 276488 | tf_op jit(solution)/shard_map/ppermute | solution.py:720
  6.8 2.6 %collective-permute-start.1 = (bf16[24,1920]{1,0:T(8,128)(2,1)S(1)}, bf16[24,1920]{1,0:T(8,128)(2,1)S(1)}, u32[]{:S(2)}, u32[]{:S(2)}) collective-permute-start(bf16[24,1920]{1,0:T(8,128)(2,1)S(1)} %pad_maximum_fusion.8), channel_id=1, source_target_pairs={{0,16},{1,17},{2,18},{3,19},{4,20},{5,21},{6,22},{7,23},{8,24},{9,... | collective-permute-start | bytes 276488 | tf_op jit(solution)/shard_map/ppermute | solution.py:720
  10.2 1.3 collective-permute-start.3
  11.5 0.9 slice_bitcast_fusion.16
  12.4 0.9 fusion.13
  13.4 0.9 convert_element_type.137
  14.4 2.3 collective-permute-done.1
  16.8 1.6 collective-permute-start.4
  18.5 1.5 collective-permute-start.5
  19.9 1.3 collective-permute-start.6
  21.3 1.5 collective-permute-start.7
  22.8 1.5 collective-permute-start.8
  25.1 1.1 collective-permute-start.9
  26.2 6.2 %collective-permute-done.5 = bf16[2,24,1536]{2,1,0:T(8,128)(2,1)S(1)} collective-permute-done((bf16[2,24,1536]{2,1,0:T(8,128)(2,1)S(1)}, bf16[2,24,1536]{2,1,0:T(8,128)(2,1)S(1)}, u32[]{:S(2)}, u32[]{:S(2)}) %collective-permute-start.5) | collective-permute-done | bytes 147488 | tf_op jit(solution)/shard_map/ppermute | solution.py:720
  32.8 7.2 %collective-permute-done.9 = bf16[4,24,1920]{2,1,0:T(8,128)(2,1)S(1)} collective-permute-done((bf16[4,24,1920]{2,1,0:T(8,128)(2,1)S(1)}, bf16[4,24,1920]{2,1,0:T(8,128)(2,1)S(1)}, u32[]{:S(2)}, u32[]{:S(2)}) %collective-permute-start.9) | collective-permute-done | bytes 368672 | tf_op jit(solution)/shard_map/ppermute | solution.py:720
  42.1 1.5 collective-permute-start.12
  43.6 1.2 collective-permute-start.13
  46.6 20.2 %conv.1 = (bf16[1024,768]{1,0:T(8,128)(2,1)}, bf16[768,1024]{1,0:T(8,128)(2,1)}, bf16[4,272,1792]{2,1,0:T(8,128)(2,1)}, f32[1024,1792]{1,0:T(8,128)}, bf16[1024,...) custom-call(s32[5]{0:T(128)} %pad_add_fusion.scal.past.token, ...), custom_call_target="tpu_custom_call" | custom-call | flops 3019898880 | bytes 6066196 | tf_op jit(solution)/shard_map/conv/pallas_call | solution.py:699
  66.8 3.3 %collective-permute-done.12 = bf16[4,2,24,1536]{3,2,1,0:T(8,128)(2,1)S(1)} collective-permute-done((bf16[4,2,24,1536]{3,2,1,0:T(8,128)(2,1)S(1)}, bf16[4,2,24,1536]{3,2,1,0:T(8,128)(2,1)S(1)}, u32[]{:S(2)}, u32[]{:S(2)}) %collective-permute-start.12) | collective-permute-done | bytes 589856 | tf_op jit(solution)/shard_map/ppermute | solution.py:720
  71.2 1.7 collective-permute-start.14
  73.0 8.0 %intra.1 = f32[1024,1536]{1,0:T(8,128)} custom-call(bf16[1024,256]{1,0:T(8,128)(2,1)} %get-tuple-element.150.bc, bf16[1024,1536]{1,0:T(8,128)(2,1)} %get-tuple-element.123.xs, f32[1024,128]{1,0:T(8,128)} %get-tuple-element.118.cum, f32[4,24,256]{2,1,0:T(8,128)} %get-tuple-element.124.cumt), custom_call_target="tpu_custom_call" | custom-call | flops 1610612736 | bytes 4292608 | tf_op jit(solution)/shard_map/intra/pallas_call | solution.py:699
  82.0 10.9 %project.1 = (f32[1024,1536]{1,0:T(8,128)S(1)}, f32[1024,1536]{1,0:T(8,128)S(1)}, bf16[1024,768]{1,0:T(8,128)(2,1)}, bf16[768,1536]{1,0:T(8,128)(2,1)}, bf16[1536,768]{1,0:T(8,128)(2,1)}) custom-call(s32[5]{0:T(128)} %pad_add_fusion.scal.past.token, bf16[1024,768]{1,0:T(8,128)(2,1)} %get-tuple-element.133.nrm, bf16[1024,768]{1,0:T(8,128)(2,1)} %bitcast.91, ...), custom_call_target="tpu_custom_call" | custom-call | flops 4831838208 | bytes 7864340 | tf_op jit(solution)/shard_map/project/pallas_call | solution.py:699
  95.6 21.0 %gate.1 = (bf16[1024,768]{1,0:T(8,128)(2,1)}, bf16[1024,1536]{1,0:T(8,128)(2,1)}, bf16[1024,1536]{1,0:T(8,128)(2,1)}, bf16[1024,1536]{1,0:T(8,128)(2,1)}, bf16[1...) custom-call(s32[5]{0:T(128)} %pad_add_fusion.scal.past.token, ...), custom_call_target="tpu_custom_call" | custom-call | flops 4831838208 | bytes 33542164 | tf_op jit(solution)/shard_map/gate/pallas_call | solution.py:699
  117.3 12.5 %early_grad.1 = (bf16[16,2,24,1536]{3,2,1,0:T(8,128)(2,1)}, bf16[16,2,24,1536]{3,2,1,0:T(8,128)(2,1)}, f32[768,128]{1,0:T(8,128)}, f32[1536,128]{1,0:T(8,128)}) custom-call(s32[5]{0:T(128)} %pad_add_fusion.scal.past.token, bf16[768,1024]{1,0:T(8,128)(2,1)} %get-tuple-element.140.nrmt, bf16[1024,1536]{1,0:T(8,128)(2,1)} %get-tuple-element.141.dz, ...), custom_call_target="tpu_custom_call" | custom-call | flops 7247757312 | bytes 14155796 | tf_op jit(solution)/shard_map/early_grad/pallas_call | solution.py:699
  129.8 1.6 collective-permute-start.18
  132.4 16.0 %intra_back.1 = (f32[1024,1536]{1,0:T(8,128)}, f32[1024,256]{1,0:T(8,128)}, f32[1024,128]{1,0:T(8,128)}) custom-call(bf16[1024,256]{1,0:T(8,128)(2,1)} %get-tuple-element.150.bc, bf16[1024,1536]{1,0:T(8,128)(2,1)} %get-tuple-element.123.xs, bf16[1024,1536]{1,0:T(8,128)(2,1)} %get-tuple-element.125.xh, bf16[1024,1536]{1,0:T(8,128)(2,1)} %get-tuple-element.151.dy, ...), custom_call_target="tpu_custom_call" | custom-call | flops 3221225472 | bytes 11898880 | tf_op jit(solution)/shard_map/intra_back/pallas_call | solution.py:699
  149.3 1.6 collective-permute-start.24
  151.0 2.6 %convert_add_fusion = (f32[16,2,24,1536]{3,2,1,0:T(8,128)S(1)}, bf16[16,2,24,1536]{3,2,1,0:T(8,128)(2,1)S(1)}) fusion(bf16[16,2,24,1536]{3,2,1,0:T(8,128)(2,1)} %collective-permute-done.18, bf16[16,2,24,1536]{3,2,1,0:T(8,128)(2,1)S(1)} %copy-done.7), kind=kLoop, calls=%fused_computation | loop fusion | flops 4718592 | bytes 11796480 | tf_op jit(solution)/shard_map/add | solution.py:755
  153.6 1.2 fusion.22
  154.8 4.4 %collective-permute-start.20 = (bf16[4,2,24,1536]{3,2,1,0:T(8,128)(2,1)}, bf16[4,2,24,1536]{3,2,1,0:T(8,128)(2,1)S(1)}, u32[]{:S(2)}, u32[]{:S(2)}) collective-permute-start(bf16[4,2,24,1536]{3,2,1,0:T(8,128)(2,1)} %get-tuple-element.219), channel_id=1, source_target_pairs={{0,2},{1,3},{2,0},{3,1},{4,6},{5,7},{6,4},{7,5},{8,10},{9,11},{10,... | collective-permute-start | bytes 1769480 | tf_op jit(solution)/shard_map/ppermute | solution.py:720
  161.6 18.6 %conv_back.1 = (bf16[1024,1920]{1,0:T(8,128)(2,1)}, f32[40,1792]{1,0:T(8,128)}, f32[16,128]{1,0:T(8,128)}, bf16[2,8,1920]{2,1,0:T(8,128)(2,1)}, f32[2,16,1920]{2,1,0:T(8,128)}) custom-call(s32[5]{0:T(128)} %pad_add_fusion.scal.past.token, f32[4,128,1536]{2,1,0:T(8,128)} %get-tuple-element.155.dloc, f32[4,8,1536]{2,1,0:T(8,128)} %get-tuple-element.156.suf, ...), custom_call_target="tpu_custom_call" | custom-call | flops 1207959552 | bytes 39284756 | tf_op jit(solution)/shard_map/conv_back/pallas_call | solution.py:699
  180.2 1.3 collective-permute-start.25
  181.5 4.9 %collective-permute-done.21 = bf16[4,2,24,1536]{3,2,1,0:T(8,128)(2,1)S(1)} collective-permute-done((bf16[4,2,24,1536]{3,2,1,0:T(8,128)(2,1)}, bf16[4,2,24,1536]{3,2,1,0:T(8,128)(2,1)S(1)}, u32[]{:S(2)}, u32[]{:S(2)}) %collective-permute-start.21) | collective-permute-done | bytes 589856 | tf_op jit(solution)/shard_map/ppermute | solution.py:720
  186.8 11.5 %late_grad.1 = (bf16[16,24,1920]{2,1,0:T(8,128)(2,1)}, bf16[16,24,1920]{2,1,0:T(8,128)(2,1)}, bf16[1024,1920]{1,0:T(8,128)(2,1)}, f32[96,128]{1,0:T(8,128)}) custom-call(s32[5]{0:T(128)} %pad_add_fusion.scal.past.token, bf16[768,1024]{1,0:T(8,128)(2,1)} %get-tuple-element.140.nrmt, bf16[1024,1920]{1,0:T(8,128)(2,1)} %get-tuple-element.176.dcv, ...), custom_call_target="tpu_custom_call" | custom-call | flops 3019898880 | bytes 10682388 | tf_op jit(solution)/shard_map/late_grad/pallas_call | solution.py:699
  198.9 5.8 %input.2 = (bf16[1024,768]{1,0:T(8,128)(2,1)}, f32[8,128]{1,0:T(8,128)}) custom-call(bf16[1024,1920]{1,0:T(8,128)(2,1)} %get-tuple-element.183.dcv, bf16[1024,1536]{1,0:T(8,128)(2,1)} %get-tuple-element.141.dz, bf16[768,1920]{1,0:T(8,128)(2,1)} %get-tuple-element.177.wc, bf16[768,1536]{1,0:T(8,128)(2,1)} %get-tuple-element.144.wzc.wz, ...), custom_call_target="tpu_custom_call" | custom-call | flops 1 | bytes 1 | tf_op jit(solution)/shard_map/input/pallas_call | solution.py:699
  205.6 1.4 collective-permute-start.29
  207.0 1.7 collective-permute-start.30
  209.4 3.6 %collective-permute-start.32 = (bf16[2,24,1536]{2,1,0:T(8,128)(2,1)S(1)}, bf16[2,24,1536]{2,1,0:T(8,128)(2,1)S(1)}, u32[]{:S(2)}, u32[]{:S(2)}) collective-permute-start(bf16[2,24,1536]{2,1,0:T(8,128)(2,1)S(1)} %get-tuple-element.199), channel_id=1, source_target_pairs={{0,16},{1,17},{2,18},{3,19},{4,20},{5,21},{6,22},{7,23},{8,24},{9,... | collective-permute-start | bytes 442376 | tf_op jit(solution)/shard_map/ppermute | solution.py:720
  213.0 9.5 %input.3 = (bf16[1024,768]{1,0:T(8,128)(2,1)}, f32[8,128]{1,0:T(8,128)}) custom-call(bf16[1024,1920]{1,0:T(8,128)(2,1)} %get-tuple-element.183.dcv, bf16[1024,1536]{1,0:T(8,128)(2,1)} %get-tuple-element.141.dz, bf16[768,1920]{1,0:T(8,128)(2,1)} %get-tuple-element.177.wc, ...), custom_call_target="tpu_custom_call", output_to_operand_aliasing={{0}: (7, {})} | custom-call | flops 1 | bytes 1 | tf_op jit(solution)/shard_map/input/pallas_call | solution.py:699
  222.7 1.0 collective-permute-done.30
  224.0 5.5 %collective-permute-done.33 = bf16[2,24,1536]{2,1,0:T(8,128)(2,1)S(1)} collective-permute-done((bf16[2,24,1536]{2,1,0:T(8,128)(2,1)S(1)}, bf16[2,24,1536]{2,1,0:T(8,128)(2,1)S(1)}, u32[]{:S(2)}, u32[]{:S(2)}) %collective-permute-start.33) | collective-permute-done | bytes 147488 | tf_op jit(solution)/shard_map/ppermute | solution.py:720
  229.7 1.4 collective-permute-start.40
  231.4 1.4 collective-permute-start.35
  232.8 1.7 collective-permute-start.36
  235.3 3.0 %collective-permute-start.42 = (bf16[24,1920]{1,0:T(8,128)(2,1)S(1)}, bf16[24,1920]{1,0:T(8,128)(2,1)S(1)}, u32[]{:S(2)}, u32[]{:S(2)}) collective-permute-start(bf16[24,1920]{1,0:T(8,128)(2,1)S(1)} %get-tuple-element.208), channel_id=1, source_target_pairs={{0,24},{1,25},{2,26},{3,27},{4,28},{5,29},{6,30},{7,31},{8,16},{9,... | collective-permute-start | bytes 276488 | tf_op jit(solution)/shard_map/ppermute | solution.py:720
  239.8 3.0 %collective-permute-start.39 = (f32[96,128]{1,0:T(8,128)S(1)}, f32[96,128]{1,0:T(8,128)S(1)}, u32[]{:S(2)}, u32[]{:S(2)}) collective-permute-start(f32[96,128]{1,0:T(8,128)S(1)} %add_add_fusion.2), channel_id=1, source_target_pairs={{0,24},{1,25},{2,26},{3,27},{4,28},{5,29},{6,30},{7,31},{8,16},{9,... | collective-permute-start | bytes 147464 | tf_op jit(solution)/shard_map/ppermute | solution.py:720
  244.5 1.7 collective-permute-done.38
  (150 shorter events, 28.0 us)
Async XLA Ops:
  3.8 10.7 %collective-permute-start = (bf16[24,1920]{1,0:T(8,128)(2,1)S(1)}, bf16[24,1920]{1,0:T(8,128)(2,1)S(1)}, u32[]{:S(2)}, u32[]{:S(2)}) collective-permute-start(bf16[24,1920]{1,0:T(8,128)(2,1)S(1)} %pad_maximum_fusion.8), channel_id=1, source_target_pairs={{0,8},{1,9},{2,10},{3,11},{4,12},{5,13},{6,14},{7,15},{8,0},{9,1},... | collective-permute-start | bytes 276488 | tf_op jit(solution)/shard_map/ppermute | solution.py:720
  6.8 10.0 %collective-permute-start.1 = (bf16[24,1920]{1,0:T(8,128)(2,1)S(1)}, bf16[24,1920]{1,0:T(8,128)(2,1)S(1)}, u32[]{:S(2)}, u32[]{:S(2)}) collective-permute-start(bf16[24,1920]{1,0:T(8,128)(2,1)S(1)} %pad_maximum_fusion.8), channel_id=1, source_target_pairs={{0,16},{1,17},{2,18},{3,19},{4,20},{5,21},{6,22},{7,23},{8,24},{9,... | collective-permute-start | bytes 276488 | tf_op jit(solution)/shard_map/ppermute | solution.py:720
  9.4 7.4 %collective-permute-start.2 = (bf16[24,1920]{1,0:T(8,128)(2,1)S(1)}, bf16[24,1920]{1,0:T(8,128)(2,1)S(1)}, u32[]{:S(2)}, u32[]{:S(2)}) collective-permute-start(bf16[24,1920]{1,0:T(8,128)(2,1)S(1)} %pad_maximum_fusion.8), channel_id=1, source_target_pairs={{0,24},{1,25},{2,26},{3,27},{4,28},{5,29},{6,30},{7,31},{8,16},{9,... | collective-permute-start | bytes 276488 | tf_op jit(solution)/shard_map/ppermute | solution.py:720
  10.2 6.6 %collective-permute-start.3 = (bf16[2,16,768]{2,1,0:T(8,128)(2,1)S(1)}, bf16[2,16,768]{2,1,0:T(8,128)(2,1)S(1)}, u32[]{:S(2)}, u32[]{:S(2)}) collective-permute-start(bf16[2,16,768]{2,1,0:T(8,128)(2,1)S(1)} %slice.126), channel_id=1, source_target_pairs={{0,1},{1,2},{2,3},{4,5},{5,6},{6,7},{8,9},{9,10},{10,11},{12,13},{... | collective-permute-start | bytes 147464 | tf_op jit(solution)/shard_map/ppermute | solution.py:846
  16.8 8.3 %collective-permute-start.4 = (bf16[2,24,1536]{2,1,0:T(8,128)(2,1)S(1)}, bf16[2,24,1536]{2,1,0:T(8,128)(2,1)S(1)}, u32[]{:S(2)}, u32[]{:S(2)}) collective-permute-start(bf16[2,24,1536]{2,1,0:T(8,128)(2,1)S(1)} %pad_maximum_fusion.5), channel_id=1, source_target_pairs={{0,8},{1,9},{2,10},{3,11},{4,12},{5,13},{6,14},{7,15},{8,0},{9,1},... | collective-permute-start | bytes 442376 | tf_op jit(solution)/shard_map/ppermute | solution.py:720
  18.5 14.0 %collective-permute-start.5 = (bf16[2,24,1536]{2,1,0:T(8,128)(2,1)S(1)}, bf16[2,24,1536]{2,1,0:T(8,128)(2,1)S(1)}, u32[]{:S(2)}, u32[]{:S(2)}) collective-permute-start(bf16[2,24,1536]{2,1,0:T(8,128)(2,1)S(1)} %pad_maximum_fusion.5), channel_id=1, source_target_pairs={{0,16},{1,17},{2,18},{3,19},{4,20},{5,21},{6,22},{7,23},{8,24},{9,... | collective-permute-start | bytes 442376 | tf_op jit(solution)/shard_map/ppermute | solution.py:720
  19.9 12.5 %collective-permute-start.6 = (bf16[2,24,1536]{2,1,0:T(8,128)(2,1)S(1)}, bf16[2,24,1536]{2,1,0:T(8,128)(2,1)S(1)}, u32[]{:S(2)}, u32[]{:S(2)}) collective-permute-start(bf16[2,24,1536]{2,1,0:T(8,128)(2,1)S(1)} %pad_maximum_fusion.5), channel_id=1, source_target_pairs={{0,24},{1,25},{2,26},{3,27},{4,28},{5,29},{6,30},{7,31},{8,16},{9,... | collective-permute-start | bytes 442376 | tf_op jit(solution)/shard_map/ppermute | solution.py:720
  21.3 11.5 %collective-permute-start.7 = (bf16[4,24,1920]{2,1,0:T(8,128)(2,1)S(1)}, bf16[4,24,1920]{2,1,0:T(8,128)(2,1)S(1)}, u32[]{:S(2)}, u32[]{:S(2)}) collective-permute-start(bf16[4,24,1920]{2,1,0:T(8,128)(2,1)S(1)} %pad_maximum_fusion.3), channel_id=1, source_target_pairs={{0,2},{1,3},{2,0},{3,1},{4,6},{5,7},{6,4},{7,5},{8,10},{9,11},{10,... | collective-permute-start | bytes 1105928 | tf_op jit(solution)/shard_map/ppermute | solution.py:720
  22.8 10.0 %collective-permute-start.8 = (bf16[4,24,1920]{2,1,0:T(8,128)(2,1)S(1)}, bf16[4,24,1920]{2,1,0:T(8,128)(2,1)S(1)}, u32[]{:S(2)}, u32[]{:S(2)}) collective-permute-start(bf16[4,24,1920]{2,1,0:T(8,128)(2,1)S(1)} %pad_maximum_fusion.3), channel_id=1, source_target_pairs={{0,4},{1,5},{2,6},{3,7},{4,0},{5,1},{6,2},{7,3},{8,12},{9,13},{10,... | collective-permute-start | bytes 1105928 | tf_op jit(solution)/shard_map/ppermute | solution.py:720
  25.1 14.9 %collective-permute-start.9 = (bf16[4,24,1920]{2,1,0:T(8,128)(2,1)S(1)}, bf16[4,24,1920]{2,1,0:T(8,128)(2,1)S(1)}, u32[]{:S(2)}, u32[]{:S(2)}) collective-permute-start(bf16[4,24,1920]{2,1,0:T(8,128)(2,1)S(1)} %pad_maximum_fusion.3), channel_id=1, source_target_pairs={{0,6},{1,7},{2,4},{3,5},{4,2},{5,3},{6,0},{7,1},{8,14},{9,15},{10,... | collective-permute-start | bytes 1105928 | tf_op jit(solution)/shard_map/ppermute | solution.py:720
  40.2 6.4 %collective-permute-start.10 = (bf16[4,4,24,1920]{3,2,1,0:T(8,128)(2,1)S(1)}, bf16[4,4,24,1920]{3,2,1,0:T(8,128)(2,1)}, u32[]{:S(2)}, u32[]{:S(2)}) collective-permute-start(bf16[4,4,24,1920]{3,2,1,0:T(8,128)(2,1)S(1)} %pad_maximum_fusion.1), channel_id=1, source_target_pairs={{0,1},{1,0},{2,3},{3,2},{4,5},{5,4},{6,7},{7,6},{8,9},{9,8},{10,11... | collective-permute-start | bytes 4423688 | tf_op jit(solution)/shard_map/ppermute | solution.py:720
  41.2 25.6 %collective-permute-start.11 = (bf16[4,2,24,1536]{3,2,1,0:T(8,128)(2,1)S(1)}, bf16[4,2,24,1536]{3,2,1,0:T(8,128)(2,1)S(1)}, u32[]{:S(2)}, u32[]{:S(2)}) collective-permute-start(bf16[4,2,24,1536]{3,2,1,0:T(8,128)(2,1)S(1)} %pad_maximum_fusion.2), channel_id=1, source_target_pairs={{0,2},{1,3},{2,0},{3,1},{4,6},{5,7},{6,4},{7,5},{8,10},{9,11},{10,... | collective-permute-start | bytes 1769480 | tf_op jit(solution)/shard_map/ppermute | solution.py:720
  42.1 28.0 %collective-permute-start.12 = (bf16[4,2,24,1536]{3,2,1,0:T(8,128)(2,1)S(1)}, bf16[4,2,24,1536]{3,2,1,0:T(8,128)(2,1)S(1)}, u32[]{:S(2)}, u32[]{:S(2)}) collective-permute-start(bf16[4,2,24,1536]{3,2,1,0:T(8,128)(2,1)S(1)} %pad_maximum_fusion.2), channel_id=1, source_target_pairs={{0,4},{1,5},{2,6},{3,7},{4,0},{5,1},{6,2},{7,3},{8,12},{9,13},{10,... | collective-permute-start | bytes 1769480 | tf_op jit(solution)/shard_map/ppermute | solution.py:720
  43.6 26.5 %collective-permute-start.13 = (bf16[4,2,24,1536]{3,2,1,0:T(8,128)(2,1)S(1)}, bf16[4,2,24,1536]{3,2,1,0:T(8,128)(2,1)S(1)}, u32[]{:S(2)}, u32[]{:S(2)}) collective-permute-start(bf16[4,2,24,1536]{3,2,1,0:T(8,128)(2,1)S(1)} %pad_maximum_fusion.2), channel_id=1, source_target_pairs={{0,6},{1,7},{2,4},{3,5},{4,2},{5,3},{6,0},{7,1},{8,14},{9,15},{10,... | collective-permute-start | bytes 1769480 | tf_op jit(solution)/shard_map/ppermute | solution.py:720
  70.4 11.6 %collective-permute-start.16 = (bf16[4,4,2,24,1536]{4,3,2,1,0:T(8,128)(2,1)S(1)}, bf16[4,4,2,24,1536]{4,3,2,1,0:T(8,128)(2,1)}, u32[]{:S(2)}, u32[]{:S(2)}) collective-permute-start(bf16[4,4,2,24,1536]{4,3,2,1,0:T(8,128)(2,1)S(1)} %pad_maximum_fusion), channel_id=1, source_target_pairs={{0,1},{1,0},{2,3},{3,2},{4,5},{5,4},{6,7},{7,6},{8,9},{9,8},{10,11... | collective-permute-start | bytes 7077896 | tf_op jit(solution)/shard_map/ppermute | solution.py:720
  71.2 9.8 %collective-permute-start.14 = (bf16[2,128,1536]{2,1,0:T(8,128)(2,1)S(1)}, bf16[2,128,1536]{2,1,0:T(8,128)(2,1)S(1)}, u32[]{:S(2)}, u32[]{:S(2)}) collective-permute-start(bf16[2,128,1536]{2,1,0:T(8,128)(2,1)S(1)} %copy-done.20), channel_id=1, source_target_pairs={{0,1},{4,5},{8,9},{12,13},{16,17},{20,21},{24,25},{28,29}} | collective-permute-start | bytes 2359304 | tf_op jit(solution)/shard_map/ppermute | solution.py:798
  81.2 11.6 %collective-permute-start.15 = (bf16[2,128,1536]{2,1,0:T(8,128)(2,1)S(1)}, bf16[2,128,1536]{2,1,0:T(8,128)(2,1)S(1)}, u32[]{:S(2)}, u32[]{:S(2)}) collective-permute-start(bf16[2,128,1536]{2,1,0:T(8,128)(2,1)S(1)} %fusion.1), channel_id=1, source_target_pairs={{1,2},{5,6},{9,10},{13,14},{17,18},{21,22},{25,26},{29,30}} | collective-permute-start | bytes 2359304 | tf_op jit(solution)/shard_map/ppermute | solution.py:798
  93.8 0.9 collective-permute-start.17
  116.5 14.9 %collective-permute-start.19 = (bf16[2,128,1536]{2,1,0:T(8,128)(2,1)}, bf16[2,128,1536]{2,1,0:T(8,128)(2,1)S(1)}, u32[]{:S(2)}, u32[]{:S(2)}) collective-permute-start(bf16[2,128,1536]{2,1,0:T(8,128)(2,1)} %get-tuple-element.147), channel_id=1, source_target_pairs={{3,2},{7,6},{11,10},{15,14},{19,18},{23,22},{27,26},{31,30}} | collective-permute-start | bytes 2359304 | tf_op jit(solution)/shard_map/ppermute | solution.py:798
  117.2 14.2 %copy-start.14 = (f32[2,1,1536]{2,1,0:T(1,128)S(1)}, f32[2,1,1536]{2,1,0:T(1,128)}, u32[]{:S(2)}) copy-start(f32[2,1,1536]{2,1,0:T(1,128)} %get-tuple-element.164) | copy-start | bytes 36868
  117.3 14.2 %copy-start.3 = (f32[2,128,1536]{2,1,0:T(8,128)S(1)}, f32[2,128,1536]{2,1,0:T(8,128)}, u32[]{:S(2)}) copy-start(f32[2,128,1536]{2,1,0:T(8,128)} %get-tuple-element.165) | copy-start | bytes 4718596
  129.8 21.2 %collective-permute-start.18 = (bf16[16,2,24,1536]{3,2,1,0:T(8,128)(2,1)}, bf16[16,2,24,1536]{3,2,1,0:T(8,128)(2,1)}, u32[]{:S(2)}, u32[]{:S(2)}) collective-permute-start(bf16[16,2,24,1536]{3,2,1,0:T(8,128)(2,1)} %get-tuple-element.146), channel_id=1, source_target_pairs={{0,1},{1,0},{2,3},{3,2},{4,5},{5,4},{6,7},{7,6},{8,9},{9,8},{10,11... | collective-permute-start | bytes 7077896 | tf_op jit(solution)/shard_map/ppermute | solution.py:720
  131.4 17.0 %copy-start = (bf16[2,128,1536]{2,1,0:T(8,128)(2,1)}, bf16[2,128,1536]{2,1,0:T(8,128)(2,1)S(1)}, u32[]{:S(2)}) copy-start(bf16[2,128,1536]{2,1,0:T(8,128)(2,1)S(1)} %collective-permute-done.19.refs_0_) | copy-start | bytes 2359300
  131.7 16.7 %collective-permute-start.23 = (bf16[2,128,1536]{2,1,0:T(8,128)(2,1)S(1)}, bf16[2,128,1536]{2,1,0:T(8,128)(2,1)S(1)}, u32[]{:S(2)}, u32[]{:S(2)}) collective-permute-start(bf16[2,128,1536]{2,1,0:T(8,128)(2,1)S(1)} %fusion.6), channel_id=1, source_target_pairs={{2,1},{6,5},{10,9},{14,13},{18,17},{22,21},{26,25},{30,29}} | collective-permute-start | bytes 2359304 | tf_op jit(solution)/shard_map/ppermute | solution.py:798
  149.3 11.4 %collective-permute-start.24 = (bf16[2,128,1536]{2,1,0:T(8,128)(2,1)S(1)}, bf16[2,128,1536]{2,1,0:T(8,128)(2,1)S(1)}, u32[]{:S(2)}, u32[]{:S(2)}) collective-permute-start(bf16[2,128,1536]{2,1,0:T(8,128)(2,1)S(1)} %fusion.9), channel_id=1, source_target_pairs={{1,0},{5,4},{9,8},{13,12},{17,16},{21,20},{25,24},{29,28}} | collective-permute-start | bytes 2359304 | tf_op jit(solution)/shard_map/ppermute | solution.py:798
  154.8 26.7 %collective-permute-start.20 = (bf16[4,2,24,1536]{3,2,1,0:T(8,128)(2,1)}, bf16[4,2,24,1536]{3,2,1,0:T(8,128)(2,1)S(1)}, u32[]{:S(2)}, u32[]{:S(2)}) collective-permute-start(bf16[4,2,24,1536]{3,2,1,0:T(8,128)(2,1)} %get-tuple-element.219), channel_id=1, source_target_pairs={{0,2},{1,3},{2,0},{3,1},{4,6},{5,7},{6,4},{7,5},{8,10},{9,11},{10,... | collective-permute-start | bytes 1769480 | tf_op jit(solution)/shard_map/ppermute | solution.py:720
  159.2 27.2 %collective-permute-start.21 = (bf16[4,2,24,1536]{3,2,1,0:T(8,128)(2,1)}, bf16[4,2,24,1536]{3,2,1,0:T(8,128)(2,1)S(1)}, u32[]{:S(2)}, u32[]{:S(2)}) collective-permute-start(bf16[4,2,24,1536]{3,2,1,0:T(8,128)(2,1)} %get-tuple-element.218), channel_id=1, source_target_pairs={{0,4},{1,5},{2,6},{3,7},{4,0},{5,1},{6,2},{7,3},{8,12},{9,13},{10,... | collective-permute-start | bytes 1769480 | tf_op jit(solution)/shard_map/ppermute | solution.py:720
  159.9 26.6 %collective-permute-start.22 = (bf16[4,2,24,1536]{3,2,1,0:T(8,128)(2,1)S(1)}, bf16[4,2,24,1536]{3,2,1,0:T(8,128)(2,1)S(1)}, u32[]{:S(2)}, u32[]{:S(2)}) collective-permute-start(bf16[4,2,24,1536]{3,2,1,0:T(8,128)(2,1)S(1)} %get-tuple-element.217), channel_id=1, source_target_pairs={{0,6},{1,7},{2,4},{3,5},{4,2},{5,3},{6,0},{7,1},{8,14},{9,15},{10,... | collective-permute-start | bytes 1769480 | tf_op jit(solution)/shard_map/ppermute | solution.py:720
  180.2 6.6 %collective-permute-start.25 = (bf16[2,8,1920]{2,1,0:T(8,128)(2,1)}, bf16[2,8,1920]{2,1,0:T(8,128)(2,1)}, u32[]{:S(2)}, u32[]{:S(2)}) collective-permute-start(bf16[2,8,1920]{2,1,0:T(8,128)(2,1)} %get-tuple-element.180), channel_id=1, source_target_pairs={{1,0},{2,1},{3,2},{5,4},{6,5},{7,6},{9,8},{10,9},{11,10},{13,12},{... | collective-permute-start | bytes 184328 | tf_op jit(solution)/shard_map/ppermute | solution.py:1178
  198.3 6.4 %collective-permute-start.26 = (bf16[16,24,1920]{2,1,0:T(8,128)(2,1)}, bf16[16,24,1920]{2,1,0:T(8,128)(2,1)S(1)}, u32[]{:S(2)}, u32[]{:S(2)}) collective-permute-start(bf16[16,24,1920]{2,1,0:T(8,128)(2,1)} %get-tuple-element.186), channel_id=1, source_target_pairs={{0,1},{1,0},{2,3},{3,2},{4,5},{5,4},{6,7},{7,6},{8,9},{9,8},{10,11... | collective-permute-start | bytes 4423688 | tf_op jit(solution)/shard_map/ppermute | solution.py:720
  198.4 10.3 %collective-permute-start.27 = (f32[96,128]{1,0:T(8,128)}, f32[96,128]{1,0:T(8,128)S(1)}, u32[]{:S(2)}, u32[]{:S(2)}) collective-permute-start(f32[96,128]{1,0:T(8,128)} %get-tuple-element.192), channel_id=1, source_target_pairs={{0,1},{1,0},{2,3},{3,2},{4,5},{5,4},{6,7},{7,6},{8,9},{9,8},{10,11... | collective-permute-start | bytes 147464 | tf_op jit(solution)/shard_map/ppermute | solution.py:720
  205.2 17.3 %collective-permute-start.28 = (bf16[4,24,1920]{2,1,0:T(8,128)(2,1)S(1)}, bf16[4,24,1920]{2,1,0:T(8,128)(2,1)S(1)}, u32[]{:S(2)}, u32[]{:S(2)}) collective-permute-start(bf16[4,24,1920]{2,1,0:T(8,128)(2,1)S(1)} %get-tuple-element.222), channel_id=1, source_target_pairs={{0,2},{1,3},{2,0},{3,1},{4,6},{5,7},{6,4},{7,5},{8,10},{9,11},{10,... | collective-permute-start | bytes 1105928 | tf_op jit(solution)/shard_map/ppermute | solution.py:720
  205.6 17.2 %collective-permute-start.29 = (bf16[4,24,1920]{2,1,0:T(8,128)(2,1)S(1)}, bf16[4,24,1920]{2,1,0:T(8,128)(2,1)S(1)}, u32[]{:S(2)}, u32[]{:S(2)}) collective-permute-start(bf16[4,24,1920]{2,1,0:T(8,128)(2,1)S(1)} %get-tuple-element.221), channel_id=1, source_target_pairs={{0,4},{1,5},{2,6},{3,7},{4,0},{5,1},{6,2},{7,3},{8,12},{9,13},{10,... | collective-permute-start | bytes 1105928 | tf_op jit(solution)/shard_map/ppermute | solution.py:720
  207.0 16.8 %collective-permute-start.30 = (bf16[4,24,1920]{2,1,0:T(8,128)(2,1)S(1)}, bf16[4,24,1920]{2,1,0:T(8,128)(2,1)S(1)}, u32[]{:S(2)}, u32[]{:S(2)}) collective-permute-start(bf16[4,24,1920]{2,1,0:T(8,128)(2,1)S(1)} %get-tuple-element.220), channel_id=1, source_target_pairs={{0,6},{1,7},{2,4},{3,5},{4,2},{5,3},{6,0},{7,1},{8,14},{9,15},{10,... | collective-permute-start | bytes 1105928 | tf_op jit(solution)/shard_map/ppermute | solution.py:720
  208.8 15.2 %collective-permute-start.31 = (bf16[2,24,1536]{2,1,0:T(8,128)(2,1)S(1)}, bf16[2,24,1536]{2,1,0:T(8,128)(2,1)S(1)}, u32[]{:S(2)}, u32[]{:S(2)}) collective-permute-start(bf16[2,24,1536]{2,1,0:T(8,128)(2,1)S(1)} %get-tuple-element.198), channel_id=1, source_target_pairs={{0,8},{1,9},{2,10},{3,11},{4,12},{5,13},{6,14},{7,15},{8,0},{9,1},... | collective-permute-start | bytes 442376 | tf_op jit(solution)/shard_map/ppermute | solution.py:720
  209.4 14.6 %collective-permute-start.32 = (bf16[2,24,1536]{2,1,0:T(8,128)(2,1)S(1)}, bf16[2,24,1536]{2,1,0:T(8,128)(2,1)S(1)}, u32[]{:S(2)}, u32[]{:S(2)}) collective-permute-start(bf16[2,24,1536]{2,1,0:T(8,128)(2,1)S(1)} %get-tuple-element.199), channel_id=1, source_target_pairs={{0,16},{1,17},{2,18},{3,19},{4,20},{5,21},{6,22},{7,23},{8,24},{9,... | collective-permute-start | bytes 442376 | tf_op jit(solution)/shard_map/ppermute | solution.py:720
  222.4 7.1 %collective-permute-start.33 = (bf16[2,24,1536]{2,1,0:T(8,128)(2,1)S(1)}, bf16[2,24,1536]{2,1,0:T(8,128)(2,1)S(1)}, u32[]{:S(2)}, u32[]{:S(2)}) collective-permute-start(bf16[2,24,1536]{2,1,0:T(8,128)(2,1)S(1)} %get-tuple-element.200), channel_id=1, source_target_pairs={{0,24},{1,25},{2,26},{3,27},{4,28},{5,29},{6,30},{7,31},{8,16},{9,... | collective-permute-start | bytes 442376 | tf_op jit(solution)/shard_map/ppermute | solution.py:720
  229.6 18.4 %copy-start.15 = (f32[48]{0:T(128)S(1)}, f32[48]{0:T(128)}, u32[]{:S(2)}) copy-start(f32[48]{0:T(128)} %param.26) | copy-start | bytes 580
  229.6 19.0 %copy-start.19 = (f32[24]{0:T(128)S(1)}, f32[24]{0:T(128)}, u32[]{:S(2)}) copy-start(f32[24]{0:T(128)} %param.19) | copy-start | bytes 292
  229.7 10.1 %collective-permute-start.40 = (bf16[24,1920]{1,0:T(8,128)(2,1)S(1)}, bf16[24,1920]{1,0:T(8,128)(2,1)S(1)}, u32[]{:S(2)}, u32[]{:S(2)}) collective-permute-start(bf16[24,1920]{1,0:T(8,128)(2,1)S(1)} %get-tuple-element.204), channel_id=1, source_target_pairs={{0,8},{1,9},{2,10},{3,11},{4,12},{5,13},{6,14},{7,15},{8,0},{9,1},... | collective-permute-start | bytes 276488 | tf_op jit(solution)/shard_map/ppermute | solution.py:720
  231.1 4.3 %collective-permute-start.34 = (f32[96,128]{1,0:T(8,128)S(1)}, f32[96,128]{1,0:T(8,128)S(1)}, u32[]{:S(2)}, u32[]{:S(2)}) collective-permute-start(f32[96,128]{1,0:T(8,128)S(1)} %add.114), channel_id=1, source_target_pairs={{0,2},{1,3},{2,0},{3,1},{4,6},{5,7},{6,4},{7,5},{8,10},{9,11},{10,... | collective-permute-start | bytes 147464 | tf_op jit(solution)/shard_map/ppermute | solution.py:720
  231.4 6.9 %collective-permute-start.35 = (f32[96,128]{1,0:T(8,128)S(1)}, f32[96,128]{1,0:T(8,128)S(1)}, u32[]{:S(2)}, u32[]{:S(2)}) collective-permute-start(f32[96,128]{1,0:T(8,128)S(1)} %add.114), channel_id=1, source_target_pairs={{0,4},{1,5},{2,6},{3,7},{4,0},{5,1},{6,2},{7,3},{8,12},{9,13},{10,... | collective-permute-start | bytes 147464 | tf_op jit(solution)/shard_map/ppermute | solution.py:720
  232.8 5.6 %collective-permute-start.36 = (f32[96,128]{1,0:T(8,128)S(1)}, f32[96,128]{1,0:T(8,128)S(1)}, u32[]{:S(2)}, u32[]{:S(2)}) collective-permute-start(f32[96,128]{1,0:T(8,128)S(1)} %add.114), channel_id=1, source_target_pairs={{0,6},{1,7},{2,4},{3,5},{4,2},{5,3},{6,0},{7,1},{8,14},{9,15},{10,... | collective-permute-start | bytes 147464 | tf_op jit(solution)/shard_map/ppermute | solution.py:720
  234.6 9.1 %collective-permute-start.41 = (bf16[24,1920]{1,0:T(8,128)(2,1)S(1)}, bf16[24,1920]{1,0:T(8,128)(2,1)S(1)}, u32[]{:S(2)}, u32[]{:S(2)}) collective-permute-start(bf16[24,1920]{1,0:T(8,128)(2,1)S(1)} %get-tuple-element.207), channel_id=1, source_target_pairs={{0,16},{1,17},{2,18},{3,19},{4,20},{5,21},{6,22},{7,23},{8,24},{9,... | collective-permute-start | bytes 276488 | tf_op jit(solution)/shard_map/ppermute | solution.py:720
  235.3 8.3 %collective-permute-start.42 = (bf16[24,1920]{1,0:T(8,128)(2,1)S(1)}, bf16[24,1920]{1,0:T(8,128)(2,1)S(1)}, u32[]{:S(2)}, u32[]{:S(2)}) collective-permute-start(bf16[24,1920]{1,0:T(8,128)(2,1)S(1)} %get-tuple-element.208), channel_id=1, source_target_pairs={{0,24},{1,25},{2,26},{3,27},{4,28},{5,29},{6,30},{7,31},{8,16},{9,... | collective-permute-start | bytes 276488 | tf_op jit(solution)/shard_map/ppermute | solution.py:720
  238.4 6.1 %collective-permute-start.37 = (f32[96,128]{1,0:T(8,128)S(1)}, f32[96,128]{1,0:T(8,128)S(1)}, u32[]{:S(2)}, u32[]{:S(2)}) collective-permute-start(f32[96,128]{1,0:T(8,128)S(1)} %add_add_fusion.2), channel_id=1, source_target_pairs={{0,8},{1,9},{2,10},{3,11},{4,12},{5,13},{6,14},{7,15},{8,0},{9,1},... | collective-permute-start | bytes 147464 | tf_op jit(solution)/shard_map/ppermute | solution.py:720
  238.9 7.3 %collective-permute-start.38 = (f32[96,128]{1,0:T(8,128)S(1)}, f32[96,128]{1,0:T(8,128)S(1)}, u32[]{:S(2)}, u32[]{:S(2)}) collective-permute-start(f32[96,128]{1,0:T(8,128)S(1)} %add_add_fusion.2), channel_id=1, source_target_pairs={{0,16},{1,17},{2,18},{3,19},{4,20},{5,21},{6,22},{7,23},{8,24},{9,... | collective-permute-start | bytes 147464 | tf_op jit(solution)/shard_map/ppermute | solution.py:720
  239.8 6.4 %collective-permute-start.39 = (f32[96,128]{1,0:T(8,128)S(1)}, f32[96,128]{1,0:T(8,128)S(1)}, u32[]{:S(2)}, u32[]{:S(2)}) collective-permute-start(f32[96,128]{1,0:T(8,128)S(1)} %add_add_fusion.2), channel_id=1, source_target_pairs={{0,24},{1,25},{2,26},{3,27},{4,28},{5,29},{6,30},{7,31},{8,16},{9,... | collective-permute-start | bytes 147464 | tf_op jit(solution)/shard_map/ppermute | solution.py:720
  (17 other events, 103.1 us)

commit v4 on v3

--- a/solution.py
+++ b/solution.py
@@ -21,6 +21,8 @@
 CH = 256
 HALF = 128
 RIM = 16
+EARLY = 3
+LATE = 3
 PIECES = 32
 NEG = -1e30
 LIMITS = {
@@ -143,7 +145,7 @@
     groups, scal, x, halo, wa, wb, t56, t48, t24, par, e,
     nrm_o, nrmt_o, cie_o, sp_o, xh_o, xs_o, wx_o, bc_o, step_o, cum_o, dtb_o, cumt_o,
     sloc_o, pre_o, r_o, rl_o, tot_o, wc_o, taps_o, gain_o, gate_o,
-    nrm, run, dec, small, *slots,
+    nrm, run, dec, small, wc_s, sem, *slots,
 ):
     block = pl.program_id(0)
     fresh = block % groups == 0
@@ -156,13 +158,14 @@
         def one(place, carry):
             chip = source_of(me, place) >> 1
             own, other = wa[place].astype(f32), wb[place].astype(f32)
-            wc_o[pl.ds(pl.multiple_of(chip * 48, 16), 48), :] = pair_rows(me, own, other).astype(low)
+            wc_s[pl.ds(pl.multiple_of(chip * 48, 16), 48), :] = pair_rows(me, own, other).astype(low)
             rows = pl.ds(pl.multiple_of(place * 8, 8), 8)
             small[0, rows, :] = own[0:8, CD:CW]
             small[1, rows, :] = other[0:8, CD:CW]
             return carry
 
         lax.fori_loop(0, PIECES // 2, one, 0)
+        pltpu.make_async_copy(wc_s, wc_o, sem).start()
         at = lax.broadcasted_iota(jnp.int32, (PIECES, 1), 0)
         slot = at & (PIECES // 2 - 1)
         ids = me ^ ((slot >> 2) << 1) ^ ((slot & 3) << 3) ^ (at >> 4)
@@ -192,7 +195,7 @@
 
     for c in range(0, CD, CH):
         cols = slice(c, c + CH)
-        conv_in = nn(nrm[...], wc_o[:, cols]).astype(low)
+        conv_in = nn(nrm[...], wc_s[:, cols]).astype(low)
         cie_o[:, cols] = conv_in
         wide = conv_in.astype(f32)
         for side in range(2):
@@ -212,7 +215,7 @@
                 else:
                     bc_o[r : r + 64, side * HALF : (side + 1) * HALF] = act
 
-    dtb = nn(nrm[RIM:, :], wc_o[:, CD:CW]) + par[0:1, :]
+    dtb = nn(nrm[RIM:, :], wc_s[:, CD:CW]) + par[0:1, :]
     step = softplus(dtb)
     cum = running_sum(-step * par[1:2, :], False)
     step_o[...] = step
@@ -244,6 +247,10 @@
         dec[:, cols] = product
         tot_o[:, cols] = product[0:1, :]
 
+    @pl.when(block == pl.num_programs(0) - 1)
+    def finish():
+        pltpu.make_async_copy(wc_s, wc_o, sem).wait()
+
 
 def block_rows(block):
     return pl.ds(pl.multiple_of(block * Q, Q), Q)
@@ -281,9 +288,16 @@
     return (at < scal[2 + seq]).astype(f32)
 
 
-def project_kernel(groups, scal, nrm, cot, wa, wb, z_all, dn_all, db_o, wz_o, wo_o):
+def project_kernel(
+    groups, scal, nrm, cot, wa, wb, z_all, dn_all, db_o, wz_o, wo_o, wz_s, wo_s, sems
+):
     block = pl.program_id(0)
     z_o, dn_o = z_all.at[block_rows(block), :], dn_all.at[block_rows(block), :]
+
+    copies = [
+        pltpu.make_async_copy(wz_s, wz_o, sems.at[0]),
+        pltpu.make_async_copy(wo_s, wo_o, sems.at[1]),
+    ]
 
     @pl.when(block == 0)
     def assemble():
@@ -295,17 +309,24 @@
         def one(place, carry):
             chip = source_of(me, place) >> 1
             own, other = wa[place, 0].astype(f32), wb[place, 0].astype(f32)
-            wz_o[pl.ds(pl.multiple_of(chip * 48, 16), 48), :] = pair_rows(me, own, other).astype(low)
+            wz_s[pl.ds(pl.multiple_of(chip * 48, 16), 48), :] = pair_rows(me, own, other).astype(low)
             own, other = halves(wa[place, 1].astype(f32)), halves(wb[place, 1].astype(f32))
-            wo_o[pl.ds(pl.multiple_of(chip * 96, 16), 96), :] = pair_rows(me, own, other).astype(low)
+            wo_s[pl.ds(pl.multiple_of(chip * 96, 16), 96), :] = pair_rows(me, own, other).astype(low)
             return carry
 
         lax.fori_loop(0, PIECES // 2, one, 0)
+        for copy in copies:
+            copy.start()
 
     db_o[...] = (cot[...].astype(f32) * valid_column(scal, groups, block)).astype(low)
     for c in range(0, DI, CH):
-        z_o[:, c : c + CH] = nn(nrm[...], wz_o[:, c : c + CH])
-        dn_o[:, c : c + CH] = nt(db_o[...], wo_o[c : c + CH, :])
+        z_o[:, c : c + CH] = nn(nrm[...], wz_s[:, c : c + CH])
+        dn_o[:, c : c + CH] = nt(db_o[...], wo_s[c : c + CH, :])
+
+    @pl.when(block == pl.num_programs(0) - 1)
+    def finish():
+        for copy in copies:
+            copy.wait()
 
 
 def gate_kernel(
@@ -591,7 +612,7 @@
 
     me = scal[0]
     refs = (g0_o, g1_o)
-    quarter = DI // 4
+    quarter = DI // EARLY
     cols = pl.ds(pl.multiple_of(at * quarter, HALF), quarter)
     part[...] = nn(nrmt[...], dz[...])
     na_o[...] += fold_lanes(part[...] * wzc[...].astype(f32))
@@ -603,7 +624,7 @@
     wide[rows, :] = tn(gn[...], db[...])
     ga_o[...] = fold_lanes(wide[rows, :] * wo[...].astype(f32))
 
-    @pl.when(at == 3)
+    @pl.when(at == EARLY - 1)
     def finish():
         for place in range(PIECES // 2):
             for which in range(2):
@@ -916,6 +937,7 @@
 
     scalars = pl.BlockSpec(memory_space=pltpu.SMEM)
     whole = pl.BlockSpec(memory_space=pltpu.VMEM)
+    away = pl.BlockSpec(memory_space=pl.ANY)
     flat_hidden = hidden.reshape(rows, width)
     flat_cot = cotangent.reshape(rows, width)
 
@@ -952,7 +974,7 @@
             (per_seq(N, DI), (seqs, N, DI), f32),
             (per_seq(N, DI), (seqs, N, DI), low),
             (per_seq(1, DI), (seqs, 1, DI), f32),
-            (kept(width, CW), (width, CW), low),
+            (away, (width, CW), low),
             (kept(8, CD), (8, CD), f32),
             (kept(8, width), (8, width), f32),
             (kept(8, DI), (8, DI), f32),
@@ -962,6 +984,8 @@
             pltpu.VMEM((N, DI), f32),
             pltpu.VMEM((8, DI), f32),
             pltpu.VMEM((2, HL, HL), f32),
+            pltpu.VMEM((width, CW), low),
+            pltpu.SemaphoreType.DMA,
             *[pltpu.VMEM((Q + RIM, HALF), f32)] * (CD // HALF),
         ],
         2.0 * rows * width * CW,
@@ -1007,10 +1031,14 @@
                 (whole, (rows, DI), f32, near),
                 (whole, (rows, DI), f32, near),
                 (tokens(width, forth), (rows, width), low),
-                (kept(width, DI), (width, DI), low),
-                (kept(DI, width), (DI, width), low),
+                (away, (width, DI), low),
+                (away, (DI, width), low),
             ],
-            [],
+            [
+                pltpu.VMEM((width, DI), low),
+                pltpu.VMEM((DI, width), low),
+                pltpu.SemaphoreType.DMA((2,)),
+            ],
             4.0 * rows * width * DI,
             "project",
         )
@@ -1102,23 +1130,23 @@
     def early_part(got):
         return call(
             early_grad_kernel,
-            4,
+            EARLY,
             [
                 (scalars, after(scal, got)),
                 (fixed(width, rows), nrmt),
-                (pl.BlockSpec((rows, DI // 4), lambda i: (0, i)), dz),
-                (pl.BlockSpec((rows, DI // 4), lambda i: (0, i)), gn),
+                (pl.BlockSpec((rows, DI // EARLY), lambda i: (0, i)), dz),
+                (pl.BlockSpec((rows, DI // EARLY), lambda i: (0, i)), gn),
                 (fixed(rows, width), db),
-                (pl.BlockSpec((width, DI // 4), lambda i: (0, i)), wz),
-                (pl.BlockSpec((DI // 4, width), lambda i: (i, 0)), wo),
+                (pl.BlockSpec((width, DI // EARLY), lambda i: (0, i)), wz),
+                (pl.BlockSpec((DI // EARLY, width), lambda i: (i, 0)), wo),
             ],
             [
                 (kept(*piece), piece, low),
                 (kept(*piece), piece, low),
                 (kept(width, HALF), (width, HALF), f32),
-                (pl.BlockSpec((DI // 4, HALF), lambda i: (i, 0)), (DI, HALF), f32),
+                (pl.BlockSpec((DI // EARLY, HALF), lambda i: (i, 0)), (DI, HALF), f32),
             ],
-            [pltpu.VMEM((width, DI // 4), f32), pltpu.VMEM((DI, width), f32)],
+            [pltpu.VMEM((width, DI // EARLY), f32), pltpu.VMEM((DI, width), f32)],
             6.0 * rows * width * DI,
             "early_grad",
         )
@@ -1178,18 +1206,18 @@
     returned = lax.ppermute(heads_out, "seq", [(i, i - 1) for i in range(1, seq_size)])
 
     late = (PIECES // 2, width // PIECES, CW)
-    late_spec = pl.BlockSpec((PIECES // 2, width // PIECES, CW // 5), lambda i: (0, 0, i))
+    late_spec = pl.BlockSpec((PIECES // 2, width // PIECES, CW // LATE), lambda i: (0, 0, i))
     (l0, l1, dcv, vector) = call(
         late_grad_kernel,
-        5,
+        LATE,
         [
             (scalars, turn),
             (fixed(width, rows), nrmt),
-            (pl.BlockSpec((rows, CW // 5), lambda i: (0, i)), dcv),
-            (pl.BlockSpec((width, CW // 5), lambda i: (0, i)), wc),
+            (pl.BlockSpec((rows, CW // LATE), lambda i: (0, i)), dcv),
+            (pl.BlockSpec((width, CW // LATE), lambda i: (0, i)), wc),
             (fixed(width, HALF), na),
-            (pl.BlockSpec((seqs, 16, CW // 5), lambda i: (0, 0, i)), tails_out),
-            (pl.BlockSpec((seqs, 8, CW // 5), lambda i: (0, 0, i)), returned),
+            (pl.BlockSpec((seqs, 16, CW // LATE), lambda i: (0, 0, i)), tails_out),
+            (pl.BlockSpec((seqs, 8, CW // LATE), lambda i: (0, 0, i)), returned),
             (fixed(8 * (KW + 1), CD), cacc),
             (fixed(16, HL), hacc),
             (fixed(8, DI), kacc),
@@ -1200,10 +1228,10 @@
         [
             (late_spec, late, low),
             (late_spec, late, low),
-            (pl.BlockSpec((rows, CW // 5), lambda i: (0, i)), (rows, CW), low),
+            (pl.BlockSpec((rows, CW // LATE), lambda i: (0, i)), (rows, CW), low),
             (kept(96, HALF), (96, HALF), f32),
         ],
-        [pltpu.VMEM((width, CW // 5), f32), pltpu.VMEM((width, HALF), f32)],
+        [pltpu.VMEM((width, CW // LATE), f32), pltpu.VMEM((width, HALF), f32)],
         2.0 * rows * width * CW,
         "late_grad",
     )
@@ -1247,10 +1275,9 @@
         gh, done2 = input_part(half_blocks, blocks - half_blocks, gh, done, late_sum[1])
         late_sum = parts_of(merge(*late_sum, (2, 4, 6), done2))
         early = merge(*early, (8, 16, 24), late_sum[1][0])
-        late_sum = tie_all(*late_sum, early)
         vector = tie(vector, late_sum[1][0])
         got = [swap(vector, mask) for mask in (2, 4, 6)]
-        vector = (vector + got[0]) + (got[1] + got[2])
+        vector = tie((vector + got[0]) + (got[1] + got[2]), early)
     else:
         gh, done = input_part(0, blocks, scal, scal, None)
 

time: 250 us -> 245 us (0.980)
  transfers between devices with their start and end apart: 43 -> 43, of which waited for: 11 -> 12; matrix products, arithmetic and copies ran while one was open for 5% -> 6% of each run, Pallas kernels for 41% -> 41%
where the time goes in v4:
time: 245 us
  Pallas kernels  132 us (54%)
  starting transfers between devices  54.2 us (22%)
  waiting for transfers between devices  33.1 us (14%)
  other arithmetic  12.2 us (5%)
  local copies, waits for them, and re-layouts  12.1 us (5%)
    pallas_call x10, Pallas kernels, call(): pl.pallas_call(kernel, grid=(grid,), in_specs=in_specs, out_specs=out_spe...  132 us
    ppermute x35, starting transfers between devices, swap(): return lax.ppermute(value, axes, [(i, i ^ mask) for i in range(PIECES)])  45.3 us
    ppermute x35, waiting for transfers between devices, swap(): return lax.ppermute(value, axes, [(i, i ^ mask) for i in range(PIECES)])  33.1 us
    ppermute x6, starting transfers between devices, relay(): arrived = lax.ppermute(value, 'seq', route)  6.34 us
  transfers between devices with their start and end apart: 43, of which 12 were waited for; matrix products, arithmetic and copies ran while one was open for 6% of the time, Pallas kernels for 41%

profile of v4, /device:TPU:0, one launch (start us, length us, event | category | flops | bytes accessed | tf_op | source)
XLA Modules:
  0.0 244.7 jit_solution(16156925520427332239)
XLA Ops:
  1.3 0.9 slice.223
  3.8 3.0 %collective-permute-start = (bf16[24,1920]{1,0:T(8,128)(2,1)S(1)}, bf16[24,1920]{1,0:T(8,128)(2,1)S(1)}, u32[]{:S(2)}, u32[]{:S(2)}) collective-permute-start(bf16[24,1920]{1,0:T(8,128)(2,1)S(1)} %pad_maximum_fusion.8), channel_id=1, source_target_pairs={{0,8},{1,9},{2,10},{3,11},{4,12},{5,13},{6,14},{7,15},{8,0},{9,1},... | collective-permute-start | bytes 276488 | tf_op jit(solution)/shard_map/ppermute | solution.py:741
  6.8 2.6 %collective-permute-start.1 = (bf16[24,1920]{1,0:T(8,128)(2,1)S(1)}, bf16[24,1920]{1,0:T(8,128)(2,1)S(1)}, u32[]{:S(2)}, u32[]{:S(2)}) collective-permute-start(bf16[24,1920]{1,0:T(8,128)(2,1)S(1)} %pad_maximum_fusion.8), channel_id=1, source_target_pairs={{0,16},{1,17},{2,18},{3,19},{4,20},{5,21},{6,22},{7,23},{8,24},{9,... | collective-permute-start | bytes 276488 | tf_op jit(solution)/shard_map/ppermute | solution.py:741
  10.2 1.3 collective-permute-start.3
  11.5 0.9 slice_bitcast_fusion.16
  12.4 0.9 fusion.13
  13.4 0.9 convert_element_type.137
  14.4 2.3 collective-permute-done.1
  16.8 1.6 collective-permute-start.4
  18.5 1.5 collective-permute-start.5
  19.9 1.3 collective-permute-start.6
  21.3 1.5 collective-permute-start.7
  22.8 1.5 collective-permute-start.8
  25.1 1.1 collective-permute-start.9
  26.2 6.2 %collective-permute-done.5 = bf16[2,24,1536]{2,1,0:T(8,128)(2,1)S(1)} collective-permute-done((bf16[2,24,1536]{2,1,0:T(8,128)(2,1)S(1)}, bf16[2,24,1536]{2,1,0:T(8,128)(2,1)S(1)}, u32[]{:S(2)}, u32[]{:S(2)}) %collective-permute-start.5) | collective-permute-done | bytes 147488 | tf_op jit(solution)/shard_map/ppermute | solution.py:741
  32.8 7.2 %collective-permute-done.9 = bf16[4,24,1920]{2,1,0:T(8,128)(2,1)S(1)} collective-permute-done((bf16[4,24,1920]{2,1,0:T(8,128)(2,1)S(1)}, bf16[4,24,1920]{2,1,0:T(8,128)(2,1)S(1)}, u32[]{:S(2)}, u32[]{:S(2)}) %collective-permute-start.9) | collective-permute-done | bytes 368672 | tf_op jit(solution)/shard_map/ppermute | solution.py:741
  42.1 1.5 collective-permute-start.12
  43.6 1.2 collective-permute-start.13
  46.6 19.8 %conv.1 = (bf16[1024,768]{1,0:T(8,128)(2,1)}, bf16[768,1024]{1,0:T(8,128)(2,1)}, bf16[4,272,1792]{2,1,0:T(8,128)(2,1)}, f32[1024,1792]{1,0:T(8,128)}, bf16[1024,...) custom-call(s32[5]{0:T(128)} %pad_add_fusion.scal.past.token, ...), custom_call_target="tpu_custom_call" | custom-call | flops 3019898880 | bytes 6066196 | tf_op jit(solution)/shard_map/conv/pallas_call | solution.py:720
  66.4 3.7 %collective-permute-done.12 = bf16[4,2,24,1536]{3,2,1,0:T(8,128)(2,1)S(1)} collective-permute-done((bf16[4,2,24,1536]{3,2,1,0:T(8,128)(2,1)S(1)}, bf16[4,2,24,1536]{3,2,1,0:T(8,128)(2,1)S(1)}, u32[]{:S(2)}, u32[]{:S(2)}) %collective-permute-start.12) | collective-permute-done | bytes 589856 | tf_op jit(solution)/shard_map/ppermute | solution.py:741
  71.2 1.7 collective-permute-start.14
  73.0 8.0 %intra.1 = f32[1024,1536]{1,0:T(8,128)} custom-call(bf16[1024,256]{1,0:T(8,128)(2,1)} %get-tuple-element.147.bc, bf16[1024,1536]{1,0:T(8,128)(2,1)} %get-tuple-element.120.xs, f32[1024,128]{1,0:T(8,128)} %get-tuple-element.115.cum, f32[4,24,256]{2,1,0:T(8,128)} %get-tuple-element.121.cumt), custom_call_target="tpu_custom_call" | custom-call | flops 1610612736 | bytes 4292608 | tf_op jit(solution)/shard_map/intra/pallas_call | solution.py:720
  82.0 10.3 %project.1 = (f32[1024,1536]{1,0:T(8,128)S(1)}, f32[1024,1536]{1,0:T(8,128)S(1)}, bf16[1024,768]{1,0:T(8,128)(2,1)}, bf16[768,1536]{1,0:T(8,128)(2,1)}, bf16[1536,768]{1,0:T(8,128)(2,1)}) custom-call(s32[5]{0:T(128)} %pad_add_fusion.scal.past.token, bf16[1024,768]{1,0:T(8,128)(2,1)} %get-tuple-element.130.nrm, bf16[1024,768]{1,0:T(8,128)(2,1)} %bitcast.91, ...), custom_call_target="tpu_custom_call" | custom-call | flops 4831838208 | bytes 7864340 | tf_op jit(solution)/shard_map/project/pallas_call | solution.py:720
  95.0 21.0 %gate.1 = (bf16[1024,768]{1,0:T(8,128)(2,1)}, bf16[1024,1536]{1,0:T(8,128)(2,1)}, bf16[1024,1536]{1,0:T(8,128)(2,1)}, bf16[1024,1536]{1,0:T(8,128)(2,1)}, bf16[1...) custom-call(s32[5]{0:T(128)} %pad_add_fusion.scal.past.token, ...), custom_call_target="tpu_custom_call" | custom-call | flops 4831838208 | bytes 33542164 | tf_op jit(solution)/shard_map/gate/pallas_call | solution.py:720
  116.7 12.0 %early_grad.1 = (bf16[16,2,24,1536]{3,2,1,0:T(8,128)(2,1)}, bf16[16,2,24,1536]{3,2,1,0:T(8,128)(2,1)}, f32[768,128]{1,0:T(8,128)}, f32[1536,128]{1,0:T(8,128)}) custom-call(s32[5]{0:T(128)} %pad_add_fusion.scal.past.token, bf16[768,1024]{1,0:T(8,128)(2,1)} %get-tuple-element.137.nrmt, bf16[1024,1536]{1,0:T(8,128)(2,1)} %get-tuple-element.138.dz, ...), custom_call_target="tpu_custom_call" | custom-call | flops 7247757312 | bytes 14155796 | tf_op jit(solution)/shard_map/early_grad/pallas_call | solution.py:720
  128.7 1.6 collective-permute-start.18
  131.3 16.0 %intra_back.1 = (f32[1024,1536]{1,0:T(8,128)}, f32[1024,256]{1,0:T(8,128)}, f32[1024,128]{1,0:T(8,128)}) custom-call(bf16[1024,256]{1,0:T(8,128)(2,1)} %get-tuple-element.147.bc, bf16[1024,1536]{1,0:T(8,128)(2,1)} %get-tuple-element.120.xs, bf16[1024,1536]{1,0:T(8,128)(2,1)} %get-tuple-element.122.xh, bf16[1024,1536]{1,0:T(8,128)(2,1)} %get-tuple-element.148.dy, ...), custom_call_target="tpu_custom_call" | custom-call | flops 3221225472 | bytes 11898880 | tf_op jit(solution)/shard_map/intra_back/pallas_call | solution.py:720
  148.2 1.6 collective-permute-start.24
  149.9 2.6 %convert_add_fusion = (f32[16,2,24,1536]{3,2,1,0:T(8,128)S(1)}, bf16[16,2,24,1536]{3,2,1,0:T(8,128)(2,1)S(1)}) fusion(bf16[16,2,24,1536]{3,2,1,0:T(8,128)(2,1)} %collective-permute-done.18, bf16[16,2,24,1536]{3,2,1,0:T(8,128)(2,1)S(1)} %copy-done.7), kind=kLoop, calls=%fused_computation | loop fusion | flops 4718592 | bytes 11796480 | tf_op jit(solution)/shard_map/add | solution.py:776
  152.5 1.2 fusion.22
  153.7 5.0 %collective-permute-start.20 = (bf16[4,2,24,1536]{3,2,1,0:T(8,128)(2,1)}, bf16[4,2,24,1536]{3,2,1,0:T(8,128)(2,1)S(1)}, u32[]{:S(2)}, u32[]{:S(2)}) collective-permute-start(bf16[4,2,24,1536]{3,2,1,0:T(8,128)(2,1)} %get-tuple-element.213), channel_id=1, source_target_pairs={{0,2},{1,3},{2,0},{3,1},{4,6},{5,7},{6,4},{7,5},{8,10},{9,11},{10,... | collective-permute-start | bytes 1769480 | tf_op jit(solution)/shard_map/ppermute | solution.py:741
  161.0 18.6 %conv_back.1 = (bf16[1024,1920]{1,0:T(8,128)(2,1)}, f32[40,1792]{1,0:T(8,128)}, f32[16,128]{1,0:T(8,128)}, bf16[2,8,1920]{2,1,0:T(8,128)(2,1)}, f32[2,16,1920]{2,1,0:T(8,128)}) custom-call(s32[5]{0:T(128)} %pad_add_fusion.scal.past.token, f32[4,128,1536]{2,1,0:T(8,128)} %get-tuple-element.152.dloc, f32[4,8,1536]{2,1,0:T(8,128)} %get-tuple-element.153.suf, ...), custom_call_target="tpu_custom_call" | custom-call | flops 1207959552 | bytes 39284756 | tf_op jit(solution)/shard_map/conv_back/pallas_call | solution.py:720
  179.6 1.3 collective-permute-start.25
  181.0 4.9 %collective-permute-done.21 = bf16[4,2,24,1536]{3,2,1,0:T(8,128)(2,1)S(1)} collective-permute-done((bf16[4,2,24,1536]{3,2,1,0:T(8,128)(2,1)}, bf16[4,2,24,1536]{3,2,1,0:T(8,128)(2,1)S(1)}, u32[]{:S(2)}, u32[]{:S(2)}) %collective-permute-start.21) | collective-permute-done | bytes 589856 | tf_op jit(solution)/shard_map/ppermute | solution.py:741
  186.2 10.7 %late_grad.1 = (bf16[16,24,1920]{2,1,0:T(8,128)(2,1)}, bf16[16,24,1920]{2,1,0:T(8,128)(2,1)}, bf16[1024,1920]{1,0:T(8,128)(2,1)}, f32[96,128]{1,0:T(8,128)}) custom-call(s32[5]{0:T(128)} %pad_add_fusion.scal.past.token, bf16[768,1024]{1,0:T(8,128)(2,1)} %get-tuple-element.137.nrmt, bf16[1024,1920]{1,0:T(8,128)(2,1)} %get-tuple-element.173.dcv, ...), custom_call_target="tpu_custom_call" | custom-call | flops 3019898880 | bytes 10682388 | tf_op jit(solution)/shard_map/late_grad/pallas_call | solution.py:720
  197.5 5.8 %input.2 = (bf16[1024,768]{1,0:T(8,128)(2,1)}, f32[8,128]{1,0:T(8,128)}) custom-call(bf16[1024,1920]{1,0:T(8,128)(2,1)} %get-tuple-element.180.dcv, bf16[1024,1536]{1,0:T(8,128)(2,1)} %get-tuple-element.138.dz, bf16[768,1920]{1,0:T(8,128)(2,1)} %get-tuple-element.174.wc, bf16[768,1536]{1,0:T(8,128)(2,1)} %get-tuple-element.141.wzc.wz, ...), custom_call_target="tpu_custom_call" | custom-call | flops 1 | bytes 1 | tf_op jit(solution)/shard_map/input/pallas_call | solution.py:720
  204.2 1.4 collective-permute-start.29
  205.6 1.8 collective-permute-start.30
  208.0 3.6 %collective-permute-start.35 = (bf16[2,24,1536]{2,1,0:T(8,128)(2,1)S(1)}, bf16[2,24,1536]{2,1,0:T(8,128)(2,1)S(1)}, u32[]{:S(2)}, u32[]{:S(2)}) collective-permute-start(bf16[2,24,1536]{2,1,0:T(8,128)(2,1)S(1)} %get-tuple-element.197), channel_id=1, source_target_pairs={{0,16},{1,17},{2,18},{3,19},{4,20},{5,21},{6,22},{7,23},{8,24},{9,... | collective-permute-start | bytes 442376 | tf_op jit(solution)/shard_map/ppermute | solution.py:741
  211.6 9.5 %input.3 = (bf16[1024,768]{1,0:T(8,128)(2,1)}, f32[8,128]{1,0:T(8,128)}) custom-call(bf16[1024,1920]{1,0:T(8,128)(2,1)} %get-tuple-element.180.dcv, bf16[1024,1536]{1,0:T(8,128)(2,1)} %get-tuple-element.138.dz, bf16[768,1920]{1,0:T(8,128)(2,1)} %get-tuple-element.174.wc, ...), custom_call_target="tpu_custom_call", output_to_operand_aliasing={{0}: (7, {})} | custom-call | flops 1 | bytes 1 | tf_op jit(solution)/shard_map/input/pallas_call | solution.py:720
  221.4 1.0 collective-permute-done.30
  223.2 1.7 collective-permute-start.31
  225.5 1.2 collective-permute-start.33
  226.7 2.3 collective-permute-done.36
  229.1 1.4 collective-permute-start.41
  232.0 1.4 collective-permute-start.37
  233.5 2.2 collective-permute-start.38
  236.5 2.9 %collective-permute-done.41 = bf16[24,1920]{1,0:T(8,128)(2,1)S(1)} collective-permute-done((bf16[24,1920]{1,0:T(8,128)(2,1)S(1)}, bf16[24,1920]{1,0:T(8,128)(2,1)S(1)}, u32[]{:S(2)}, u32[]{:S(2)}) %collective-permute-start.41) | collective-permute-done | bytes 92192 | tf_op jit(solution)/shard_map/ppermute | solution.py:741
  (150 shorter events, 29.8 us)
Async XLA Ops:
  3.8 10.7 %collective-permute-start = (bf16[24,1920]{1,0:T(8,128)(2,1)S(1)}, bf16[24,1920]{1,0:T(8,128)(2,1)S(1)}, u32[]{:S(2)}, u32[]{:S(2)}) collective-permute-start(bf16[24,1920]{1,0:T(8,128)(2,1)S(1)} %pad_maximum_fusion.8), channel_id=1, source_target_pairs={{0,8},{1,9},{2,10},{3,11},{4,12},{5,13},{6,14},{7,15},{8,0},{9,1},... | collective-permute-start | bytes 276488 | tf_op jit(solution)/shard_map/ppermute | solution.py:741
  6.8 10.0 %collective-permute-start.1 = (bf16[24,1920]{1,0:T(8,128)(2,1)S(1)}, bf16[24,1920]{1,0:T(8,128)(2,1)S(1)}, u32[]{:S(2)}, u32[]{:S(2)}) collective-permute-start(bf16[24,1920]{1,0:T(8,128)(2,1)S(1)} %pad_maximum_fusion.8), channel_id=1, source_target_pairs={{0,16},{1,17},{2,18},{3,19},{4,20},{5,21},{6,22},{7,23},{8,24},{9,... | collective-permute-start | bytes 276488 | tf_op jit(solution)/shard_map/ppermute | solution.py:741
  9.4 7.4 %collective-permute-start.2 = (bf16[24,1920]{1,0:T(8,128)(2,1)S(1)}, bf16[24,1920]{1,0:T(8,128)(2,1)S(1)}, u32[]{:S(2)}, u32[]{:S(2)}) collective-permute-start(bf16[24,1920]{1,0:T(8,128)(2,1)S(1)} %pad_maximum_fusion.8), channel_id=1, source_target_pairs={{0,24},{1,25},{2,26},{3,27},{4,28},{5,29},{6,30},{7,31},{8,16},{9,... | collective-permute-start | bytes 276488 | tf_op jit(solution)/shard_map/ppermute | solution.py:741
  10.2 6.6 %collective-permute-start.3 = (bf16[2,16,768]{2,1,0:T(8,128)(2,1)S(1)}, bf16[2,16,768]{2,1,0:T(8,128)(2,1)S(1)}, u32[]{:S(2)}, u32[]{:S(2)}) collective-permute-start(bf16[2,16,768]{2,1,0:T(8,128)(2,1)S(1)} %slice.126), channel_id=1, source_target_pairs={{0,1},{1,2},{2,3},{4,5},{5,6},{6,7},{8,9},{9,10},{10,11},{12,13},{... | collective-permute-start | bytes 147464 | tf_op jit(solution)/shard_map/ppermute | solution.py:867
  16.8 8.3 %collective-permute-start.4 = (bf16[2,24,1536]{2,1,0:T(8,128)(2,1)S(1)}, bf16[2,24,1536]{2,1,0:T(8,128)(2,1)S(1)}, u32[]{:S(2)}, u32[]{:S(2)}) collective-permute-start(bf16[2,24,1536]{2,1,0:T(8,128)(2,1)S(1)} %pad_maximum_fusion.5), channel_id=1, source_target_pairs={{0,8},{1,9},{2,10},{3,11},{4,12},{5,13},{6,14},{7,15},{8,0},{9,1},... | collective-permute-start | bytes 442376 | tf_op jit(solution)/shard_map/ppermute | solution.py:741
  18.5 14.0 %collective-permute-start.5 = (bf16[2,24,1536]{2,1,0:T(8,128)(2,1)S(1)}, bf16[2,24,1536]{2,1,0:T(8,128)(2,1)S(1)}, u32[]{:S(2)}, u32[]{:S(2)}) collective-permute-start(bf16[2,24,1536]{2,1,0:T(8,128)(2,1)S(1)} %pad_maximum_fusion.5), channel_id=1, source_target_pairs={{0,16},{1,17},{2,18},{3,19},{4,20},{5,21},{6,22},{7,23},{8,24},{9,... | collective-permute-start | bytes 442376 | tf_op jit(solution)/shard_map/ppermute | solution.py:741
  19.9 12.5 %collective-permute-start.6 = (bf16[2,24,1536]{2,1,0:T(8,128)(2,1)S(1)}, bf16[2,24,1536]{2,1,0:T(8,128)(2,1)S(1)}, u32[]{:S(2)}, u32[]{:S(2)}) collective-permute-start(bf16[2,24,1536]{2,1,0:T(8,128)(2,1)S(1)} %pad_maximum_fusion.5), channel_id=1, source_target_pairs={{0,24},{1,25},{2,26},{3,27},{4,28},{5,29},{6,30},{7,31},{8,16},{9,... | collective-permute-start | bytes 442376 | tf_op jit(solution)/shard_map/ppermute | solution.py:741
  21.3 11.5 %collective-permute-start.7 = (bf16[4,24,1920]{2,1,0:T(8,128)(2,1)S(1)}, bf16[4,24,1920]{2,1,0:T(8,128)(2,1)S(1)}, u32[]{:S(2)}, u32[]{:S(2)}) collective-permute-start(bf16[4,24,1920]{2,1,0:T(8,128)(2,1)S(1)} %pad_maximum_fusion.3), channel_id=1, source_target_pairs={{0,2},{1,3},{2,0},{3,1},{4,6},{5,7},{6,4},{7,5},{8,10},{9,11},{10,... | collective-permute-start | bytes 1105928 | tf_op jit(solution)/shard_map/ppermute | solution.py:741
  22.8 10.0 %collective-permute-start.8 = (bf16[4,24,1920]{2,1,0:T(8,128)(2,1)S(1)}, bf16[4,24,1920]{2,1,0:T(8,128)(2,1)S(1)}, u32[]{:S(2)}, u32[]{:S(2)}) collective-permute-start(bf16[4,24,1920]{2,1,0:T(8,128)(2,1)S(1)} %pad_maximum_fusion.3), channel_id=1, source_target_pairs={{0,4},{1,5},{2,6},{3,7},{4,0},{5,1},{6,2},{7,3},{8,12},{9,13},{10,... | collective-permute-start | bytes 1105928 | tf_op jit(solution)/shard_map/ppermute | solution.py:741
  25.1 14.9 %collective-permute-start.9 = (bf16[4,24,1920]{2,1,0:T(8,128)(2,1)S(1)}, bf16[4,24,1920]{2,1,0:T(8,128)(2,1)S(1)}, u32[]{:S(2)}, u32[]{:S(2)}) collective-permute-start(bf16[4,24,1920]{2,1,0:T(8,128)(2,1)S(1)} %pad_maximum_fusion.3), channel_id=1, source_target_pairs={{0,6},{1,7},{2,4},{3,5},{4,2},{5,3},{6,0},{7,1},{8,14},{9,15},{10,... | collective-permute-start | bytes 1105928 | tf_op jit(solution)/shard_map/ppermute | solution.py:741
  40.2 6.4 %collective-permute-start.10 = (bf16[4,4,24,1920]{3,2,1,0:T(8,128)(2,1)S(1)}, bf16[4,4,24,1920]{3,2,1,0:T(8,128)(2,1)}, u32[]{:S(2)}, u32[]{:S(2)}) collective-permute-start(bf16[4,4,24,1920]{3,2,1,0:T(8,128)(2,1)S(1)} %pad_maximum_fusion.1), channel_id=1, source_target_pairs={{0,1},{1,0},{2,3},{3,2},{4,5},{5,4},{6,7},{7,6},{8,9},{9,8},{10,11... | collective-permute-start | bytes 4423688 | tf_op jit(solution)/shard_map/ppermute | solution.py:741
  41.2 25.2 %collective-permute-start.11 = (bf16[4,2,24,1536]{3,2,1,0:T(8,128)(2,1)S(1)}, bf16[4,2,24,1536]{3,2,1,0:T(8,128)(2,1)S(1)}, u32[]{:S(2)}, u32[]{:S(2)}) collective-permute-start(bf16[4,2,24,1536]{3,2,1,0:T(8,128)(2,1)S(1)} %pad_maximum_fusion.2), channel_id=1, source_target_pairs={{0,2},{1,3},{2,0},{3,1},{4,6},{5,7},{6,4},{7,5},{8,10},{9,11},{10,... | collective-permute-start | bytes 1769480 | tf_op jit(solution)/shard_map/ppermute | solution.py:741
  42.1 28.0 %collective-permute-start.12 = (bf16[4,2,24,1536]{3,2,1,0:T(8,128)(2,1)S(1)}, bf16[4,2,24,1536]{3,2,1,0:T(8,128)(2,1)S(1)}, u32[]{:S(2)}, u32[]{:S(2)}) collective-permute-start(bf16[4,2,24,1536]{3,2,1,0:T(8,128)(2,1)S(1)} %pad_maximum_fusion.2), channel_id=1, source_target_pairs={{0,4},{1,5},{2,6},{3,7},{4,0},{5,1},{6,2},{7,3},{8,12},{9,13},{10,... | collective-permute-start | bytes 1769480 | tf_op jit(solution)/shard_map/ppermute | solution.py:741
  43.6 26.5 %collective-permute-start.13 = (bf16[4,2,24,1536]{3,2,1,0:T(8,128)(2,1)S(1)}, bf16[4,2,24,1536]{3,2,1,0:T(8,128)(2,1)S(1)}, u32[]{:S(2)}, u32[]{:S(2)}) collective-permute-start(bf16[4,2,24,1536]{3,2,1,0:T(8,128)(2,1)S(1)} %pad_maximum_fusion.2), channel_id=1, source_target_pairs={{0,6},{1,7},{2,4},{3,5},{4,2},{5,3},{6,0},{7,1},{8,14},{9,15},{10,... | collective-permute-start | bytes 1769480 | tf_op jit(solution)/shard_map/ppermute | solution.py:741
  70.4 11.6 %collective-permute-start.16 = (bf16[4,4,2,24,1536]{4,3,2,1,0:T(8,128)(2,1)S(1)}, bf16[4,4,2,24,1536]{4,3,2,1,0:T(8,128)(2,1)}, u32[]{:S(2)}, u32[]{:S(2)}) collective-permute-start(bf16[4,4,2,24,1536]{4,3,2,1,0:T(8,128)(2,1)S(1)} %pad_maximum_fusion), channel_id=1, source_target_pairs={{0,1},{1,0},{2,3},{3,2},{4,5},{5,4},{6,7},{7,6},{8,9},{9,8},{10,11... | collective-permute-start | bytes 7077896 | tf_op jit(solution)/shard_map/ppermute | solution.py:741
  71.2 9.8 %collective-permute-start.14 = (bf16[2,128,1536]{2,1,0:T(8,128)(2,1)S(1)}, bf16[2,128,1536]{2,1,0:T(8,128)(2,1)S(1)}, u32[]{:S(2)}, u32[]{:S(2)}) collective-permute-start(bf16[2,128,1536]{2,1,0:T(8,128)(2,1)S(1)} %copy-done.20), channel_id=1, source_target_pairs={{0,1},{4,5},{8,9},{12,13},{16,17},{20,21},{24,25},{28,29}} | collective-permute-start | bytes 2359304 | tf_op jit(solution)/shard_map/ppermute | solution.py:819
  81.2 11.1 %collective-permute-start.15 = (bf16[2,128,1536]{2,1,0:T(8,128)(2,1)S(1)}, bf16[2,128,1536]{2,1,0:T(8,128)(2,1)S(1)}, u32[]{:S(2)}, u32[]{:S(2)}) collective-permute-start(bf16[2,128,1536]{2,1,0:T(8,128)(2,1)S(1)} %fusion.1), channel_id=1, source_target_pairs={{1,2},{5,6},{9,10},{13,14},{17,18},{21,22},{25,26},{29,30}} | collective-permute-start | bytes 2359304 | tf_op jit(solution)/shard_map/ppermute | solution.py:819
  93.2 0.9 collective-permute-start.17
  116.0 14.4 %collective-permute-start.19 = (bf16[2,128,1536]{2,1,0:T(8,128)(2,1)}, bf16[2,128,1536]{2,1,0:T(8,128)(2,1)S(1)}, u32[]{:S(2)}, u32[]{:S(2)}) collective-permute-start(bf16[2,128,1536]{2,1,0:T(8,128)(2,1)} %get-tuple-element.144), channel_id=1, source_target_pairs={{3,2},{7,6},{11,10},{15,14},{19,18},{23,22},{27,26},{31,30}} | collective-permute-start | bytes 2359304 | tf_op jit(solution)/shard_map/ppermute | solution.py:819
  116.7 13.7 %copy-start.14 = (f32[2,1,1536]{2,1,0:T(1,128)S(1)}, f32[2,1,1536]{2,1,0:T(1,128)}, u32[]{:S(2)}) copy-start(f32[2,1,1536]{2,1,0:T(1,128)} %get-tuple-element.161) | copy-start | bytes 36868
  116.7 13.7 %copy-start.3 = (f32[2,128,1536]{2,1,0:T(8,128)S(1)}, f32[2,128,1536]{2,1,0:T(8,128)}, u32[]{:S(2)}) copy-start(f32[2,128,1536]{2,1,0:T(8,128)} %get-tuple-element.162) | copy-start | bytes 4718596
  128.7 21.2 %collective-permute-start.18 = (bf16[16,2,24,1536]{3,2,1,0:T(8,128)(2,1)}, bf16[16,2,24,1536]{3,2,1,0:T(8,128)(2,1)}, u32[]{:S(2)}, u32[]{:S(2)}) collective-permute-start(bf16[16,2,24,1536]{3,2,1,0:T(8,128)(2,1)} %get-tuple-element.143), channel_id=1, source_target_pairs={{0,1},{1,0},{2,3},{3,2},{4,5},{5,4},{6,7},{7,6},{8,9},{9,8},{10,11... | collective-permute-start | bytes 7077896 | tf_op jit(solution)/shard_map/ppermute | solution.py:741
  130.4 17.0 %copy-start = (bf16[2,128,1536]{2,1,0:T(8,128)(2,1)}, bf16[2,128,1536]{2,1,0:T(8,128)(2,1)S(1)}, u32[]{:S(2)}) copy-start(bf16[2,128,1536]{2,1,0:T(8,128)(2,1)S(1)} %collective-permute-done.19.refs_0_) | copy-start | bytes 2359300
  130.6 16.7 %collective-permute-start.23 = (bf16[2,128,1536]{2,1,0:T(8,128)(2,1)S(1)}, bf16[2,128,1536]{2,1,0:T(8,128)(2,1)S(1)}, u32[]{:S(2)}, u32[]{:S(2)}) collective-permute-start(bf16[2,128,1536]{2,1,0:T(8,128)(2,1)S(1)} %fusion.6), channel_id=1, source_target_pairs={{2,1},{6,5},{10,9},{14,13},{18,17},{22,21},{26,25},{30,29}} | collective-permute-start | bytes 2359304 | tf_op jit(solution)/shard_map/ppermute | solution.py:819
  148.2 11.9 %collective-permute-start.24 = (bf16[2,128,1536]{2,1,0:T(8,128)(2,1)S(1)}, bf16[2,128,1536]{2,1,0:T(8,128)(2,1)S(1)}, u32[]{:S(2)}, u32[]{:S(2)}) collective-permute-start(bf16[2,128,1536]{2,1,0:T(8,128)(2,1)S(1)} %fusion.9), channel_id=1, source_target_pairs={{1,0},{5,4},{9,8},{13,12},{17,16},{21,20},{25,24},{29,28}} | collective-permute-start | bytes 2359304 | tf_op jit(solution)/shard_map/ppermute | solution.py:819
  153.7 27.2 %collective-permute-start.20 = (bf16[4,2,24,1536]{3,2,1,0:T(8,128)(2,1)}, bf16[4,2,24,1536]{3,2,1,0:T(8,128)(2,1)S(1)}, u32[]{:S(2)}, u32[]{:S(2)}) collective-permute-start(bf16[4,2,24,1536]{3,2,1,0:T(8,128)(2,1)} %get-tuple-element.213), channel_id=1, source_target_pairs={{0,2},{1,3},{2,0},{3,1},{4,6},{5,7},{6,4},{7,5},{8,10},{9,11},{10,... | collective-permute-start | bytes 1769480 | tf_op jit(solution)/shard_map/ppermute | solution.py:741
  158.7 27.2 %collective-permute-start.21 = (bf16[4,2,24,1536]{3,2,1,0:T(8,128)(2,1)}, bf16[4,2,24,1536]{3,2,1,0:T(8,128)(2,1)S(1)}, u32[]{:S(2)}, u32[]{:S(2)}) collective-permute-start(bf16[4,2,24,1536]{3,2,1,0:T(8,128)(2,1)} %get-tuple-element.212), channel_id=1, source_target_pairs={{0,4},{1,5},{2,6},{3,7},{4,0},{5,1},{6,2},{7,3},{8,12},{9,13},{10,... | collective-permute-start | bytes 1769480 | tf_op jit(solution)/shard_map/ppermute | solution.py:741
  159.3 26.6 %collective-permute-start.22 = (bf16[4,2,24,1536]{3,2,1,0:T(8,128)(2,1)S(1)}, bf16[4,2,24,1536]{3,2,1,0:T(8,128)(2,1)S(1)}, u32[]{:S(2)}, u32[]{:S(2)}) collective-permute-start(bf16[4,2,24,1536]{3,2,1,0:T(8,128)(2,1)S(1)} %get-tuple-element.211), channel_id=1, source_target_pairs={{0,6},{1,7},{2,4},{3,5},{4,2},{5,3},{6,0},{7,1},{8,14},{9,15},{10,... | collective-permute-start | bytes 1769480 | tf_op jit(solution)/shard_map/ppermute | solution.py:741
  179.6 6.6 %collective-permute-start.25 = (bf16[2,8,1920]{2,1,0:T(8,128)(2,1)}, bf16[2,8,1920]{2,1,0:T(8,128)(2,1)}, u32[]{:S(2)}, u32[]{:S(2)}) collective-permute-start(bf16[2,8,1920]{2,1,0:T(8,128)(2,1)} %get-tuple-element.177), channel_id=1, source_target_pairs={{1,0},{2,1},{3,2},{5,4},{6,5},{7,6},{9,8},{10,9},{11,10},{13,12},{... | collective-permute-start | bytes 184328 | tf_op jit(solution)/shard_map/ppermute | solution.py:1206
  196.9 6.4 %collective-permute-start.26 = (bf16[16,24,1920]{2,1,0:T(8,128)(2,1)}, bf16[16,24,1920]{2,1,0:T(8,128)(2,1)S(1)}, u32[]{:S(2)}, u32[]{:S(2)}) collective-permute-start(bf16[16,24,1920]{2,1,0:T(8,128)(2,1)} %get-tuple-element.183), channel_id=1, source_target_pairs={{0,1},{1,0},{2,3},{3,2},{4,5},{5,4},{6,7},{7,6},{8,9},{9,8},{10,11... | collective-permute-start | bytes 4423688 | tf_op jit(solution)/shard_map/ppermute | solution.py:741
  197.0 10.4 %collective-permute-start.27 = (f32[96,128]{1,0:T(8,128)}, f32[96,128]{1,0:T(8,128)S(1)}, u32[]{:S(2)}, u32[]{:S(2)}) collective-permute-start(f32[96,128]{1,0:T(8,128)} %get-tuple-element.189), channel_id=1, source_target_pairs={{0,1},{1,0},{2,3},{3,2},{4,5},{5,4},{6,7},{7,6},{8,9},{9,8},{10,11... | collective-permute-start | bytes 147464 | tf_op jit(solution)/shard_map/ppermute | solution.py:741
  203.8 17.3 %collective-permute-start.28 = (bf16[4,24,1920]{2,1,0:T(8,128)(2,1)S(1)}, bf16[4,24,1920]{2,1,0:T(8,128)(2,1)S(1)}, u32[]{:S(2)}, u32[]{:S(2)}) collective-permute-start(bf16[4,24,1920]{2,1,0:T(8,128)(2,1)S(1)} %get-tuple-element.216), channel_id=1, source_target_pairs={{0,2},{1,3},{2,0},{3,1},{4,6},{5,7},{6,4},{7,5},{8,10},{9,11},{10,... | collective-permute-start | bytes 1105928 | tf_op jit(solution)/shard_map/ppermute | solution.py:741
  204.2 17.2 %collective-permute-start.29 = (bf16[4,24,1920]{2,1,0:T(8,128)(2,1)S(1)}, bf16[4,24,1920]{2,1,0:T(8,128)(2,1)S(1)}, u32[]{:S(2)}, u32[]{:S(2)}) collective-permute-start(bf16[4,24,1920]{2,1,0:T(8,128)(2,1)S(1)} %get-tuple-element.215), channel_id=1, source_target_pairs={{0,4},{1,5},{2,6},{3,7},{4,0},{5,1},{6,2},{7,3},{8,12},{9,13},{10,... | collective-permute-start | bytes 1105928 | tf_op jit(solution)/shard_map/ppermute | solution.py:741
  205.6 16.8 %collective-permute-start.30 = (bf16[4,24,1920]{2,1,0:T(8,128)(2,1)S(1)}, bf16[4,24,1920]{2,1,0:T(8,128)(2,1)S(1)}, u32[]{:S(2)}, u32[]{:S(2)}) collective-permute-start(bf16[4,24,1920]{2,1,0:T(8,128)(2,1)S(1)} %get-tuple-element.214), channel_id=1, source_target_pairs={{0,6},{1,7},{2,4},{3,5},{4,2},{5,3},{6,0},{7,1},{8,14},{9,15},{10,... | collective-permute-start | bytes 1105928 | tf_op jit(solution)/shard_map/ppermute | solution.py:741
  207.4 17.5 %collective-permute-start.34 = (bf16[2,24,1536]{2,1,0:T(8,128)(2,1)S(1)}, bf16[2,24,1536]{2,1,0:T(8,128)(2,1)S(1)}, u32[]{:S(2)}, u32[]{:S(2)}) collective-permute-start(bf16[2,24,1536]{2,1,0:T(8,128)(2,1)S(1)} %get-tuple-element.196), channel_id=1, source_target_pairs={{0,8},{1,9},{2,10},{3,11},{4,12},{5,13},{6,14},{7,15},{8,0},{9,1},... | collective-permute-start | bytes 442376 | tf_op jit(solution)/shard_map/ppermute | solution.py:741
  208.0 17.5 %collective-permute-start.35 = (bf16[2,24,1536]{2,1,0:T(8,128)(2,1)S(1)}, bf16[2,24,1536]{2,1,0:T(8,128)(2,1)S(1)}, u32[]{:S(2)}, u32[]{:S(2)}) collective-permute-start(bf16[2,24,1536]{2,1,0:T(8,128)(2,1)S(1)} %get-tuple-element.197), channel_id=1, source_target_pairs={{0,16},{1,17},{2,18},{3,19},{4,20},{5,21},{6,22},{7,23},{8,24},{9,... | collective-permute-start | bytes 442376 | tf_op jit(solution)/shard_map/ppermute | solution.py:741
  221.0 7.9 %collective-permute-start.36 = (bf16[2,24,1536]{2,1,0:T(8,128)(2,1)S(1)}, bf16[2,24,1536]{2,1,0:T(8,128)(2,1)S(1)}, u32[]{:S(2)}, u32[]{:S(2)}) collective-permute-start(bf16[2,24,1536]{2,1,0:T(8,128)(2,1)S(1)} %get-tuple-element.198), channel_id=1, source_target_pairs={{0,24},{1,25},{2,26},{3,27},{4,28},{5,29},{6,30},{7,31},{8,16},{9,... | collective-permute-start | bytes 442376 | tf_op jit(solution)/shard_map/ppermute | solution.py:741
  222.6 13.1 %collective-permute-start.40 = (bf16[24,1920]{1,0:T(8,128)(2,1)S(1)}, bf16[24,1920]{1,0:T(8,128)(2,1)S(1)}, u32[]{:S(2)}, u32[]{:S(2)}) collective-permute-start(bf16[24,1920]{1,0:T(8,128)(2,1)S(1)} %get-tuple-element.222), channel_id=1, source_target_pairs={{0,8},{1,9},{2,10},{3,11},{4,12},{5,13},{6,14},{7,15},{8,0},{9,1},... | collective-permute-start | bytes 276488 | tf_op jit(solution)/shard_map/ppermute | solution.py:741
  223.2 8.0 %collective-permute-start.31 = (f32[96,128]{1,0:T(8,128)S(1)}, f32[96,128]{1,0:T(8,128)S(1)}, u32[]{:S(2)}, u32[]{:S(2)}) collective-permute-start(f32[96,128]{1,0:T(8,128)S(1)} %add.114), channel_id=1, source_target_pairs={{0,2},{1,3},{2,0},{3,1},{4,6},{5,7},{6,4},{7,5},{8,10},{9,11},{10,... | collective-permute-start | bytes 147464 | tf_op jit(solution)/shard_map/ppermute | solution.py:741
  224.9 7.1 %collective-permute-start.32 = (f32[96,128]{1,0:T(8,128)S(1)}, f32[96,128]{1,0:T(8,128)S(1)}, u32[]{:S(2)}, u32[]{:S(2)}) collective-permute-start(f32[96,128]{1,0:T(8,128)S(1)} %add.114), channel_id=1, source_target_pairs={{0,4},{1,5},{2,6},{3,7},{4,0},{5,1},{6,2},{7,3},{8,12},{9,13},{10,... | collective-permute-start | bytes 147464 | tf_op jit(solution)/shard_map/ppermute | solution.py:741
  225.5 6.5 %collective-permute-start.33 = (f32[96,128]{1,0:T(8,128)S(1)}, f32[96,128]{1,0:T(8,128)S(1)}, u32[]{:S(2)}, u32[]{:S(2)}) collective-permute-start(f32[96,128]{1,0:T(8,128)S(1)} %add.114), channel_id=1, source_target_pairs={{0,6},{1,7},{2,4},{3,5},{4,2},{5,3},{6,0},{7,1},{8,14},{9,15},{10,... | collective-permute-start | bytes 147464 | tf_op jit(solution)/shard_map/ppermute | solution.py:741
  229.1 14.4 %copy-start.15 = (f32[48]{0:T(128)S(1)}, f32[48]{0:T(128)}, u32[]{:S(2)}) copy-start(f32[48]{0:T(128)} %param.26) | copy-start | bytes 580
  229.1 15.0 %copy-start.19 = (f32[24]{0:T(128)S(1)}, f32[24]{0:T(128)}, u32[]{:S(2)}) copy-start(f32[24]{0:T(128)} %param.19) | copy-start | bytes 292
  229.1 10.2 %collective-permute-start.41 = (bf16[24,1920]{1,0:T(8,128)(2,1)S(1)}, bf16[24,1920]{1,0:T(8,128)(2,1)S(1)}, u32[]{:S(2)}, u32[]{:S(2)}) collective-permute-start(bf16[24,1920]{1,0:T(8,128)(2,1)S(1)} %get-tuple-element.220), channel_id=1, source_target_pairs={{0,16},{1,17},{2,18},{3,19},{4,20},{5,21},{6,22},{7,23},{8,24},{9,... | collective-permute-start | bytes 276488 | tf_op jit(solution)/shard_map/ppermute | solution.py:741
  231.2 8.2 %collective-permute-start.42 = (bf16[24,1920]{1,0:T(8,128)(2,1)S(1)}, bf16[24,1920]{1,0:T(8,128)(2,1)S(1)}, u32[]{:S(2)}, u32[]{:S(2)}) collective-permute-start(bf16[24,1920]{1,0:T(8,128)(2,1)S(1)} %get-tuple-element.221), channel_id=1, source_target_pairs={{0,24},{1,25},{2,26},{3,27},{4,28},{5,29},{6,30},{7,31},{8,16},{9,... | collective-permute-start | bytes 276488 | tf_op jit(solution)/shard_map/ppermute | solution.py:741
  232.0 8.1 %collective-permute-start.37 = (f32[96,128]{1,0:T(8,128)S(1)}, f32[96,128]{1,0:T(8,128)S(1)}, u32[]{:S(2)}, u32[]{:S(2)}) collective-permute-start(f32[96,128]{1,0:T(8,128)S(1)} %add_add_fusion.2), channel_id=1, source_target_pairs={{0,8},{1,9},{2,10},{3,11},{4,12},{5,13},{6,14},{7,15},{8,0},{9,1},... | collective-permute-start | bytes 147464 | tf_op jit(solution)/shard_map/ppermute | solution.py:741
  233.5 7.5 %collective-permute-start.38 = (f32[96,128]{1,0:T(8,128)S(1)}, f32[96,128]{1,0:T(8,128)S(1)}, u32[]{:S(2)}, u32[]{:S(2)}) collective-permute-start(f32[96,128]{1,0:T(8,128)S(1)} %add_add_fusion.2), channel_id=1, source_target_pairs={{0,16},{1,17},{2,18},{3,19},{4,20},{5,21},{6,22},{7,23},{8,24},{9,... | collective-permute-start | bytes 147464 | tf_op jit(solution)/shard_map/ppermute | solution.py:741
  235.7 6.0 %collective-permute-start.39 = (f32[96,128]{1,0:T(8,128)S(1)}, f32[96,128]{1,0:T(8,128)S(1)}, u32[]{:S(2)}, u32[]{:S(2)}) collective-permute-start(f32[96,128]{1,0:T(8,128)S(1)} %add_add_fusion.2), channel_id=1, source_target_pairs={{0,24},{1,25},{2,26},{3,27},{4,28},{5,29},{6,30},{7,31},{8,16},{9,... | collective-permute-start | bytes 147464 | tf_op jit(solution)/shard_map/ppermute | solution.py:741
  (17 other events, 102.5 us)

commit v5 on v4

--- a/solution.py
+++ b/solution.py
@@ -31,8 +31,8 @@
     "project": 48,
     "gate": 48,
     "early_grad": 56,
-    "intra_back": 56,
-    "conv_back": 56,
+    "intra_back": 51,
+    "conv_back": 54,
     "late_grad": 56,
     "input": 56,
 }
@@ -983,7 +983,7 @@
             pltpu.VMEM((Q + RIM, width), low),
             pltpu.VMEM((N, DI), f32),
             pltpu.VMEM((8, DI), f32),
-            pltpu.VMEM((2, HL, HL), f32),
+            pltpu.VMEM((2, HL + 16, HL), f32),
             pltpu.VMEM((width, CW), low),
             pltpu.SemaphoreType.DMA,
             *[pltpu.VMEM((Q + RIM, HALF), f32)] * (CD // HALF),

time: 245 us -> 244 us (level)
    unnamed x46 -> x64, local copies, waits for them, and re-layouts: 3.73 us -> 5.21 us
  transfers between devices with their start and end apart: 43 -> 43, of which waited for: 12 -> 12; matrix products, arithmetic and copies ran while one was open for 6% -> 5% of each run, Pallas kernels for 41% -> 41%
where the time goes in v5:
time: 244 us; the launch traced here: 243 us
  Pallas kernels  131 us (54%)
  starting transfers between devices  53.8 us (22%)
  waiting for transfers between devices  33.5 us (14%)
  local copies, waits for them, and re-layouts  12.6 us (5%)
  other arithmetic  10.6 us (4%)
    pallas_call x10, Pallas kernels, call(): pl.pallas_call(kernel, grid=(grid,), in_specs=in_specs, out_specs=out_spe...  131 us
    ppermute x35, starting transfers between devices, swap(): return lax.ppermute(value, axes, [(i, i ^ mask) for i in range(PIECES)])  44.8 us
    ppermute x35, waiting for transfers between devices, swap(): return lax.ppermute(value, axes, [(i, i ^ mask) for i in range(PIECES)])  33.4 us
    ppermute x6, starting transfers between devices, relay(): arrived = lax.ppermute(value, 'seq', route)  6.48 us
    unnamed x64, local copies, waits for them, and re-layouts  5.21 us
  transfers between devices with their start and end apart: 43, of which 12 were waited for; matrix products, arithmetic and copies ran while one was open for 5% of the time, Pallas kernels for 41%

profile of v5, /device:TPU:0, one launch (start us, length us, event | category | flops | bytes accessed | tf_op | source)
XLA Modules:
  0.0 242.8 jit_solution(12073645581608998166)
XLA Ops:
  1.3 0.9 slice.223
  3.8 3.0 %collective-permute-start = (bf16[24,1920]{1,0:T(8,128)(2,1)S(1)}, bf16[24,1920]{1,0:T(8,128)(2,1)S(1)}, u32[]{:S(2)}, u32[]{:S(2)}) collective-permute-start(bf16[24,1920]{1,0:T(8,128)(2,1)S(1)} %pad_maximum_fusion.8), channel_id=1, source_target_pairs={{0,8},{1,9},{2,10},{3,11},{4,12},{5,13},{6,14},{7,15},{8,0},{9,1},... | collective-permute-start | bytes 276488 | tf_op jit(solution)/shard_map/ppermute | solution.py:741
  6.8 2.6 %collective-permute-start.1 = (bf16[24,1920]{1,0:T(8,128)(2,1)S(1)}, bf16[24,1920]{1,0:T(8,128)(2,1)S(1)}, u32[]{:S(2)}, u32[]{:S(2)}) collective-permute-start(bf16[24,1920]{1,0:T(8,128)(2,1)S(1)} %pad_maximum_fusion.8), channel_id=1, source_target_pairs={{0,16},{1,17},{2,18},{3,19},{4,20},{5,21},{6,22},{7,23},{8,24},{9,... | collective-permute-start | bytes 276488 | tf_op jit(solution)/shard_map/ppermute | solution.py:741
  10.2 1.3 collective-permute-start.3
  11.5 0.9 slice_bitcast_fusion.16
  12.4 0.9 fusion.13
  13.4 0.9 convert_element_type.137
  14.4 2.3 collective-permute-done.1
  16.8 1.6 collective-permute-start.4
  18.5 1.5 collective-permute-start.5
  19.9 1.3 collective-permute-start.6
  21.3 1.5 collective-permute-start.7
  22.8 1.5 collective-permute-start.8
  25.1 1.1 collective-permute-start.9
  26.2 6.2 %collective-permute-done.5 = bf16[2,24,1536]{2,1,0:T(8,128)(2,1)S(1)} collective-permute-done((bf16[2,24,1536]{2,1,0:T(8,128)(2,1)S(1)}, bf16[2,24,1536]{2,1,0:T(8,128)(2,1)S(1)}, u32[]{:S(2)}, u32[]{:S(2)}) %collective-permute-start.5) | collective-permute-done | bytes 147488 | tf_op jit(solution)/shard_map/ppermute | solution.py:741
  32.8 7.2 %collective-permute-done.9 = bf16[4,24,1920]{2,1,0:T(8,128)(2,1)S(1)} collective-permute-done((bf16[4,24,1920]{2,1,0:T(8,128)(2,1)S(1)}, bf16[4,24,1920]{2,1,0:T(8,128)(2,1)S(1)}, u32[]{:S(2)}, u32[]{:S(2)}) %collective-permute-start.9) | collective-permute-done | bytes 368672 | tf_op jit(solution)/shard_map/ppermute | solution.py:741
  42.1 1.5 collective-permute-start.12
  43.6 1.2 collective-permute-start.13
  46.6 19.8 %conv.1 = (bf16[1024,768]{1,0:T(8,128)(2,1)}, bf16[768,1024]{1,0:T(8,128)(2,1)}, bf16[4,272,1792]{2,1,0:T(8,128)(2,1)}, f32[1024,1792]{1,0:T(8,128)}, bf16[1024,...) custom-call(s32[5]{0:T(128)} %pad_add_fusion.scal.past.token, ...), custom_call_target="tpu_custom_call" | custom-call | flops 3019898880 | bytes 6066196 | tf_op jit(solution)/shard_map/conv/pallas_call | solution.py:720
  66.4 3.7 %collective-permute-done.12 = bf16[4,2,24,1536]{3,2,1,0:T(8,128)(2,1)S(1)} collective-permute-done((bf16[4,2,24,1536]{3,2,1,0:T(8,128)(2,1)S(1)}, bf16[4,2,24,1536]{3,2,1,0:T(8,128)(2,1)S(1)}, u32[]{:S(2)}, u32[]{:S(2)}) %collective-permute-start.12) | collective-permute-done | bytes 589856 | tf_op jit(solution)/shard_map/ppermute | solution.py:741
  71.2 1.7 collective-permute-start.14
  73.0 8.0 %intra.1 = f32[1024,1536]{1,0:T(8,128)} custom-call(bf16[1024,256]{1,0:T(8,128)(2,1)} %get-tuple-element.147.bc, bf16[1024,1536]{1,0:T(8,128)(2,1)} %get-tuple-element.120.xs, f32[1024,128]{1,0:T(8,128)} %get-tuple-element.115.cum, f32[4,24,256]{2,1,0:T(8,128)} %get-tuple-element.121.cumt), custom_call_target="tpu_custom_call" | custom-call | flops 1610612736 | bytes 4292608 | tf_op jit(solution)/shard_map/intra/pallas_call | solution.py:720
  82.0 10.3 %project.1 = (f32[1024,1536]{1,0:T(8,128)S(1)}, f32[1024,1536]{1,0:T(8,128)S(1)}, bf16[1024,768]{1,0:T(8,128)(2,1)}, bf16[768,1536]{1,0:T(8,128)(2,1)}, bf16[1536,768]{1,0:T(8,128)(2,1)}) custom-call(s32[5]{0:T(128)} %pad_add_fusion.scal.past.token, bf16[1024,768]{1,0:T(8,128)(2,1)} %get-tuple-element.130.nrm, bf16[1024,768]{1,0:T(8,128)(2,1)} %bitcast.91, ...), custom_call_target="tpu_custom_call" | custom-call | flops 4831838208 | bytes 7864340 | tf_op jit(solution)/shard_map/project/pallas_call | solution.py:720
  95.0 20.9 %gate.1 = (bf16[1024,768]{1,0:T(8,128)(2,1)}, bf16[1024,1536]{1,0:T(8,128)(2,1)}, bf16[1024,1536]{1,0:T(8,128)(2,1)}, bf16[1024,1536]{1,0:T(8,128)(2,1)}, bf16[1...) custom-call(s32[5]{0:T(128)} %pad_add_fusion.scal.past.token, ...), custom_call_target="tpu_custom_call" | custom-call | flops 4831838208 | bytes 33542164 | tf_op jit(solution)/shard_map/gate/pallas_call | solution.py:720
  116.7 12.0 %early_grad.1 = (bf16[16,2,24,1536]{3,2,1,0:T(8,128)(2,1)}, bf16[16,2,24,1536]{3,2,1,0:T(8,128)(2,1)}, f32[768,128]{1,0:T(8,128)}, f32[1536,128]{1,0:T(8,128)}) custom-call(s32[5]{0:T(128)} %pad_add_fusion.scal.past.token, bf16[768,1024]{1,0:T(8,128)(2,1)} %get-tuple-element.137.nrmt, bf16[1024,1536]{1,0:T(8,128)(2,1)} %get-tuple-element.138.dz, ...), custom_call_target="tpu_custom_call" | custom-call | flops 7247757312 | bytes 14155796 | tf_op jit(solution)/shard_map/early_grad/pallas_call | solution.py:720
  128.7 1.6 collective-permute-start.18
  132.2 15.1 %intra_back.1 = (f32[1024,1536]{1,0:T(8,128)}, f32[1024,256]{1,0:T(8,128)}, f32[1024,128]{1,0:T(8,128)S(1)}) custom-call(bf16[1024,256]{1,0:T(8,128)(2,1)S(1)} %copy-done, bf16[1024,1536]{1,0:T(8,128)(2,1)} %get-tuple-element.120.xs, bf16[1024,1536]{1,0:T(8,128)(2,1)} %get-tuple-element.122.xh, bf16[1024,1536]{1,0:T(8,128)(2,1)} %get-tuple-element.148.dy, ...), custom_call_target="tpu_custom_call" | custom-call | flops 3221225472 | bytes 11898880 | tf_op jit(solution)/shard_map/intra_back/pallas_call | solution.py:720
  148.4 1.6 collective-permute-start.24
  150.1 0.9 convert_add_fusion
  151.2 4.4 %collective-permute-start.20 = (bf16[4,2,24,1536]{3,2,1,0:T(8,128)(2,1)S(1)}, bf16[4,2,24,1536]{3,2,1,0:T(8,128)(2,1)S(1)}, u32[]{:S(2)}, u32[]{:S(2)}) collective-permute-start(bf16[4,2,24,1536]{3,2,1,0:T(8,128)(2,1)S(1)} %get-tuple-element.213), channel_id=1, source_target_pairs={{0,2},{1,3},{2,0},{3,1},{4,6},{5,7},{6,4},{7,5},{8,10},{9,11},{10,... | collective-permute-start | bytes 1769480 | tf_op jit(solution)/shard_map/ppermute | solution.py:741
  156.2 0.9 collective-permute-start.22
  158.0 18.6 %conv_back.1 = (bf16[1024,1920]{1,0:T(8,128)(2,1)}, f32[40,1792]{1,0:T(8,128)}, f32[16,128]{1,0:T(8,128)}, bf16[2,8,1920]{2,1,0:T(8,128)(2,1)}, f32[2,16,1920]{2,1,0:T(8,128)}) custom-call(s32[5]{0:T(128)} %pad_add_fusion.scal.past.token, f32[4,128,1536]{2,1,0:T(8,128)} %get-tuple-element.152.dloc, f32[4,8,1536]{2,1,0:T(8,128)} %get-tuple-element.153.suf, ...), custom_call_target="tpu_custom_call" | custom-call | flops 1207959552 | bytes 39284756 | tf_op jit(solution)/shard_map/conv_back/pallas_call | solution.py:720
  176.6 1.3 collective-permute-start.25
  178.0 5.2 %collective-permute-done.21 = bf16[4,2,24,1536]{3,2,1,0:T(8,128)(2,1)S(1)} collective-permute-done((bf16[4,2,24,1536]{3,2,1,0:T(8,128)(2,1)S(1)}, bf16[4,2,24,1536]{3,2,1,0:T(8,128)(2,1)S(1)}, u32[]{:S(2)}, u32[]{:S(2)}) %collective-permute-start.21) | collective-permute-done | bytes 589856 | tf_op jit(solution)/shard_map/ppermute | solution.py:741
  184.2 10.8 %late_grad.1 = (bf16[16,24,1920]{2,1,0:T(8,128)(2,1)}, bf16[16,24,1920]{2,1,0:T(8,128)(2,1)}, bf16[1024,1920]{1,0:T(8,128)(2,1)}, f32[96,128]{1,0:T(8,128)}) custom-call(s32[5]{0:T(128)} %pad_add_fusion.scal.past.token, bf16[768,1024]{1,0:T(8,128)(2,1)} %get-tuple-element.137.nrmt, bf16[1024,1920]{1,0:T(8,128)(2,1)} %get-tuple-element.173.dcv, ...), custom_call_target="tpu_custom_call" | custom-call | flops 3019898880 | bytes 10682388 | tf_op jit(solution)/shard_map/late_grad/pallas_call | solution.py:720
  195.6 5.8 %input.2 = (bf16[1024,768]{1,0:T(8,128)(2,1)}, f32[8,128]{1,0:T(8,128)}) custom-call(bf16[1024,1920]{1,0:T(8,128)(2,1)} %get-tuple-element.180.dcv, bf16[1024,1536]{1,0:T(8,128)(2,1)} %get-tuple-element.138.dz, bf16[768,1920]{1,0:T(8,128)(2,1)} %get-tuple-element.174.wc, bf16[768,1536]{1,0:T(8,128)(2,1)} %get-tuple-element.141.wzc.wz, ...), custom_call_target="tpu_custom_call" | custom-call | flops 1 | bytes 1 | tf_op jit(solution)/shard_map/input/pallas_call | solution.py:720
  202.2 1.4 collective-permute-start.29
  203.6 1.8 collective-permute-start.30
  206.1 3.6 %collective-permute-start.35 = (bf16[2,24,1536]{2,1,0:T(8,128)(2,1)S(1)}, bf16[2,24,1536]{2,1,0:T(8,128)(2,1)S(1)}, u32[]{:S(2)}, u32[]{:S(2)}) collective-permute-start(bf16[2,24,1536]{2,1,0:T(8,128)(2,1)S(1)} %get-tuple-element.197), channel_id=1, source_target_pairs={{0,16},{1,17},{2,18},{3,19},{4,20},{5,21},{6,22},{7,23},{8,24},{9,... | collective-permute-start | bytes 442376 | tf_op jit(solution)/shard_map/ppermute | solution.py:741
  209.6 9.5 %input.3 = (bf16[1024,768]{1,0:T(8,128)(2,1)}, f32[8,128]{1,0:T(8,128)}) custom-call(bf16[1024,1920]{1,0:T(8,128)(2,1)} %get-tuple-element.180.dcv, bf16[1024,1536]{1,0:T(8,128)(2,1)} %get-tuple-element.138.dz, bf16[768,1920]{1,0:T(8,128)(2,1)} %get-tuple-element.174.wc, ...), custom_call_target="tpu_custom_call", output_to_operand_aliasing={{0}: (7, {})} | custom-call | flops 1 | bytes 1 | tf_op jit(solution)/shard_map/input/pallas_call | solution.py:720
  219.4 1.0 collective-permute-done.30
  221.3 1.7 collective-permute-start.31
  223.6 1.2 collective-permute-start.33
  224.8 2.3 collective-permute-done.36
  227.2 1.4 collective-permute-start.41
  230.1 1.5 collective-permute-start.37
  231.5 2.2 collective-permute-start.38
  234.5 2.9 %collective-permute-done.41 = bf16[24,1920]{1,0:T(8,128)(2,1)S(1)} collective-permute-done((bf16[24,1920]{1,0:T(8,128)(2,1)S(1)}, bf16[24,1920]{1,0:T(8,128)(2,1)S(1)}, u32[]{:S(2)}, u32[]{:S(2)}) %collective-permute-start.41) | collective-permute-done | bytes 92192 | tf_op jit(solution)/shard_map/ppermute | solution.py:741
  (168 shorter events, 30.7 us)
Async XLA Ops:
  3.8 10.7 %collective-permute-start = (bf16[24,1920]{1,0:T(8,128)(2,1)S(1)}, bf16[24,1920]{1,0:T(8,128)(2,1)S(1)}, u32[]{:S(2)}, u32[]{:S(2)}) collective-permute-start(bf16[24,1920]{1,0:T(8,128)(2,1)S(1)} %pad_maximum_fusion.8), channel_id=1, source_target_pairs={{0,8},{1,9},{2,10},{3,11},{4,12},{5,13},{6,14},{7,15},{8,0},{9,1},... | collective-permute-start | bytes 276488 | tf_op jit(solution)/shard_map/ppermute | solution.py:741
  6.8 10.0 %collective-permute-start.1 = (bf16[24,1920]{1,0:T(8,128)(2,1)S(1)}, bf16[24,1920]{1,0:T(8,128)(2,1)S(1)}, u32[]{:S(2)}, u32[]{:S(2)}) collective-permute-start(bf16[24,1920]{1,0:T(8,128)(2,1)S(1)} %pad_maximum_fusion.8), channel_id=1, source_target_pairs={{0,16},{1,17},{2,18},{3,19},{4,20},{5,21},{6,22},{7,23},{8,24},{9,... | collective-permute-start | bytes 276488 | tf_op jit(solution)/shard_map/ppermute | solution.py:741
  9.4 7.4 %collective-permute-start.2 = (bf16[24,1920]{1,0:T(8,128)(2,1)S(1)}, bf16[24,1920]{1,0:T(8,128)(2,1)S(1)}, u32[]{:S(2)}, u32[]{:S(2)}) collective-permute-start(bf16[24,1920]{1,0:T(8,128)(2,1)S(1)} %pad_maximum_fusion.8), channel_id=1, source_target_pairs={{0,24},{1,25},{2,26},{3,27},{4,28},{5,29},{6,30},{7,31},{8,16},{9,... | collective-permute-start | bytes 276488 | tf_op jit(solution)/shard_map/ppermute | solution.py:741
  10.2 6.6 %collective-permute-start.3 = (bf16[2,16,768]{2,1,0:T(8,128)(2,1)S(1)}, bf16[2,16,768]{2,1,0:T(8,128)(2,1)S(1)}, u32[]{:S(2)}, u32[]{:S(2)}) collective-permute-start(bf16[2,16,768]{2,1,0:T(8,128)(2,1)S(1)} %slice.126), channel_id=1, source_target_pairs={{0,1},{1,2},{2,3},{4,5},{5,6},{6,7},{8,9},{9,10},{10,11},{12,13},{... | collective-permute-start | bytes 147464 | tf_op jit(solution)/shard_map/ppermute | solution.py:867
  16.8 8.3 %collective-permute-start.4 = (bf16[2,24,1536]{2,1,0:T(8,128)(2,1)S(1)}, bf16[2,24,1536]{2,1,0:T(8,128)(2,1)S(1)}, u32[]{:S(2)}, u32[]{:S(2)}) collective-permute-start(bf16[2,24,1536]{2,1,0:T(8,128)(2,1)S(1)} %pad_maximum_fusion.5), channel_id=1, source_target_pairs={{0,8},{1,9},{2,10},{3,11},{4,12},{5,13},{6,14},{7,15},{8,0},{9,1},... | collective-permute-start | bytes 442376 | tf_op jit(solution)/shard_map/ppermute | solution.py:741
  18.5 14.0 %collective-permute-start.5 = (bf16[2,24,1536]{2,1,0:T(8,128)(2,1)S(1)}, bf16[2,24,1536]{2,1,0:T(8,128)(2,1)S(1)}, u32[]{:S(2)}, u32[]{:S(2)}) collective-permute-start(bf16[2,24,1536]{2,1,0:T(8,128)(2,1)S(1)} %pad_maximum_fusion.5), channel_id=1, source_target_pairs={{0,16},{1,17},{2,18},{3,19},{4,20},{5,21},{6,22},{7,23},{8,24},{9,... | collective-permute-start | bytes 442376 | tf_op jit(solution)/shard_map/ppermute | solution.py:741
  19.9 12.5 %collective-permute-start.6 = (bf16[2,24,1536]{2,1,0:T(8,128)(2,1)S(1)}, bf16[2,24,1536]{2,1,0:T(8,128)(2,1)S(1)}, u32[]{:S(2)}, u32[]{:S(2)}) collective-permute-start(bf16[2,24,1536]{2,1,0:T(8,128)(2,1)S(1)} %pad_maximum_fusion.5), channel_id=1, source_target_pairs={{0,24},{1,25},{2,26},{3,27},{4,28},{5,29},{6,30},{7,31},{8,16},{9,... | collective-permute-start | bytes 442376 | tf_op jit(solution)/shard_map/ppermute | solution.py:741
  21.3 11.5 %collective-permute-start.7 = (bf16[4,24,1920]{2,1,0:T(8,128)(2,1)S(1)}, bf16[4,24,1920]{2,1,0:T(8,128)(2,1)S(1)}, u32[]{:S(2)}, u32[]{:S(2)}) collective-permute-start(bf16[4,24,1920]{2,1,0:T(8,128)(2,1)S(1)} %pad_maximum_fusion.3), channel_id=1, source_target_pairs={{0,2},{1,3},{2,0},{3,1},{4,6},{5,7},{6,4},{7,5},{8,10},{9,11},{10,... | collective-permute-start | bytes 1105928 | tf_op jit(solution)/shard_map/ppermute | solution.py:741
  22.8 10.0 %collective-permute-start.8 = (bf16[4,24,1920]{2,1,0:T(8,128)(2,1)S(1)}, bf16[4,24,1920]{2,1,0:T(8,128)(2,1)S(1)}, u32[]{:S(2)}, u32[]{:S(2)}) collective-permute-start(bf16[4,24,1920]{2,1,0:T(8,128)(2,1)S(1)} %pad_maximum_fusion.3), channel_id=1, source_target_pairs={{0,4},{1,5},{2,6},{3,7},{4,0},{5,1},{6,2},{7,3},{8,12},{9,13},{10,... | collective-permute-start | bytes 1105928 | tf_op jit(solution)/shard_map/ppermute | solution.py:741
  25.1 14.9 %collective-permute-start.9 = (bf16[4,24,1920]{2,1,0:T(8,128)(2,1)S(1)}, bf16[4,24,1920]{2,1,0:T(8,128)(2,1)S(1)}, u32[]{:S(2)}, u32[]{:S(2)}) collective-permute-start(bf16[4,24,1920]{2,1,0:T(8,128)(2,1)S(1)} %pad_maximum_fusion.3), channel_id=1, source_target_pairs={{0,6},{1,7},{2,4},{3,5},{4,2},{5,3},{6,0},{7,1},{8,14},{9,15},{10,... | collective-permute-start | bytes 1105928 | tf_op jit(solution)/shard_map/ppermute | solution.py:741
  40.2 6.4 %collective-permute-start.10 = (bf16[4,4,24,1920]{3,2,1,0:T(8,128)(2,1)S(1)}, bf16[4,4,24,1920]{3,2,1,0:T(8,128)(2,1)}, u32[]{:S(2)}, u32[]{:S(2)}) collective-permute-start(bf16[4,4,24,1920]{3,2,1,0:T(8,128)(2,1)S(1)} %pad_maximum_fusion.1), channel_id=1, source_target_pairs={{0,1},{1,0},{2,3},{3,2},{4,5},{5,4},{6,7},{7,6},{8,9},{9,8},{10,11... | collective-permute-start | bytes 4423688 | tf_op jit(solution)/shard_map/ppermute | solution.py:741
  41.2 25.2 %collective-permute-start.11 = (bf16[4,2,24,1536]{3,2,1,0:T(8,128)(2,1)S(1)}, bf16[4,2,24,1536]{3,2,1,0:T(8,128)(2,1)S(1)}, u32[]{:S(2)}, u32[]{:S(2)}) collective-permute-start(bf16[4,2,24,1536]{3,2,1,0:T(8,128)(2,1)S(1)} %pad_maximum_fusion.2), channel_id=1, source_target_pairs={{0,2},{1,3},{2,0},{3,1},{4,6},{5,7},{6,4},{7,5},{8,10},{9,11},{10,... | collective-permute-start | bytes 1769480 | tf_op jit(solution)/shard_map/ppermute | solution.py:741
  42.1 28.0 %collective-permute-start.12 = (bf16[4,2,24,1536]{3,2,1,0:T(8,128)(2,1)S(1)}, bf16[4,2,24,1536]{3,2,1,0:T(8,128)(2,1)S(1)}, u32[]{:S(2)}, u32[]{:S(2)}) collective-permute-start(bf16[4,2,24,1536]{3,2,1,0:T(8,128)(2,1)S(1)} %pad_maximum_fusion.2), channel_id=1, source_target_pairs={{0,4},{1,5},{2,6},{3,7},{4,0},{5,1},{6,2},{7,3},{8,12},{9,13},{10,... | collective-permute-start | bytes 1769480 | tf_op jit(solution)/shard_map/ppermute | solution.py:741
  43.6 26.5 %collective-permute-start.13 = (bf16[4,2,24,1536]{3,2,1,0:T(8,128)(2,1)S(1)}, bf16[4,2,24,1536]{3,2,1,0:T(8,128)(2,1)S(1)}, u32[]{:S(2)}, u32[]{:S(2)}) collective-permute-start(bf16[4,2,24,1536]{3,2,1,0:T(8,128)(2,1)S(1)} %pad_maximum_fusion.2), channel_id=1, source_target_pairs={{0,6},{1,7},{2,4},{3,5},{4,2},{5,3},{6,0},{7,1},{8,14},{9,15},{10,... | collective-permute-start | bytes 1769480 | tf_op jit(solution)/shard_map/ppermute | solution.py:741
  70.4 11.6 %collective-permute-start.16 = (bf16[4,4,2,24,1536]{4,3,2,1,0:T(8,128)(2,1)S(1)}, bf16[4,4,2,24,1536]{4,3,2,1,0:T(8,128)(2,1)}, u32[]{:S(2)}, u32[]{:S(2)}) collective-permute-start(bf16[4,4,2,24,1536]{4,3,2,1,0:T(8,128)(2,1)S(1)} %pad_maximum_fusion), channel_id=1, source_target_pairs={{0,1},{1,0},{2,3},{3,2},{4,5},{5,4},{6,7},{7,6},{8,9},{9,8},{10,11... | collective-permute-start | bytes 7077896 | tf_op jit(solution)/shard_map/ppermute | solution.py:741
  71.2 9.8 %collective-permute-start.14 = (bf16[2,128,1536]{2,1,0:T(8,128)(2,1)S(1)}, bf16[2,128,1536]{2,1,0:T(8,128)(2,1)S(1)}, u32[]{:S(2)}, u32[]{:S(2)}) collective-permute-start(bf16[2,128,1536]{2,1,0:T(8,128)(2,1)S(1)} %copy-done.28), channel_id=1, source_target_pairs={{0,1},{4,5},{8,9},{12,13},{16,17},{20,21},{24,25},{28,29}} | collective-permute-start | bytes 2359304 | tf_op jit(solution)/shard_map/ppermute | solution.py:819
  81.2 11.1 %collective-permute-start.15 = (bf16[2,128,1536]{2,1,0:T(8,128)(2,1)S(1)}, bf16[2,128,1536]{2,1,0:T(8,128)(2,1)S(1)}, u32[]{:S(2)}, u32[]{:S(2)}) collective-permute-start(bf16[2,128,1536]{2,1,0:T(8,128)(2,1)S(1)} %fusion.1), channel_id=1, source_target_pairs={{1,2},{5,6},{9,10},{13,14},{17,18},{21,22},{25,26},{29,30}} | collective-permute-start | bytes 2359304 | tf_op jit(solution)/shard_map/ppermute | solution.py:819
  93.3 0.9 collective-permute-start.17
  115.9 14.4 %collective-permute-start.19 = (bf16[2,128,1536]{2,1,0:T(8,128)(2,1)}, bf16[2,128,1536]{2,1,0:T(8,128)(2,1)S(1)}, u32[]{:S(2)}, u32[]{:S(2)}) collective-permute-start(bf16[2,128,1536]{2,1,0:T(8,128)(2,1)} %get-tuple-element.144), channel_id=1, source_target_pairs={{3,2},{7,6},{11,10},{15,14},{19,18},{23,22},{27,26},{31,30}} | collective-permute-start | bytes 2359304 | tf_op jit(solution)/shard_map/ppermute | solution.py:819
  116.7 13.6 %copy-start.22 = (f32[2,1,1536]{2,1,0:T(1,128)S(1)}, f32[2,1,1536]{2,1,0:T(1,128)}, u32[]{:S(2)}) copy-start(f32[2,1,1536]{2,1,0:T(1,128)} %get-tuple-element.161) | copy-start | bytes 36868
  116.7 13.7 %copy-start.11 = (f32[2,128,1536]{2,1,0:T(8,128)S(1)}, f32[2,128,1536]{2,1,0:T(8,128)}, u32[]{:S(2)}) copy-start(f32[2,128,1536]{2,1,0:T(8,128)} %get-tuple-element.162) | copy-start | bytes 4718596
  128.7 21.4 %collective-permute-start.18 = (bf16[16,2,24,1536]{3,2,1,0:T(8,128)(2,1)}, bf16[16,2,24,1536]{3,2,1,0:T(8,128)(2,1)S(1)}, u32[]{:S(2)}, u32[]{:S(2)}) collective-permute-start(bf16[16,2,24,1536]{3,2,1,0:T(8,128)(2,1)} %get-tuple-element.143), channel_id=1, source_target_pairs={{0,1},{1,0},{2,3},{3,2},{4,5},{5,4},{6,7},{7,6},{8,9},{9,8},{10,11... | collective-permute-start | bytes 7077896 | tf_op jit(solution)/shard_map/ppermute | solution.py:741
  130.3 17.1 %copy-start.8 = (bf16[2,128,1536]{2,1,0:T(8,128)(2,1)}, bf16[2,128,1536]{2,1,0:T(8,128)(2,1)S(1)}, u32[]{:S(2)}) copy-start(bf16[2,128,1536]{2,1,0:T(8,128)(2,1)S(1)} %collective-permute-done.19.refs_0_) | copy-start | bytes 2359300
  130.7 16.7 %collective-permute-start.23 = (bf16[2,128,1536]{2,1,0:T(8,128)(2,1)S(1)}, bf16[2,128,1536]{2,1,0:T(8,128)(2,1)S(1)}, u32[]{:S(2)}, u32[]{:S(2)}) collective-permute-start(bf16[2,128,1536]{2,1,0:T(8,128)(2,1)S(1)} %fusion.6), channel_id=1, source_target_pairs={{2,1},{6,5},{10,9},{14,13},{18,17},{22,21},{26,25},{30,29}} | collective-permute-start | bytes 2359304 | tf_op jit(solution)/shard_map/ppermute | solution.py:819
  148.4 8.7 %collective-permute-start.24 = (bf16[2,128,1536]{2,1,0:T(8,128)(2,1)S(1)}, bf16[2,128,1536]{2,1,0:T(8,128)(2,1)S(1)}, u32[]{:S(2)}, u32[]{:S(2)}) collective-permute-start(bf16[2,128,1536]{2,1,0:T(8,128)(2,1)S(1)} %fusion.9), channel_id=1, source_target_pairs={{1,0},{5,4},{9,8},{13,12},{17,16},{21,20},{25,24},{29,28}} | collective-permute-start | bytes 2359304 | tf_op jit(solution)/shard_map/ppermute | solution.py:819
  151.2 26.8 %collective-permute-start.20 = (bf16[4,2,24,1536]{3,2,1,0:T(8,128)(2,1)S(1)}, bf16[4,2,24,1536]{3,2,1,0:T(8,128)(2,1)S(1)}, u32[]{:S(2)}, u32[]{:S(2)}) collective-permute-start(bf16[4,2,24,1536]{3,2,1,0:T(8,128)(2,1)S(1)} %get-tuple-element.213), channel_id=1, source_target_pairs={{0,2},{1,3},{2,0},{3,1},{4,6},{5,7},{6,4},{7,5},{8,10},{9,11},{10,... | collective-permute-start | bytes 1769480 | tf_op jit(solution)/shard_map/ppermute | solution.py:741
  155.6 27.6 %collective-permute-start.21 = (bf16[4,2,24,1536]{3,2,1,0:T(8,128)(2,1)S(1)}, bf16[4,2,24,1536]{3,2,1,0:T(8,128)(2,1)S(1)}, u32[]{:S(2)}, u32[]{:S(2)}) collective-permute-start(bf16[4,2,24,1536]{3,2,1,0:T(8,128)(2,1)S(1)} %get-tuple-element.212), channel_id=1, source_target_pairs={{0,4},{1,5},{2,6},{3,7},{4,0},{5,1},{6,2},{7,3},{8,12},{9,13},{10,... | collective-permute-start | bytes 1769480 | tf_op jit(solution)/shard_map/ppermute | solution.py:741
  156.2 27.0 %collective-permute-start.22 = (bf16[4,2,24,1536]{3,2,1,0:T(8,128)(2,1)S(1)}, bf16[4,2,24,1536]{3,2,1,0:T(8,128)(2,1)S(1)}, u32[]{:S(2)}, u32[]{:S(2)}) collective-permute-start(bf16[4,2,24,1536]{3,2,1,0:T(8,128)(2,1)S(1)} %get-tuple-element.211), channel_id=1, source_target_pairs={{0,6},{1,7},{2,4},{3,5},{4,2},{5,3},{6,0},{7,1},{8,14},{9,15},{10,... | collective-permute-start | bytes 1769480 | tf_op jit(solution)/shard_map/ppermute | solution.py:741
  176.6 6.9 %collective-permute-start.25 = (bf16[2,8,1920]{2,1,0:T(8,128)(2,1)}, bf16[2,8,1920]{2,1,0:T(8,128)(2,1)S(1)}, u32[]{:S(2)}, u32[]{:S(2)}) collective-permute-start(bf16[2,8,1920]{2,1,0:T(8,128)(2,1)} %get-tuple-element.177), channel_id=1, source_target_pairs={{1,0},{2,1},{3,2},{5,4},{6,5},{7,6},{9,8},{10,9},{11,10},{13,12},{... | collective-permute-start | bytes 184328 | tf_op jit(solution)/shard_map/ppermute | solution.py:1206
  195.0 6.4 %collective-permute-start.26 = (bf16[16,24,1920]{2,1,0:T(8,128)(2,1)}, bf16[16,24,1920]{2,1,0:T(8,128)(2,1)S(1)}, u32[]{:S(2)}, u32[]{:S(2)}) collective-permute-start(bf16[16,24,1920]{2,1,0:T(8,128)(2,1)} %get-tuple-element.183), channel_id=1, source_target_pairs={{0,1},{1,0},{2,3},{3,2},{4,5},{5,4},{6,7},{7,6},{8,9},{9,8},{10,11... | collective-permute-start | bytes 4423688 | tf_op jit(solution)/shard_map/ppermute | solution.py:741
  195.1 10.4 %collective-permute-start.27 = (f32[96,128]{1,0:T(8,128)}, f32[96,128]{1,0:T(8,128)S(1)}, u32[]{:S(2)}, u32[]{:S(2)}) collective-permute-start(f32[96,128]{1,0:T(8,128)} %get-tuple-element.189), channel_id=1, source_target_pairs={{0,1},{1,0},{2,3},{3,2},{4,5},{5,4},{6,7},{7,6},{8,9},{9,8},{10,11... | collective-permute-start | bytes 147464 | tf_op jit(solution)/shard_map/ppermute | solution.py:741
  201.8 17.3 %collective-permute-start.28 = (bf16[4,24,1920]{2,1,0:T(8,128)(2,1)S(1)}, bf16[4,24,1920]{2,1,0:T(8,128)(2,1)S(1)}, u32[]{:S(2)}, u32[]{:S(2)}) collective-permute-start(bf16[4,24,1920]{2,1,0:T(8,128)(2,1)S(1)} %get-tuple-element.216), channel_id=1, source_target_pairs={{0,2},{1,3},{2,0},{3,1},{4,6},{5,7},{6,4},{7,5},{8,10},{9,11},{10,... | collective-permute-start | bytes 1105928 | tf_op jit(solution)/shard_map/ppermute | solution.py:741
  202.2 17.2 %collective-permute-start.29 = (bf16[4,24,1920]{2,1,0:T(8,128)(2,1)S(1)}, bf16[4,24,1920]{2,1,0:T(8,128)(2,1)S(1)}, u32[]{:S(2)}, u32[]{:S(2)}) collective-permute-start(bf16[4,24,1920]{2,1,0:T(8,128)(2,1)S(1)} %get-tuple-element.215), channel_id=1, source_target_pairs={{0,4},{1,5},{2,6},{3,7},{4,0},{5,1},{6,2},{7,3},{8,12},{9,13},{10,... | collective-permute-start | bytes 1105928 | tf_op jit(solution)/shard_map/ppermute | solution.py:741
  203.6 16.8 %collective-permute-start.30 = (bf16[4,24,1920]{2,1,0:T(8,128)(2,1)S(1)}, bf16[4,24,1920]{2,1,0:T(8,128)(2,1)S(1)}, u32[]{:S(2)}, u32[]{:S(2)}) collective-permute-start(bf16[4,24,1920]{2,1,0:T(8,128)(2,1)S(1)} %get-tuple-element.214), channel_id=1, source_target_pairs={{0,6},{1,7},{2,4},{3,5},{4,2},{5,3},{6,0},{7,1},{8,14},{9,15},{10,... | collective-permute-start | bytes 1105928 | tf_op jit(solution)/shard_map/ppermute | solution.py:741
  205.5 17.5 %collective-permute-start.34 = (bf16[2,24,1536]{2,1,0:T(8,128)(2,1)S(1)}, bf16[2,24,1536]{2,1,0:T(8,128)(2,1)S(1)}, u32[]{:S(2)}, u32[]{:S(2)}) collective-permute-start(bf16[2,24,1536]{2,1,0:T(8,128)(2,1)S(1)} %get-tuple-element.196), channel_id=1, source_target_pairs={{0,8},{1,9},{2,10},{3,11},{4,12},{5,13},{6,14},{7,15},{8,0},{9,1},... | collective-permute-start | bytes 442376 | tf_op jit(solution)/shard_map/ppermute | solution.py:741
  206.1 17.5 %collective-permute-start.35 = (bf16[2,24,1536]{2,1,0:T(8,128)(2,1)S(1)}, bf16[2,24,1536]{2,1,0:T(8,128)(2,1)S(1)}, u32[]{:S(2)}, u32[]{:S(2)}) collective-permute-start(bf16[2,24,1536]{2,1,0:T(8,128)(2,1)S(1)} %get-tuple-element.197), channel_id=1, source_target_pairs={{0,16},{1,17},{2,18},{3,19},{4,20},{5,21},{6,22},{7,23},{8,24},{9,... | collective-permute-start | bytes 442376 | tf_op jit(solution)/shard_map/ppermute | solution.py:741
  219.1 7.9 %collective-permute-start.36 = (bf16[2,24,1536]{2,1,0:T(8,128)(2,1)S(1)}, bf16[2,24,1536]{2,1,0:T(8,128)(2,1)S(1)}, u32[]{:S(2)}, u32[]{:S(2)}) collective-permute-start(bf16[2,24,1536]{2,1,0:T(8,128)(2,1)S(1)} %get-tuple-element.198), channel_id=1, source_target_pairs={{0,24},{1,25},{2,26},{3,27},{4,28},{5,29},{6,30},{7,31},{8,16},{9,... | collective-permute-start | bytes 442376 | tf_op jit(solution)/shard_map/ppermute | solution.py:741
  220.7 13.1 %collective-permute-start.40 = (bf16[24,1920]{1,0:T(8,128)(2,1)S(1)}, bf16[24,1920]{1,0:T(8,128)(2,1)S(1)}, u32[]{:S(2)}, u32[]{:S(2)}) collective-permute-start(bf16[24,1920]{1,0:T(8,128)(2,1)S(1)} %get-tuple-element.222), channel_id=1, source_target_pairs={{0,8},{1,9},{2,10},{3,11},{4,12},{5,13},{6,14},{7,15},{8,0},{9,1},... | collective-permute-start | bytes 276488 | tf_op jit(solution)/shard_map/ppermute | solution.py:741
  221.3 8.0 %collective-permute-start.31 = (f32[96,128]{1,0:T(8,128)S(1)}, f32[96,128]{1,0:T(8,128)S(1)}, u32[]{:S(2)}, u32[]{:S(2)}) collective-permute-start(f32[96,128]{1,0:T(8,128)S(1)} %add.114), channel_id=1, source_target_pairs={{0,2},{1,3},{2,0},{3,1},{4,6},{5,7},{6,4},{7,5},{8,10},{9,11},{10,... | collective-permute-start | bytes 147464 | tf_op jit(solution)/shard_map/ppermute | solution.py:741
  223.0 7.1 %collective-permute-start.32 = (f32[96,128]{1,0:T(8,128)S(1)}, f32[96,128]{1,0:T(8,128)S(1)}, u32[]{:S(2)}, u32[]{:S(2)}) collective-permute-start(f32[96,128]{1,0:T(8,128)S(1)} %add.114), channel_id=1, source_target_pairs={{0,4},{1,5},{2,6},{3,7},{4,0},{5,1},{6,2},{7,3},{8,12},{9,13},{10,... | collective-permute-start | bytes 147464 | tf_op jit(solution)/shard_map/ppermute | solution.py:741
  223.6 6.4 %collective-permute-start.33 = (f32[96,128]{1,0:T(8,128)S(1)}, f32[96,128]{1,0:T(8,128)S(1)}, u32[]{:S(2)}, u32[]{:S(2)}) collective-permute-start(f32[96,128]{1,0:T(8,128)S(1)} %add.114), channel_id=1, source_target_pairs={{0,6},{1,7},{2,4},{3,5},{4,2},{5,3},{6,0},{7,1},{8,14},{9,15},{10,... | collective-permute-start | bytes 147464 | tf_op jit(solution)/shard_map/ppermute | solution.py:741
  227.1 14.4 %copy-start.23 = (f32[48]{0:T(128)S(1)}, f32[48]{0:T(128)}, u32[]{:S(2)}) copy-start(f32[48]{0:T(128)} %param.26) | copy-start | bytes 580
  227.2 15.0 %copy-start.27 = (f32[24]{0:T(128)S(1)}, f32[24]{0:T(128)}, u32[]{:S(2)}) copy-start(f32[24]{0:T(128)} %param.19) | copy-start | bytes 292
  227.2 10.2 %collective-permute-start.41 = (bf16[24,1920]{1,0:T(8,128)(2,1)S(1)}, bf16[24,1920]{1,0:T(8,128)(2,1)S(1)}, u32[]{:S(2)}, u32[]{:S(2)}) collective-permute-start(bf16[24,1920]{1,0:T(8,128)(2,1)S(1)} %get-tuple-element.220), channel_id=1, source_target_pairs={{0,16},{1,17},{2,18},{3,19},{4,20},{5,21},{6,22},{7,23},{8,24},{9,... | collective-permute-start | bytes 276488 | tf_op jit(solution)/shard_map/ppermute | solution.py:741
  229.3 8.1 %collective-permute-start.42 = (bf16[24,1920]{1,0:T(8,128)(2,1)S(1)}, bf16[24,1920]{1,0:T(8,128)(2,1)S(1)}, u32[]{:S(2)}, u32[]{:S(2)}) collective-permute-start(bf16[24,1920]{1,0:T(8,128)(2,1)S(1)} %get-tuple-element.221), channel_id=1, source_target_pairs={{0,24},{1,25},{2,26},{3,27},{4,28},{5,29},{6,30},{7,31},{8,16},{9,... | collective-permute-start | bytes 276488 | tf_op jit(solution)/shard_map/ppermute | solution.py:741
  230.1 8.1 %collective-permute-start.37 = (f32[96,128]{1,0:T(8,128)S(1)}, f32[96,128]{1,0:T(8,128)S(1)}, u32[]{:S(2)}, u32[]{:S(2)}) collective-permute-start(f32[96,128]{1,0:T(8,128)S(1)} %add_add_fusion.2), channel_id=1, source_target_pairs={{0,8},{1,9},{2,10},{3,11},{4,12},{5,13},{6,14},{7,15},{8,0},{9,1},... | collective-permute-start | bytes 147464 | tf_op jit(solution)/shard_map/ppermute | solution.py:741
  231.5 7.5 %collective-permute-start.38 = (f32[96,128]{1,0:T(8,128)S(1)}, f32[96,128]{1,0:T(8,128)S(1)}, u32[]{:S(2)}, u32[]{:S(2)}) collective-permute-start(f32[96,128]{1,0:T(8,128)S(1)} %add_add_fusion.2), channel_id=1, source_target_pairs={{0,16},{1,17},{2,18},{3,19},{4,20},{5,21},{6,22},{7,23},{8,24},{9,... | collective-permute-start | bytes 147464 | tf_op jit(solution)/shard_map/ppermute | solution.py:741
  233.7 6.0 %collective-permute-start.39 = (f32[96,128]{1,0:T(8,128)S(1)}, f32[96,128]{1,0:T(8,128)S(1)}, u32[]{:S(2)}, u32[]{:S(2)}) collective-permute-start(f32[96,128]{1,0:T(8,128)S(1)} %add_add_fusion.2), channel_id=1, source_target_pairs={{0,24},{1,25},{2,26},{3,27},{4,28},{5,29},{6,30},{7,31},{8,16},{9,... | collective-permute-start | bytes 147464 | tf_op jit(solution)/shard_map/ppermute | solution.py:741
  (26 other events, 115.9 us)
